TPU v7x, 128 devices: a whole 4x4x4 slice. The times are simulated.
128 devices in a mesh: tm: 2 (over core), space: 64 (over x, y, z).
Axes of the slice: x: 4, y: 4, z: 4, core: 2. Of those that a mesh axis runs over, the one named last changes fastest.
Arguments:
- winds: bfloat16 [4, 64, 2, 3, 384, 128], P('tm', 'space'), may hold values from -0.44921875 to 0.44921875
- mixing: float32 [128, 128], replicated, may hold values from -0.5 to 0.5
- innovations: float32 [2, 64, 64, 8, 384], P('tm', 'space'), may hold values from -6 to 6
- obs_weight: float32 [2, 64, 64, 8, 384], P('tm', 'space'), may hold values from 0.3 to 3
- obs_sub: int32 [2, 64, 64, 8], P('tm', 'space'), may hold values from 0 to 1
- obs_col: int32 [2, 64, 64, 8], P('tm', 'space'), may hold values from 0 to 1151
- obs_count: int32 [2, 64, 64], P('tm', 'space'), may hold values from 1 to 8, as said below
Outputs:
- increment: float32 [4, 64, 3, 3, 384, 128], P('tm', 'space')
- residual: float32 [4, 64, 3, 3, 384, 128], P('tm', 'space')
Inputs may be any that keep to these rules, and one draw needn't show every extreme that they name: `obs_count`: slots at or above the count are empty; in every draw some owner of each group receives 8 live slots from every observer.
All inputs are finite; a program needn't handle non-finite values.
Results may differ from a plain program's by a relative error of at most 0.022.
Values sent between devices are 32-bit elements; how exact they have to be, the bound alone decides.
No kernel may reach another device: no remote copies, remote signals or barrier semaphores. Data moves between devices by JAX's collectives and lax.ppermute only.
A program may use at most 128 MiB of HBM per device.

v0:
```python
import jax
import jax.numpy as jnp
from jax import lax
from jax.sharding import PartitionSpec as P

FIELDS = 3
ITERS = 2


MIXC = 0.25
SCALE_B = 1.0
SCALE_Q = 0.5


def shifted(value, axis, steps):
    count = lax.axis_size(axis)
    initial, last = (max(0, -steps), min(count, count - steps))
    return lax.ppermute(value, axis, [(source, source + steps) for source in range(initial, last)])


def moved(padded, wind_pair, mixing):
    values = padded[:, 1:-1, 1:-1]
    zonal_courant = wind_pair[0:1].astype(jnp.float32)
    merid_courant = wind_pair[1:2].astype(jnp.float32)
    westward = padded[:, 1:-1, :-2]
    eastward = padded[:, 1:-1, 2:]
    southern = padded[:, :-2, 1:-1]
    northern = padded[:, 2:, 1:-1]
    result = values - jnp.maximum(zonal_courant, 0.0) * (values - westward)
    result = result - jnp.maximum(-zonal_courant, 0.0) * (values - eastward)
    result = result - jnp.maximum(merid_courant, 0.0) * (values - southern)
    result = result - jnp.maximum(-merid_courant, 0.0) * (values - northern)
    return result + MIXC * jnp.einsum(
        "aijl,kl->aijk", result, mixing, precision=lax.Precision.HIGHEST
    )


def step_forward(state, wind_pair, mixing):
    middle = jnp.concatenate([state[:, :, -1:], state, state[:, :, :1]], axis=2)
    south_row = shifted(state[:, -1:], "space", 1)
    north_row = shifted(state[:, :1], "space", -1)
    corner = jnp.zeros((state.shape[0], 1, 1, state.shape[3]), jnp.float32)
    south_full = jnp.concatenate([corner, south_row, corner], axis=2)
    north_full = jnp.concatenate([corner, north_row, corner], axis=2)
    padded = jnp.concatenate([south_full, middle, north_full], axis=1)
    return moved(padded, wind_pair, mixing)


def step_adjoint(cotangent, wind_pair, mixing):
    fields, rows_here, cols_here, levels = cotangent.shape
    blank_pad = jnp.zeros((fields, rows_here + 2, cols_here + 2, levels), jnp.float32)

    def local_step(padded):
        return moved(padded, wind_pair, mixing)

    _, pull_back = jax.vjp(local_step, blank_pad)
    spread_pad = pull_back(cotangent)[0]
    inner = spread_pad[:, 1:-1, 1:-1]
    south_pad = spread_pad[:, :1, 1:-1]
    north_pad = spread_pad[:, -1:, 1:-1]
    west_pad = spread_pad[:, 1:-1, :1]
    east_pad = spread_pad[:, 1:-1, -1:]
    from_south = shifted(north_pad, "space", 1)
    from_north = shifted(south_pad, "space", -1)
    inner = inner.at[:, :1].add(from_south)
    inner = inner.at[:, -1:].add(from_north)
    inner = inner.at[:, :, -1:].add(west_pad)
    return inner.at[:, :, :1].add(east_pad)


def window_scale(group_pos, count_sub, window):
    global_pos = group_pos * count_sub + window
    return jnp.where(global_pos == 0, SCALE_B, SCALE_Q)


def forward_local(control, winds, mixing, group_pos):
    count_sub = control.shape[0]
    states = []
    current = jnp.zeros(control.shape[1:], jnp.float32)
    for window in range(count_sub):
        weight_now = window_scale(group_pos, count_sub, window)
        current = step_forward(current + weight_now * control[window], winds[window], mixing)
        states.append(current)
    carried = states[-1]
    carried = shifted(carried, "tm", 1)
    for window in range(count_sub):
        carried = step_forward(carried, winds[window], mixing)
        states[window] = states[window] + carried
    return jnp.stack(states)


def adjoint_local(forcing, winds, mixing, group_pos):
    count_sub = forcing.shape[0]
    results = [None] * count_sub
    carried = jnp.zeros(forcing.shape[1:], jnp.float32)
    for window in reversed(range(count_sub)):
        carried = step_adjoint(forcing[window] + carried, winds[window], mixing)
        results[window] = carried
    carried = results[0]
    carried = shifted(carried, "tm", -1)
    for window in reversed(range(count_sub)):
        carried = step_adjoint(carried, winds[window], mixing)
        results[window] = results[window] + carried
    scaled = [
        window_scale(group_pos, count_sub, window) * results[window] for window in range(count_sub)
    ]
    return jnp.stack(scaled)


def residual_norm(vector):
    return lax.psum(jnp.sum(vector * vector), ("tm", "space"))


def per_device(winds, mixing, innovations, obs_weight, obs_sub, obs_col, obs_count):
    group_pos = lax.axis_index("tm")
    owners = obs_sub.shape[2]
    per_pair = obs_sub.shape[3]
    levels = mixing.shape[0]
    winds_mine = winds[:, 0]
    tile_rows = winds.shape[3]
    tile_cols = winds.shape[4]
    state_shape = (winds.shape[0], FIELDS, tile_rows, tile_cols, levels)
    sub_mine = obs_sub.reshape(owners, per_pair)
    col_mine = obs_col.reshape(owners, per_pair)
    count_mine = obs_count.reshape(owners)
    live_slot = jnp.arange(per_pair, dtype=jnp.int32)[None, :] < count_mine[:, None]
    weights_mine = jnp.where(live_slot[..., None], obs_weight.reshape(owners, per_pair, -1), 0.0)
    innov_mine = innovations.reshape(owners, per_pair, -1)
    sub_owned, col_owned = (
        lax.all_to_all(sub_mine, "space", split_axis=0, concat_axis=0, tiled=True),
        lax.all_to_all(col_mine, "space", split_axis=0, concat_axis=0, tiled=True),
    )
    lat_owned = col_owned // tile_cols
    lon_owned = col_owned % tile_cols

    def spread_profiles(profiles):
        shaped = profiles.reshape(owners, per_pair, FIELDS, levels)
        return (
            jnp.zeros(state_shape, jnp.float32)
            .at[sub_owned, :, lat_owned, lon_owned, :]
            .add(shaped)
        )

    def send_back(profiles):
        return lax.all_to_all(profiles, "space", split_axis=0, concat_axis=0, tiled=True)

    start_forcing = spread_profiles(send_back(weights_mine * innov_mine))
    gradient = adjoint_local(start_forcing, winds_mine, mixing, group_pos)
    increment = jnp.zeros(state_shape, jnp.float32)
    residual = gradient
    direction = gradient
    norm_now = residual_norm(residual)
    for step_num in range(ITERS):
        hessian_states = forward_local(direction, winds_mine, mixing, group_pos)
        seen = lax.all_to_all(
            hessian_states[sub_owned, :, lat_owned, lon_owned, :].reshape(owners, per_pair, -1),
            "space",
            split_axis=0,
            concat_axis=0,
            tiled=True,
        )
        image_vec = direction + adjoint_local(
            spread_profiles(send_back(weights_mine * seen)), winds_mine, mixing, group_pos
        )
        step_size = norm_now / lax.psum(jnp.sum(direction * image_vec), ("tm", "space"))
        increment = increment + step_size * direction
        residual = residual - step_size * image_vec
        norm_next = residual_norm(residual)
        direction = residual + norm_next / norm_now * direction
        norm_now = norm_next
    return (increment[:, None], residual[:, None])


def solution(mesh):
    in_specs = (
        P("tm", "space", None, None, None, None),
        P(),
        P("tm", "space", None, None, None),
        P("tm", "space", None, None, None),
        P("tm", "space", None, None),
        P("tm", "space", None, None),
        P("tm", "space", None),
    )
    out_specs = (P("tm", "space", None, None, None, None), P("tm", "space", None, None, None, None))
    return jax.shard_map(
        per_device, mesh=mesh, in_specs=in_specs, out_specs=out_specs, check_vma=False
    )
```

profile of v0, /device:TPU:1, one launch (start us, length us, event | category | flops | bytes accessed | tf_op | source)
XLA Modules:
  0.0 1228.6 jit_solution(12332198214788693122)
XLA Ops:
  2.1 12.0 all-to-all-start
  16.2 6.2 all-to-all-done
  29.4 5.9 all-to-all-done.1
  43.8 9.5 all-to-all-done.2
  58.4 52.7 %scatter_fusion = f32[2,3,3,384,128]{4,1,3,2,0:T(4,128)} fusion(f32[2,3,3,384,128]{4,1,3,2,0:T(4,128)} %broadcast.922.clone.1, s32[512]{0:T(512)S(1)} %reshape.2122, f32[512,3,128]{2,1,0:T(4,128)} %reshape.2124), kind=kCustom, calls=%fused_computation.2 | custom fusion | flops 196608 | bytes 2365440 | tf_op jit(solution)/shard_map/scatter-add | solution.py:141
  123.1 7.0 collective-permute-done
  139.1 6.0 fusion.216
  164.2 8.6 collective-permute-start.4
  187.0 10.6 collective-permute-done.5
  224.6 7.8 collective-permute-done.7
  255.5 7.8 collective-permute-done.10
  264.2 13.2 %multiply_add_fusion.8 = (f32[3,3,384,128]{3,2,1,0:T(8,128)S(1)}, f32[3,3,384,128]{3,2,1,0:T(8,128)}, f32[3,3,384,128]{3,2,1,0:T(8,128)}) fusion(f32[]{:T(128)S(6)} %select_n.94, f32[3,3,384,128]{3,2,1,0:T(8,128)} %scatter-add.186, f32[3,3,384,128]{3,2,1,0:T(8,128)} %scatter-add.200, f32[128,128]{1,0:T(8,128)S(1)} %copy-done, ...), kind=kOutput, calls=%fused_computation.280 | convolution fusion | flops 703365120 | bytes 14232068 | tf_op jit(solution)/shard_map/aijl,kl->aijk/dot_general | solution.py:33
  283.1 7.8 collective-permute-done.11
  300.8 7.1 collective-permute-done.13
  314.5 11.2 collective-permute-done.14
  325.8 7.0 collective-permute-done.15
  338.5 6.3 collective-permute-start.16
  349.5 6.5 collective-permute-done.16
  360.6 7.4 add_bitcast_fusion.2
  372.9 5.8 gather_fusion
  381.1 43.0 %all_to_all.46 = f32[64,8,384]{2,1,0:T(8,128)S(1)} all-to-all(f32[64,8,384]{2,1,0:T(8,128)} %reshape.2106), channel_id=1, replica_groups=mesh['tm'=2,'space'=64] {'space'}, dimensions={0} | all-to-all | bytes 1572864 | tf_op jit(solution)/shard_map/all_to_all | solution.py:155
  424.3 19.3 %all_to_all.47 = f32[64,8,384]{2,1,0:T(8,128)} all-to-all(f32[64,8,384]{2,1,0:T(8,128)S(1)} %fusion.275), channel_id=1, replica_groups=mesh['tm'=2,'space'=64] {'space'}, dimensions={0} | all-to-all | bytes 1572864 | tf_op jit(solution)/shard_map/all_to_all | solution.py:145
  448.6 52.5 %scatter_fusion.1 = f32[2,3,3,384,128]{4,1,3,2,0:T(4,128)} fusion(f32[2,3,3,384,128]{4,1,3,2,0:T(4,128)} %broadcast.922.clone, s32[512]{0:T(512)S(1)} %reshape.2122, f32[512,3,128]{2,1,0:T(4,128)} %reshape.2130), kind=kCustom, calls=%fused_computation.3 | custom fusion | flops 196608 | bytes 2365440 | tf_op jit(solution)/shard_map/scatter-add | solution.py:141
  514.1 8.2 collective-permute-done.18
  531.2 6.2 fusion.204
  541.3 6.6 collective-permute-done.20
  557.3 7.4 collective-permute-start.22
  580.1 10.4 collective-permute-done.23
  610.9 9.9 collective-permute-done.25
  637.3 76.4 %all-reduce.60 = (f32[]{:T(128)}, f32[]{:T(128)}) all-reduce(f32[]{:T(128)} %get-tuple-element.579, f32[]{:T(128)} %get-tuple-element.578), channel_id=1, replica_groups=mesh['tm'=2,'space'=64] {'tm','space'}, use_global_device_ids=true, to_apply=%region_2.3 | all-reduce | flops 2 | bytes 16 | tf_op jit(solution)/shard_map/psum | solution.py:111
  719.0 62.8 %psum.30 = f32[]{:T(128)} all-reduce(f32[]{:T(128)} %multiply_reduce_fusion), channel_id=1, replica_groups=mesh['tm'=2,'space'=64] {'tm','space'}, use_global_device_ids=true, to_apply=%region_7.8 | all-reduce | flops 1 | bytes 8 | tf_op jit(solution)/shard_map/psum | solution.py:111
  790.7 10.2 collective-permute-done.27
  812.7 9.4 collective-permute-done.29
  830.9 6.2 collective-permute-done.31
  843.4 11.2 collective-permute-done.32
  868.1 9.9 collective-permute-done.34
  890.3 5.8 gather_fusion.1
  898.5 33.2 %all_to_all.48 = f32[64,8,384]{2,1,0:T(8,128)S(1)} all-to-all(f32[64,8,384]{2,1,0:T(8,128)} %reshape.2108), channel_id=1, replica_groups=mesh['tm'=2,'space'=64] {'space'}, dimensions={0} | all-to-all | bytes 1572864 | tf_op jit(solution)/shard_map/all_to_all | solution.py:155
  931.9 19.7 %all_to_all.49 = f32[64,8,384]{2,1,0:T(8,128)} all-to-all(f32[64,8,384]{2,1,0:T(8,128)S(1)} %fusion.274), channel_id=1, replica_groups=mesh['tm'=2,'space'=64] {'space'}, dimensions={0} | all-to-all | bytes 1572864 | tf_op jit(solution)/shard_map/all_to_all | solution.py:145
  956.6 52.6 %scatter_fusion.2 = f32[2,3,3,384,128]{4,1,3,2,0:T(4,128)} fusion(f32[2,3,3,384,128]{4,1,3,2,0:T(4,128)} %broadcast.922, s32[512]{0:T(512)S(1)} %reshape.2122, f32[512,3,128]{2,1,0:T(4,128)} %reshape.2136), kind=kCustom, calls=%fused_computation.4 | custom fusion | flops 196608 | bytes 2365440 | tf_op jit(solution)/shard_map/scatter-add | solution.py:141
  1021.9 8.4 collective-permute-done.36
  1039.2 6.1 fusion.192
  1049.3 6.8 collective-permute-done.38
  1065.0 7.7 collective-permute-start.40
  1087.4 10.8 collective-permute-done.41
  1121.1 7.7 collective-permute-done.43
  1144.2 76.7 %psum.31 = f32[]{:T(128)} all-reduce(f32[]{:T(128)} %fusion), channel_id=1, replica_groups=mesh['tm'=2,'space'=64] {'tm','space'}, use_global_device_ids=true, to_apply=%region_10.11 | all-reduce | flops 1 | bytes 8 | tf_op jit(solution)/shard_map/psum | solution.py:165
  1222.3 6.1 fusion.4
  (492 shorter events, 423.2 us)
Async XLA Ops:
  2.1 20.3 %all-to-all-start = ((s32[64,1,8]{2,1,0:T(1,128)}), s32[64,1,8]{2,1,0:T(1,128)S(1)}, u32[]{:S(2)}, u32[]{:S(2)}) async-start(s32[64,1,8]{2,1,0:T(1,128)} %bitcast.1), calls=%async_computation | async-start | bytes 65536 | tf_op jit(solution)/shard_map/all_to_all | solution.py:130
  22.4 13.0 %all-to-all-start.1 = ((s32[64,1,8]{2,1,0:T(1,128)}), s32[64,1,8]{2,1,0:T(1,128)S(1)}, u32[]{:S(2)}, u32[]{:S(2)}) async-start(s32[64,1,8]{2,1,0:T(1,128)} %bitcast.3), calls=%async_computation.1 | async-start | bytes 65536 | tf_op jit(solution)/shard_map/all_to_all | solution.py:131
  35.4 17.9 %all-to-all-start.2 = ((f32[64,8,384]{2,1,0:T(8,128)}), f32[64,8,384]{2,1,0:T(8,128)}, u32[]{:S(2)}, u32[]{:S(2)}) async-start(f32[64,8,384]{2,1,0:T(8,128)} %bitcast_multiply_fusion), calls=%async_computation.2 | async-start | bytes 1572864 | tf_op jit(solution)/shard_map/all_to_all | solution.py:145
  119.2 10.9 collective-permute-start
  121.5 12.5 %collective-permute-start.1 = (f32[3,1,384,128]{3,2,1,0:T(8,128)S(1)}, f32[3,1,384,128]{3,2,1,0:T(8,128)S(1)}, u32[]{:S(2)}, u32[]{:S(2)}) collective-permute-start(f32[3,1,384,128]{3,2,1,0:T(8,128)S(1)} %get-tuple-element.624), channel_id=1, source_target_pairs={{1,0},{2,1},{3,2},{4,3},{5,4},{6,5},{7,6},{8,7},{9,8},{10,9},{11,1... | collective-permute-start | bytes 1769480 | tf_op jit(solution)/shard_map/ppermute | solution.py:18
  146.0 9.2 collective-permute-start.2
  148.1 11.0 collective-permute-start.3
  164.2 12.0 collective-permute-start.4
  180.9 16.7 %collective-permute-start.5 = (f32[3,1,384,128]{3,2,1,0:T(8,128)S(1)}, f32[3,1,384,128]{3,2,1,0:T(8,128)S(1)}, u32[]{:S(2)}, u32[]{:S(2)}) collective-permute-start(f32[3,1,384,128]{3,2,1,0:T(8,128)S(1)} %get-tuple-element.621), channel_id=1, source_target_pairs={{0,1},{1,2},{2,3},{3,4},{4,5},{5,6},{6,7},{7,8},{8,9},{9,10},{10,1... | collective-permute-start | bytes 1769480 | tf_op jit(solution)/shard_map/ppermute | solution.py:18
  185.3 16.5 %collective-permute-start.6 = (f32[3,1,384,128]{3,2,1,0:T(8,128)S(1)}, f32[3,1,384,128]{3,2,1,0:T(8,128)S(1)}, u32[]{:S(2)}, u32[]{:S(2)}) collective-permute-start(f32[3,1,384,128]{3,2,1,0:T(8,128)S(1)} %get-tuple-element.620), channel_id=1, source_target_pairs={{1,0},{2,1},{3,2},{4,3},{5,4},{6,5},{7,6},{8,7},{9,8},{10,9},{11,1... | collective-permute-start | bytes 1769480 | tf_op jit(solution)/shard_map/ppermute | solution.py:18
  216.8 15.6 %collective-permute-start.7 = (f32[3,1,384,128]{3,2,1,0:T(8,128)}, f32[3,1,384,128]{3,2,1,0:T(8,128)}, u32[]{:S(2)}, u32[]{:S(2)}) collective-permute-start(f32[3,1,384,128]{3,2,1,0:T(8,128)} %get-tuple-element.619), channel_id=1, source_target_pairs={{0,1},{1,2},{2,3},{3,4},{4,5},{5,6},{6,7},{7,8},{8,9},{9,10},{10,1... | collective-permute-start | bytes 1769480 | tf_op jit(solution)/shard_map/ppermute | solution.py:18
  221.5 15.5 %collective-permute-start.8 = (f32[3,1,384,128]{3,2,1,0:T(8,128)}, f32[3,1,384,128]{3,2,1,0:T(8,128)}, u32[]{:S(2)}, u32[]{:S(2)}) collective-permute-start(f32[3,1,384,128]{3,2,1,0:T(8,128)} %get-tuple-element.618), channel_id=1, source_target_pairs={{1,0},{2,1},{3,2},{4,3},{5,4},{6,5},{7,6},{8,7},{9,8},{10,9},{11,1... | collective-permute-start | bytes 1769480 | tf_op jit(solution)/shard_map/ppermute | solution.py:18
  248.4 14.9 %collective-permute-start.10 = (f32[3,1,384,128]{3,2,1,0:T(8,128)}, f32[3,1,384,128]{3,2,1,0:T(8,128)}, u32[]{:S(2)}, u32[]{:S(2)}) collective-permute-start(f32[3,1,384,128]{3,2,1,0:T(8,128)} %get-tuple-element.715), channel_id=1, source_target_pairs={{1,0},{2,1},{3,2},{4,3},{5,4},{6,5},{7,6},{8,7},{9,8},{10,9},{11,1... | collective-permute-start | bytes 1769480 | tf_op jit(solution)/shard_map/ppermute | solution.py:18
  249.7 14.5 %collective-permute-start.9 = (f32[3,1,384,128]{3,2,1,0:T(8,128)}, f32[3,1,384,128]{3,2,1,0:T(8,128)}, u32[]{:S(2)}, u32[]{:S(2)}) collective-permute-start(f32[3,1,384,128]{3,2,1,0:T(8,128)} %get-tuple-element.714), channel_id=1, source_target_pairs={{0,1},{1,2},{2,3},{3,4},{4,5},{5,6},{6,7},{7,8},{8,9},{9,10},{10,1... | collective-permute-start | bytes 1769480 | tf_op jit(solution)/shard_map/ppermute | solution.py:18
  277.5 13.4 %collective-permute-start.11 = (f32[3,1,384,128]{3,2,1,0:T(8,128)S(1)}, f32[3,1,384,128]{3,2,1,0:T(8,128)S(1)}, u32[]{:S(2)}, u32[]{:S(2)}) collective-permute-start(f32[3,1,384,128]{3,2,1,0:T(8,128)S(1)} %get-tuple-element.710), channel_id=1, source_target_pairs={{0,1},{1,2},{2,3},{3,4},{4,5},{5,6},{6,7},{7,8},{8,9},{9,10},{10,1... | collective-permute-start | bytes 1769480 | tf_op jit(solution)/shard_map/ppermute | solution.py:18
  281.8 13.6 %collective-permute-start.12 = (f32[3,1,384,128]{3,2,1,0:T(8,128)S(1)}, f32[3,1,384,128]{3,2,1,0:T(8,128)S(1)}, u32[]{:S(2)}, u32[]{:S(2)}) collective-permute-start(f32[3,1,384,128]{3,2,1,0:T(8,128)S(1)} %get-tuple-element.711), channel_id=1, source_target_pairs={{1,0},{2,1},{3,2},{4,3},{5,4},{6,5},{7,6},{8,7},{9,8},{10,9},{11,1... | collective-permute-start | bytes 1769480 | tf_op jit(solution)/shard_map/ppermute | solution.py:18
  298.8 9.1 collective-permute-start.13
  308.0 17.8 %collective-permute-start.14 = (f32[3,1,384,128]{3,2,1,0:T(8,128)S(1)}, f32[3,1,384,128]{3,2,1,0:T(8,128)S(1)}, u32[]{:S(2)}, u32[]{:S(2)}) collective-permute-start(f32[3,1,384,128]{3,2,1,0:T(8,128)S(1)} %get-tuple-element.706), channel_id=1, source_target_pairs={{0,1},{1,2},{2,3},{3,4},{4,5},{5,6},{6,7},{7,8},{8,9},{9,10},{10,1... | collective-permute-start | bytes 1769480 | tf_op jit(solution)/shard_map/ppermute | solution.py:18
  313.2 19.5 %collective-permute-start.15 = (f32[3,1,384,128]{3,2,1,0:T(8,128)S(1)}, f32[3,1,384,128]{3,2,1,0:T(8,128)S(1)}, u32[]{:S(2)}, u32[]{:S(2)}) collective-permute-start(f32[3,1,384,128]{3,2,1,0:T(8,128)S(1)} %get-tuple-element.707), channel_id=1, source_target_pairs={{1,0},{2,1},{3,2},{4,3},{5,4},{6,5},{7,6},{8,7},{9,8},{10,9},{11,1... | collective-permute-start | bytes 1769480 | tf_op jit(solution)/shard_map/ppermute | solution.py:18
  338.5 17.4 %collective-permute-start.16 = (f32[3,1,384,128]{3,2,1,0:T(8,128)}, f32[3,1,384,128]{3,2,1,0:T(8,128)}, u32[]{:S(2)}, u32[]{:S(2)}) collective-permute-start(f32[3,1,384,128]{3,2,1,0:T(8,128)} %get-tuple-element.702), channel_id=1, source_target_pairs={{0,1},{1,2},{2,3},{3,4},{4,5},{5,6},{6,7},{7,8},{8,9},{9,10},{10,1... | collective-permute-start | bytes 1769480 | tf_op jit(solution)/shard_map/ppermute | solution.py:18
  344.8 15.8 %collective-permute-start.17 = (f32[3,1,384,128]{3,2,1,0:T(8,128)}, f32[3,1,384,128]{3,2,1,0:T(8,128)}, u32[]{:S(2)}, u32[]{:S(2)}) collective-permute-start(f32[3,1,384,128]{3,2,1,0:T(8,128)} %get-tuple-element.703), channel_id=1, source_target_pairs={{1,0},{2,1},{3,2},{4,3},{5,4},{6,5},{7,6},{8,7},{9,8},{10,9},{11,1... | collective-permute-start | bytes 1769480 | tf_op jit(solution)/shard_map/ppermute | solution.py:18
  509.2 13.1 %collective-permute-start.18 = (f32[3,1,384,128]{3,2,1,0:T(8,128)S(1)}, f32[3,1,384,128]{3,2,1,0:T(8,128)S(1)}, u32[]{:S(2)}, u32[]{:S(2)}) collective-permute-start(f32[3,1,384,128]{3,2,1,0:T(8,128)S(1)} %get-tuple-element.617), channel_id=1, source_target_pairs={{0,1},{1,2},{2,3},{3,4},{4,5},{5,6},{6,7},{7,8},{8,9},{9,10},{10,1... | collective-permute-start | bytes 1769480 | tf_op jit(solution)/shard_map/ppermute | solution.py:18
  512.5 13.7 %collective-permute-start.19 = (f32[3,1,384,128]{3,2,1,0:T(8,128)S(1)}, f32[3,1,384,128]{3,2,1,0:T(8,128)S(1)}, u32[]{:S(2)}, u32[]{:S(2)}) collective-permute-start(f32[3,1,384,128]{3,2,1,0:T(8,128)S(1)} %get-tuple-element.616), channel_id=1, source_target_pairs={{1,0},{2,1},{3,2},{4,3},{5,4},{6,5},{7,6},{8,7},{9,8},{10,9},{11,1... | collective-permute-start | bytes 1769480 | tf_op jit(solution)/shard_map/ppermute | solution.py:18
  538.4 9.5 collective-permute-start.20
  539.8 12.4 %collective-permute-start.21 = (f32[3,1,384,128]{3,2,1,0:T(8,128)S(1)}, f32[3,1,384,128]{3,2,1,0:T(8,128)S(1)}, u32[]{:S(2)}, u32[]{:S(2)}) collective-permute-start(f32[3,1,384,128]{3,2,1,0:T(8,128)S(1)} %get-tuple-element.614), channel_id=1, source_target_pairs={{1,0},{2,1},{3,2},{4,3},{5,4},{6,5},{7,6},{8,7},{9,8},{10,9},{11,1... | collective-permute-start | bytes 1769480 | tf_op jit(solution)/shard_map/ppermute | solution.py:18
  557.3 10.9 collective-permute-start.22
  573.0 17.5 %collective-permute-start.23 = (f32[3,1,384,128]{3,2,1,0:T(8,128)S(1)}, f32[3,1,384,128]{3,2,1,0:T(8,128)S(1)}, u32[]{:S(2)}, u32[]{:S(2)}) collective-permute-start(f32[3,1,384,128]{3,2,1,0:T(8,128)S(1)} %get-tuple-element.613), channel_id=1, source_target_pairs={{0,1},{1,2},{2,3},{3,4},{4,5},{5,6},{6,7},{7,8},{8,9},{9,10},{10,1... | collective-permute-start | bytes 1769480 | tf_op jit(solution)/shard_map/ppermute | solution.py:18
  578.2 16.1 %collective-permute-start.24 = (f32[3,1,384,128]{3,2,1,0:T(8,128)S(1)}, f32[3,1,384,128]{3,2,1,0:T(8,128)S(1)}, u32[]{:S(2)}, u32[]{:S(2)}) collective-permute-start(f32[3,1,384,128]{3,2,1,0:T(8,128)S(1)} %get-tuple-element.612), channel_id=1, source_target_pairs={{1,0},{2,1},{3,2},{4,3},{5,4},{6,5},{7,6},{8,7},{9,8},{10,9},{11,1... | collective-permute-start | bytes 1769480 | tf_op jit(solution)/shard_map/ppermute | solution.py:18
  605.2 15.7 %collective-permute-start.25 = (f32[3,1,384,128]{3,2,1,0:T(8,128)S(1)}, f32[3,1,384,128]{3,2,1,0:T(8,128)S(1)}, u32[]{:S(2)}, u32[]{:S(2)}) collective-permute-start(f32[3,1,384,128]{3,2,1,0:T(8,128)S(1)} %get-tuple-element.611), channel_id=1, source_target_pairs={{0,1},{1,2},{2,3},{3,4},{4,5},{5,6},{6,7},{7,8},{8,9},{9,10},{10,1... | collective-permute-start | bytes 1769480 | tf_op jit(solution)/shard_map/ppermute | solution.py:18
  609.5 15.2 %collective-permute-start.26 = (f32[3,1,384,128]{3,2,1,0:T(8,128)S(1)}, f32[3,1,384,128]{3,2,1,0:T(8,128)S(1)}, u32[]{:S(2)}, u32[]{:S(2)}) collective-permute-start(f32[3,1,384,128]{3,2,1,0:T(8,128)S(1)} %get-tuple-element.610), channel_id=1, source_target_pairs={{1,0},{2,1},{3,2},{4,3},{5,4},{6,5},{7,6},{8,7},{9,8},{10,9},{11,1... | collective-permute-start | bytes 1769480 | tf_op jit(solution)/shard_map/ppermute | solution.py:18
  786.6 14.3 %collective-permute-start.27 = (f32[3,1,384,128]{3,2,1,0:T(8,128)S(1)}, f32[3,1,384,128]{3,2,1,0:T(8,128)S(1)}, u32[]{:S(2)}, u32[]{:S(2)}) collective-permute-start(f32[3,1,384,128]{3,2,1,0:T(8,128)S(1)} %get-tuple-element.698), channel_id=1, source_target_pairs={{0,1},{1,2},{2,3},{3,4},{4,5},{5,6},{6,7},{7,8},{8,9},{9,10},{10,1... | collective-permute-start | bytes 1769480 | tf_op jit(solution)/shard_map/ppermute | solution.py:18
  789.2 15.5 %collective-permute-start.28 = (f32[3,1,384,128]{3,2,1,0:T(8,128)S(1)}, f32[3,1,384,128]{3,2,1,0:T(8,128)S(1)}, u32[]{:S(2)}, u32[]{:S(2)}) collective-permute-start(f32[3,1,384,128]{3,2,1,0:T(8,128)S(1)} %get-tuple-element.699), channel_id=1, source_target_pairs={{1,0},{2,1},{3,2},{4,3},{5,4},{6,5},{7,6},{8,7},{9,8},{10,9},{11,1... | collective-permute-start | bytes 1769480 | tf_op jit(solution)/shard_map/ppermute | solution.py:18
  808.4 13.7 %collective-permute-start.29 = (f32[3,1,384,128]{3,2,1,0:T(8,128)S(1)}, f32[3,1,384,128]{3,2,1,0:T(8,128)S(1)}, u32[]{:S(2)}, u32[]{:S(2)}) collective-permute-start(f32[3,1,384,128]{3,2,1,0:T(8,128)S(1)} %get-tuple-element.694), channel_id=1, source_target_pairs={{0,1},{1,2},{2,3},{3,4},{4,5},{5,6},{6,7},{7,8},{8,9},{9,10},{10,1... | collective-permute-start | bytes 1769480 | tf_op jit(solution)/shard_map/ppermute | solution.py:18
  811.4 14.6 %collective-permute-start.30 = (f32[3,1,384,128]{3,2,1,0:T(8,128)S(1)}, f32[3,1,384,128]{3,2,1,0:T(8,128)S(1)}, u32[]{:S(2)}, u32[]{:S(2)}) collective-permute-start(f32[3,1,384,128]{3,2,1,0:T(8,128)S(1)} %get-tuple-element.695), channel_id=1, source_target_pairs={{1,0},{2,1},{3,2},{4,3},{5,4},{6,5},{7,6},{8,7},{9,8},{10,9},{11,1... | collective-permute-start | bytes 1769480 | tf_op jit(solution)/shard_map/ppermute | solution.py:18
  829.6 7.5 collective-permute-start.31
  837.2 17.5 %collective-permute-start.32 = (f32[3,1,384,128]{3,2,1,0:T(8,128)S(1)}, f32[3,1,384,128]{3,2,1,0:T(8,128)S(1)}, u32[]{:S(2)}, u32[]{:S(2)}) collective-permute-start(f32[3,1,384,128]{3,2,1,0:T(8,128)S(1)} %get-tuple-element.690), channel_id=1, source_target_pairs={{0,1},{1,2},{2,3},{3,4},{4,5},{5,6},{6,7},{7,8},{8,9},{9,10},{10,1... | collective-permute-start | bytes 1769480 | tf_op jit(solution)/shard_map/ppermute | solution.py:18
  842.1 16.4 %collective-permute-start.33 = (f32[3,1,384,128]{3,2,1,0:T(8,128)S(1)}, f32[3,1,384,128]{3,2,1,0:T(8,128)S(1)}, u32[]{:S(2)}, u32[]{:S(2)}) collective-permute-start(f32[3,1,384,128]{3,2,1,0:T(8,128)S(1)} %get-tuple-element.691), channel_id=1, source_target_pairs={{1,0},{2,1},{3,2},{4,3},{5,4},{6,5},{7,6},{8,7},{9,8},{10,9},{11,1... | collective-permute-start | bytes 1769480 | tf_op jit(solution)/shard_map/ppermute | solution.py:18
  862.0 16.0 %collective-permute-start.34 = (f32[3,1,384,128]{3,2,1,0:T(8,128)S(1)}, f32[3,1,384,128]{3,2,1,0:T(8,128)S(1)}, u32[]{:S(2)}, u32[]{:S(2)}) collective-permute-start(f32[3,1,384,128]{3,2,1,0:T(8,128)S(1)} %get-tuple-element.686), channel_id=1, source_target_pairs={{0,1},{1,2},{2,3},{3,4},{4,5},{5,6},{6,7},{7,8},{8,9},{9,10},{10,1... | collective-permute-start | bytes 1769480 | tf_op jit(solution)/shard_map/ppermute | solution.py:18
  866.4 15.5 %collective-permute-start.35 = (f32[3,1,384,128]{3,2,1,0:T(8,128)S(1)}, f32[3,1,384,128]{3,2,1,0:T(8,128)S(1)}, u32[]{:S(2)}, u32[]{:S(2)}) collective-permute-start(f32[3,1,384,128]{3,2,1,0:T(8,128)S(1)} %get-tuple-element.687), channel_id=1, source_target_pairs={{1,0},{2,1},{3,2},{4,3},{5,4},{6,5},{7,6},{8,7},{9,8},{10,9},{11,1... | collective-permute-start | bytes 1769480 | tf_op jit(solution)/shard_map/ppermute | solution.py:18
  1017.2 13.1 %collective-permute-start.36 = (f32[3,1,384,128]{3,2,1,0:T(8,128)S(1)}, f32[3,1,384,128]{3,2,1,0:T(8,128)S(1)}, u32[]{:S(2)}, u32[]{:S(2)}) collective-permute-start(f32[3,1,384,128]{3,2,1,0:T(8,128)S(1)} %get-tuple-element.609), channel_id=1, source_target_pairs={{0,1},{1,2},{2,3},{3,4},{4,5},{5,6},{6,7},{7,8},{8,9},{9,10},{10,1... | collective-permute-start | bytes 1769480 | tf_op jit(solution)/shard_map/ppermute | solution.py:18
  1020.4 13.7 %collective-permute-start.37 = (f32[3,1,384,128]{3,2,1,0:T(8,128)S(1)}, f32[3,1,384,128]{3,2,1,0:T(8,128)S(1)}, u32[]{:S(2)}, u32[]{:S(2)}) collective-permute-start(f32[3,1,384,128]{3,2,1,0:T(8,128)S(1)} %get-tuple-element.608), channel_id=1, source_target_pairs={{1,0},{2,1},{3,2},{4,3},{5,4},{6,5},{7,6},{8,7},{9,8},{10,9},{11,1... | collective-permute-start | bytes 1769480 | tf_op jit(solution)/shard_map/ppermute | solution.py:18
  1046.3 9.7 collective-permute-start.38
  1047.8 12.1 collective-permute-start.39
  1065.0 10.9 collective-permute-start.40
  1080.8 17.5 %collective-permute-start.41 = (f32[3,1,384,128]{3,2,1,0:T(8,128)S(1)}, f32[3,1,384,128]{3,2,1,0:T(8,128)S(1)}, u32[]{:S(2)}, u32[]{:S(2)}) collective-permute-start(f32[3,1,384,128]{3,2,1,0:T(8,128)S(1)} %get-tuple-element.605), channel_id=1, source_target_pairs={{0,1},{1,2},{2,3},{3,4},{4,5},{5,6},{6,7},{7,8},{8,9},{9,10},{10,1... | collective-permute-start | bytes 1769480 | tf_op jit(solution)/shard_map/ppermute | solution.py:18
  1086.0 16.1 %collective-permute-start.42 = (f32[3,1,384,128]{3,2,1,0:T(8,128)S(1)}, f32[3,1,384,128]{3,2,1,0:T(8,128)S(1)}, u32[]{:S(2)}, u32[]{:S(2)}) collective-permute-start(f32[3,1,384,128]{3,2,1,0:T(8,128)S(1)} %get-tuple-element.604), channel_id=1, source_target_pairs={{1,0},{2,1},{3,2},{4,3},{5,4},{6,5},{7,6},{8,7},{9,8},{10,9},{11,1... | collective-permute-start | bytes 1769480 | tf_op jit(solution)/shard_map/ppermute | solution.py:18
  1112.8 16.0 %collective-permute-start.43 = (f32[3,1,384,128]{3,2,1,0:T(8,128)S(1)}, f32[3,1,384,128]{3,2,1,0:T(8,128)S(1)}, u32[]{:S(2)}, u32[]{:S(2)}) collective-permute-start(f32[3,1,384,128]{3,2,1,0:T(8,128)S(1)} %get-tuple-element.603), channel_id=1, source_target_pairs={{0,1},{1,2},{2,3},{3,4},{4,5},{5,6},{6,7},{7,8},{8,9},{9,10},{10,1... | collective-permute-start | bytes 1769480 | tf_op jit(solution)/shard_map/ppermute | solution.py:18
  1117.6 15.2 %collective-permute-start.44 = (f32[3,1,384,128]{3,2,1,0:T(8,128)S(1)}, f32[3,1,384,128]{3,2,1,0:T(8,128)S(1)}, u32[]{:S(2)}, u32[]{:S(2)}) collective-permute-start(f32[3,1,384,128]{3,2,1,0:T(8,128)S(1)} %get-tuple-element.602), channel_id=1, source_target_pairs={{1,0},{2,1},{3,2},{4,3},{5,4},{6,5},{7,6},{8,7},{9,8},{10,9},{11,1... | collective-permute-start | bytes 1769480 | tf_op jit(solution)/shard_map/ppermute | solution.py:18
  (123 other events, 2211.7 us)
where the time goes:
time: 1250 us; the launch traced here: 1230 us
  blocking collectives  331 us (26%)
  waiting for transfers between devices  297 us (24%)
  other arithmetic  223 us (18%)
  starting transfers between devices  154 us (12%)
  local copies, waits for them, and re-layouts  124 us (10%)
  matrix products  92.1 us (7%)
    ppermute x45, waiting for transfers between devices, shifted(): lax.ppermute(value, axis, [(source, source + steps) for source in range(i...  276 us
    scatter-add x3, other arithmetic, spread_profiles(): return jnp.zeros(state_shape, jnp.float32).at[sub_owned, :, lat_owned, lo...  158 us
    psum x2, blocking collectives, residual_norm(): return lax.psum(jnp.sum(vector * vector), ('tm', 'space'))  139 us
    ppermute x45, starting transfers between devices, shifted(): lax.ppermute(value, axis, [(source, source + steps) for source in range(i...  132 us
    dot_general x20, matrix products, moved(): jnp.einsum('aijl,kl->aijk', result, mixing, precision=lax.Precision.HIGHEST)  92.1 us
    psum x1, blocking collectives, per_device(): lax.psum(jnp.sum(direction * image_vec), ('tm', 'space'))  76.7 us
    all_to_all x2, blocking collectives, per_device(): lax.all_to_all(hessian_states[sub_owned, :, lat_owned, lon_owned, :].resh...  76.2 us
    all_to_all x2, blocking collectives, send_back(): lax.all_to_all(profiles, 'space', split_axis=0, concat_axis=0, tiled=True)  39 us
  transfers between devices with their start and end apart: 48, of which 48 were waited for; matrix products, arithmetic and copies ran while one was open for 2% of the time, Pallas kernels for 0%

commit v1 on v0

v1 whole, which is shorter than its diff:
```python
import functools
import jax
import jax.numpy as jnp
from jax import lax
from jax.experimental import pallas as pl
from jax.experimental.pallas import tpu as pltpu
from jax.sharding import PartitionSpec as P

FIELDS = 3
MIXC = 0.25
SCALE_Q = 0.5
PAD = 8
F32 = jnp.float32
BF16 = jnp.bfloat16

VM = pl.BlockSpec(memory_space=pltpu.VMEM)
SM = pl.BlockSpec(memory_space=pltpu.SMEM)


def call(body, ins, specs, outs, vmem=None, flops=1e8, scratch=()):
    nbytes = sum(a.size * a.dtype.itemsize for a in ins)
    nbytes += sum(o.size * o.dtype.itemsize for o in outs)
    return pl.pallas_call(
        body,
        out_shape=outs,
        in_specs=specs,
        out_specs=[VM] * len(outs),
        scratch_shapes=list(scratch),
        compiler_params=pltpu.CompilerParams(vmem_limit_bytes=vmem or 40 * 2**20),
        cost_estimate=pl.CostEstimate(
            flops=int(flops), bytes_accessed=int(nbytes), transcendentals=0
        ),
    )(*ins)


def sds(*shape, dtype=F32):
    return jax.ShapeDtypeStruct(shape, dtype)


def later(x):
    return pltpu.roll(x, 1, 0)


def earlier(x):
    return pltpu.roll(x, x.shape[0] - 1, 0)


def coef(w_ref, i):
    a = w_ref[0, i]
    b = w_ref[1, i]
    ap = jnp.maximum(a, 0.0)
    am = ap - a
    bp = jnp.maximum(b, 0.0)
    bm = bp - b
    return ap, am, bp, bm, 1.0 - (ap + am) - (bp + bm)


def mixed(v, rhs):
    lev = v.shape[1]
    hi = v.astype(BF16)
    lo = (v - hi.astype(F32)).astype(BF16)
    o = jnp.dot(jnp.concatenate([hi, lo], axis=1), rhs, preferred_element_type=F32)
    return v + (o[:, :lev] + o[:, lev:])


def adj_local(w, c):
    ap, am, _, _, c0 = c
    return c0 * w + earlier(ap * w) + later(am * w)


def fwd_local(u, c):
    ap, am, _, _, c0 = c
    return c0 * u + ap * later(u) + am * earlier(u)


def adj_pre(f, rows, w_ref, rhs, mid_ref, ss_ref, sn_ref):
    w = [mixed(x, rhs) for x in rows]
    c = [coef(w_ref, i) for i in range(3)]
    mid_ref[f] = adj_local(w[1], c[1]) + c[2][2] * w[2] + c[0][3] * w[0]
    ss_ref[0, f] = adj_local(w[0], c[0]) + c[1][2] * w[1]
    ss_ref[1, f] = c[0][2] * w[0]
    sn_ref[0, f] = adj_local(w[2], c[2]) + c[1][3] * w[1]
    sn_ref[1, f] = c[2][3] * w[2]


def adj_post(f, mid_ref, ss_ref, sn_ref, rs_ref, rn_ref, fs, fn):
    return [
        (rs_ref[0, f] + ss_ref[1, f]) * fs,
        ss_ref[0, f] + rs_ref[1, f] * fs,
        mid_ref[f],
        sn_ref[0, f] + rn_ref[1, f] * fn,
        (rn_ref[0, f] + sn_ref[1, f]) * fn,
    ]


def adj_second(rows5, w_ref, wh_ref, rhs):
    w = [mixed(x, rhs) for x in rows5]
    c = [coef(w_ref, i) for i in range(3)]
    up = [c[1][2], c[2][2], wh_ref[1]]
    down = [wh_ref[0], c[0][3], c[1][3]]
    return [
        adj_local(w[i + 1], c[i]) + up[i] * w[i + 2] + down[i] * w[i] for i in range(3)
    ]


def fwd_pre(f, u, w_ref, mid_ref, ss_ref, sn_ref):
    c = [coef(w_ref, i) for i in range(3)]
    mid_ref[f] = fwd_local(u[1], c[1]) + c[1][2] * u[0] + c[1][3] * u[2]
    ss_ref[0, f] = u[0]
    ss_ref[1, f] = fwd_local(u[0], c[0]) + c[0][3] * u[1]
    sn_ref[0, f] = u[2]
    sn_ref[1, f] = fwd_local(u[2], c[2]) + c[2][2] * u[1]


def fwd_post(f, mid_ref, ss_ref, sn_ref, rs_ref, rn_ref, w_ref, wh_ref, fs, fn, rhs):
    b0 = w_ref[1, 0]
    b2 = w_ref[1, 2]
    m = [
        rs_ref[1, f] * fs + wh_ref[0] * ss_ref[0, f],
        ss_ref[1, f] + jnp.maximum(b0, 0.0) * (rs_ref[0, f] * fs),
        mid_ref[f],
        sn_ref[1, f] + jnp.maximum(-b2, 0.0) * (rn_ref[0, f] * fn),
        rn_ref[1, f] * fn + wh_ref[1] * sn_ref[0, f],
    ]
    return [mixed(x, rhs) for x in m]


def fwd_second(u5, w_ref, rhs):
    out = []
    for i in range(3):
        c = coef(w_ref, i)
        m = fwd_local(u5[i + 1], c) + c[2] * u5[i] + c[3] * u5[i + 2]
        out.append(mixed(m, rhs))
    return out


def fields(body):
    def step(f, carry):
        body(f)
        return carry

    lax.fori_loop(0, FIELDS, step, 0)


def fold(x):
    own = x[PAD:-PAD]
    return jnp.sum(own.reshape(own.shape[0] // 8, 8, own.shape[1]), axis=0)


def split_store(x, half, c, own_ref, snd_ref, idx):
    n = x.shape[0]
    low = jnp.concatenate([x[n - PAD :], x[: half + PAD]], axis=0)
    high = jnp.concatenate([x[half - PAD :], x[:PAD]], axis=0)

    @pl.when(c == 0)
    def _():
        own_ref[idx] = low
        snd_ref[idx] = high

    @pl.when(c != 0)
    def _():
        own_ref[idx] = high
        snd_ref[idx] = low


def pack_body(w_ref, d_ref, i_ref, o_ref):
    lev = o_ref.shape[-1]
    live = i_ref[...] >= 0.0
    for f in range(FIELDS):
        w = jnp.where(live, w_ref[:, :, f * lev : (f + 1) * lev], 0.0)
        o_ref[:, f] = w
        o_ref[:, FIELDS + f] = w * d_ref[:, :, f * lev : (f + 1) * lev]
    o_ref[:, 2 * FIELDS] = i_ref[...]


def scatter_body(half, c_ref, idx_ref, p_ref, do_ref, ds_ref, go_ref, gs_ref, acc):
    owners, slots = idx_ref.shape
    blocks = 2 * FIELDS + 1
    lev = p_ref.shape[1]
    cells = acc.shape[0] // 8
    cols = 2 * half
    c = c_ref[0]
    chunk = 64

    def clear(t, carry):
        acc[pl.ds(pl.multiple_of(t * (8 * chunk), 8 * chunk), 8 * chunk), :] = jnp.zeros(
            (8 * chunk, lev), F32
        )
        return carry

    lax.fori_loop(0, cells // chunk, clear, 0)

    def put(o, carry):
        for s in range(slots):
            row = pl.multiple_of(idx_ref[o, s] * 8, 8)
            x = p_ref[pl.ds(o * (blocks * slots) + s, blocks, stride=slots), :]
            acc[pl.ds(row, blocks), :] += x
        return carry

    lax.fori_loop(0, owners, put, 0)

    for w in range(2):

        def one(i, carry):
            base = (w * 3 + i) * (cols * 8)
            for f in range(FIELDS):
                x = acc[pl.ds(base + f, cols, stride=8), :]
                split_store(x, half, c, do_ref, ds_ref, (w, f, i))
                y = acc[pl.ds(base + FIELDS + f, cols, stride=8), :]
                split_store(y, half, c, go_ref, gs_ref, (w, f, i))
            return carry

        lax.fori_loop(0, 3, one, 0)


def wind_body(half, c_ref, w_ref, m_ref, o_ref, s_ref, ra_ref, rf_ref):
    c = c_ref[0]
    for w in range(2):

        def one(i, carry):
            for k in range(2):
                split_store(w_ref[w, k, i].astype(F32), half, c, o_ref, s_ref, (w, k, i))
            return carry

        lax.fori_loop(0, 3, one, 0)
    for m, ref in ((m_ref[...] * MIXC, ra_ref), (m_ref[...].T * MIXC, rf_ref)):
        hi = m.astype(BF16)
        lo = (m - hi.astype(F32)).astype(BF16)
        line = jnp.concatenate([hi, lo], axis=1)
        ref[...] = jnp.concatenate([line, line], axis=0)


def turn_first_body(g3_ref, g2_ref, w3_ref, ra_ref, mid_ref, ss_ref, sn_ref):
    rhs = ra_ref[...]

    def one(f):
        adj_pre(f, [g3_ref[f, i] for i in range(3)], w3_ref, rhs, mid_ref, ss_ref, sn_ref)
        ss_ref[2, f] = g2_ref[f, 0]
        sn_ref[2, f] = g2_ref[f, 2]

    fields(one)


def five(f, f_ref, rs_ref, rn_ref, ext):
    if ext:
        return [rs_ref[2, f]] + [f_ref[f, i] for i in range(3)] + [rn_ref[2, f]]
    return [f_ref[f, i] for i in range(5)]


def adj_mid_body(ext, *refs):
    (fl, mid, ss, sn, rs, rn, f2, f1, w2, wh2, w1, ra) = refs[:12]
    n = 12
    if ext:
        g0 = refs[n]
        n += 1
    g3, g2, mid_o, ss_o, sn_o = refs[n:]
    fs, fn = fl[0], fl[1]
    rhs = ra[...]

    def one(f):
        lam = adj_post(f, mid, ss, sn, rs, rn, fs, fn)
        for i in range(5):
            g3[f, i] = lam[i] * SCALE_Q
        src = five(f, f2, rs, rn, ext)
        out = adj_second([lam[i] + src[i] for i in range(5)], w2, wh2, rhs)
        for i in range(3):
            g2[f, i] = out[i] * SCALE_Q
        adj_pre(f, [out[i] + f1[f, i] for i in range(3)], w1, rhs, mid_o, ss_o, sn_o)
        if ext:
            ss_o[2, f] = g0[f, 0]
            sn_o[2, f] = g0[f, 2]

    fields(one)


def adj_last_body(mode, *refs):
    ext = mode == 0
    (fl, mid, ss, sn, rs, rn, f0, w0, wh0, ra) = refs[:10]
    n = 10
    if mode == 1:
        sc, g0, g1 = refs[n : n + 3]
        n += 3
    outs = refs[n:]
    fs, fn = fl[0], fl[1]
    rhs = ra[...]

    def one(f):
        lam = adj_post(f, mid, ss, sn, rs, rn, fs, fn)
        src = five(f, f0, rs, rn, ext)
        out = adj_second([lam[i] + src[i] for i in range(5)], w0, wh0, rhs)
        one_half = [x * SCALE_Q for x in lam]
        if mode == 1:
            a = sc[0]
            one_half = [(1.0 - a) * g1[f, i] - a * one_half[i] for i in range(5)]
            out = [(1.0 - a) * g0[f, i] - a * out[i] for i in range(3)]
        for i in range(5):
            outs[1][f, i] = one_half[i]
        for i in range(3):
            outs[0][f, i] = out[i]
        if mode < 2:
            fwd_pre(f, out, w0, *outs[2:5])

    fields(one)


def fwd_first_body(fl, mid, ss, sn, rs, rn, v1, v2, w0, wh0, w1, w2, rf, *outs):
    x0, x1, mid_o, ss_o, sn_o = outs
    fs, fn = fl[0], fl[1]
    rhs = rf[...]

    def one(f):
        x5 = fwd_post(f, mid, ss, sn, rs, rn, w0, wh0, fs, fn, rhs)
        for i in range(5):
            x0[f, i] = x5[i]
        x3 = fwd_second([x5[i] + SCALE_Q * v1[f, i] for i in range(5)], w1, rhs)
        for i in range(3):
            x1[f, i] = x3[i]
        fwd_pre(f, [x3[i] + SCALE_Q * v2[f, i] for i in range(3)], w2, mid_o, ss_o, sn_o)

    fields(one)


def edge(x, half):
    return jnp.concatenate([x[half : half + PAD], x[PAD : 2 * PAD]], axis=0)


def fwd_last_body(half, fl, mid, ss, sn, rs, rn, v3, x0, x1, w2, wh2, w3, rf, *outs):
    x2, x3, eg = outs
    fs, fn = fl[0], fl[1]
    rhs = rf[...]

    def one(f):
        x5 = fwd_post(f, mid, ss, sn, rs, rn, w2, wh2, fs, fn, rhs)
        for i in range(5):
            x2[f, i] = x5[i]
            eg[f, 8 + i] = edge(x5[i], half)
            eg[f, i] = edge(x0[f, i], half)
        y3 = fwd_second([x5[i] + SCALE_Q * v3[f, i] for i in range(5)], w3, rhs)
        for i in range(3):
            x3[f, i] = y3[i]
            eg[f, 13 + i] = edge(y3[i], half)
            eg[f, 5 + i] = edge(x1[f, i], half)

    fields(one)


def fixed(x, e):
    return jnp.concatenate([e[:PAD], x[PAD:-PAD], e[PAD:]], axis=0)


def turn_body(second, *refs):
    x3, eg, d3, w3, ra = refs[:5]
    n = 5
    if second:
        sc, old = refs[n : n + 2]
        n += 2
    y3, mid, ss, sn, q = refs[n:]
    rhs = ra[...]
    q[...] = jnp.zeros_like(q)

    def one(f):
        rows = []
        for i in range(3):
            y = fixed(x3[f, i], eg[f, 13 + i])
            if second:
                y = y + sc[0] * old[f, i]
            y3[f, i] = y
            t = d3[f, i] * y
            q[...] += fold(t * y)
            rows.append(t)
        adj_pre(f, rows, w3, rhs, mid, ss, sn)

    fields(one)


def rest_body(second, *refs):
    x0, x1, x2, eg, d0, d1, d2, ds, dn = refs[:9]
    n = 9
    if second:
        sc, old0, old1, old2 = refs[n : n + 4]
        n += 4
    else:
        old0 = old1 = old2 = None
    y0, y1, y2, f0, f1, f2, q = refs[n:]
    q[...] = jnp.zeros_like(q)

    def one(f):
        for x, rows, at, d, w, old, y_o, f_o in (
            (x0, 5, 0, d0, 0, old0, y0, f0),
            (x1, 3, 5, d1, None, old1, y1, f1),
            (x2, 5, 8, d2, 1, old2, y2, f2),
        ):
            for i in range(rows):
                y = fixed(x[f, i], eg[f, at + i])
                if second:
                    y = y + sc[0] * old[f, i]
                y_o[f, i] = y
                if rows == 3:
                    t = d[f, i] * y
                    q[...] += fold(t * y)
                elif i == 0:
                    t = ds[w, f] * y
                elif i == 4:
                    t = dn[w, f] * y
                else:
                    t = d[f, i - 1] * y
                    q[...] += fold(t * y)
                f_o[f, i] = t

    fields(one)


def norm_body(v0, v1, v2, v3, q):
    q[...] = jnp.zeros_like(q)

    def one(f):
        for v, off in ((v0, 0), (v1, 1), (v2, 0), (v3, 1)):
            for i in range(3):
                x = v[f, i + off]
                q[...] += fold(x * x)

    fields(one)


def resid_body(sc, v0, v1, g0, g1, g2, g3, z2, z3, r2, r3, q):
    a = sc[0]
    q[...] = jnp.zeros_like(q)

    def dots(r, g):
        q[0] += fold(r * r)
        q[1] += fold(r * g)

    def one(f):
        for i in range(5):
            r = (1.0 - a) * g3[f, i] - a * z3[f, i]
            r3[f, i] = r
            if 0 < i < 4:
                dots(r, g3[f, i])
                dots(v1[f, i], g1[f, i])
        for i in range(3):
            r = (1.0 - a) * g2[f, i] - a * z2[f, i]
            r2[f, i] = r
            dots(r, g2[f, i])
            dots(v0[f, i], g0[f, i])

    fields(one)


def final_body(kind, c_ref, sc, *refs):
    r = refs[0:4]
    g = refs[4:8]
    n = 8
    if kind == "res":
        z = refs[8:12]
        n = 12
    keep, send = refs[n:]
    c = c_ref[0]
    beta, a0, a1 = sc[0], sc[1], sc[2]

    def one(f):
        for k in range(4):
            off = k % 2
            for i in range(3):
                res = r[k][f, i + off][PAD:-PAD]
                grad = g[k][f, i + off][PAD:-PAD]
                d = res + beta * grad
                if kind == "res":
                    val = res - a1 * (d + z[k][f, i + off][PAD:-PAD])
                else:
                    val = a0 * grad + a1 * d

                @pl.when(c == k // 2)
                def _():
                    keep[k % 2, f, i] = val

                @pl.when(c != k // 2)
                def _():
                    send[k % 2, f, i] = val

    fields(one)


def per_device(winds, mixing, innovations, obs_weight, obs_sub, obs_col, obs_count):
    owners, slots = obs_sub.shape[2], obs_sub.shape[3]
    lev = mixing.shape[0]
    cols = winds.shape[4]
    half = cols // 2
    wide = half + 2 * PAD
    cells = winds.shape[3] * cols
    c = lax.axis_index("tm").astype(jnp.int32)
    pos = lax.axis_index("space")
    bands = lax.axis_size("space")
    c_arr = c.reshape(1)
    flags = jnp.stack([(pos > 0), (pos < bands - 1)]).astype(F32)
    north = [(i, (i + 1) % bands) for i in range(bands)]
    south = [((i + 1) % bands, i) for i in range(bands)]

    def swap(x):
        return lax.ppermute(x, "tm", [(0, 1), (1, 0)])

    def exchange(ss, sn):
        return lax.ppermute(sn, "space", north), lax.ppermute(ss, "space", south)

    def total(parts):
        vals = jnp.stack([jnp.sum(p) for p in parts])
        vals = vals + swap(vals)
        msg = jnp.broadcast_to(
            jnp.pad(vals, (0, lev - len(parts)))[None, None, :], (bands, 1, lev)
        )
        got = lax.all_to_all(msg, "space", split_axis=0, concat_axis=0, tiled=True)
        return jnp.sum(got, axis=(0, 1))

    live = (
        jnp.arange(slots, dtype=jnp.int32)[None, :] < obs_count.reshape(owners)[:, None]
    )
    place = (obs_sub * cells + obs_col).reshape(owners, slots)
    place = jnp.where(live, place, -1).astype(F32)
    place = jnp.broadcast_to(place[..., None], (owners, slots, lev))
    blocks = 2 * FIELDS + 1
    packed = call(
        pack_body,
        (
            obs_weight.reshape(owners, slots, -1),
            innovations.reshape(owners, slots, -1),
            place,
        ),
        [VM] * 3,
        [sds(owners, blocks, slots, lev)],
    )[0]
    got = lax.all_to_all(packed, "space", split_axis=0, concat_axis=0, tiled=True)

    w_own, w_snd, ra, rf = call(
        functools.partial(wind_body, half),
        (c_arr, winds[:, 0], mixing),
        [SM, VM, VM],
        [sds(2, 2, 3, wide, lev)] * 2 + [sds(2 * lev, 2 * lev, dtype=BF16)] * 2,
    )
    w_got = swap(w_snd)
    first = c == 0
    w01 = jnp.where(first, w_own, w_got)
    w23 = jnp.where(first, w_got, w_own)
    w0, w1, w2, w3 = w01[0], w01[1], w23[0], w23[1]
    up = jnp.stack([jnp.maximum(-w0[1, 2], 0.0), jnp.maximum(-w2[1, 2], 0.0)])
    down = jnp.stack([jnp.maximum(w0[1, 0], 0.0), jnp.maximum(w2[1, 0], 0.0)])
    from_s, from_n = exchange(down, up)
    from_s = jnp.where(pos > 0, from_s, 0.0)
    from_n = jnp.where(pos < bands - 1, from_n, 0.0)
    wh0 = jnp.stack([from_s[0], from_n[0]])
    wh2 = jnp.stack([from_s[1], from_n[1]])

    idx = jnp.maximum(got[:, 2 * FIELDS, :, 0], 0.0).astype(jnp.int32)
    d_own, d_snd, g_own, g_snd = call(
        functools.partial(scatter_body, half),
        (c_arr, idx, got.reshape(owners * blocks * slots, lev)),
        [SM, SM, VM],
        [sds(2, FIELDS, 3, wide, lev)] * 4,
        scratch=[pltpu.VMEM((2 * cells * 8, lev), F32)],
    )
    g_got = swap(g_snd)
    f01 = jnp.where(first, g_own, g_got)
    f23 = jnp.where(first, g_got, g_own)
    d_got = swap(d_snd)
    d01 = jnp.where(first, d_own, d_got)
    d23 = jnp.where(first, d_got, d_own)
    dd0, dd1, dd2, dd3 = d01[0], d01[1], d23[0], d23[1]
    ds, dn = exchange(
        jnp.stack([dd0[:, 0], dd2[:, 0]]), jnp.stack([dd0[:, 2], dd2[:, 2]])
    )

    row3 = sds(FIELDS, 3, wide, lev)
    row5 = sds(FIELDS, 5, wide, lev)
    mid_t = sds(FIELDS, wide, lev)

    def msg(n):
        return sds(n, FIELDS, wide, lev)

    part = sds(8, lev)

    def adj_mid(state, f2, f1, g0=None):
        mid, ss, sn = state
        rs, rn = exchange(ss, sn)
        ext = g0 is not None
        n = 3 if ext else 2
        ins = (flags, mid, ss, sn, rs, rn, f2, f1, w2, wh2, w1, ra) + ((g0,) if ext else ())
        o = call(
            functools.partial(adj_mid_body, ext),
            ins,
            [SM] + [VM] * (len(ins) - 1),
            [row5, row3, mid_t, msg(n), msg(n)],
        )
        return o[0], o[1], tuple(o[2:])

    def adj_last(mode, state, f0, extra=()):
        mid, ss, sn = state
        rs, rn = exchange(ss, sn)
        ins = (flags, mid, ss, sn, rs, rn, f0, w0, wh0, ra) + extra
        specs = [SM] + [VM] * 9 + ([SM, VM, VM] if extra else [])
        outs = [row3, row5] + ([mid_t, msg(2), msg(2)] if mode < 2 else [])
        o = call(functools.partial(adj_last_body, mode), ins, specs, outs)
        return o[0], o[1], tuple(o[2:])

    def fwd_first(state, v1, v2):
        mid, ss, sn = state
        rs, rn = exchange(ss, sn)
        ins = (flags, mid, ss, sn, rs, rn, v1, v2, w0, wh0, w1, w2, rf)
        o = call(
            fwd_first_body, ins, [SM] + [VM] * 12, [row5, row3, mid_t, msg(2), msg(2)]
        )
        return o[0], o[1], tuple(o[2:])

    def fwd_last(state, v3, x0, x1):
        mid, ss, sn = state
        rs, rn = exchange(ss, sn)
        ins = (flags, mid, ss, sn, rs, rn, v3, x0, x1, w2, wh2, w3, rf)
        return call(
            functools.partial(fwd_last_body, half),
            ins,
            [SM] + [VM] * 12,
            [row5, row3, sds(FIELDS, 16, 2 * PAD, lev)],
        )

    def turn(xs, eg, beta=None, old=None):
        eg = swap(eg)
        second = beta is not None
        x0, x1, x2, x3 = xs
        ex = (beta, old[3]) if second else ()
        o = call(
            functools.partial(turn_body, second),
            (x3, eg, dd3, w3, ra) + ex,
            [VM] * 5 + ([SM, VM] if second else []),
            [row3, mid_t, msg(2), msg(2), part],
        )
        y3, state, q3 = o[0], tuple(o[1:4]), o[4]
        ex = (beta,) + old[:3] if second else ()
        y0, y1, y2, f0, f1, f2, q = call(
            functools.partial(rest_body, second),
            (x0, x1, x2, eg, dd0, dd1, dd2, ds, dn) + ex,
            [VM] * 9 + ([SM] + [VM] * 3 if second else []),
            [row5, row3, row5, row5, row3, row5, part],
        )
        return state, (y0, y1, y2, y3), (f0, f1, f2), q3 + q

    o = call(
        turn_first_body,
        (f23[1], f23[0], w3, ra),
        [VM] * 4,
        [mid_t, msg(3), msg(3)],
    )
    g3, g2, state = adj_mid(tuple(o), f23[0], f01[1], f01[0])
    g0, g1, state = adj_last(0, state, f01[0])
    rr_part = call(norm_body, (g0, g1, g2, g3), [VM] * 4, [part])[0]

    x0, x1, state = fwd_first(state, g1, g2)
    x2, x3, eg = fwd_last(state, g3, x0, x1)
    state, ys, fs, q = turn((x0, x1, x2, x3), eg)
    sums = total([rr_part, q])
    rr0 = sums[0]
    a0 = rr0 / (rr0 + sums[1])
    z3, z2, state = adj_mid(state, fs[2], fs[1])
    a0_arr = a0.reshape(1)
    v0, v1, state = adj_last(1, state, fs[0], (a0_arr, g0, g1))
    v2, v3, q = call(
        resid_body,
        (a0_arr, v0, v1, g0, g1, g2, g3, z2, z3),
        [SM] + [VM] * 8,
        [row3, row5, sds(2, 8, lev)],
    )
    sums = total([q[0], q[1]])
    rr1 = sums[0]
    beta = rr1 / rr0
    dd = rr1 + beta * (2.0 * sums[1] + beta * rr0)

    x0, x1, state = fwd_first(state, v1, v2)
    x2, x3, eg = fwd_last(state, v3, x0, x1)
    state, _, fs, q = turn((x0, x1, x2, x3), eg, beta.reshape(1), ys)
    a1 = rr1 / (dd + total([q])[0])
    scal = jnp.stack([beta, a0, a1])
    z3, z2, state = adj_mid(state, fs[2], fs[1])
    z0, z1, _ = adj_last(2, state, fs[0])

    shape = sds(2, FIELDS, 3, half, lev)
    keep_i, send_i = call(
        functools.partial(final_body, "inc"),
        (c_arr, scal, v0, v1, v2, v3, g0, g1, g2, g3),
        [SM, SM] + [VM] * 8,
        [shape, shape],
    )
    keep_r, send_r = call(
        functools.partial(final_body, "res"),
        (c_arr, scal, v0, v1, v2, v3, g0, g1, g2, g3, z0, z1, z2, z3),
        [SM, SM] + [VM] * 12,
        [shape, shape],
    )

    def whole(keep, send):
        other = swap(send)
        return jnp.where(
            first,
            jnp.concatenate([keep, other], axis=3),
            jnp.concatenate([other, keep], axis=3),
        )[:, None]

    return whole(keep_i, send_i), whole(keep_r, send_r)


def solution(mesh):
    in_specs = (
        P("tm", "space", None, None, None, None),
        P(),
        P("tm", "space", None, None, None),
        P("tm", "space", None, None, None),
        P("tm", "space", None, None),
        P("tm", "space", None, None),
        P("tm", "space", None),
    )
    out_specs = (P("tm", "space", None, None, None, None), P("tm", "space", None, None, None, None))
    return jax.shard_map(
        per_device, mesh=mesh, in_specs=in_specs, out_specs=out_specs, check_vma=False
    )
```

time: 1250 us -> 427 us (0.34); the launches traced: 1230 us -> 426 us
  blocking collectives: 331 us -> 29.6 us
  other arithmetic: 223 us -> 18.3 us
  waiting for transfers between devices: 297 us -> 129 us
  matrix products: 92.1 us -> 0 us
  Pallas kernels: 0 us -> 64.4 us
  local copies, waits for them, and re-layouts: 124 us -> 61.5 us
  starting transfers between devices: 154 us -> 114 us
    psum x3 -> x0, blocking collectives: 216 us -> none  [the longest x2 139 us: residual_norm(): return lax.psum(jnp.sum(vector * vector), ('tm', 'space'))]
    ppermute x45 -> x34, waiting for transfers between devices: 276 us -> 101 us  [the longest x24 96.7 us: exchange(): return (lax.ppermute(sn, 'space', north), lax.ppermute(ss, 'space', south))]
    scatter-add x27 -> x0, other arithmetic: 163 us -> none  [the longest x3 158 us: spread_profiles(): return jnp.zeros(state_shape, jnp.float32).at[sub_owned, :, lat_owned, lo...]
    dot_general x20 -> x0, matrix products: 92.1 us -> none  [moved(): jnp.einsum('aijl,kl->aijk', result, mixing, precision=lax.Precision.HIGHEST)]
    all_to_all x4 -> x2, blocking collectives: 115 us -> 29.6 us  [total(): got = lax.all_to_all(msg, 'space', split_axis=0, concat_axis=0, tiled=True)]
    pallas_call x0 -> x22, Pallas kernels: none -> 64.4 us  [call(): pl.pallas_call(body, out_shape=outs, in_specs=specs, out_specs=[VM] * len...]
    ppermute x45 -> x34, starting transfers between devices: 132 us -> 97.5 us  [the longest x24 78.7 us: exchange(): return (lax.ppermute(sn, 'space', north), lax.ppermute(ss, 'space', south))]
    scatter-add x24 -> x0, local copies, waits for them, and re-layouts: 33.8 us -> none  [the longest x12 17 us: step_adjoint(): inner = inner.at[:, :, -1:].add(west_pad)]
  transfers between devices with their start and end apart: 48 -> 36, of which waited for: 48 -> 16; matrix products, arithmetic and copies ran while one was open for 2% -> 6% of each run, Pallas kernels for 0% -> 9%
where the time goes in v1:
time: 427 us; the launch traced here: 426 us
  waiting for transfers between devices  129 us (30%)
  starting transfers between devices  114 us (27%)
  Pallas kernels  64.4 us (15%)
  local copies, waits for them, and re-layouts  61.5 us (14%)
  blocking collectives  29.6 us (7%)
  other arithmetic  18.3 us (4%)
  between operations  8.53 us (2%)
    ppermute x24, waiting for transfers between devices, exchange(): return (lax.ppermute(sn, 'space', north), lax.ppermute(ss, 'space', south))  96.7 us
    ppermute x24, starting transfers between devices, exchange(): return (lax.ppermute(sn, 'space', north), lax.ppermute(ss, 'space', south))  78.7 us
    pallas_call x22, Pallas kernels, call(): pl.pallas_call(body, out_shape=outs, in_specs=specs, out_specs=[VM] * len...  64.4 us
    unnamed x207, local copies, waits for them, and re-layouts  53.6 us
    all_to_all x2, blocking collectives, total(): got = lax.all_to_all(msg, 'space', split_axis=0, concat_axis=0, tiled=True)  29.6 us
    all_to_all x1, waiting for transfers between devices, per_device(): lax.all_to_all(packed, 'space', split_axis=0, concat_axis=0, tiled=True)  21.3 us
    ppermute x10, starting transfers between devices, swap(): return lax.ppermute(x, 'tm', [(0, 1), (1, 0)])  18.8 us
    all_to_all x1, starting transfers between devices, per_device(): lax.all_to_all(packed, 'space', split_axis=0, concat_axis=0, tiled=True)  12.1 us
  transfers between devices with their start and end apart: 36, of which 16 were waited for; matrix products, arithmetic and copies ran while one was open for 6% of the time, Pallas kernels for 9%

profile of v1, /device:TPU:1, one launch (start us, length us, event | category | flops | bytes accessed | tf_op | source)
XLA Modules:
  0.0 425.7 jit_solution(1033819259023016907)
XLA Ops:
  5.2 12.1 %all-to-all-start = ((f32[64,7,8,128]{3,2,1,0:T(8,128)}), f32[64,7,8,128]{3,2,1,0:T(8,128)S(1)}, u32[]{:S(2)}, u32[]{:S(2)}) async-start(f32[64,7,8,128]{3,2,1,0:T(8,128)} %copy-done.47), calls=%async_computation | async-start | bytes 3670016 | tf_op jit(solution)/shard_map/all_to_all | solution.py:530
  20.9 21.3 %all-to-all-done = f32[64,7,8,128]{3,2,1,0:T(8,128)S(1)} async-done(((f32[64,7,8,128]{3,2,1,0:T(8,128)}), f32[64,7,8,128]{3,2,1,0:T(8,128)S(1)}, u32[]{:S(2)}, u32[]{:S(2)}) %all-to-all-start) | async-done | bytes 1835040 | tf_op jit(solution)/shard_map/all_to_all | solution.py:530
  44.3 6.5 %shard_map.87 = (f32[2,3,3,208,128]{4,3,2,1,0:T(8,128)S(1)}, f32[2,3,3,208,128]{4,3,2,1,0:T(8,128)S(1)}, f32[2,3,3,208,128]{4,3,2,1,0:T(8,128)S(1)}, f32[2,3,3,208,128]{4,3,2,1,0:T(8,128)S(1)}) custom-call(s32[1]{0:T(128)} %bitcast.c_ref, s32[64,8]{1,0:T(8,128)S(1)} %convert_bitcast_fusion.idx_ref, f32[3584,128]{1,0:T(8,128)S(1)} %bitcast.79), custom_call_target="tpu_custom_call" | custom-call | flops 100000000 | bytes 9504772 | tf_op jit(solution)/shard_map/pallas_call | solution.py:23
  54.6 2.6 collective-permute-start
  59.1 2.2 collective-permute-start.5
  65.0 6.9 %collective-permute-start.3 = (f32[3,3,208,128]{3,2,1,0:T(8,128)S(1)}, f32[3,3,208,128]{3,2,1,0:T(8,128)S(1)}, u32[]{:S(2)}, u32[]{:S(2)}) collective-permute-start(f32[3,3,208,128]{3,2,1,0:T(8,128)S(1)} %get-tuple-element.89.refs_2_), channel_id=1, source_target_pairs={{1,0},{2,1},{3,2},{4,3},{5,4},{6,5},{7,6},{8,7},{9,8},{10,9},{11,1... | collective-permute-start | bytes 2875400 | tf_op jit(solution)/shard_map/ppermute | solution.py:502
  76.8 17.1 %collective-permute-done.2.refs_4_ = f32[3,3,208,128]{3,2,1,0:T(8,128)S(1)} collective-permute-done((f32[3,3,208,128]{3,2,1,0:T(8,128)S(1)}, f32[3,3,208,128]{3,2,1,0:T(8,128)S(1)}, u32[]{:S(2)}, u32[]{:S(2)}) %collective-permute-start.2) | collective-permute-done | bytes 958496 | tf_op jit(solution)/shard_map/ppermute | solution.py:502
  94.0 3.0 shard_map.90
  97.1 6.9 %collective-permute-start.7 = (f32[3,3,208,128]{3,2,1,0:T(8,128)S(1)}, f32[3,3,208,128]{3,2,1,0:T(8,128)S(1)}, u32[]{:S(2)}, u32[]{:S(2)}) collective-permute-start(f32[3,3,208,128]{3,2,1,0:T(8,128)S(1)} %get-tuple-element.92.refs_2_), channel_id=1, source_target_pairs={{1,0},{2,1},{3,2},{4,3},{5,4},{6,5},{7,6},{8,7},{9,8},{10,9},{11,1... | collective-permute-start | bytes 2875400 | tf_op jit(solution)/shard_map/ppermute | solution.py:502
  104.0 20.1 %collective-permute-done.6.refs_4_ = f32[3,3,208,128]{3,2,1,0:T(8,128)S(1)} collective-permute-done((f32[3,3,208,128]{3,2,1,0:T(8,128)S(1)}, f32[3,3,208,128]{3,2,1,0:T(8,128)S(1)}, u32[]{:S(2)}, u32[]{:S(2)}) %collective-permute-start.6) | collective-permute-done | bytes 958496 | tf_op jit(solution)/shard_map/ppermute | solution.py:502
  125.1 2.6 shard_map.91
  127.8 6.9 %collective-permute-start.9 = (f32[2,3,208,128]{3,2,1,0:T(8,128)S(1)}, f32[2,3,208,128]{3,2,1,0:T(8,128)S(1)}, u32[]{:S(2)}, u32[]{:S(2)}) collective-permute-start(f32[2,3,208,128]{3,2,1,0:T(8,128)S(1)} %get-tuple-element.99.ss), channel_id=1, source_target_pairs={{1,0},{2,1},{3,2},{4,3},{5,4},{6,5},{7,6},{8,7},{9,8},{10,9},{11,1... | collective-permute-start | bytes 1916936 | tf_op jit(solution)/shard_map/ppermute | solution.py:502
  134.7 12.4 %collective-permute-done.8.rs = f32[2,3,208,128]{3,2,1,0:T(8,128)S(1)} collective-permute-done((f32[2,3,208,128]{3,2,1,0:T(8,128)S(1)}, f32[2,3,208,128]{3,2,1,0:T(8,128)S(1)}, u32[]{:S(2)}, u32[]{:S(2)}) %collective-permute-start.8) | collective-permute-done | bytes 639008 | tf_op jit(solution)/shard_map/ppermute | solution.py:502
  147.1 3.1 shard_map.93
  150.2 6.9 %collective-permute-start.11 = (f32[2,3,208,128]{3,2,1,0:T(8,128)S(1)}, f32[2,3,208,128]{3,2,1,0:T(8,128)S(1)}, u32[]{:S(2)}, u32[]{:S(2)}) collective-permute-start(f32[2,3,208,128]{3,2,1,0:T(8,128)S(1)} %get-tuple-element.103.ss), channel_id=1, source_target_pairs={{1,0},{2,1},{3,2},{4,3},{5,4},{6,5},{7,6},{8,7},{9,8},{10,9},{11,1... | collective-permute-start | bytes 1916936 | tf_op jit(solution)/shard_map/ppermute | solution.py:502
  160.3 8.2 %collective-permute-done.10.rs = f32[2,3,208,128]{3,2,1,0:T(8,128)S(1)} collective-permute-done((f32[2,3,208,128]{3,2,1,0:T(8,128)S(1)}, f32[2,3,208,128]{3,2,1,0:T(8,128)S(1)}, u32[]{:S(2)}, u32[]{:S(2)}) %collective-permute-start.10) | collective-permute-done | bytes 639008 | tf_op jit(solution)/shard_map/ppermute | solution.py:502
  168.6 2.7 shard_map.94
  171.3 3.9 collective-permute-start.12
  175.5 7.0 %collective-permute-start.15 = (f32[2,3,208,128]{3,2,1,0:T(8,128)S(1)}, f32[2,3,208,128]{3,2,1,0:T(8,128)S(1)}, u32[]{:S(2)}, u32[]{:S(2)}) collective-permute-start(f32[2,3,208,128]{3,2,1,0:T(8,128)S(1)} %pad_maximum_fusion.1), channel_id=1, source_target_pairs={{1,0},{2,1},{3,2},{4,3},{5,4},{6,5},{7,6},{8,7},{9,8},{10,9},{11,1... | collective-permute-start | bytes 1916936 | tf_op jit(solution)/shard_map/ppermute | solution.py:502
  184.6 6.9 %collective-permute-start.18 = (f32[2,3,208,128]{3,2,1,0:T(8,128)S(1)}, f32[2,3,208,128]{3,2,1,0:T(8,128)S(1)}, u32[]{:S(2)}, u32[]{:S(2)}) collective-permute-start(f32[2,3,208,128]{3,2,1,0:T(8,128)S(1)} %get-tuple-element.115.refs_2_), channel_id=1, source_target_pairs={{1,0},{2,1},{3,2},{4,3},{5,4},{6,5},{7,6},{8,7},{9,8},{10,9},{11,1... | collective-permute-start | bytes 1916936 | tf_op jit(solution)/shard_map/ppermute | solution.py:502
  191.8 5.0 %collective-permute-done.14.refs_7_ = f32[2,3,208,128]{3,2,1,0:T(8,128)S(1)} collective-permute-done((f32[2,3,208,128]{3,2,1,0:T(8,128)S(1)}, f32[2,3,208,128]{3,2,1,0:T(8,128)S(1)}, u32[]{:S(2)}, u32[]{:S(2)}) %collective-permute-start.14) | collective-permute-done | bytes 639008 | tf_op jit(solution)/shard_map/ppermute | solution.py:502
  196.8 3.1 shard_map.96
  203.5 7.0 %collective-permute-done.17.refs_4_ = f32[2,3,208,128]{3,2,1,0:T(8,128)S(1)} collective-permute-done((f32[2,3,208,128]{3,2,1,0:T(8,128)S(1)}, f32[2,3,208,128]{3,2,1,0:T(8,128)S(1)}, u32[]{:S(2)}, u32[]{:S(2)}) %collective-permute-start.17) | collective-permute-done | bytes 639008 | tf_op jit(solution)/shard_map/ppermute | solution.py:502
  214.3 4.0 shard_map.97
  221.2 6.9 %collective-permute-start.20 = (f32[2,3,208,128]{3,2,1,0:T(8,128)}, f32[2,3,208,128]{3,2,1,0:T(8,128)}, u32[]{:S(2)}, u32[]{:S(2)}) collective-permute-start(f32[2,3,208,128]{3,2,1,0:T(8,128)} %get-tuple-element.120.refs_2_), channel_id=1, source_target_pairs={{1,0},{2,1},{3,2},{4,3},{5,4},{6,5},{7,6},{8,7},{9,8},{10,9},{11,1... | collective-permute-start | bytes 1916936 | tf_op jit(solution)/shard_map/ppermute | solution.py:502
  234.4 12.2 %all_to_all.20 = f32[64,1,128]{2,1,0:T(1,128)S(1)} all-to-all(f32[64,1,128]{2,1,0:T(1,128)S(1)} %broadcast_in_dim.20), channel_id=1, replica_groups=mesh['tm'=2,'space'=64] {'space'}, dimensions={0} | all-to-all | bytes 65536 | tf_op jit(solution)/shard_map/all_to_all | solution.py:510
  254.5 4.2 shard_map.98
  259.0 6.6 %collective-permute-start.23 = (f32[2,3,208,128]{3,2,1,0:T(8,128)S(1)}, f32[2,3,208,128]{3,2,1,0:T(8,128)S(1)}, u32[]{:S(2)}, u32[]{:S(2)}) collective-permute-start(f32[2,3,208,128]{3,2,1,0:T(8,128)S(1)} %get-tuple-element.129.ss), channel_id=1, source_target_pairs={{1,0},{2,1},{3,2},{4,3},{5,4},{6,5},{7,6},{8,7},{9,8},{10,9},{11,1... | collective-permute-start | bytes 1916936 | tf_op jit(solution)/shard_map/ppermute | solution.py:502
  266.7 11.9 %collective-permute-done.22.rs = f32[2,3,208,128]{3,2,1,0:T(8,128)S(1)} collective-permute-done((f32[2,3,208,128]{3,2,1,0:T(8,128)S(1)}, f32[2,3,208,128]{3,2,1,0:T(8,128)S(1)}, u32[]{:S(2)}, u32[]{:S(2)}) %collective-permute-start.22) | collective-permute-done | bytes 639008 | tf_op jit(solution)/shard_map/ppermute | solution.py:502
  278.6 3.1 shard_map.100
  281.8 6.9 %collective-permute-start.25 = (f32[2,3,208,128]{3,2,1,0:T(8,128)S(1)}, f32[2,3,208,128]{3,2,1,0:T(8,128)S(1)}, u32[]{:S(2)}, u32[]{:S(2)}) collective-permute-start(f32[2,3,208,128]{3,2,1,0:T(8,128)S(1)} %get-tuple-element.133.ss), channel_id=1, source_target_pairs={{1,0},{2,1},{3,2},{4,3},{5,4},{6,5},{7,6},{8,7},{9,8},{10,9},{11,1... | collective-permute-start | bytes 1916936 | tf_op jit(solution)/shard_map/ppermute | solution.py:502
  289.3 11.4 %collective-permute-done.24.rs = f32[2,3,208,128]{3,2,1,0:T(8,128)S(1)} collective-permute-done((f32[2,3,208,128]{3,2,1,0:T(8,128)S(1)}, f32[2,3,208,128]{3,2,1,0:T(8,128)S(1)}, u32[]{:S(2)}, u32[]{:S(2)}) %collective-permute-start.24) | collective-permute-done | bytes 639008 | tf_op jit(solution)/shard_map/ppermute | solution.py:502
  300.7 3.5 shard_map.101
  306.3 3.3 collective-permute-start.26
  313.5 17.4 %all_to_all.21 = f32[64,1,128]{2,1,0:T(1,128)S(1)} all-to-all(f32[64,1,128]{2,1,0:T(1,128)S(1)} %broadcast_in_dim.21), channel_id=1, replica_groups=mesh['tm'=2,'space'=64] {'space'}, dimensions={0} | all-to-all | bytes 65536 | tf_op jit(solution)/shard_map/all_to_all | solution.py:510
  337.2 3.1 shard_map.102
  340.6 6.6 %collective-permute-start.30 = (f32[2,3,208,128]{3,2,1,0:T(8,128)S(1)}, f32[2,3,208,128]{3,2,1,0:T(8,128)S(1)}, u32[]{:S(2)}, u32[]{:S(2)}) collective-permute-start(f32[2,3,208,128]{3,2,1,0:T(8,128)S(1)} %get-tuple-element.150.refs_2_), channel_id=1, source_target_pairs={{1,0},{2,1},{3,2},{4,3},{5,4},{6,5},{7,6},{8,7},{9,8},{10,9},{11,1... | collective-permute-start | bytes 1916936 | tf_op jit(solution)/shard_map/ppermute | solution.py:502
  350.6 6.2 %shard_map.103 = (f32[3,5,208,128]{3,2,1,0:T(8,128)}, f32[3,3,208,128]{3,2,1,0:T(8,128)}, f32[3,5,208,128]{3,2,1,0:T(8,128)}, f32[3,5,208,128]{3,2,1,0:T(8,128)S...) custom-call(f32[3,5,208,128]{3,2,1,0:T(8,128)} %copy-done.49, ...), custom_call_target="tpu_custom_call" | custom-call | flops 100000000 | bytes 21164036 | tf_op jit(solution)/shard_map/pallas_call | solution.py:23
  361.4 4.0 shard_map.105
  368.3 6.9 %collective-permute-start.32 = (f32[2,3,208,128]{3,2,1,0:T(8,128)}, f32[2,3,208,128]{3,2,1,0:T(8,128)}, u32[]{:S(2)}, u32[]{:S(2)}) collective-permute-start(f32[2,3,208,128]{3,2,1,0:T(8,128)} %get-tuple-element.155.refs_2_), channel_id=1, source_target_pairs={{1,0},{2,1},{3,2},{4,3},{5,4},{6,5},{7,6},{8,7},{9,8},{10,9},{11,1... | collective-permute-start | bytes 1916936 | tf_op jit(solution)/shard_map/ppermute | solution.py:502
  375.8 3.1 collective-permute-start.27
  381.9 4.6 %all-to-all-start.3 = ((f32[64,1,128]{2,1,0:T(1,128)}), f32[64,1,128]{2,1,0:T(1,128)S(1)}, u32[]{:S(2)}, u32[]{:S(2)}) async-start(f32[64,1,128]{2,1,0:T(1,128)} %broadcast_in_dim.22), calls=%async_computation.3 | async-start | bytes 65536 | tf_op jit(solution)/shard_map/all_to_all | solution.py:510
  388.3 6.5 %all-to-all-done.3 = f32[64,1,128]{2,1,0:T(1,128)S(1)} async-done(((f32[64,1,128]{2,1,0:T(1,128)}), f32[64,1,128]{2,1,0:T(1,128)S(1)}, u32[]{:S(2)}, u32[]{:S(2)}) %all-to-all-start.3) | async-done | bytes 32800 | tf_op jit(solution)/shard_map/all_to_all | solution.py:510
  404.7 2.8 shard_map.104
  410.9 3.1 shard_map.106
  415.3 4.3 %shard_map.107 = (f32[2,3,3,192,128]{4,3,2,1,0:T(8,128)}, f32[2,3,3,192,128]{4,3,2,1,0:T(8,128)}) custom-call(s32[1]{0:T(128)} %bitcast.c_ref, f32[3]{0:T(128)S(1)} %pad_maximum_fusion.8.sc, f32[3,3,208,128]{3,2,1,0:T(8,128)S(1)} %copy-done.29, f32[3,5,208,128]{3,2,1,0:T(8,128)S(1)} %copy-done.6, f32[3,3,208,128]{3,2,1,0:T(8,128)S(1)} %copy-done.34, ...), custom_call_target="tpu_custom_call" | custom-call | flops 100000000 | bytes 18874384 | tf_op jit(solution)/shard_map/pallas_call | solution.py:23
  419.6 2.2 fusion
  423.5 2.2 fusion.1
  (314 shorter events, 95.8 us)
Async XLA Ops:
  5.2 37.0 %all-to-all-start = ((f32[64,7,8,128]{3,2,1,0:T(8,128)}), f32[64,7,8,128]{3,2,1,0:T(8,128)S(1)}, u32[]{:S(2)}, u32[]{:S(2)}) async-start(f32[64,7,8,128]{3,2,1,0:T(8,128)} %copy-done.47), calls=%async_computation | async-start | bytes 3670016 | tf_op jit(solution)/shard_map/all_to_all | solution.py:530
  20.0 33.6 %copy-start.56 = (bf16[256,256]{1,0:T(8,128)(2,1)}, bf16[256,256]{1,0:T(8,128)(2,1)S(1)}, u32[]{:S(2)}) copy-start(bf16[256,256]{1,0:T(8,128)(2,1)S(1)} %get-tuple-element.101.rf) | copy-start | bytes 393220
  20.0 74.0 %copy-start.21 = (bf16[256,256]{1,0:T(8,128)(2,1)}, bf16[256,256]{1,0:T(8,128)(2,1)S(1)}, u32[]{:S(2)}) copy-start(bf16[256,256]{1,0:T(8,128)(2,1)S(1)} %get-tuple-element.87.ra_ref.refs_11_.refs_9_.refs_4_) | copy-start | bytes 393220
  20.0 37.4 %collective-permute-start.1 = (f32[2,2,3,208,128]{4,3,2,1,0:T(8,128)}, f32[2,2,3,208,128]{4,3,2,1,0:T(8,128)}, u32[]{:S(2)}, u32[]{:S(2)}) collective-permute-start(f32[2,2,3,208,128]{4,3,2,1,0:T(8,128)} %get-tuple-element.85), channel_id=1, source_target_pairs={{0,64},{64,0},{1,65},{65,1},{2,66},{66,2},{3,67},{67,3},{4,68},{68... | collective-permute-start | bytes 3833864 | tf_op jit(solution)/shard_map/ppermute | solution.py:499
  54.6 6.8 %collective-permute-start = (f32[2,3,3,208,128]{4,3,1,2,0:T(8,128)}, f32[2,3,3,208,128]{4,3,1,2,0:T(8,128)}, u32[]{:S(2)}, u32[]{:S(2)}) collective-permute-start(f32[2,3,3,208,128]{4,3,1,2,0:T(8,128)} %copy.84), channel_id=1, source_target_pairs={{0,64},{64,0},{1,65},{65,1},{2,66},{66,2},{3,67},{67,3},{4,68},{68... | collective-permute-start | bytes 5750792 | tf_op jit(solution)/shard_map/ppermute | solution.py:499
  59.1 153.1 %copy-start.15 = (f32[2,3,208,128]{3,2,1,0:T(8,128)}, f32[2,3,208,128]{3,2,1,0:T(8,128)S(1)}, u32[]{:S(2)}) copy-start(f32[2,3,208,128]{3,2,1,0:T(8,128)S(1)} %get-tuple-element.188.refs_10_.w1) | copy-start | bytes 1916932
  59.1 12.8 %collective-permute-start.5 = (f32[2,208,128]{2,1,0:T(8,128)S(1)}, f32[2,208,128]{2,1,0:T(8,128)S(1)}, u32[]{:S(2)}, u32[]{:S(2)}) collective-permute-start(f32[2,208,128]{2,1,0:T(8,128)S(1)} %pad_maximum_fusion.3), channel_id=1, source_target_pairs={{1,0},{2,1},{3,2},{4,3},{5,4},{6,5},{7,6},{8,7},{9,8},{10,9},{11,1... | collective-permute-start | bytes 638984 | tf_op jit(solution)/shard_map/ppermute | solution.py:502
  61.4 12.1 %collective-permute-start.4 = (f32[2,208,128]{2,1,0:T(8,128)S(1)}, f32[2,208,128]{2,1,0:T(8,128)S(1)}, u32[]{:S(2)}, u32[]{:S(2)}) collective-permute-start(f32[2,208,128]{2,1,0:T(8,128)S(1)} %pad_maximum_fusion.2), channel_id=1, source_target_pairs={{0,1},{1,2},{2,3},{3,4},{4,5},{5,6},{6,7},{7,8},{8,9},{9,10},{10,1... | collective-permute-start | bytes 638984 | tf_op jit(solution)/shard_map/ppermute | solution.py:502
  64.9 29.0 %collective-permute-start.2 = (f32[3,3,208,128]{3,2,1,0:T(8,128)S(1)}, f32[3,3,208,128]{3,2,1,0:T(8,128)S(1)}, u32[]{:S(2)}, u32[]{:S(2)}) collective-permute-start(f32[3,3,208,128]{3,2,1,0:T(8,128)S(1)} %get-tuple-element.90.refs_3_), channel_id=1, source_target_pairs={{0,1},{1,2},{2,3},{3,4},{4,5},{5,6},{6,7},{7,8},{8,9},{9,10},{10,1... | collective-permute-start | bytes 2875400 | tf_op jit(solution)/shard_map/ppermute | solution.py:502
  65.0 28.9 %collective-permute-start.3 = (f32[3,3,208,128]{3,2,1,0:T(8,128)S(1)}, f32[3,3,208,128]{3,2,1,0:T(8,128)S(1)}, u32[]{:S(2)}, u32[]{:S(2)}) collective-permute-start(f32[3,3,208,128]{3,2,1,0:T(8,128)S(1)} %get-tuple-element.89.refs_2_), channel_id=1, source_target_pairs={{1,0},{2,1},{3,2},{4,3},{5,4},{6,5},{7,6},{8,7},{9,8},{10,9},{11,1... | collective-permute-start | bytes 2875400 | tf_op jit(solution)/shard_map/ppermute | solution.py:502
  74.8 82.3 %collective-permute-start.13 = (f32[2,3,3,208,128]{4,3,1,2,0:T(8,128)}, f32[2,3,3,208,128]{4,3,1,2,0:T(8,128)}, u32[]{:S(2)}, u32[]{:S(2)}) collective-permute-start(f32[2,3,3,208,128]{4,3,1,2,0:T(8,128)} %copy.93), channel_id=1, source_target_pairs={{0,64},{64,0},{1,65},{65,1},{2,66},{66,2},{3,67},{67,3},{4,68},{68... | collective-permute-start | bytes 5750792 | tf_op jit(solution)/shard_map/ppermute | solution.py:499
  76.7 135.5 %copy-start.44 = (f32[2,208,128]{2,1,0:T(8,128)}, f32[2,208,128]{2,1,0:T(8,128)S(1)}, u32[]{:S(2)}) copy-start(f32[2,208,128]{2,1,0:T(8,128)S(1)} %pad_maximum_fusion.4.refs_9_.wh2) | copy-start | bytes 638980
  97.0 131.1 %copy-start = (f32[3,5,208,128]{3,2,1,0:T(8,128)}, f32[3,5,208,128]{3,2,1,0:T(8,128)S(1)}, u32[]{:S(2)}) copy-start(f32[3,5,208,128]{3,2,1,0:T(8,128)S(1)} %get-tuple-element.97.v3.g3.refs_7_) | copy-start | bytes 4792324
  97.0 131.0 %copy-start.7 = (f32[3,3,208,128]{3,2,1,0:T(8,128)}, f32[3,3,208,128]{3,2,1,0:T(8,128)S(1)}, u32[]{:S(2)}) copy-start(f32[3,3,208,128]{3,2,1,0:T(8,128)S(1)} %get-tuple-element.96.v2.g2.refs_6_) | copy-start | bytes 2875396
  97.0 27.1 %collective-permute-start.6 = (f32[3,3,208,128]{3,2,1,0:T(8,128)S(1)}, f32[3,3,208,128]{3,2,1,0:T(8,128)S(1)}, u32[]{:S(2)}, u32[]{:S(2)}) collective-permute-start(f32[3,3,208,128]{3,2,1,0:T(8,128)S(1)} %get-tuple-element.93.refs_3_), channel_id=1, source_target_pairs={{0,1},{1,2},{2,3},{3,4},{4,5},{5,6},{6,7},{7,8},{8,9},{9,10},{10,1... | collective-permute-start | bytes 2875400 | tf_op jit(solution)/shard_map/ppermute | solution.py:502
  97.1 27.1 %collective-permute-start.7 = (f32[3,3,208,128]{3,2,1,0:T(8,128)S(1)}, f32[3,3,208,128]{3,2,1,0:T(8,128)S(1)}, u32[]{:S(2)}, u32[]{:S(2)}) collective-permute-start(f32[3,3,208,128]{3,2,1,0:T(8,128)S(1)} %get-tuple-element.92.refs_2_), channel_id=1, source_target_pairs={{1,0},{2,1},{3,2},{4,3},{5,4},{6,5},{7,6},{8,7},{9,8},{10,9},{11,1... | collective-permute-start | bytes 2875400 | tf_op jit(solution)/shard_map/ppermute | solution.py:502
  104.0 43.0 %copy-start.41 = (f32[2,208,128]{2,1,0:T(8,128)}, f32[2,208,128]{2,1,0:T(8,128)S(1)}, u32[]{:S(2)}) copy-start(f32[2,208,128]{2,1,0:T(8,128)S(1)} %pad_maximum_fusion.5.refs_8_.wh0) | copy-start | bytes 638980
  127.7 100.4 %copy-start.11 = (f32[3,3,208,128]{3,2,1,0:T(8,128)}, f32[3,3,208,128]{3,2,1,0:T(8,128)S(1)}, u32[]{:S(2)}) copy-start(f32[3,3,208,128]{3,2,1,0:T(8,128)S(1)} %get-tuple-element.94.v0.refs_11_.g0.refs_4_) | copy-start | bytes 2875396
  127.7 19.4 %collective-permute-start.8 = (f32[2,3,208,128]{3,2,1,0:T(8,128)S(1)}, f32[2,3,208,128]{3,2,1,0:T(8,128)S(1)}, u32[]{:S(2)}, u32[]{:S(2)}) collective-permute-start(f32[2,3,208,128]{3,2,1,0:T(8,128)S(1)} %get-tuple-element.100.sn), channel_id=1, source_target_pairs={{0,1},{1,2},{2,3},{3,4},{4,5},{5,6},{6,7},{7,8},{8,9},{9,10},{10,1... | collective-permute-start | bytes 1916936 | tf_op jit(solution)/shard_map/ppermute | solution.py:502
  127.8 19.3 %collective-permute-start.9 = (f32[2,3,208,128]{3,2,1,0:T(8,128)S(1)}, f32[2,3,208,128]{3,2,1,0:T(8,128)S(1)}, u32[]{:S(2)}, u32[]{:S(2)}) collective-permute-start(f32[2,3,208,128]{3,2,1,0:T(8,128)S(1)} %get-tuple-element.99.ss), channel_id=1, source_target_pairs={{1,0},{2,1},{3,2},{4,3},{5,4},{6,5},{7,6},{8,7},{9,8},{10,9},{11,1... | collective-permute-start | bytes 1916936 | tf_op jit(solution)/shard_map/ppermute | solution.py:502
  150.1 18.4 %collective-permute-start.10 = (f32[2,3,208,128]{3,2,1,0:T(8,128)S(1)}, f32[2,3,208,128]{3,2,1,0:T(8,128)S(1)}, u32[]{:S(2)}, u32[]{:S(2)}) collective-permute-start(f32[2,3,208,128]{3,2,1,0:T(8,128)S(1)} %get-tuple-element.104.sn), channel_id=1, source_target_pairs={{0,1},{1,2},{2,3},{3,4},{4,5},{5,6},{6,7},{7,8},{8,9},{9,10},{10,1... | collective-permute-start | bytes 1916936 | tf_op jit(solution)/shard_map/ppermute | solution.py:502
  150.2 18.4 %collective-permute-start.11 = (f32[2,3,208,128]{3,2,1,0:T(8,128)S(1)}, f32[2,3,208,128]{3,2,1,0:T(8,128)S(1)}, u32[]{:S(2)}, u32[]{:S(2)}) collective-permute-start(f32[2,3,208,128]{3,2,1,0:T(8,128)S(1)} %get-tuple-element.103.ss), channel_id=1, source_target_pairs={{1,0},{2,1},{3,2},{4,3},{5,4},{6,5},{7,6},{8,7},{9,8},{10,9},{11,1... | collective-permute-start | bytes 1916936 | tf_op jit(solution)/shard_map/ppermute | solution.py:502
  160.3 22.1 %copy-start.30 = (f32[3,3,208,128]{3,2,1,0:T(8,128)}, f32[3,3,208,128]{3,2,1,0:T(8,128)S(1)}, u32[]{:S(2)}) copy-start(f32[3,3,208,128]{3,2,1,0:T(8,128)S(1)} %copy.95.refs_2_) | copy-start | bytes 2875396
  171.3 11.2 %collective-permute-start.12 = (f32[3,16,16,128]{3,2,1,0:T(8,128)S(1)}, f32[3,16,16,128]{3,2,1,0:T(8,128)S(1)}, u32[]{:S(2)}, u32[]{:S(2)}) collective-permute-start(f32[3,16,16,128]{3,2,1,0:T(8,128)S(1)} %get-tuple-element.108), channel_id=1, source_target_pairs={{0,64},{64,0},{1,65},{65,1},{2,66},{66,2},{3,67},{67,3},{4,68},{68... | collective-permute-start | bytes 1179656 | tf_op jit(solution)/shard_map/ppermute | solution.py:499
  175.3 21.5 %collective-permute-start.14 = (f32[2,3,208,128]{3,2,1,0:T(8,128)S(1)}, f32[2,3,208,128]{3,2,1,0:T(8,128)S(1)}, u32[]{:S(2)}, u32[]{:S(2)}) collective-permute-start(f32[2,3,208,128]{3,2,1,0:T(8,128)S(1)} %pad_maximum_fusion), channel_id=1, source_target_pairs={{0,1},{1,2},{2,3},{3,4},{4,5},{5,6},{6,7},{7,8},{8,9},{9,10},{10,1... | collective-permute-start | bytes 1916936 | tf_op jit(solution)/shard_map/ppermute | solution.py:502
  175.5 21.3 %collective-permute-start.15 = (f32[2,3,208,128]{3,2,1,0:T(8,128)S(1)}, f32[2,3,208,128]{3,2,1,0:T(8,128)S(1)}, u32[]{:S(2)}, u32[]{:S(2)}) collective-permute-start(f32[2,3,208,128]{3,2,1,0:T(8,128)S(1)} %pad_maximum_fusion.1), channel_id=1, source_target_pairs={{1,0},{2,1},{3,2},{4,3},{5,4},{6,5},{7,6},{8,7},{9,8},{10,9},{11,1... | collective-permute-start | bytes 1916936 | tf_op jit(solution)/shard_map/ppermute | solution.py:502
  184.6 25.9 %collective-permute-start.17 = (f32[2,3,208,128]{3,2,1,0:T(8,128)S(1)}, f32[2,3,208,128]{3,2,1,0:T(8,128)S(1)}, u32[]{:S(2)}, u32[]{:S(2)}) collective-permute-start(f32[2,3,208,128]{3,2,1,0:T(8,128)S(1)} %get-tuple-element.116.refs_3_), channel_id=1, source_target_pairs={{0,1},{1,2},{2,3},{3,4},{4,5},{5,6},{6,7},{7,8},{8,9},{9,10},{10,1... | collective-permute-start | bytes 1916936 | tf_op jit(solution)/shard_map/ppermute | solution.py:502
  184.6 26.7 %collective-permute-start.18 = (f32[2,3,208,128]{3,2,1,0:T(8,128)S(1)}, f32[2,3,208,128]{3,2,1,0:T(8,128)S(1)}, u32[]{:S(2)}, u32[]{:S(2)}) collective-permute-start(f32[2,3,208,128]{3,2,1,0:T(8,128)S(1)} %get-tuple-element.115.refs_2_), channel_id=1, source_target_pairs={{1,0},{2,1},{3,2},{4,3},{5,4},{6,5},{7,6},{8,7},{9,8},{10,9},{11,1... | collective-permute-start | bytes 1916936 | tf_op jit(solution)/shard_map/ppermute | solution.py:502
  221.2 27.9 %collective-permute-start.19 = (f32[2,3,208,128]{3,2,1,0:T(8,128)}, f32[2,3,208,128]{3,2,1,0:T(8,128)}, u32[]{:S(2)}, u32[]{:S(2)}) collective-permute-start(f32[2,3,208,128]{3,2,1,0:T(8,128)} %get-tuple-element.121.refs_3_), channel_id=1, source_target_pairs={{0,1},{1,2},{2,3},{3,4},{4,5},{5,6},{6,7},{7,8},{8,9},{9,10},{10,1... | collective-permute-start | bytes 1916936 | tf_op jit(solution)/shard_map/ppermute | solution.py:502
  221.2 27.9 %collective-permute-start.20 = (f32[2,3,208,128]{3,2,1,0:T(8,128)}, f32[2,3,208,128]{3,2,1,0:T(8,128)}, u32[]{:S(2)}, u32[]{:S(2)}) collective-permute-start(f32[2,3,208,128]{3,2,1,0:T(8,128)} %get-tuple-element.120.refs_2_), channel_id=1, source_target_pairs={{1,0},{2,1},{3,2},{4,3},{5,4},{6,5},{7,6},{8,7},{9,8},{10,9},{11,1... | collective-permute-start | bytes 1916936 | tf_op jit(solution)/shard_map/ppermute | solution.py:502
  230.9 2.2 collective-permute-start.16
  258.7 19.9 %collective-permute-start.22 = (f32[2,3,208,128]{3,2,1,0:T(8,128)S(1)}, f32[2,3,208,128]{3,2,1,0:T(8,128)S(1)}, u32[]{:S(2)}, u32[]{:S(2)}) collective-permute-start(f32[2,3,208,128]{3,2,1,0:T(8,128)S(1)} %get-tuple-element.130.sn), channel_id=1, source_target_pairs={{0,1},{1,2},{2,3},{3,4},{4,5},{5,6},{6,7},{7,8},{8,9},{9,10},{10,1... | collective-permute-start | bytes 1916936 | tf_op jit(solution)/shard_map/ppermute | solution.py:502
  259.0 19.6 %collective-permute-start.23 = (f32[2,3,208,128]{3,2,1,0:T(8,128)S(1)}, f32[2,3,208,128]{3,2,1,0:T(8,128)S(1)}, u32[]{:S(2)}, u32[]{:S(2)}) collective-permute-start(f32[2,3,208,128]{3,2,1,0:T(8,128)S(1)} %get-tuple-element.129.ss), channel_id=1, source_target_pairs={{1,0},{2,1},{3,2},{4,3},{5,4},{6,5},{7,6},{8,7},{9,8},{10,9},{11,1... | collective-permute-start | bytes 1916936 | tf_op jit(solution)/shard_map/ppermute | solution.py:502
  266.7 34.0 %copy-start.18 = (f32[3,5,208,128]{3,2,1,0:T(8,128)}, f32[3,5,208,128]{3,2,1,0:T(8,128)S(1)}, u32[]{:S(2)}) copy-start(f32[3,5,208,128]{3,2,1,0:T(8,128)S(1)} %get-tuple-element.135.v3.refs_3_) | copy-start | bytes 4792324
  281.7 22.5 %copy-start.49 = (f32[3,5,208,128]{3,2,1,0:T(8,128)}, f32[3,5,208,128]{3,2,1,0:T(8,128)S(1)}, u32[]{:S(2)}) copy-start(f32[3,5,208,128]{3,2,1,0:T(8,128)S(1)} %get-tuple-element.136.x0.refs_0_) | copy-start | bytes 4792324
  281.7 22.5 %copy-start.50 = (f32[3,3,208,128]{3,2,1,0:T(8,128)}, f32[3,3,208,128]{3,2,1,0:T(8,128)S(1)}, u32[]{:S(2)}) copy-start(f32[3,3,208,128]{3,2,1,0:T(8,128)S(1)} %get-tuple-element.137.x1.refs_1_) | copy-start | bytes 2875396
  281.7 19.0 %collective-permute-start.24 = (f32[2,3,208,128]{3,2,1,0:T(8,128)S(1)}, f32[2,3,208,128]{3,2,1,0:T(8,128)S(1)}, u32[]{:S(2)}, u32[]{:S(2)}) collective-permute-start(f32[2,3,208,128]{3,2,1,0:T(8,128)S(1)} %get-tuple-element.134.sn), channel_id=1, source_target_pairs={{0,1},{1,2},{2,3},{3,4},{4,5},{5,6},{6,7},{7,8},{8,9},{9,10},{10,1... | collective-permute-start | bytes 1916936 | tf_op jit(solution)/shard_map/ppermute | solution.py:502
  281.8 18.9 %collective-permute-start.25 = (f32[2,3,208,128]{3,2,1,0:T(8,128)S(1)}, f32[2,3,208,128]{3,2,1,0:T(8,128)S(1)}, u32[]{:S(2)}, u32[]{:S(2)}) collective-permute-start(f32[2,3,208,128]{3,2,1,0:T(8,128)S(1)} %get-tuple-element.133.ss), channel_id=1, source_target_pairs={{1,0},{2,1},{3,2},{4,3},{5,4},{6,5},{7,6},{8,7},{9,8},{10,9},{11,1... | collective-permute-start | bytes 1916936 | tf_op jit(solution)/shard_map/ppermute | solution.py:502
  306.3 26.4 %collective-permute-start.26 = (f32[3,16,16,128]{3,2,1,0:T(8,128)}, f32[3,16,16,128]{3,2,1,0:T(8,128)}, u32[]{:S(2)}, u32[]{:S(2)}) collective-permute-start(f32[3,16,16,128]{3,2,1,0:T(8,128)} %get-tuple-element.139), channel_id=1, source_target_pairs={{0,64},{64,0},{1,65},{65,1},{2,66},{66,2},{3,67},{67,3},{4,68},{68... | collective-permute-start | bytes 1179656 | tf_op jit(solution)/shard_map/ppermute | solution.py:499
  310.8 1.4 collective-permute-start.21
  340.3 19.7 %collective-permute-start.29 = (f32[2,3,208,128]{3,2,1,0:T(8,128)S(1)}, f32[2,3,208,128]{3,2,1,0:T(8,128)S(1)}, u32[]{:S(2)}, u32[]{:S(2)}) collective-permute-start(f32[2,3,208,128]{3,2,1,0:T(8,128)S(1)} %get-tuple-element.151.refs_3_), channel_id=1, source_target_pairs={{0,1},{1,2},{2,3},{3,4},{4,5},{5,6},{6,7},{7,8},{8,9},{9,10},{10,1... | collective-permute-start | bytes 1916936 | tf_op jit(solution)/shard_map/ppermute | solution.py:502
  340.6 19.4 %collective-permute-start.30 = (f32[2,3,208,128]{3,2,1,0:T(8,128)S(1)}, f32[2,3,208,128]{3,2,1,0:T(8,128)S(1)}, u32[]{:S(2)}, u32[]{:S(2)}) collective-permute-start(f32[2,3,208,128]{3,2,1,0:T(8,128)S(1)} %get-tuple-element.150.refs_2_), channel_id=1, source_target_pairs={{1,0},{2,1},{3,2},{4,3},{5,4},{6,5},{7,6},{8,7},{9,8},{10,9},{11,1... | collective-permute-start | bytes 1916936 | tf_op jit(solution)/shard_map/ppermute | solution.py:502
  368.3 40.7 %collective-permute-start.31 = (f32[2,3,208,128]{3,2,1,0:T(8,128)}, f32[2,3,208,128]{3,2,1,0:T(8,128)S(1)}, u32[]{:S(2)}, u32[]{:S(2)}) collective-permute-start(f32[2,3,208,128]{3,2,1,0:T(8,128)} %get-tuple-element.156.refs_3_), channel_id=1, source_target_pairs={{0,1},{1,2},{2,3},{3,4},{4,5},{5,6},{6,7},{7,8},{8,9},{9,10},{10,1... | collective-permute-start | bytes 1916936 | tf_op jit(solution)/shard_map/ppermute | solution.py:502
  368.3 41.5 %collective-permute-start.32 = (f32[2,3,208,128]{3,2,1,0:T(8,128)}, f32[2,3,208,128]{3,2,1,0:T(8,128)}, u32[]{:S(2)}, u32[]{:S(2)}) collective-permute-start(f32[2,3,208,128]{3,2,1,0:T(8,128)} %get-tuple-element.155.refs_2_), channel_id=1, source_target_pairs={{1,0},{2,1},{3,2},{4,3},{5,4},{6,5},{7,6},{8,7},{9,8},{10,9},{11,1... | collective-permute-start | bytes 1916936 | tf_op jit(solution)/shard_map/ppermute | solution.py:502
  375.8 4.2 collective-permute-start.27
  381.9 12.9 %all-to-all-start.3 = ((f32[64,1,128]{2,1,0:T(1,128)}), f32[64,1,128]{2,1,0:T(1,128)S(1)}, u32[]{:S(2)}, u32[]{:S(2)}) async-start(f32[64,1,128]{2,1,0:T(1,128)} %broadcast_in_dim.22), calls=%async_computation.3 | async-start | bytes 65536 | tf_op jit(solution)/shard_map/all_to_all | solution.py:510
  407.5 12.1 %collective-permute-start.28 = (f32[2,3,3,192,128]{4,3,2,1,0:T(8,128)}, f32[2,3,3,192,128]{4,3,2,1,0:T(8,128)S(1)}, u32[]{:S(2)}, u32[]{:S(2)}) collective-permute-start(f32[2,3,3,192,128]{4,3,2,1,0:T(8,128)} %get-tuple-element.148), channel_id=1, source_target_pairs={{0,64},{64,0},{1,65},{65,1},{2,66},{66,2},{3,67},{67,3},{4,68},{68... | collective-permute-start | bytes 5308424 | tf_op jit(solution)/shard_map/ppermute | solution.py:499
  419.6 3.9 collective-permute-start.33
  (91 other events, 455.4 us)

commit v2 on v1

--- a/solution.py
+++ b/solution.py
@@ -9,6 +9,7 @@
 FIELDS = 3
 MIXC = 0.25
 SCALE_Q = 0.5
+GROUPS = (3,)
 PAD = 8
 F32 = jnp.float32
 BF16 = jnp.bfloat16
@@ -17,16 +18,16 @@
 SM = pl.BlockSpec(memory_space=pltpu.SMEM)
 
 
-def call(body, ins, specs, outs, vmem=None, flops=1e8, scratch=()):
+def call(body, ins, specs, outs, vmem=None, flops=1e8, scratch=(), out_specs=None):
     nbytes = sum(a.size * a.dtype.itemsize for a in ins)
     nbytes += sum(o.size * o.dtype.itemsize for o in outs)
     return pl.pallas_call(
         body,
         out_shape=outs,
         in_specs=specs,
-        out_specs=[VM] * len(outs),
+        out_specs=out_specs or [VM] * len(outs),
         scratch_shapes=list(scratch),
-        compiler_params=pltpu.CompilerParams(vmem_limit_bytes=vmem or 40 * 2**20),
+        compiler_params=pltpu.CompilerParams(vmem_limit_bytes=vmem or 6 * 2**20),
         cost_estimate=pl.CostEstimate(
             flops=int(flops), bytes_accessed=int(nbytes), transcendentals=0
         ),
@@ -134,12 +135,25 @@
     return out
 
 
-def fields(body):
+def fields(n, body):
+    if n == 1:
+        body(0)
+        return
+
     def step(f, carry):
         body(f)
         return carry
 
-    lax.fori_loop(0, FIELDS, step, 0)
+    lax.fori_loop(0, n, step, 0)
+
+
+def tot(s_ref, i):
+    return jnp.sum(s_ref[i], keepdims=True)
+
+
+def first_step(s_ref):
+    rr = tot(s_ref, 0)
+    return rr / (rr + tot(s_ref, 1))
 
 
 def fold(x):
@@ -230,6 +244,33 @@
         ref[...] = jnp.concatenate([line, line], axis=0)
 
 
+def pick_body(f0, c_ref, own_ref, got_ref, *outs):
+    c = c_ref[0]
+    nf = outs[0].shape[0]
+
+    def put(src, dst):
+        for w in range(2):
+            for f in range(nf):
+                dst[w][f] = src[w, f0 + f]
+
+    @pl.when(c == 0)
+    def _():
+        put(own_ref, outs[:2])
+        put(got_ref, outs[2:4])
+
+    @pl.when(c != 0)
+    def _():
+        put(got_ref, outs[:2])
+        put(own_ref, outs[2:4])
+
+
+def pick_wind_body(c_ref, own_ref, got_ref, w0, w1, w2, w3, ss, sn):
+    pick_body(0, c_ref, own_ref, got_ref, w0, w1, w2, w3)
+    for k, w in enumerate((w0, w2)):
+        ss[k] = jnp.maximum(w[1, 0], 0.0)
+        sn[k] = jnp.maximum(-w[1, 2], 0.0)
+
+
 def turn_first_body(g3_ref, g2_ref, w3_ref, ra_ref, mid_ref, ss_ref, sn_ref):
     rhs = ra_ref[...]
 
@@ -238,7 +279,7 @@
         ss_ref[2, f] = g2_ref[f, 0]
         sn_ref[2, f] = g2_ref[f, 2]
 
-    fields(one)
+    fields(g3_ref.shape[0], one)
 
 
 def five(f, f_ref, rs_ref, rn_ref, ext):
@@ -270,7 +311,7 @@
             ss_o[2, f] = g0[f, 0]
             sn_o[2, f] = g0[f, 2]
 
-    fields(one)
+    fields(mid.shape[0], one)
 
 
 def adj_last_body(mode, *refs):
@@ -283,6 +324,8 @@
     outs = refs[n:]
     fs, fn = fl[0], fl[1]
     rhs = ra[...]
+    if mode == 1:
+        a = first_step(sc)
 
     def one(f):
         lam = adj_post(f, mid, ss, sn, rs, rn, fs, fn)
@@ -290,7 +333,6 @@
         out = adj_second([lam[i] + src[i] for i in range(5)], w0, wh0, rhs)
         one_half = [x * SCALE_Q for x in lam]
         if mode == 1:
-            a = sc[0]
             one_half = [(1.0 - a) * g1[f, i] - a * one_half[i] for i in range(5)]
             out = [(1.0 - a) * g0[f, i] - a * out[i] for i in range(3)]
         for i in range(5):
@@ -300,7 +342,7 @@
         if mode < 2:
             fwd_pre(f, out, w0, *outs[2:5])
 
-    fields(one)
+    fields(mid.shape[0], one)
 
 
 def fwd_first_body(fl, mid, ss, sn, rs, rn, v1, v2, w0, wh0, w1, w2, rf, *outs):
@@ -317,7 +359,7 @@
             x1[f, i] = x3[i]
         fwd_pre(f, [x3[i] + SCALE_Q * v2[f, i] for i in range(3)], w2, mid_o, ss_o, sn_o)
 
-    fields(one)
+    fields(mid.shape[0], one)
 
 
 def edge(x, half):
@@ -341,7 +383,7 @@
             eg[f, 13 + i] = edge(y3[i], half)
             eg[f, 5 + i] = edge(x1[f, i], half)
 
-    fields(one)
+    fields(mid.shape[0], one)
 
 
 def fixed(x, e):
@@ -352,8 +394,9 @@
     x3, eg, d3, w3, ra = refs[:5]
     n = 5
     if second:
-        sc, old = refs[n : n + 2]
-        n += 2
+        s1, s2, old = refs[n : n + 3]
+        n += 3
+        beta = tot(s2, 0) / tot(s1, 0)
     y3, mid, ss, sn, q = refs[n:]
     rhs = ra[...]
     q[...] = jnp.zeros_like(q)
@@ -363,22 +406,23 @@
         for i in range(3):
             y = fixed(x3[f, i], eg[f, 13 + i])
             if second:
-                y = y + sc[0] * old[f, i]
+                y = y + beta * old[f, i]
             y3[f, i] = y
             t = d3[f, i] * y
             q[...] += fold(t * y)
             rows.append(t)
         adj_pre(f, rows, w3, rhs, mid, ss, sn)
 
-    fields(one)
+    fields(x3.shape[0], one)
 
 
 def rest_body(second, *refs):
     x0, x1, x2, eg, d0, d1, d2, ds, dn = refs[:9]
     n = 9
     if second:
-        sc, old0, old1, old2 = refs[n : n + 4]
-        n += 4
+        s1, s2, old0, old1, old2 = refs[n : n + 5]
+        n += 5
+        beta = tot(s2, 0) / tot(s1, 0)
     else:
         old0 = old1 = old2 = None
     y0, y1, y2, f0, f1, f2, q = refs[n:]
@@ -393,7 +437,7 @@
             for i in range(rows):
                 y = fixed(x[f, i], eg[f, at + i])
                 if second:
-                    y = y + sc[0] * old[f, i]
+                    y = y + beta * old[f, i]
                 y_o[f, i] = y
                 if rows == 3:
                     t = d[f, i] * y
@@ -407,7 +451,7 @@
                     q[...] += fold(t * y)
                 f_o[f, i] = t
 
-    fields(one)
+    fields(x0.shape[0], one)
 
 
 def norm_body(v0, v1, v2, v3, q):
@@ -419,11 +463,11 @@
                 x = v[f, i + off]
                 q[...] += fold(x * x)
 
-    fields(one)
+    fields(v0.shape[0], one)
 
 
 def resid_body(sc, v0, v1, g0, g1, g2, g3, z2, z3, r2, r3, q):
-    a = sc[0]
+    a = first_step(sc)
     q[...] = jnp.zeros_like(q)
 
     def dots(r, g):
@@ -443,10 +487,10 @@
             dots(r, g2[f, i])
             dots(v0[f, i], g0[f, i])
 
-    fields(one)
-
-
-def final_body(kind, c_ref, sc, *refs):
+    fields(v0.shape[0], one)
+
+
+def final_body(kind, c_ref, s1, s2, s3, *refs):
     r = refs[0:4]
     g = refs[4:8]
     n = 8
@@ -455,7 +499,10 @@
         n = 12
     keep, send = refs[n:]
     c = c_ref[0]
-    beta, a0, a1 = sc[0], sc[1], sc[2]
+    rr0, rr1 = tot(s1, 0), tot(s2, 0)
+    a0 = rr0 / (rr0 + tot(s1, 1))
+    beta = rr1 / rr0
+    a1 = rr1 / (rr1 + beta * (2.0 * tot(s2, 1) + beta * rr0) + tot(s3, 0))
 
     def one(f):
         for k in range(4):
@@ -477,7 +524,31 @@
                 def _():
                     send[k % 2, f, i] = val
 
-    fields(one)
+    fields(g[0].shape[0], one)
+
+
+def join_body(half, n, c_ref, *refs):
+    keep, other, out, sem = refs[:n], refs[n : 2 * n], refs[2 * n], refs[2 * n + 1]
+    mine = pl.multiple_of(c_ref[0] * half, PAD)
+    theirs = pl.multiple_of((1 - c_ref[0]) * half, PAD)
+    copies = []
+    for src, at in ((keep, mine), (other, theirs)):
+        f0 = 0
+        for s in src:
+            nf = s.shape[1]
+            for w in range(2):
+                copies.append(
+                    pltpu.make_async_copy(
+                        s.at[w],
+                        out.at[w, 0, pl.ds(f0, nf), :, pl.ds(at, half), :],
+                        sem.at[len(copies)],
+                    )
+                )
+            f0 += nf
+    for cp in copies:
+        cp.start()
+    for cp in copies:
+        cp.wait()
 
 
 def per_device(winds, mixing, innovations, obs_weight, obs_sub, obs_col, obs_count):
@@ -502,13 +573,14 @@
         return lax.ppermute(sn, "space", north), lax.ppermute(ss, "space", south)
 
     def total(parts):
-        vals = jnp.stack([jnp.sum(p) for p in parts])
-        vals = vals + swap(vals)
-        msg = jnp.broadcast_to(
-            jnp.pad(vals, (0, lev - len(parts)))[None, None, :], (bands, 1, lev)
-        )
-        got = lax.all_to_all(msg, "space", split_axis=0, concat_axis=0, tiled=True)
-        return jnp.sum(got, axis=(0, 1))
+        vals = swap(parts) + parts
+        step = 1
+        while step < bands:
+            vals = vals + lax.ppermute(
+                vals, "space", [(i, i ^ step) for i in range(bands)]
+            )
+            step *= 2
+        return vals
 
     live = (
         jnp.arange(slots, dtype=jnp.int32)[None, :] < obs_count.reshape(owners)[:, None]
@@ -536,12 +608,12 @@
         [sds(2, 2, 3, wide, lev)] * 2 + [sds(2 * lev, 2 * lev, dtype=BF16)] * 2,
     )
     w_got = swap(w_snd)
-    first = c == 0
-    w01 = jnp.where(first, w_own, w_got)
-    w23 = jnp.where(first, w_got, w_own)
-    w0, w1, w2, w3 = w01[0], w01[1], w23[0], w23[1]
-    up = jnp.stack([jnp.maximum(-w0[1, 2], 0.0), jnp.maximum(-w2[1, 2], 0.0)])
-    down = jnp.stack([jnp.maximum(w0[1, 0], 0.0), jnp.maximum(w2[1, 0], 0.0)])
+    w0, w1, w2, w3, down, up = call(
+        pick_wind_body,
+        (c_arr, w_own, w_got),
+        [SM, VM, VM],
+        [sds(2, 3, wide, lev)] * 4 + [sds(2, wide, lev)] * 2,
+    )
     from_s, from_n = exchange(down, up)
     from_s = jnp.where(pos > 0, from_s, 0.0)
     from_n = jnp.where(pos < bands - 1, from_n, 0.0)
@@ -555,29 +627,37 @@
         [SM, SM, VM],
         [sds(2, FIELDS, 3, wide, lev)] * 4,
         scratch=[pltpu.VMEM((2 * cells * 8, lev), F32)],
+        vmem=16 * 2**20,
     )
     g_got = swap(g_snd)
-    f01 = jnp.where(first, g_own, g_got)
-    f23 = jnp.where(first, g_got, g_own)
     d_got = swap(d_snd)
-    d01 = jnp.where(first, d_own, d_got)
-    d23 = jnp.where(first, d_got, d_own)
-    dd0, dd1, dd2, dd3 = d01[0], d01[1], d23[0], d23[1]
-    ds, dn = exchange(
-        jnp.stack([dd0[:, 0], dd2[:, 0]]), jnp.stack([dd0[:, 2], dd2[:, 2]])
-    )
-
-    row3 = sds(FIELDS, 3, wide, lev)
-    row5 = sds(FIELDS, 5, wide, lev)
-    mid_t = sds(FIELDS, wide, lev)
-
-    def msg(n):
-        return sds(n, FIELDS, wide, lev)
+    groups = []
+    f0 = 0
+    for nf in GROUPS:
+        shapes = [sds(nf, 3, wide, lev)] * 4
+        pick = functools.partial(pick_body, f0)
+        gg = call(pick, (c_arr, g_own, g_got), [SM, VM, VM], shapes)
+        dd = call(pick, (c_arr, d_own, d_got), [SM, VM, VM], shapes)
+        ds, dn = exchange(
+            jnp.stack([dd[0][:, 0], dd[2][:, 0]]), jnp.stack([dd[0][:, 2], dd[2][:, 2]])
+        )
+        groups.append((nf, gg, dd, ds, dn))
+        f0 += nf
 
     part = sds(8, lev)
+
+    def row3(nf):
+        return sds(nf, 3, wide, lev)
+
+    def row5(nf):
+        return sds(nf, 5, wide, lev)
+
+    def state_of(nf, n):
+        return [sds(nf, wide, lev)] + [sds(n, nf, wide, lev)] * 2
 
     def adj_mid(state, f2, f1, g0=None):
         mid, ss, sn = state
+        nf = mid.shape[0]
         rs, rn = exchange(ss, sn)
         ext = g0 is not None
         n = 3 if ext else 2
@@ -586,121 +666,139 @@
             functools.partial(adj_mid_body, ext),
             ins,
             [SM] + [VM] * (len(ins) - 1),
-            [row5, row3, mid_t, msg(n), msg(n)],
+            [row5(nf), row3(nf)] + state_of(nf, n),
         )
         return o[0], o[1], tuple(o[2:])
 
     def adj_last(mode, state, f0, extra=()):
         mid, ss, sn = state
+        nf = mid.shape[0]
         rs, rn = exchange(ss, sn)
         ins = (flags, mid, ss, sn, rs, rn, f0, w0, wh0, ra) + extra
-        specs = [SM] + [VM] * 9 + ([SM, VM, VM] if extra else [])
-        outs = [row3, row5] + ([mid_t, msg(2), msg(2)] if mode < 2 else [])
+        specs = [SM] + [VM] * 9 + ([VM] * 3 if extra else [])
+        outs = [row3(nf), row5(nf)] + (state_of(nf, 2) if mode < 2 else [])
         o = call(functools.partial(adj_last_body, mode), ins, specs, outs)
         return o[0], o[1], tuple(o[2:])
 
     def fwd_first(state, v1, v2):
         mid, ss, sn = state
+        nf = mid.shape[0]
         rs, rn = exchange(ss, sn)
         ins = (flags, mid, ss, sn, rs, rn, v1, v2, w0, wh0, w1, w2, rf)
         o = call(
-            fwd_first_body, ins, [SM] + [VM] * 12, [row5, row3, mid_t, msg(2), msg(2)]
+            fwd_first_body,
+            ins,
+            [SM] + [VM] * 12,
+            [row5(nf), row3(nf)] + state_of(nf, 2),
         )
         return o[0], o[1], tuple(o[2:])
 
     def fwd_last(state, v3, x0, x1):
         mid, ss, sn = state
+        nf = mid.shape[0]
         rs, rn = exchange(ss, sn)
         ins = (flags, mid, ss, sn, rs, rn, v3, x0, x1, w2, wh2, w3, rf)
         return call(
             functools.partial(fwd_last_body, half),
             ins,
             [SM] + [VM] * 12,
-            [row5, row3, sds(FIELDS, 16, 2 * PAD, lev)],
-        )
-
-    def turn(xs, eg, beta=None, old=None):
+            [row5(nf), row3(nf), sds(nf, 16, 2 * PAD, lev)],
+        )
+
+    def turn(xs, eg, dd, ds, dn, sums=(), old=None):
         eg = swap(eg)
-        second = beta is not None
+        second = old is not None
         x0, x1, x2, x3 = xs
-        ex = (beta, old[3]) if second else ()
+        nf = x3.shape[0]
+        ex = sums + (old[3],) if second else ()
         o = call(
             functools.partial(turn_body, second),
-            (x3, eg, dd3, w3, ra) + ex,
-            [VM] * 5 + ([SM, VM] if second else []),
-            [row3, mid_t, msg(2), msg(2), part],
+            (x3, eg, dd[3], w3, ra) + ex,
+            [VM] * (5 + len(ex)),
+            [row3(nf)] + state_of(nf, 2) + [part],
         )
         y3, state, q3 = o[0], tuple(o[1:4]), o[4]
-        ex = (beta,) + old[:3] if second else ()
+        ex = sums + tuple(old[:3]) if second else ()
         y0, y1, y2, f0, f1, f2, q = call(
             functools.partial(rest_body, second),
-            (x0, x1, x2, eg, dd0, dd1, dd2, ds, dn) + ex,
-            [VM] * 9 + ([SM] + [VM] * 3 if second else []),
-            [row5, row3, row5, row5, row3, row5, part],
+            (x0, x1, x2, eg, dd[0], dd[1], dd[2], ds, dn) + ex,
+            [VM] * (9 + len(ex)),
+            [row5(nf), row3(nf), row5(nf)] * 2 + [part],
         )
         return state, (y0, y1, y2, y3), (f0, f1, f2), q3 + q
 
-    o = call(
-        turn_first_body,
-        (f23[1], f23[0], w3, ra),
-        [VM] * 4,
-        [mid_t, msg(3), msg(3)],
-    )
-    g3, g2, state = adj_mid(tuple(o), f23[0], f01[1], f01[0])
-    g0, g1, state = adj_last(0, state, f01[0])
-    rr_part = call(norm_body, (g0, g1, g2, g3), [VM] * 4, [part])[0]
-
-    x0, x1, state = fwd_first(state, g1, g2)
-    x2, x3, eg = fwd_last(state, g3, x0, x1)
-    state, ys, fs, q = turn((x0, x1, x2, x3), eg)
-    sums = total([rr_part, q])
-    rr0 = sums[0]
-    a0 = rr0 / (rr0 + sums[1])
-    z3, z2, state = adj_mid(state, fs[2], fs[1])
-    a0_arr = a0.reshape(1)
-    v0, v1, state = adj_last(1, state, fs[0], (a0_arr, g0, g1))
-    v2, v3, q = call(
-        resid_body,
-        (a0_arr, v0, v1, g0, g1, g2, g3, z2, z3),
-        [SM] + [VM] * 8,
-        [row3, row5, sds(2, 8, lev)],
-    )
-    sums = total([q[0], q[1]])
-    rr1 = sums[0]
-    beta = rr1 / rr0
-    dd = rr1 + beta * (2.0 * sums[1] + beta * rr0)
-
-    x0, x1, state = fwd_first(state, v1, v2)
-    x2, x3, eg = fwd_last(state, v3, x0, x1)
-    state, _, fs, q = turn((x0, x1, x2, x3), eg, beta.reshape(1), ys)
-    a1 = rr1 / (dd + total([q])[0])
-    scal = jnp.stack([beta, a0, a1])
-    z3, z2, state = adj_mid(state, fs[2], fs[1])
-    z0, z1, _ = adj_last(2, state, fs[0])
-
-    shape = sds(2, FIELDS, 3, half, lev)
-    keep_i, send_i = call(
-        functools.partial(final_body, "inc"),
-        (c_arr, scal, v0, v1, v2, v3, g0, g1, g2, g3),
-        [SM, SM] + [VM] * 8,
-        [shape, shape],
-    )
-    keep_r, send_r = call(
-        functools.partial(final_body, "res"),
-        (c_arr, scal, v0, v1, v2, v3, g0, g1, g2, g3, z0, z1, z2, z3),
-        [SM, SM] + [VM] * 12,
-        [shape, shape],
-    )
-
-    def whole(keep, send):
-        other = swap(send)
-        return jnp.where(
-            first,
-            jnp.concatenate([keep, other], axis=3),
-            jnp.concatenate([other, keep], axis=3),
-        )[:, None]
-
-    return whole(keep_i, send_i), whole(keep_r, send_r)
+    def forward(state, v):
+        x0, x1, state = fwd_first(state, v[1], v[2])
+        x2, x3, eg = fwd_last(state, v[3], x0, x1)
+        return (x0, x1, x2, x3), eg
+
+    grads, mids = [], []
+    for nf, gg, dd, ds, dn in groups:
+        state = tuple(
+            call(turn_first_body, (gg[3], gg[2], w3, ra), [VM] * 4, state_of(nf, 3))
+        )
+        g3, g2, state = adj_mid(state, gg[2], gg[1], gg[0])
+        g0, g1, state = adj_last(0, state, gg[0])
+        g = (g0, g1, g2, g3)
+        rr = call(norm_body, g, [VM] * 4, [part])[0]
+        xs, eg = forward(state, g)
+        state, ys, fs, q = turn(xs, eg, dd, ds, dn)
+        grads.append(g)
+        mids.append((state, ys, fs, rr, q))
+    s1 = total(jnp.stack([sum(m[3] for m in mids), sum(m[4] for m in mids)]))
+
+    resid, ends = [], []
+    for g, (state, _, fs, _, _) in zip(grads, mids):
+        nf = g[0].shape[0]
+        z3, z2, state = adj_mid(state, fs[2], fs[1])
+        v0, v1, state = adj_last(1, state, fs[0], (s1, g[0], g[1]))
+        v2, v3, q = call(
+            resid_body,
+            (s1, v0, v1) + g + (z2, z3),
+            [VM] * 9,
+            [row3(nf), row5(nf), sds(2, 8, lev)],
+        )
+        v = (v0, v1, v2, v3)
+        resid.append(v)
+        ends.append((forward(state, v), q))
+    s2 = total(sum(e[1] for e in ends))
+
+    turns = []
+    for ((xs, eg), _), (_, ys, _, _, _), (nf, gg, dd, ds, dn) in zip(ends, mids, groups):
+        turns.append(turn(xs, eg, dd, ds, dn, (s1, s2), ys))
+    s3 = total(sum(t[3] for t in turns)[None])
+
+    def final(kind, v, g, z=()):
+        nf = g[0].shape[0]
+        ins = (c_arr, s1, s2, s3) + tuple(v) + tuple(g) + tuple(z)
+        shape = sds(2, nf, 3, half, lev)
+        keep, send = call(
+            functools.partial(final_body, kind),
+            ins,
+            [SM] + [VM] * (len(ins) - 1),
+            [shape, shape],
+        )
+        return keep, swap(send)
+
+    def join(parts):
+        n = len(parts)
+        ins = (c_arr,) + tuple(p[0] for p in parts) + tuple(p[1] for p in parts)
+        return call(
+            functools.partial(join_body, half, n),
+            ins,
+            [SM] + [VM] * (2 * n),
+            [sds(2, 1, FIELDS, 3, cols, lev)],
+            scratch=[pltpu.SemaphoreType.DMA((4 * n,))],
+            out_specs=[pl.BlockSpec(memory_space=pl.ANY)],
+        )[0]
+
+    increment = join([final("inc", v, g) for v, g in zip(resid, grads)])
+    parts = []
+    for v, g, (state, _, fs, _) in zip(resid, grads, turns):
+        z3, z2, state = adj_mid(state, fs[2], fs[1])
+        z0, z1, _ = adj_last(2, state, fs[0])
+        parts.append(final("res", v, g, (z0, z1, z2, z3)))
+    return increment, join(parts)
 
 
 def solution(mesh):

time: 427 us -> 388 us (0.909)
  waiting for transfers between devices: 129 us -> 192 us
  local copies, waits for them, and re-layouts: 61.5 us -> 9.64 us
  blocking collectives: 29.6 us -> 0 us
  other arithmetic: 18.3 us -> 1.06 us
  starting transfers between devices: 114 us -> 130 us
  Pallas kernels: 64.4 us -> 53.8 us
  between operations: 8.53 us -> 1.27 us
    ppermute x0 -> x18, waiting for transfers between devices: none -> 60.9 us  [total(): lax.ppermute(vals, 'space', [(i, i ^ step) for i in range(bands)])]
    unnamed x207 -> x23, local copies, waits for them, and re-layouts: 53.6 us -> 9.28 us
    all_to_all x2 -> x0, blocking collectives: 29.6 us -> none  [total(): got = lax.all_to_all(msg, 'space', split_axis=0, concat_axis=0, tiled=True)]
    ppermute x10, starting transfers between devices: 18.8 us -> 36.6 us  [swap(): return lax.ppermute(x, 'tm', [(0, 1), (1, 0)])]
    pallas_call x22 -> x27, Pallas kernels: 64.4 us -> 53.8 us  [call(): pl.pallas_call(body, out_shape=outs, in_specs=specs, out_specs=out_specs...]
    all_to_all x1 -> x0, waiting for transfers between devices: 6.53 us -> none  [total(): got = lax.all_to_all(msg, 'space', split_axis=0, concat_axis=0, tiled=True)]
    select_n x3 -> x0, other arithmetic: 5.22 us -> none  [the longest x1 1.89 us: per_device(): d01 = jnp.where(first, d_own, d_got)]
    all_to_all x1 -> x0, starting transfers between devices: 4.59 us -> none  [total(): got = lax.all_to_all(msg, 'space', split_axis=0, concat_axis=0, tiled=True)]
  transfers between devices with their start and end apart: 36 -> 53, of which waited for: 16 -> 33; matrix products, arithmetic and copies ran while one was open for 6% -> 0% of each run, Pallas kernels for 9% -> 6%
where the time goes in v2:
time: 388 us
  waiting for transfers between devices  192 us (49%)
  starting transfers between devices  130 us (34%)
  Pallas kernels  53.8 us (14%)
  local copies, waits for them, and re-layouts  9.64 us (2%)
    ppermute x24, waiting for transfers between devices, exchange(): return (lax.ppermute(sn, 'space', north), lax.ppermute(ss, 'space', south))  98.7 us
    ppermute x24, starting transfers between devices, exchange(): return (lax.ppermute(sn, 'space', north), lax.ppermute(ss, 'space', south))  79.5 us
    ppermute x18, waiting for transfers between devices, total(): lax.ppermute(vals, 'space', [(i, i ^ step) for i in range(bands)])  60.9 us
    pallas_call x27, Pallas kernels, call(): pl.pallas_call(body, out_shape=outs, in_specs=specs, out_specs=out_specs...  53.8 us
    ppermute x10, starting transfers between devices, swap(): return lax.ppermute(x, 'tm', [(0, 1), (1, 0)])  36.6 us
    all_to_all x1, waiting for transfers between devices, per_device(): lax.all_to_all(packed, 'space', split_axis=0, concat_axis=0, tiled=True)  24.9 us
    all_to_all x1, starting transfers between devices, per_device(): lax.all_to_all(packed, 'space', split_axis=0, concat_axis=0, tiled=True)  12 us
    unnamed x23, local copies, waits for them, and re-layouts  9.28 us
  transfers between devices with their start and end apart: 53, of which 33 were waited for; matrix products, arithmetic and copies ran while one was open for 0% of the time, Pallas kernels for 6%

profile of v2, /device:TPU:1, one launch (start us, length us, event | category | flops | bytes accessed | tf_op | source)
XLA Modules:
  0.0 388.0 jit_solution(5432003922880278624)
XLA Ops:
  5.2 12.0 %all-to-all-start = ((f32[64,7,8,128]{3,2,1,0:T(8,128)}), f32[64,7,8,128]{3,2,1,0:T(8,128)S(1)}, u32[]{:S(2)}, u32[]{:S(2)}) async-start(f32[64,7,8,128]{3,2,1,0:T(8,128)} %copy-done), calls=%async_computation | async-start | bytes 3670016 | tf_op jit(solution)/shard_map/all_to_all | solution.py:602
  17.2 24.9 %all-to-all-done = f32[64,7,8,128]{3,2,1,0:T(8,128)S(1)} async-done(((f32[64,7,8,128]{3,2,1,0:T(8,128)}), f32[64,7,8,128]{3,2,1,0:T(8,128)S(1)}, u32[]{:S(2)}, u32[]{:S(2)}) %all-to-all-start) | async-done | bytes 1835040 | tf_op jit(solution)/shard_map/all_to_all | solution.py:602
  42.6 7.7 %shard_map.87 = (f32[2,3,3,208,128]{4,3,2,1,0:T(8,128)S(1)}, f32[2,3,3,208,128]{4,3,2,1,0:T(8,128)S(1)}, f32[2,3,3,208,128]{4,3,2,1,0:T(8,128)S(1)}, f32[2,3,3,208,128]{4,3,2,1,0:T(8,128)}) custom-call(s32[1]{0:T(128)} %bitcast.c_ref, s32[64,8]{1,0:T(8,128)S(1)} %convert_bitcast_fusion.idx_ref, f32[3584,128]{1,0:T(8,128)S(1)} %bitcast.27), custom_call_target="tpu_custom_call" | custom-call | flops 100000000 | bytes 9504772 | tf_op jit(solution)/shard_map/pallas_call | solution.py:24
  52.8 2.6 collective-permute-start
  57.9 2.9 collective-permute-done.1.got_ref
  68.1 6.9 %collective-permute-start.3 = (f32[3,3,208,128]{3,2,1,0:T(8,128)S(1)}, f32[3,3,208,128]{3,2,1,0:T(8,128)S(1)}, u32[]{:S(2)}, u32[]{:S(2)}) collective-permute-start(f32[3,3,208,128]{3,2,1,0:T(8,128)S(1)} %get-tuple-element.106.refs_2_), channel_id=1, source_target_pairs={{1,0},{2,1},{3,2},{4,3},{5,4},{6,5},{7,6},{8,7},{9,8},{10,9},{11,1... | collective-permute-start | bytes 2875400 | tf_op jit(solution)/shard_map/ppermute | solution.py:573
  75.1 20.4 %collective-permute-done.2.refs_4_ = f32[3,3,208,128]{3,2,1,0:T(8,128)S(1)} collective-permute-done((f32[3,3,208,128]{3,2,1,0:T(8,128)S(1)}, f32[3,3,208,128]{3,2,1,0:T(8,128)S(1)}, u32[]{:S(2)}, u32[]{:S(2)}) %collective-permute-start.2) | collective-permute-done | bytes 958496 | tf_op jit(solution)/shard_map/ppermute | solution.py:573
  95.6 2.9 shard_map.92
  98.6 6.9 %collective-permute-start.7 = (f32[3,3,208,128]{3,2,1,0:T(8,128)S(1)}, f32[3,3,208,128]{3,2,1,0:T(8,128)S(1)}, u32[]{:S(2)}, u32[]{:S(2)}) collective-permute-start(f32[3,3,208,128]{3,2,1,0:T(8,128)S(1)} %get-tuple-element.115.refs_2_), channel_id=1, source_target_pairs={{1,0},{2,1},{3,2},{4,3},{5,4},{6,5},{7,6},{8,7},{9,8},{10,9},{11,1... | collective-permute-start | bytes 2875400 | tf_op jit(solution)/shard_map/ppermute | solution.py:573
  107.6 17.6 %collective-permute-done.6.refs_4_ = f32[3,3,208,128]{3,2,1,0:T(8,128)S(1)} collective-permute-done((f32[3,3,208,128]{3,2,1,0:T(8,128)S(1)}, f32[3,3,208,128]{3,2,1,0:T(8,128)S(1)}, u32[]{:S(2)}, u32[]{:S(2)}) %collective-permute-start.6) | collective-permute-done | bytes 958496 | tf_op jit(solution)/shard_map/ppermute | solution.py:573
  127.9 6.9 %collective-permute-start.9 = (f32[2,3,208,128]{3,2,1,0:T(8,128)S(1)}, f32[2,3,208,128]{3,2,1,0:T(8,128)S(1)}, u32[]{:S(2)}, u32[]{:S(2)}) collective-permute-start(f32[2,3,208,128]{3,2,1,0:T(8,128)S(1)} %get-tuple-element.123.ss), channel_id=1, source_target_pairs={{1,0},{2,1},{3,2},{4,3},{5,4},{6,5},{7,6},{8,7},{9,8},{10,9},{11,1... | collective-permute-start | bytes 1916936 | tf_op jit(solution)/shard_map/ppermute | solution.py:573
  134.7 11.9 %collective-permute-done.8.rs = f32[2,3,208,128]{3,2,1,0:T(8,128)S(1)} collective-permute-done((f32[2,3,208,128]{3,2,1,0:T(8,128)S(1)}, f32[2,3,208,128]{3,2,1,0:T(8,128)S(1)}, u32[]{:S(2)}, u32[]{:S(2)}) %collective-permute-start.8) | collective-permute-done | bytes 639008 | tf_op jit(solution)/shard_map/ppermute | solution.py:573
  146.7 3.0 shard_map.95
  149.8 6.9 %collective-permute-start.11 = (f32[2,3,208,128]{3,2,1,0:T(8,128)S(1)}, f32[2,3,208,128]{3,2,1,0:T(8,128)S(1)}, u32[]{:S(2)}, u32[]{:S(2)}) collective-permute-start(f32[2,3,208,128]{3,2,1,0:T(8,128)S(1)} %get-tuple-element.127.ss), channel_id=1, source_target_pairs={{1,0},{2,1},{3,2},{4,3},{5,4},{6,5},{7,6},{8,7},{9,8},{10,9},{11,1... | collective-permute-start | bytes 1916936 | tf_op jit(solution)/shard_map/ppermute | solution.py:573
  157.1 10.6 %collective-permute-done.10.rs = f32[2,3,208,128]{3,2,1,0:T(8,128)S(1)} collective-permute-done((f32[2,3,208,128]{3,2,1,0:T(8,128)S(1)}, f32[2,3,208,128]{3,2,1,0:T(8,128)S(1)}, u32[]{:S(2)}, u32[]{:S(2)}) %collective-permute-start.10) | collective-permute-done | bytes 639008 | tf_op jit(solution)/shard_map/ppermute | solution.py:573
  167.7 2.6 shard_map.96
  170.3 4.4 %collective-permute-start.12 = (f32[3,16,16,128]{3,2,1,0:T(8,128)S(1)}, f32[3,16,16,128]{3,2,1,0:T(8,128)S(1)}, u32[]{:S(2)}, u32[]{:S(2)}) collective-permute-start(f32[3,16,16,128]{3,2,1,0:T(8,128)S(1)} %get-tuple-element.132), channel_id=1, source_target_pairs={{0,64},{64,0},{1,65},{65,1},{2,66},{66,2},{3,67},{67,3},{4,68},{68... | collective-permute-start | bytes 1179656 | tf_op jit(solution)/shard_map/ppermute | solution.py:570
  175.0 7.0 %collective-permute-start.15 = (f32[2,3,208,128]{3,2,1,0:T(8,128)S(1)}, f32[2,3,208,128]{3,2,1,0:T(8,128)S(1)}, u32[]{:S(2)}, u32[]{:S(2)}) collective-permute-start(f32[2,3,208,128]{3,2,1,0:T(8,128)S(1)} %pad_maximum_fusion.1), channel_id=1, source_target_pairs={{1,0},{2,1},{3,2},{4,3},{5,4},{6,5},{7,6},{8,7},{9,8},{10,9},{11,1... | collective-permute-start | bytes 1916936 | tf_op jit(solution)/shard_map/ppermute | solution.py:573
  183.2 6.9 %collective-permute-start.24 = (f32[2,3,208,128]{3,2,1,0:T(8,128)S(1)}, f32[2,3,208,128]{3,2,1,0:T(8,128)S(1)}, u32[]{:S(2)}, u32[]{:S(2)}) collective-permute-start(f32[2,3,208,128]{3,2,1,0:T(8,128)S(1)} %get-tuple-element.143.refs_2_), channel_id=1, source_target_pairs={{1,0},{2,1},{3,2},{4,3},{5,4},{6,5},{7,6},{8,7},{9,8},{10,9},{11,1... | collective-permute-start | bytes 1916936 | tf_op jit(solution)/shard_map/ppermute | solution.py:573
  190.4 6.0 %collective-permute-done.14.refs_7_ = f32[2,3,208,128]{3,2,1,0:T(8,128)S(1)} collective-permute-done((f32[2,3,208,128]{3,2,1,0:T(8,128)S(1)}, f32[2,3,208,128]{3,2,1,0:T(8,128)S(1)}, u32[]{:S(2)}, u32[]{:S(2)}) %collective-permute-start.14) | collective-permute-done | bytes 639008 | tf_op jit(solution)/shard_map/ppermute | solution.py:573
  197.1 13.0 %collective-permute-done.23.refs_4_ = f32[2,3,208,128]{3,2,1,0:T(8,128)S(1)} collective-permute-done((f32[2,3,208,128]{3,2,1,0:T(8,128)S(1)}, f32[2,3,208,128]{3,2,1,0:T(8,128)S(1)}, u32[]{:S(2)}, u32[]{:S(2)}) %collective-permute-start.23) | collective-permute-done | bytes 639008 | tf_op jit(solution)/shard_map/ppermute | solution.py:573
  210.0 2.9 shard_map.100
  213.0 6.9 %collective-permute-start.26 = (f32[2,3,208,128]{3,2,1,0:T(8,128)S(1)}, f32[2,3,208,128]{3,2,1,0:T(8,128)S(1)}, u32[]{:S(2)}, u32[]{:S(2)}) collective-permute-start(f32[2,3,208,128]{3,2,1,0:T(8,128)S(1)} %get-tuple-element.148.refs_2_), channel_id=1, source_target_pairs={{1,0},{2,1},{3,2},{4,3},{5,4},{6,5},{7,6},{8,7},{9,8},{10,9},{11,1... | collective-permute-start | bytes 1916936 | tf_op jit(solution)/shard_map/ppermute | solution.py:573
  222.1 6.3 %collective-permute-done.17 = f32[2,8,128]{2,1,0:T(8,128)S(1)} collective-permute-done((f32[2,8,128]{2,1,0:T(8,128)S(1)}, f32[2,8,128]{2,1,0:T(8,128)S(1)}, u32[]{:S(2)}, u32[]{:S(2)}) %collective-permute-start.17) | collective-permute-done | bytes 8224 | tf_op jit(solution)/shard_map/ppermute | solution.py:579
  228.4 4.3 %collective-permute-done.18 = f32[2,8,128]{2,1,0:T(8,128)S(1)} collective-permute-done((f32[2,8,128]{2,1,0:T(8,128)S(1)}, f32[2,8,128]{2,1,0:T(8,128)S(1)}, u32[]{:S(2)}, u32[]{:S(2)}) %collective-permute-start.18) | collective-permute-done | bytes 8224 | tf_op jit(solution)/shard_map/ppermute | solution.py:579
  235.2 4.0 %collective-permute-done.20 = f32[2,8,128]{2,1,0:T(8,128)S(1)} collective-permute-done((f32[2,8,128]{2,1,0:T(8,128)S(1)}, f32[2,8,128]{2,1,0:T(8,128)S(1)}, u32[]{:S(2)}, u32[]{:S(2)}) %collective-permute-start.20) | collective-permute-done | bytes 8224 | tf_op jit(solution)/shard_map/ppermute | solution.py:579
  242.7 3.0 collective-permute-done.22
  245.7 2.9 shard_map.101
  248.8 6.9 %collective-permute-start.35 = (f32[2,3,208,128]{3,2,1,0:T(8,128)S(1)}, f32[2,3,208,128]{3,2,1,0:T(8,128)S(1)}, u32[]{:S(2)}, u32[]{:S(2)}) collective-permute-start(f32[2,3,208,128]{3,2,1,0:T(8,128)S(1)} %get-tuple-element.157.ss), channel_id=1, source_target_pairs={{1,0},{2,1},{3,2},{4,3},{5,4},{6,5},{7,6},{8,7},{9,8},{10,9},{11,1... | collective-permute-start | bytes 1916936 | tf_op jit(solution)/shard_map/ppermute | solution.py:573
  256.8 6.7 %collective-permute-done.34.rs = f32[2,3,208,128]{3,2,1,0:T(8,128)S(1)} collective-permute-done((f32[2,3,208,128]{3,2,1,0:T(8,128)S(1)}, f32[2,3,208,128]{3,2,1,0:T(8,128)S(1)}, u32[]{:S(2)}, u32[]{:S(2)}) %collective-permute-start.34) | collective-permute-done | bytes 639008 | tf_op jit(solution)/shard_map/ppermute | solution.py:573
  263.5 3.0 shard_map.103
  266.5 7.0 %collective-permute-start.37 = (f32[2,3,208,128]{3,2,1,0:T(8,128)S(1)}, f32[2,3,208,128]{3,2,1,0:T(8,128)S(1)}, u32[]{:S(2)}, u32[]{:S(2)}) collective-permute-start(f32[2,3,208,128]{3,2,1,0:T(8,128)S(1)} %get-tuple-element.161.ss), channel_id=1, source_target_pairs={{1,0},{2,1},{3,2},{4,3},{5,4},{6,5},{7,6},{8,7},{9,8},{10,9},{11,1... | collective-permute-start | bytes 1916936 | tf_op jit(solution)/shard_map/ppermute | solution.py:573
  273.5 7.7 %collective-permute-done.36.rs = f32[2,3,208,128]{3,2,1,0:T(8,128)S(1)} collective-permute-done((f32[2,3,208,128]{3,2,1,0:T(8,128)S(1)}, f32[2,3,208,128]{3,2,1,0:T(8,128)S(1)}, u32[]{:S(2)}, u32[]{:S(2)}) %collective-permute-start.36) | collective-permute-done | bytes 639008 | tf_op jit(solution)/shard_map/ppermute | solution.py:573
  283.8 9.7 %collective-permute-start.38 = (f32[3,16,16,128]{3,2,1,0:T(8,128)S(1)}, f32[3,16,16,128]{3,2,1,0:T(8,128)S(1)}, u32[]{:S(2)}, u32[]{:S(2)}) collective-permute-start(f32[3,16,16,128]{3,2,1,0:T(8,128)S(1)} %get-tuple-element.167), channel_id=1, source_target_pairs={{0,64},{64,0},{1,65},{65,1},{2,66},{66,2},{3,67},{67,3},{4,68},{68... | collective-permute-start | bytes 1179656 | tf_op jit(solution)/shard_map/ppermute | solution.py:570
  297.4 4.0 %collective-permute-done.29 = f32[2,8,128]{2,1,0:T(8,128)S(1)} collective-permute-done((f32[2,8,128]{2,1,0:T(8,128)S(1)}, f32[2,8,128]{2,1,0:T(8,128)S(1)}, u32[]{:S(2)}, u32[]{:S(2)}) %collective-permute-start.29) | collective-permute-done | bytes 8224 | tf_op jit(solution)/shard_map/ppermute | solution.py:579
  303.9 4.0 %collective-permute-done.31 = f32[2,8,128]{2,1,0:T(8,128)S(1)} collective-permute-done((f32[2,8,128]{2,1,0:T(8,128)S(1)}, f32[2,8,128]{2,1,0:T(8,128)S(1)}, u32[]{:S(2)}, u32[]{:S(2)}) %collective-permute-start.31) | collective-permute-done | bytes 8224 | tf_op jit(solution)/shard_map/ppermute | solution.py:579
  311.4 3.0 collective-permute-done.33
  316.7 7.2 %collective-permute-start.48 = (f32[2,3,208,128]{3,2,1,0:T(8,128)S(1)}, f32[2,3,208,128]{3,2,1,0:T(8,128)S(1)}, u32[]{:S(2)}, u32[]{:S(2)}) collective-permute-start(f32[2,3,208,128]{3,2,1,0:T(8,128)S(1)} %get-tuple-element.178.refs_2_), channel_id=1, source_target_pairs={{1,0},{2,1},{3,2},{4,3},{5,4},{6,5},{7,6},{8,7},{9,8},{10,9},{11,1... | collective-permute-start | bytes 1916936 | tf_op jit(solution)/shard_map/ppermute | solution.py:573
  323.9 3.0 shard_map.106
  326.9 4.8 %collective-permute-done.47.refs_4_ = f32[2,3,208,128]{3,2,1,0:T(8,128)S(1)} collective-permute-done((f32[2,3,208,128]{3,2,1,0:T(8,128)S(1)}, f32[2,3,208,128]{3,2,1,0:T(8,128)S(1)}, u32[]{:S(2)}, u32[]{:S(2)}) %collective-permute-start.47) | collective-permute-done | bytes 639008 | tf_op jit(solution)/shard_map/ppermute | solution.py:573
  331.7 2.9 shard_map.109
  334.7 7.0 %collective-permute-start.50 = (f32[2,3,208,128]{3,2,1,0:T(8,128)S(1)}, f32[2,3,208,128]{3,2,1,0:T(8,128)S(1)}, u32[]{:S(2)}, u32[]{:S(2)}) collective-permute-start(f32[2,3,208,128]{3,2,1,0:T(8,128)S(1)} %get-tuple-element.183.refs_2_), channel_id=1, source_target_pairs={{1,0},{2,1},{3,2},{4,3},{5,4},{6,5},{7,6},{8,7},{9,8},{10,9},{11,1... | collective-permute-start | bytes 1916936 | tf_op jit(solution)/shard_map/ppermute | solution.py:573
  341.7 8.7 %collective-permute-start.39 = (f32[1,8,128]{2,1,0:T(8,128)S(1)}, f32[1,8,128]{2,1,0:T(8,128)S(1)}, u32[]{:S(2)}, u32[]{:S(2)}) collective-permute-start(f32[1,8,128]{2,1,0:T(8,128)S(1)} %add_bitcast_fusion), channel_id=1, source_target_pairs={{0,64},{64,0},{1,65},{65,1},{2,66},{66,2},{3,67},{67,3},{4,68},{68... | collective-permute-start | bytes 12296 | tf_op jit(solution)/shard_map/ppermute | solution.py:570
  351.2 2.7 collective-permute-done.40
  354.0 4.3 %collective-permute-done.41 = f32[1,8,128]{2,1,0:T(8,128)S(1)} collective-permute-done((f32[1,8,128]{2,1,0:T(8,128)S(1)}, f32[1,8,128]{2,1,0:T(8,128)S(1)}, u32[]{:S(2)}, u32[]{:S(2)}) %collective-permute-start.41) | collective-permute-done | bytes 4128 | tf_op jit(solution)/shard_map/ppermute | solution.py:579
  360.7 4.0 %collective-permute-done.43 = f32[1,8,128]{2,1,0:T(8,128)S(1)} collective-permute-done((f32[1,8,128]{2,1,0:T(8,128)S(1)}, f32[1,8,128]{2,1,0:T(8,128)S(1)}, u32[]{:S(2)}, u32[]{:S(2)}) %collective-permute-start.43) | collective-permute-done | bytes 4128 | tf_op jit(solution)/shard_map/ppermute | solution.py:579
  367.1 4.0 %collective-permute-done.45 = f32[1,8,128]{2,1,0:T(8,128)S(1)} collective-permute-done((f32[1,8,128]{2,1,0:T(8,128)S(1)}, f32[1,8,128]{2,1,0:T(8,128)S(1)}, u32[]{:S(2)}, u32[]{:S(2)}) %collective-permute-start.45) | collective-permute-done | bytes 4128 | tf_op jit(solution)/shard_map/ppermute | solution.py:579
  372.3 6.7 %collective-permute-start.46 = (f32[2,3,3,192,128]{4,3,2,1,0:T(8,128)S(1)}, f32[2,3,3,192,128]{4,3,2,1,0:T(8,128)S(1)}, u32[]{:S(2)}, u32[]{:S(2)}) collective-permute-start(f32[2,3,3,192,128]{4,3,2,1,0:T(8,128)S(1)} %get-tuple-element.176), channel_id=1, source_target_pairs={{0,64},{64,0},{1,65},{65,1},{2,66},{66,2},{3,67},{67,3},{4,68},{68... | collective-permute-start | bytes 5308424 | tf_op jit(solution)/shard_map/ppermute | solution.py:570
  (147 shorter events, 65.3 us)
Async XLA Ops:
  5.2 36.9 %all-to-all-start = ((f32[64,7,8,128]{3,2,1,0:T(8,128)}), f32[64,7,8,128]{3,2,1,0:T(8,128)S(1)}, u32[]{:S(2)}, u32[]{:S(2)}) async-start(f32[64,7,8,128]{3,2,1,0:T(8,128)} %copy-done), calls=%async_computation | async-start | bytes 3670016 | tf_op jit(solution)/shard_map/all_to_all | solution.py:602
  52.8 10.7 %collective-permute-start = (f32[2,3,3,208,128]{4,3,2,1,0:T(8,128)}, f32[2,3,3,208,128]{4,3,2,1,0:T(8,128)}, u32[]{:S(2)}, u32[]{:S(2)}) collective-permute-start(f32[2,3,3,208,128]{4,3,2,1,0:T(8,128)} %get-tuple-element.98), channel_id=1, source_target_pairs={{0,64},{64,0},{1,65},{65,1},{2,66},{66,2},{3,67},{67,3},{4,68},{68... | collective-permute-start | bytes 5750792 | tf_op jit(solution)/shard_map/ppermute | solution.py:570
  57.1 3.7 collective-permute-start.1
  61.0 14.0 %collective-permute-start.5 = (f32[2,208,128]{2,1,0:T(8,128)S(1)}, f32[2,208,128]{2,1,0:T(8,128)S(1)}, u32[]{:S(2)}, u32[]{:S(2)}) collective-permute-start(f32[2,208,128]{2,1,0:T(8,128)S(1)} %get-tuple-element.111), channel_id=1, source_target_pairs={{1,0},{2,1},{3,2},{4,3},{5,4},{6,5},{7,6},{8,7},{9,8},{10,9},{11,1... | collective-permute-start | bytes 638984 | tf_op jit(solution)/shard_map/ppermute | solution.py:573
  63.4 11.6 %collective-permute-start.4 = (f32[2,208,128]{2,1,0:T(8,128)S(1)}, f32[2,208,128]{2,1,0:T(8,128)S(1)}, u32[]{:S(2)}, u32[]{:S(2)}) collective-permute-start(f32[2,208,128]{2,1,0:T(8,128)S(1)} %get-tuple-element.110), channel_id=1, source_target_pairs={{0,1},{1,2},{2,3},{3,4},{4,5},{5,6},{6,7},{7,8},{8,9},{9,10},{10,1... | collective-permute-start | bytes 638984 | tf_op jit(solution)/shard_map/ppermute | solution.py:573
  68.0 27.6 %collective-permute-start.2 = (f32[3,3,208,128]{3,2,1,0:T(8,128)S(1)}, f32[3,3,208,128]{3,2,1,0:T(8,128)S(1)}, u32[]{:S(2)}, u32[]{:S(2)}) collective-permute-start(f32[3,3,208,128]{3,2,1,0:T(8,128)S(1)} %get-tuple-element.107.refs_3_), channel_id=1, source_target_pairs={{0,1},{1,2},{2,3},{3,4},{4,5},{5,6},{6,7},{7,8},{8,9},{9,10},{10,1... | collective-permute-start | bytes 2875400 | tf_op jit(solution)/shard_map/ppermute | solution.py:573
  68.1 27.5 %collective-permute-start.3 = (f32[3,3,208,128]{3,2,1,0:T(8,128)S(1)}, f32[3,3,208,128]{3,2,1,0:T(8,128)S(1)}, u32[]{:S(2)}, u32[]{:S(2)}) collective-permute-start(f32[3,3,208,128]{3,2,1,0:T(8,128)S(1)} %get-tuple-element.106.refs_2_), channel_id=1, source_target_pairs={{1,0},{2,1},{3,2},{4,3},{5,4},{6,5},{7,6},{8,7},{9,8},{10,9},{11,1... | collective-permute-start | bytes 2875400 | tf_op jit(solution)/shard_map/ppermute | solution.py:573
  98.5 26.7 %collective-permute-start.6 = (f32[3,3,208,128]{3,2,1,0:T(8,128)S(1)}, f32[3,3,208,128]{3,2,1,0:T(8,128)S(1)}, u32[]{:S(2)}, u32[]{:S(2)}) collective-permute-start(f32[3,3,208,128]{3,2,1,0:T(8,128)S(1)} %get-tuple-element.116.refs_3_), channel_id=1, source_target_pairs={{0,1},{1,2},{2,3},{3,4},{4,5},{5,6},{6,7},{7,8},{8,9},{9,10},{10,1... | collective-permute-start | bytes 2875400 | tf_op jit(solution)/shard_map/ppermute | solution.py:573
  98.6 26.6 %collective-permute-start.7 = (f32[3,3,208,128]{3,2,1,0:T(8,128)S(1)}, f32[3,3,208,128]{3,2,1,0:T(8,128)S(1)}, u32[]{:S(2)}, u32[]{:S(2)}) collective-permute-start(f32[3,3,208,128]{3,2,1,0:T(8,128)S(1)} %get-tuple-element.115.refs_2_), channel_id=1, source_target_pairs={{1,0},{2,1},{3,2},{4,3},{5,4},{6,5},{7,6},{8,7},{9,8},{10,9},{11,1... | collective-permute-start | bytes 2875400 | tf_op jit(solution)/shard_map/ppermute | solution.py:573
  105.5 51.1 %collective-permute-start.13 = (f32[2,3,3,208,128]{4,3,2,1,0:T(8,128)S(1)}, f32[2,3,3,208,128]{4,3,2,1,0:T(8,128)S(1)}, u32[]{:S(2)}, u32[]{:S(2)}) collective-permute-start(f32[2,3,3,208,128]{4,3,2,1,0:T(8,128)S(1)} %copy-done.10), channel_id=1, source_target_pairs={{0,64},{64,0},{1,65},{65,1},{2,66},{66,2},{3,67},{67,3},{4,68},{68... | collective-permute-start | bytes 5750792 | tf_op jit(solution)/shard_map/ppermute | solution.py:570
  127.8 18.9 %collective-permute-start.8 = (f32[2,3,208,128]{3,2,1,0:T(8,128)S(1)}, f32[2,3,208,128]{3,2,1,0:T(8,128)S(1)}, u32[]{:S(2)}, u32[]{:S(2)}) collective-permute-start(f32[2,3,208,128]{3,2,1,0:T(8,128)S(1)} %get-tuple-element.124.sn), channel_id=1, source_target_pairs={{0,1},{1,2},{2,3},{3,4},{4,5},{5,6},{6,7},{7,8},{8,9},{9,10},{10,1... | collective-permute-start | bytes 1916936 | tf_op jit(solution)/shard_map/ppermute | solution.py:573
  127.9 18.8 %collective-permute-start.9 = (f32[2,3,208,128]{3,2,1,0:T(8,128)S(1)}, f32[2,3,208,128]{3,2,1,0:T(8,128)S(1)}, u32[]{:S(2)}, u32[]{:S(2)}) collective-permute-start(f32[2,3,208,128]{3,2,1,0:T(8,128)S(1)} %get-tuple-element.123.ss), channel_id=1, source_target_pairs={{1,0},{2,1},{3,2},{4,3},{5,4},{6,5},{7,6},{8,7},{9,8},{10,9},{11,1... | collective-permute-start | bytes 1916936 | tf_op jit(solution)/shard_map/ppermute | solution.py:573
  149.7 18.0 %collective-permute-start.10 = (f32[2,3,208,128]{3,2,1,0:T(8,128)S(1)}, f32[2,3,208,128]{3,2,1,0:T(8,128)S(1)}, u32[]{:S(2)}, u32[]{:S(2)}) collective-permute-start(f32[2,3,208,128]{3,2,1,0:T(8,128)S(1)} %get-tuple-element.128.sn), channel_id=1, source_target_pairs={{0,1},{1,2},{2,3},{3,4},{4,5},{5,6},{6,7},{7,8},{8,9},{9,10},{10,1... | collective-permute-start | bytes 1916936 | tf_op jit(solution)/shard_map/ppermute | solution.py:573
  149.8 17.9 %collective-permute-start.11 = (f32[2,3,208,128]{3,2,1,0:T(8,128)S(1)}, f32[2,3,208,128]{3,2,1,0:T(8,128)S(1)}, u32[]{:S(2)}, u32[]{:S(2)}) collective-permute-start(f32[2,3,208,128]{3,2,1,0:T(8,128)S(1)} %get-tuple-element.127.ss), channel_id=1, source_target_pairs={{1,0},{2,1},{3,2},{4,3},{5,4},{6,5},{7,6},{8,7},{9,8},{10,9},{11,1... | collective-permute-start | bytes 1916936 | tf_op jit(solution)/shard_map/ppermute | solution.py:573
  170.3 11.7 %collective-permute-start.12 = (f32[3,16,16,128]{3,2,1,0:T(8,128)S(1)}, f32[3,16,16,128]{3,2,1,0:T(8,128)S(1)}, u32[]{:S(2)}, u32[]{:S(2)}) collective-permute-start(f32[3,16,16,128]{3,2,1,0:T(8,128)S(1)} %get-tuple-element.132), channel_id=1, source_target_pairs={{0,64},{64,0},{1,65},{65,1},{2,66},{66,2},{3,67},{67,3},{4,68},{68... | collective-permute-start | bytes 1179656 | tf_op jit(solution)/shard_map/ppermute | solution.py:570
  174.8 21.5 %collective-permute-start.14 = (f32[2,3,208,128]{3,2,1,0:T(8,128)S(1)}, f32[2,3,208,128]{3,2,1,0:T(8,128)S(1)}, u32[]{:S(2)}, u32[]{:S(2)}) collective-permute-start(f32[2,3,208,128]{3,2,1,0:T(8,128)S(1)} %pad_maximum_fusion), channel_id=1, source_target_pairs={{0,1},{1,2},{2,3},{3,4},{4,5},{5,6},{6,7},{7,8},{8,9},{9,10},{10,1... | collective-permute-start | bytes 1916936 | tf_op jit(solution)/shard_map/ppermute | solution.py:573
  175.0 21.4 %collective-permute-start.15 = (f32[2,3,208,128]{3,2,1,0:T(8,128)S(1)}, f32[2,3,208,128]{3,2,1,0:T(8,128)S(1)}, u32[]{:S(2)}, u32[]{:S(2)}) collective-permute-start(f32[2,3,208,128]{3,2,1,0:T(8,128)S(1)} %pad_maximum_fusion.1), channel_id=1, source_target_pairs={{1,0},{2,1},{3,2},{4,3},{5,4},{6,5},{7,6},{8,7},{9,8},{10,9},{11,1... | collective-permute-start | bytes 1916936 | tf_op jit(solution)/shard_map/ppermute | solution.py:573
  183.1 26.9 %collective-permute-start.23 = (f32[2,3,208,128]{3,2,1,0:T(8,128)S(1)}, f32[2,3,208,128]{3,2,1,0:T(8,128)S(1)}, u32[]{:S(2)}, u32[]{:S(2)}) collective-permute-start(f32[2,3,208,128]{3,2,1,0:T(8,128)S(1)} %get-tuple-element.144.refs_3_), channel_id=1, source_target_pairs={{0,1},{1,2},{2,3},{3,4},{4,5},{5,6},{6,7},{7,8},{8,9},{9,10},{10,1... | collective-permute-start | bytes 1916936 | tf_op jit(solution)/shard_map/ppermute | solution.py:573
  183.2 26.8 %collective-permute-start.24 = (f32[2,3,208,128]{3,2,1,0:T(8,128)S(1)}, f32[2,3,208,128]{3,2,1,0:T(8,128)S(1)}, u32[]{:S(2)}, u32[]{:S(2)}) collective-permute-start(f32[2,3,208,128]{3,2,1,0:T(8,128)S(1)} %get-tuple-element.143.refs_2_), channel_id=1, source_target_pairs={{1,0},{2,1},{3,2},{4,3},{5,4},{6,5},{7,6},{8,7},{9,8},{10,9},{11,1... | collective-permute-start | bytes 1916936 | tf_op jit(solution)/shard_map/ppermute | solution.py:573
  212.9 32.8 %collective-permute-start.25 = (f32[2,3,208,128]{3,2,1,0:T(8,128)S(1)}, f32[2,3,208,128]{3,2,1,0:T(8,128)S(1)}, u32[]{:S(2)}, u32[]{:S(2)}) collective-permute-start(f32[2,3,208,128]{3,2,1,0:T(8,128)S(1)} %get-tuple-element.149.refs_3_), channel_id=1, source_target_pairs={{0,1},{1,2},{2,3},{3,4},{4,5},{5,6},{6,7},{7,8},{8,9},{9,10},{10,1... | collective-permute-start | bytes 1916936 | tf_op jit(solution)/shard_map/ppermute | solution.py:573
  213.0 32.7 %collective-permute-start.26 = (f32[2,3,208,128]{3,2,1,0:T(8,128)S(1)}, f32[2,3,208,128]{3,2,1,0:T(8,128)S(1)}, u32[]{:S(2)}, u32[]{:S(2)}) collective-permute-start(f32[2,3,208,128]{3,2,1,0:T(8,128)S(1)} %get-tuple-element.148.refs_2_), channel_id=1, source_target_pairs={{1,0},{2,1},{3,2},{4,3},{5,4},{6,5},{7,6},{8,7},{9,8},{10,9},{11,1... | collective-permute-start | bytes 1916936 | tf_op jit(solution)/shard_map/ppermute | solution.py:573
  222.1 6.3 %collective-permute-start.17 = (f32[2,8,128]{2,1,0:T(8,128)S(1)}, f32[2,8,128]{2,1,0:T(8,128)S(1)}, u32[]{:S(2)}, u32[]{:S(2)}) collective-permute-start(f32[2,8,128]{2,1,0:T(8,128)S(1)} %fusion.1), channel_id=1, source_target_pairs={{0,1},{1,0},{2,3},{3,2},{4,5},{5,4},{6,7},{7,6},{8,9},{9,8},{10,11... | collective-permute-start | bytes 24584 | tf_op jit(solution)/shard_map/ppermute | solution.py:579
  228.4 4.3 %collective-permute-start.18 = (f32[2,8,128]{2,1,0:T(8,128)S(1)}, f32[2,8,128]{2,1,0:T(8,128)S(1)}, u32[]{:S(2)}, u32[]{:S(2)}) collective-permute-start(f32[2,8,128]{2,1,0:T(8,128)S(1)} %fusion.4), channel_id=1, source_target_pairs={{0,2},{1,3},{2,0},{3,1},{4,6},{5,7},{6,4},{7,5},{8,10},{9,11},{10,... | collective-permute-start | bytes 24584 | tf_op jit(solution)/shard_map/ppermute | solution.py:579
  232.7 2.5 collective-permute-start.19
  235.2 4.0 %collective-permute-start.20 = (f32[2,8,128]{2,1,0:T(8,128)S(1)}, f32[2,8,128]{2,1,0:T(8,128)S(1)}, u32[]{:S(2)}, u32[]{:S(2)}) collective-permute-start(f32[2,8,128]{2,1,0:T(8,128)S(1)} %add.77), channel_id=1, source_target_pairs={{0,8},{1,9},{2,10},{3,11},{4,12},{5,13},{6,14},{7,15},{8,0},{9,1},... | collective-permute-start | bytes 24584 | tf_op jit(solution)/shard_map/ppermute | solution.py:579
  239.2 2.5 collective-permute-start.21
  241.7 4.0 %collective-permute-start.22 = (f32[2,8,128]{2,1,0:T(8,128)S(1)}, f32[2,8,128]{2,1,0:T(8,128)S(1)}, u32[]{:S(2)}, u32[]{:S(2)}) collective-permute-start(f32[2,8,128]{2,1,0:T(8,128)S(1)} %add.79), channel_id=1, source_target_pairs={{0,32},{1,33},{2,34},{3,35},{4,36},{5,37},{6,38},{7,39},{8,40},{9,... | collective-permute-start | bytes 24584 | tf_op jit(solution)/shard_map/ppermute | solution.py:579
  248.7 14.8 %collective-permute-start.34 = (f32[2,3,208,128]{3,2,1,0:T(8,128)S(1)}, f32[2,3,208,128]{3,2,1,0:T(8,128)S(1)}, u32[]{:S(2)}, u32[]{:S(2)}) collective-permute-start(f32[2,3,208,128]{3,2,1,0:T(8,128)S(1)} %get-tuple-element.158.sn), channel_id=1, source_target_pairs={{0,1},{1,2},{2,3},{3,4},{4,5},{5,6},{6,7},{7,8},{8,9},{9,10},{10,1... | collective-permute-start | bytes 1916936 | tf_op jit(solution)/shard_map/ppermute | solution.py:573
  248.8 14.7 %collective-permute-start.35 = (f32[2,3,208,128]{3,2,1,0:T(8,128)S(1)}, f32[2,3,208,128]{3,2,1,0:T(8,128)S(1)}, u32[]{:S(2)}, u32[]{:S(2)}) collective-permute-start(f32[2,3,208,128]{3,2,1,0:T(8,128)S(1)} %get-tuple-element.157.ss), channel_id=1, source_target_pairs={{1,0},{2,1},{3,2},{4,3},{5,4},{6,5},{7,6},{8,7},{9,8},{10,9},{11,1... | collective-permute-start | bytes 1916936 | tf_op jit(solution)/shard_map/ppermute | solution.py:573
  266.5 14.8 %collective-permute-start.36 = (f32[2,3,208,128]{3,2,1,0:T(8,128)S(1)}, f32[2,3,208,128]{3,2,1,0:T(8,128)S(1)}, u32[]{:S(2)}, u32[]{:S(2)}) collective-permute-start(f32[2,3,208,128]{3,2,1,0:T(8,128)S(1)} %get-tuple-element.162.sn), channel_id=1, source_target_pairs={{0,1},{1,2},{2,3},{3,4},{4,5},{5,6},{6,7},{7,8},{8,9},{9,10},{10,1... | collective-permute-start | bytes 1916936 | tf_op jit(solution)/shard_map/ppermute | solution.py:573
  266.5 14.7 %collective-permute-start.37 = (f32[2,3,208,128]{3,2,1,0:T(8,128)S(1)}, f32[2,3,208,128]{3,2,1,0:T(8,128)S(1)}, u32[]{:S(2)}, u32[]{:S(2)}) collective-permute-start(f32[2,3,208,128]{3,2,1,0:T(8,128)S(1)} %get-tuple-element.161.ss), channel_id=1, source_target_pairs={{1,0},{2,1},{3,2},{4,3},{5,4},{6,5},{7,6},{8,7},{9,8},{10,9},{11,1... | collective-permute-start | bytes 1916936 | tf_op jit(solution)/shard_map/ppermute | solution.py:573
  283.8 30.6 %collective-permute-start.38 = (f32[3,16,16,128]{3,2,1,0:T(8,128)S(1)}, f32[3,16,16,128]{3,2,1,0:T(8,128)S(1)}, u32[]{:S(2)}, u32[]{:S(2)}) collective-permute-start(f32[3,16,16,128]{3,2,1,0:T(8,128)S(1)} %get-tuple-element.167), channel_id=1, source_target_pairs={{0,64},{64,0},{1,65},{65,1},{2,66},{66,2},{3,67},{67,3},{4,68},{68... | collective-permute-start | bytes 1179656 | tf_op jit(solution)/shard_map/ppermute | solution.py:570
  294.9 2.5 collective-permute-start.28
  297.4 4.0 %collective-permute-start.29 = (f32[2,8,128]{2,1,0:T(8,128)S(1)}, f32[2,8,128]{2,1,0:T(8,128)S(1)}, u32[]{:S(2)}, u32[]{:S(2)}) collective-permute-start(f32[2,8,128]{2,1,0:T(8,128)S(1)} %add.82), channel_id=1, source_target_pairs={{0,2},{1,3},{2,0},{3,1},{4,6},{5,7},{6,4},{7,5},{8,10},{9,11},{10,... | collective-permute-start | bytes 24584 | tf_op jit(solution)/shard_map/ppermute | solution.py:579
  301.4 2.5 collective-permute-start.30
  303.9 4.0 %collective-permute-start.31 = (f32[2,8,128]{2,1,0:T(8,128)S(1)}, f32[2,8,128]{2,1,0:T(8,128)S(1)}, u32[]{:S(2)}, u32[]{:S(2)}) collective-permute-start(f32[2,8,128]{2,1,0:T(8,128)S(1)} %add.84), channel_id=1, source_target_pairs={{0,8},{1,9},{2,10},{3,11},{4,12},{5,13},{6,14},{7,15},{8,0},{9,1},... | collective-permute-start | bytes 24584 | tf_op jit(solution)/shard_map/ppermute | solution.py:579
  310.4 4.0 %collective-permute-start.33 = (f32[2,8,128]{2,1,0:T(8,128)S(1)}, f32[2,8,128]{2,1,0:T(8,128)S(1)}, u32[]{:S(2)}, u32[]{:S(2)}) collective-permute-start(f32[2,8,128]{2,1,0:T(8,128)S(1)} %add.86), channel_id=1, source_target_pairs={{0,32},{1,33},{2,34},{3,35},{4,36},{5,37},{6,38},{7,39},{8,40},{9,... | collective-permute-start | bytes 24584 | tf_op jit(solution)/shard_map/ppermute | solution.py:579
  316.7 15.0 %collective-permute-start.47 = (f32[2,3,208,128]{3,2,1,0:T(8,128)S(1)}, f32[2,3,208,128]{3,2,1,0:T(8,128)S(1)}, u32[]{:S(2)}, u32[]{:S(2)}) collective-permute-start(f32[2,3,208,128]{3,2,1,0:T(8,128)S(1)} %get-tuple-element.179.refs_3_), channel_id=1, source_target_pairs={{0,1},{1,2},{2,3},{3,4},{4,5},{5,6},{6,7},{7,8},{8,9},{9,10},{10,1... | collective-permute-start | bytes 1916936 | tf_op jit(solution)/shard_map/ppermute | solution.py:573
  316.7 15.0 %collective-permute-start.48 = (f32[2,3,208,128]{3,2,1,0:T(8,128)S(1)}, f32[2,3,208,128]{3,2,1,0:T(8,128)S(1)}, u32[]{:S(2)}, u32[]{:S(2)}) collective-permute-start(f32[2,3,208,128]{3,2,1,0:T(8,128)S(1)} %get-tuple-element.178.refs_2_), channel_id=1, source_target_pairs={{1,0},{2,1},{3,2},{4,3},{5,4},{6,5},{7,6},{8,7},{9,8},{10,9},{11,1... | collective-permute-start | bytes 1916936 | tf_op jit(solution)/shard_map/ppermute | solution.py:573
  334.6 44.4 %collective-permute-start.49 = (f32[2,3,208,128]{3,2,1,0:T(8,128)S(1)}, f32[2,3,208,128]{3,2,1,0:T(8,128)S(1)}, u32[]{:S(2)}, u32[]{:S(2)}) collective-permute-start(f32[2,3,208,128]{3,2,1,0:T(8,128)S(1)} %get-tuple-element.184.refs_3_), channel_id=1, source_target_pairs={{0,1},{1,2},{2,3},{3,4},{4,5},{5,6},{6,7},{7,8},{8,9},{9,10},{10,1... | collective-permute-start | bytes 1916936 | tf_op jit(solution)/shard_map/ppermute | solution.py:573
  334.7 44.3 %collective-permute-start.50 = (f32[2,3,208,128]{3,2,1,0:T(8,128)S(1)}, f32[2,3,208,128]{3,2,1,0:T(8,128)S(1)}, u32[]{:S(2)}, u32[]{:S(2)}) collective-permute-start(f32[2,3,208,128]{3,2,1,0:T(8,128)S(1)} %get-tuple-element.183.refs_2_), channel_id=1, source_target_pairs={{1,0},{2,1},{3,2},{4,3},{5,4},{6,5},{7,6},{8,7},{9,8},{10,9},{11,1... | collective-permute-start | bytes 1916936 | tf_op jit(solution)/shard_map/ppermute | solution.py:573
  341.7 9.5 %collective-permute-start.39 = (f32[1,8,128]{2,1,0:T(8,128)S(1)}, f32[1,8,128]{2,1,0:T(8,128)S(1)}, u32[]{:S(2)}, u32[]{:S(2)}) collective-permute-start(f32[1,8,128]{2,1,0:T(8,128)S(1)} %add_bitcast_fusion), channel_id=1, source_target_pairs={{0,64},{64,0},{1,65},{65,1},{2,66},{66,2},{3,67},{67,3},{4,68},{68... | collective-permute-start | bytes 12296 | tf_op jit(solution)/shard_map/ppermute | solution.py:570
  351.2 2.8 collective-permute-start.40
  354.0 4.3 %collective-permute-start.41 = (f32[1,8,128]{2,1,0:T(8,128)S(1)}, f32[1,8,128]{2,1,0:T(8,128)S(1)}, u32[]{:S(2)}, u32[]{:S(2)}) collective-permute-start(f32[1,8,128]{2,1,0:T(8,128)S(1)} %add.90), channel_id=1, source_target_pairs={{0,2},{1,3},{2,0},{3,1},{4,6},{5,7},{6,4},{7,5},{8,10},{9,11},{10,... | collective-permute-start | bytes 12296 | tf_op jit(solution)/shard_map/ppermute | solution.py:579
  360.7 4.0 %collective-permute-start.43 = (f32[1,8,128]{2,1,0:T(8,128)S(1)}, f32[1,8,128]{2,1,0:T(8,128)S(1)}, u32[]{:S(2)}, u32[]{:S(2)}) collective-permute-start(f32[1,8,128]{2,1,0:T(8,128)S(1)} %add.92), channel_id=1, source_target_pairs={{0,8},{1,9},{2,10},{3,11},{4,12},{5,13},{6,14},{7,15},{8,0},{9,1},... | collective-permute-start | bytes 12296 | tf_op jit(solution)/shard_map/ppermute | solution.py:579
  367.1 4.0 %collective-permute-start.45 = (f32[1,8,128]{2,1,0:T(8,128)S(1)}, f32[1,8,128]{2,1,0:T(8,128)S(1)}, u32[]{:S(2)}, u32[]{:S(2)}) collective-permute-start(f32[1,8,128]{2,1,0:T(8,128)S(1)} %add.94), channel_id=1, source_target_pairs={{0,32},{1,33},{2,34},{3,35},{4,36},{5,37},{6,38},{7,39},{8,40},{9,... | collective-permute-start | bytes 12296 | tf_op jit(solution)/shard_map/ppermute | solution.py:579
  372.3 10.0 %collective-permute-start.46 = (f32[2,3,3,192,128]{4,3,2,1,0:T(8,128)S(1)}, f32[2,3,3,192,128]{4,3,2,1,0:T(8,128)S(1)}, u32[]{:S(2)}, u32[]{:S(2)}) collective-permute-start(f32[2,3,3,192,128]{4,3,2,1,0:T(8,128)S(1)} %get-tuple-element.176), channel_id=1, source_target_pairs={{0,64},{64,0},{1,65},{65,1},{2,66},{66,2},{3,67},{67,3},{4,68},{68... | collective-permute-start | bytes 5308424 | tf_op jit(solution)/shard_map/ppermute | solution.py:570
  382.2 3.8 collective-permute-start.51
  (16 other events, 86.1 us)

commit v3 on v2

--- a/solution.py
+++ b/solution.py
@@ -147,15 +147,6 @@
     lax.fori_loop(0, n, step, 0)
 
 
-def tot(s_ref, i):
-    return jnp.sum(s_ref[i], keepdims=True)
-
-
-def first_step(s_ref):
-    rr = tot(s_ref, 0)
-    return rr / (rr + tot(s_ref, 1))
-
-
 def fold(x):
     own = x[PAD:-PAD]
     return jnp.sum(own.reshape(own.shape[0] // 8, 8, own.shape[1]), axis=0)
@@ -187,13 +178,25 @@
     o_ref[:, 2 * FIELDS] = i_ref[...]
 
 
-def scatter_body(half, c_ref, idx_ref, p_ref, do_ref, ds_ref, go_ref, gs_ref, acc):
+def emit(half, c, acc, at, own_ref, snd_ref):
+    cols = 2 * half
+    for w in range(2):
+
+        def one(i, carry):
+            base = (w * 3 + i) * (cols * 8) + at
+            for f in range(FIELDS):
+                x = acc[pl.ds(base + f, cols, stride=8), :]
+                split_store(x, half, c, own_ref, snd_ref, (w, f, i))
+            return carry
+
+        lax.fori_loop(0, 3, one, 0)
+
+
+def scatter_body(half, c_ref, idx_ref, p_ref, acc, go_ref, gs_ref):
     owners, slots = idx_ref.shape
     blocks = 2 * FIELDS + 1
     lev = p_ref.shape[1]
     cells = acc.shape[0] // 8
-    cols = 2 * half
-    c = c_ref[0]
     chunk = 64
 
     def clear(t, carry):
@@ -212,19 +215,11 @@
         return carry
 
     lax.fori_loop(0, owners, put, 0)
-
-    for w in range(2):
-
-        def one(i, carry):
-            base = (w * 3 + i) * (cols * 8)
-            for f in range(FIELDS):
-                x = acc[pl.ds(base + f, cols, stride=8), :]
-                split_store(x, half, c, do_ref, ds_ref, (w, f, i))
-                y = acc[pl.ds(base + FIELDS + f, cols, stride=8), :]
-                split_store(y, half, c, go_ref, gs_ref, (w, f, i))
-            return carry
-
-        lax.fori_loop(0, 3, one, 0)
+    emit(half, c_ref[0], acc, FIELDS, go_ref, gs_ref)
+
+
+def diag_body(half, c_ref, acc, do_ref, ds_ref):
+    emit(half, c_ref[0], acc, 0, do_ref, ds_ref)
 
 
 def wind_body(half, c_ref, w_ref, m_ref, o_ref, s_ref, ra_ref, rf_ref):
@@ -288,7 +283,10 @@
     return [f_ref[f, i] for i in range(5)]
 
 
-def adj_mid_body(ext, *refs):
+def adj_mid_body(ext, carry, *refs):
+    if carry:
+        refs[-1][...] = refs[12][...]
+        refs = refs[:12] + refs[13:-1]
     (fl, mid, ss, sn, rs, rn, f2, f1, w2, wh2, w1, ra) = refs[:12]
     n = 12
     if ext:
@@ -315,28 +313,17 @@
 
 
 def adj_last_body(mode, *refs):
-    ext = mode == 0
     (fl, mid, ss, sn, rs, rn, f0, w0, wh0, ra) = refs[:10]
-    n = 10
-    if mode == 1:
-        sc, g0, g1 = refs[n : n + 3]
-        n += 3
-    outs = refs[n:]
+    outs = refs[10:]
     fs, fn = fl[0], fl[1]
     rhs = ra[...]
-    if mode == 1:
-        a = first_step(sc)
 
     def one(f):
         lam = adj_post(f, mid, ss, sn, rs, rn, fs, fn)
-        src = five(f, f0, rs, rn, ext)
+        src = five(f, f0, rs, rn, mode == 0)
         out = adj_second([lam[i] + src[i] for i in range(5)], w0, wh0, rhs)
-        one_half = [x * SCALE_Q for x in lam]
-        if mode == 1:
-            one_half = [(1.0 - a) * g1[f, i] - a * one_half[i] for i in range(5)]
-            out = [(1.0 - a) * g0[f, i] - a * out[i] for i in range(3)]
         for i in range(5):
-            outs[1][f, i] = one_half[i]
+            outs[1][f, i] = lam[i] * SCALE_Q
         for i in range(3):
             outs[0][f, i] = out[i]
         if mode < 2:
@@ -390,66 +377,52 @@
     return jnp.concatenate([e[:PAD], x[PAD:-PAD], e[PAD:]], axis=0)
 
 
-def turn_body(second, *refs):
-    x3, eg, d3, w3, ra = refs[:5]
-    n = 5
-    if second:
-        s1, s2, old = refs[n : n + 3]
-        n += 3
-        beta = tot(s2, 0) / tot(s1, 0)
-    y3, mid, ss, sn, q = refs[n:]
+def turn_body(carry, sc, x3, eg, d3, w3, ra, *outs):
+    if carry:
+        outs[4][...] = outs[0][...]
+        outs = outs[1:4]
+    mid, ss, sn = outs[:3]
+    q = None if carry else outs[3]
     rhs = ra[...]
-    q[...] = jnp.zeros_like(q)
+    if q is not None:
+        q[...] = jnp.zeros_like(q)
+    scale = sc[0]
 
     def one(f):
         rows = []
         for i in range(3):
             y = fixed(x3[f, i], eg[f, 13 + i])
-            if second:
-                y = y + beta * old[f, i]
-            y3[f, i] = y
             t = d3[f, i] * y
-            q[...] += fold(t * y)
-            rows.append(t)
+            if q is not None:
+                q[...] += fold(t * y)
+            rows.append(t * scale)
         adj_pre(f, rows, w3, rhs, mid, ss, sn)
 
     fields(x3.shape[0], one)
 
 
-def rest_body(second, *refs):
-    x0, x1, x2, eg, d0, d1, d2, ds, dn = refs[:9]
-    n = 9
-    if second:
-        s1, s2, old0, old1, old2 = refs[n : n + 5]
-        n += 5
-        beta = tot(s2, 0) / tot(s1, 0)
-    else:
-        old0 = old1 = old2 = None
-    y0, y1, y2, f0, f1, f2, q = refs[n:]
-    q[...] = jnp.zeros_like(q)
+def rest_body(sc, x0, x1, x2, eg, d0, d1, d2, ds, dn, f0, f1, f2, q=None):
+    if q is not None:
+        q[...] = jnp.zeros_like(q)
+    scale = sc[0]
 
     def one(f):
-        for x, rows, at, d, w, old, y_o, f_o in (
-            (x0, 5, 0, d0, 0, old0, y0, f0),
-            (x1, 3, 5, d1, None, old1, y1, f1),
-            (x2, 5, 8, d2, 1, old2, y2, f2),
+        for x, rows, at, d, w, f_o in (
+            (x0, 5, 0, d0, 0, f0),
+            (x1, 3, 5, d1, None, f1),
+            (x2, 5, 8, d2, 1, f2),
         ):
             for i in range(rows):
                 y = fixed(x[f, i], eg[f, at + i])
-                if second:
-                    y = y + beta * old[f, i]
-                y_o[f, i] = y
-                if rows == 3:
-                    t = d[f, i] * y
-                    q[...] += fold(t * y)
-                elif i == 0:
+                if rows == 5 and i == 0:
                     t = ds[w, f] * y
-                elif i == 4:
+                elif rows == 5 and i == 4:
                     t = dn[w, f] * y
                 else:
-                    t = d[f, i - 1] * y
-                    q[...] += fold(t * y)
-                f_o[f, i] = t
+                    t = d[f, i - (rows == 5)] * y
+                    if q is not None:
+                        q[...] += fold(t * y)
+                f_o[f, i] = t * scale
 
     fields(x0.shape[0], one)
 
@@ -466,55 +439,112 @@
     fields(v0.shape[0], one)
 
 
-def resid_body(sc, v0, v1, g0, g1, g2, g3, z2, z3, r2, r3, q):
-    a = first_step(sc)
-    q[...] = jnp.zeros_like(q)
-
-    def dots(r, g):
-        q[0] += fold(r * r)
-        q[1] += fold(r * g)
-
-    def one(f):
-        for i in range(5):
-            r = (1.0 - a) * g3[f, i] - a * z3[f, i]
-            r3[f, i] = r
-            if 0 < i < 4:
-                dots(r, g3[f, i])
-                dots(v1[f, i], g1[f, i])
-        for i in range(3):
-            r = (1.0 - a) * g2[f, i] - a * z2[f, i]
-            r2[f, i] = r
-            dots(r, g2[f, i])
-            dots(v0[f, i], g0[f, i])
-
-    fields(v0.shape[0], one)
-
-
-def final_body(kind, c_ref, s1, s2, s3, *refs):
-    r = refs[0:4]
-    g = refs[4:8]
+def lanes(shape):
+    return lax.broadcasted_iota(jnp.int32, shape, len(shape) - 1)
+
+
+def sums_body(n, *refs):
+    out = refs[-1]
+    parts = [refs[:n], refs[n : 3 * n], refs[3 * n : 4 * n]]
+    acc = jnp.zeros(refs[0].shape, F32)
+    at = 4 * n
+    for _ in range(n):
+        xs, ds = refs[at : at + 4], refs[at + 4 : at + 8]
+        at += 8
+
+        def one(f, acc):
+            for x, d in zip(xs, ds):
+                off = (x.shape[1] - 3) // 2
+                for i in range(3):
+                    v = x[f, i + off]
+                    acc = acc + fold(d[f, i] * v * v)
+            return acc
+
+        nf = xs[0].shape[0]
+        acc = one(0, acc) if nf == 1 else lax.fori_loop(0, nf, one, acc)
+    lane = lanes(out.shape)
+    row = jnp.where(lane == 3, jnp.sum(acc, keepdims=True), 0.0)
+    for k in range(3):
+        val = parts[k][0][...]
+        for p in parts[k][1:]:
+            val = val + p[...]
+        row = jnp.where(lane == k, jnp.sum(val, keepdims=True), row)
+    out[...] = row
+
+
+def add_body(a, b, out):
+    out[...] = a[...] + b[...]
+
+
+def ring_body(step, pos_ref, a, b, c, d, out):
+    mine = lax.rem(lax.div(pos_ref[0], step), 4)
+    rows = [a[...], b[...], c[...], d[...]]
+    total = jnp.zeros(out.shape, F32)
+    for place in range(4):
+        gap = lax.rem(mine + 4 - place, 4)
+        term = rows[0]
+        for k in (1, 2, 3):
+            term = jnp.where(gap == k, rows[k], term)
+        total = total + term
+    out[...] = total
+
+
+def solve_body(hs, got, out):
+    row = got[...]
+    at = lanes(row.shape)
+
+    def pick(k):
+        return jnp.sum(jnp.where(at == k, row, 0.0), axis=1, keepdims=True)
+
+    rr, bg, zz, bz = [pick(k) for k in range(4)]
+    sig, inv = hs[0], hs[1]
+    a0 = rr / (rr + bg)
+    left = bg / (rr + bg)
+    c = a0 * inv
+    sbg = bg * sig
+    rr1 = c * (c * (zz - sbg * (sbg / rr)))
+    beta = rr1 / rr
+    p = left + beta
+    curve = p * (p * bg) - 2.0 * (p * (c * (inv * zz))) + c * (c * bz)
+    a1 = rr1 / (rr1 + beta * beta * rr + curve)
+    terms = (
+        a0 + a1 * p,
+        -(a1 * c),
+        left - a1 * p,
+        a1 * c - c - a1 * (p * inv),
+        a1 * c,
+    )
+    w = jnp.zeros(row.shape, F32)
+    for k, t in enumerate(terms):
+        w = jnp.where(at == k, t, w)
+    out[...] = w
+
+
+def final_body(kind, c_ref, k_ref, *refs):
+    row = k_ref[...]
+    at = lanes(row.shape)
+
+    def pick(k):
+        return jnp.sum(jnp.where(at == k, row, 0.0), axis=1, keepdims=True)
+
+    g, z = refs[0:4], refs[4:8]
     n = 8
     if kind == "res":
-        z = refs[8:12]
+        w = refs[8:12]
         n = 12
+        kg, kz, kw = pick(2), pick(3), pick(4)
+    else:
+        kg, kz = pick(0), pick(1)
     keep, send = refs[n:]
     c = c_ref[0]
-    rr0, rr1 = tot(s1, 0), tot(s2, 0)
-    a0 = rr0 / (rr0 + tot(s1, 1))
-    beta = rr1 / rr0
-    a1 = rr1 / (rr1 + beta * (2.0 * tot(s2, 1) + beta * rr0) + tot(s3, 0))
 
     def one(f):
         for k in range(4):
             off = k % 2
             for i in range(3):
-                res = r[k][f, i + off][PAD:-PAD]
-                grad = g[k][f, i + off][PAD:-PAD]
-                d = res + beta * grad
+                val = kg * g[k][f, i + off][PAD:-PAD] + kz * z[k][f, i + off][PAD:-PAD]
                 if kind == "res":
-                    val = res - a1 * (d + z[k][f, i + off][PAD:-PAD])
-                else:
-                    val = a0 * grad + a1 * d
+                    val = val + kw * w[k][f, i + off][PAD:-PAD]
 
                 @pl.when(c == k // 2)
                 def _():
@@ -562,6 +592,7 @@
     pos = lax.axis_index("space")
     bands = lax.axis_size("space")
     c_arr = c.reshape(1)
+    pos_arr = pos.astype(jnp.int32).reshape(1)
     flags = jnp.stack([(pos > 0), (pos < bands - 1)]).astype(F32)
     north = [(i, (i + 1) % bands) for i in range(bands)]
     south = [((i + 1) % bands, i) for i in range(bands)]
@@ -572,15 +603,22 @@
     def exchange(ss, sn):
         return lax.ppermute(sn, "space", north), lax.ppermute(ss, "space", south)
 
-    def total(parts):
-        vals = swap(parts) + parts
-        step = 1
-        while step < bands:
-            vals = vals + lax.ppermute(
-                vals, "space", [(i, i ^ step) for i in range(bands)]
-            )
-            step *= 2
-        return vals
+    def ring_sum(row, step):
+        shifts = []
+        for k in (1, 2, 3):
+            pairs = []
+            for i in range(bands):
+                digit = (i // step) % 4
+                pairs.append((i, i + ((digit + k) % 4 - digit) * step))
+            shifts.append(pairs)
+        got = tuple(lax.ppermute(row, "space", p) for p in shifts)
+        return call(
+            functools.partial(ring_body, step),
+            (pos_arr, row) + got,
+            [SM] + [VM] * 4,
+            [sds(1, lev)],
+            flops=1e5,
+        )[0]
 
     live = (
         jnp.arange(slots, dtype=jnp.int32)[None, :] < obs_count.reshape(owners)[:, None]
@@ -620,16 +658,28 @@
     wh0 = jnp.stack([from_s[0], from_n[0]])
     wh2 = jnp.stack([from_s[1], from_n[1]])
 
+    size = jnp.abs(mixing)
+    grow = (1.0 + MIXC * jnp.max(jnp.sum(size, 0))) * (1.0 + MIXC * jnp.max(jnp.sum(size, 1)))
+    grow = grow * grow
+    inv = grow * grow
+    sig = 1.0 / inv
+    sig_arr = sig.reshape(1)
+    one_arr = jnp.ones((1,), F32)
+    span = jnp.stack([sig, 1.0 / sig])
+
     idx = jnp.maximum(got[:, 2 * FIELDS, :, 0], 0.0).astype(jnp.int32)
-    d_own, d_snd, g_own, g_snd = call(
+    idx, wh0, wh2, w0, w1, w2, w3, sig_arr, span = lax.optimization_barrier(
+        (idx, wh0, wh2, w0, w1, w2, w3, sig_arr, span)
+    )
+    halves = [sds(2, FIELDS, 3, wide, lev)] * 2
+    acc, g_own, g_snd = call(
         functools.partial(scatter_body, half),
         (c_arr, idx, got.reshape(owners * blocks * slots, lev)),
         [SM, SM, VM],
-        [sds(2, FIELDS, 3, wide, lev)] * 4,
-        scratch=[pltpu.VMEM((2 * cells * 8, lev), F32)],
-        vmem=16 * 2**20,
+        [sds(2 * cells * 8, lev)] + halves,
     )
     g_got = swap(g_snd)
+    d_own, d_snd = call(functools.partial(diag_body, half), (c_arr, acc), [SM, VM], halves)
     d_got = swap(d_snd)
     groups = []
     f0 = 0
@@ -655,27 +705,31 @@
     def state_of(nf, n):
         return [sds(nf, wide, lev)] + [sds(n, nf, wide, lev)] * 2
 
-    def adj_mid(state, f2, f1, g0=None):
+    def adj_mid(state, f2, f1, g0=None, row=None):
         mid, ss, sn = state
         nf = mid.shape[0]
         rs, rn = exchange(ss, sn)
         ext = g0 is not None
+        carry = row is not None
         n = 3 if ext else 2
         ins = (flags, mid, ss, sn, rs, rn, f2, f1, w2, wh2, w1, ra) + ((g0,) if ext else ())
+        ins += (row,) if carry else ()
         o = call(
-            functools.partial(adj_mid_body, ext),
+            functools.partial(adj_mid_body, ext, carry),
             ins,
             [SM] + [VM] * (len(ins) - 1),
-            [row5(nf), row3(nf)] + state_of(nf, n),
+            [row5(nf), row3(nf)] + state_of(nf, n) + ([sds(1, lev)] if carry else []),
         )
+        if carry:
+            return o[0], o[1], tuple(o[2:5]), o[5]
         return o[0], o[1], tuple(o[2:])
 
-    def adj_last(mode, state, f0, extra=()):
+    def adj_last(mode, state, f0):
         mid, ss, sn = state
         nf = mid.shape[0]
         rs, rn = exchange(ss, sn)
-        ins = (flags, mid, ss, sn, rs, rn, f0, w0, wh0, ra) + extra
-        specs = [SM] + [VM] * 9 + ([VM] * 3 if extra else [])
+        ins = (flags, mid, ss, sn, rs, rn, f0, w0, wh0, ra)
+        specs = [SM] + [VM] * 9
         outs = [row3(nf), row5(nf)] + (state_of(nf, 2) if mode < 2 else [])
         o = call(functools.partial(adj_last_body, mode), ins, specs, outs)
         return o[0], o[1], tuple(o[2:])
@@ -705,34 +759,34 @@
             [row5(nf), row3(nf), sds(nf, 16, 2 * PAD, lev)],
         )
 
-    def turn(xs, eg, dd, ds, dn, sums=(), old=None):
+    def turn(xs, eg, dd, ds, dn, scale, row=None):
         eg = swap(eg)
-        second = old is not None
         x0, x1, x2, x3 = xs
         nf = x3.shape[0]
-        ex = sums + (old[3],) if second else ()
+        carry = row is not None
         o = call(
-            functools.partial(turn_body, second),
-            (x3, eg, dd[3], w3, ra) + ex,
-            [VM] * (5 + len(ex)),
-            [row3(nf)] + state_of(nf, 2) + [part],
+            functools.partial(turn_body, carry),
+            (scale, x3, eg, dd[3], w3, ra) + ((row,) if carry else ()),
+            [SM] + [VM] * (6 if carry else 5),
+            state_of(nf, 2) + [sds(1, lev) if carry else part],
         )
-        y3, state, q3 = o[0], tuple(o[1:4]), o[4]
-        ex = sums + tuple(old[:3]) if second else ()
-        y0, y1, y2, f0, f1, f2, q = call(
-            functools.partial(rest_body, second),
-            (x0, x1, x2, eg, dd[0], dd[1], dd[2], ds, dn) + ex,
-            [VM] * (9 + len(ex)),
-            [row5(nf), row3(nf), row5(nf)] * 2 + [part],
+        r = call(
+            rest_body,
+            (scale, x0, x1, x2, eg, dd[0], dd[1], dd[2], ds, dn),
+            [SM] + [VM] * 9,
+            [row5(nf), row3(nf), row5(nf)] + ([] if carry else [part]),
         )
-        return state, (y0, y1, y2, y3), (f0, f1, f2), q3 + q
+        return tuple(o[:3]), tuple(r[:3]), (o[3] if carry else (o[3], r[3]))
 
     def forward(state, v):
         x0, x1, state = fwd_first(state, v[1], v[2])
         x2, x3, eg = fwd_last(state, v[3], x0, x1)
         return (x0, x1, x2, x3), eg
 
-    grads, mids = [], []
+    def norm(v):
+        return call(norm_body, tuple(v), [VM] * 4, [part])[0]
+
+    chains = []
     for nf, gg, dd, ds, dn in groups:
         state = tuple(
             call(turn_first_body, (gg[3], gg[2], w3, ra), [VM] * 4, state_of(nf, 3))
@@ -740,37 +794,37 @@
         g3, g2, state = adj_mid(state, gg[2], gg[1], gg[0])
         g0, g1, state = adj_last(0, state, gg[0])
         g = (g0, g1, g2, g3)
-        rr = call(norm_body, g, [VM] * 4, [part])[0]
         xs, eg = forward(state, g)
-        state, ys, fs, q = turn(xs, eg, dd, ds, dn)
-        grads.append(g)
-        mids.append((state, ys, fs, rr, q))
-    s1 = total(jnp.stack([sum(m[3] for m in mids), sum(m[4] for m in mids)]))
-
-    resid, ends = [], []
-    for g, (state, _, fs, _, _) in zip(grads, mids):
-        nf = g[0].shape[0]
+        state, fs, bg = turn(xs, eg, dd, ds, dn, sig_arr)
         z3, z2, state = adj_mid(state, fs[2], fs[1])
-        v0, v1, state = adj_last(1, state, fs[0], (s1, g[0], g[1]))
-        v2, v3, q = call(
-            resid_body,
-            (s1, v0, v1) + g + (z2, z3),
-            [VM] * 9,
-            [row3(nf), row5(nf), sds(2, 8, lev)],
-        )
-        v = (v0, v1, v2, v3)
-        resid.append(v)
-        ends.append((forward(state, v), q))
-    s2 = total(sum(e[1] for e in ends))
-
-    turns = []
-    for ((xs, eg), _), (_, ys, _, _, _), (nf, gg, dd, ds, dn) in zip(ends, mids, groups):
-        turns.append(turn(xs, eg, dd, ds, dn, (s1, s2), ys))
-    s3 = total(sum(t[3] for t in turns)[None])
-
-    def final(kind, v, g, z=()):
-        nf = g[0].shape[0]
-        ins = (c_arr, s1, s2, s3) + tuple(v) + tuple(g) + tuple(z)
+        z0, z1, state = adj_last(1, state, fs[0])
+        z = (z0, z1, z2, z3)
+        xs, eg = forward(state, z)
+        chains.append((g, z, xs, eg, norm(g), bg, norm(z)))
+    ins = [ch[4] for ch in chains] + [q for ch in chains for q in ch[5]]
+    ins += [ch[6] for ch in chains]
+    for ch, (_, _, dd, _, _) in zip(chains, groups):
+        ins += list(ch[2]) + list(dd)
+    row = call(
+        functools.partial(sums_body, len(chains)), tuple(ins), [VM] * len(ins), [sds(1, lev)]
+    )[0]
+    row = call(add_body, (row, swap(row)), [VM] * 2, [sds(1, lev)], flops=1e5)[0]
+    row = ring_sum(row, 1)
+    states = []
+    for ch, (nf, gg, dd, ds, dn) in zip(chains, groups):
+        state, fs, row = turn(ch[2], ch[3], dd, ds, dn, one_arr, row)
+        states.append((state, fs))
+    row = ring_sum(row, 4)
+    mids = []
+    for state, fs in states:
+        w3z, w2z, state, row = adj_mid(state, fs[2], fs[1], None, row)
+        mids.append((w3z, w2z, state, fs))
+    row = ring_sum(row, 16)
+    weights = call(solve_body, (span, row), [SM, VM], [sds(1, lev)], flops=1e5)[0]
+
+    def final(kind, *vecs):
+        nf = vecs[0][0].shape[0]
+        ins = (c_arr, weights) + tuple(x for v in vecs for x in v)
         shape = sds(2, nf, 3, half, lev)
         keep, send = call(
             functools.partial(final_body, kind),
@@ -792,13 +846,12 @@
             out_specs=[pl.BlockSpec(memory_space=pl.ANY)],
         )[0]
 
-    increment = join([final("inc", v, g) for v, g in zip(resid, grads)])
-    parts = []
-    for v, g, (state, _, fs, _) in zip(resid, grads, turns):
-        z3, z2, state = adj_mid(state, fs[2], fs[1])
-        z0, z1, _ = adj_last(2, state, fs[0])
-        parts.append(final("res", v, g, (z0, z1, z2, z3)))
-    return increment, join(parts)
+    increment = join([final("inc", ch[0], ch[1]) for ch in chains])
+    ends = []
+    for ch, (w3z, w2z, state, fs) in zip(chains, mids):
+        w0z, w1z, _ = adj_last(2, state, fs[0])
+        ends.append(final("res", ch[0], ch[1], (w0z, w1z, w2z, w3z)))
+    return increment, join(ends)
 
 
 def solution(mesh):

time: 388 us -> 352 us (0.907)
  waiting for transfers between devices: 192 us -> 168 us
  starting transfers between devices: 130 us -> 120 us
  Pallas kernels: 53.8 us -> 49.7 us
    ppermute x24, waiting for transfers between devices: 98.7 us -> 146 us  [exchange(): return (lax.ppermute(sn, 'space', north), lax.ppermute(ss, 'space', south))]
    ppermute x18 -> x9, waiting for transfers between devices: 60.9 us -> 15.6 us  [ring_sum(): got = tuple((lax.ppermute(row, 'space', p) for p in shifts))]
    all_to_all x1, waiting for transfers between devices: 24.9 us -> 0.01 us  [per_device(): lax.all_to_all(packed, 'space', split_axis=0, concat_axis=0, tiled=True)]
    ppermute x10 -> x8, starting transfers between devices: 36.6 us -> 15.7 us  [swap(): return lax.ppermute(x, 'tm', [(0, 1), (1, 0)])]
    ppermute x18 -> x9, starting transfers between devices: 2.04 us -> 8.03 us  [ring_sum(): got = tuple((lax.ppermute(row, 'space', p) for p in shifts))]
    ppermute x24, starting transfers between devices: 79.5 us -> 84.3 us  [exchange(): return (lax.ppermute(sn, 'space', north), lax.ppermute(ss, 'space', south))]
    pallas_call x27 -> x34, Pallas kernels: 53.8 us -> 49.7 us  [call(): pl.pallas_call(body, out_shape=outs, in_specs=specs, out_specs=out_specs...]
    unnamed x23 -> x19, local copies, waits for them, and re-layouts: 9.28 us -> 8.38 us
  transfers between devices with their start and end apart: 53 -> 42, of which waited for: 33 -> 25; matrix products, arithmetic and copies ran while one was open for 0% -> 1% of each run, Pallas kernels for 6% -> 5%
where the time goes in v3:
time: 352 us
  waiting for transfers between devices  168 us (48%)
  starting transfers between devices  120 us (34%)
  Pallas kernels  49.7 us (14%)
  local copies, waits for them, and re-layouts  9.67 us (3%)
    ppermute x24, waiting for transfers between devices, exchange(): return (lax.ppermute(sn, 'space', north), lax.ppermute(ss, 'space', south))  146 us
    ppermute x24, starting transfers between devices, exchange(): return (lax.ppermute(sn, 'space', north), lax.ppermute(ss, 'space', south))  84.3 us
    pallas_call x34, Pallas kernels, call(): pl.pallas_call(body, out_shape=outs, in_specs=specs, out_specs=out_specs...  49.7 us
    ppermute x8, starting transfers between devices, swap(): return lax.ppermute(x, 'tm', [(0, 1), (1, 0)])  15.7 us
    ppermute x9, waiting for transfers between devices, ring_sum(): got = tuple((lax.ppermute(row, 'space', p) for p in shifts))  15.6 us
    all_to_all x1, starting transfers between devices, per_device(): lax.all_to_all(packed, 'space', split_axis=0, concat_axis=0, tiled=True)  11.6 us
    unnamed x19, local copies, waits for them, and re-layouts  8.38 us
    ppermute x9, starting transfers between devices, ring_sum(): got = tuple((lax.ppermute(row, 'space', p) for p in shifts))  8.03 us
  transfers between devices with their start and end apart: 42, of which 25 were waited for; matrix products, arithmetic and copies ran while one was open for 1% of the time, Pallas kernels for 5%

profile of v3, /device:TPU:1, one launch (start us, length us, event | category | flops | bytes accessed | tf_op | source)
XLA Modules:
  0.0 351.9 jit_solution(6750898880075397292)
XLA Ops:
  10.0 11.6 %all-to-all-start = ((f32[64,7,8,128]{3,2,1,0:T(8,128)}), f32[64,7,8,128]{3,2,1,0:T(8,128)}, u32[]{:S(2)}, u32[]{:S(2)}) async-start(f32[64,7,8,128]{3,2,1,0:T(8,128)} %shard_map.86), calls=%async_computation | async-start | bytes 3670016 | tf_op jit(solution)/shard_map/all_to_all | solution.py:640
  29.1 6.0 %collective-permute-start.2 = (f32[2,208,128]{2,1,0:T(8,128)S(1)}, f32[2,208,128]{2,1,0:T(8,128)S(1)}, u32[]{:S(2)}, u32[]{:S(2)}) collective-permute-start(f32[2,208,128]{2,1,0:T(8,128)S(1)} %get-tuple-element.103), channel_id=1, source_target_pairs={{1,0},{2,1},{3,2},{4,3},{5,4},{6,5},{7,6},{8,7},{9,8},{10,9},{11,1... | collective-permute-start | bytes 638984 | tf_op jit(solution)/shard_map/ppermute | solution.py:604
  35.1 17.8 %collective-permute-done.1 = f32[2,208,128]{2,1,0:T(8,128)S(1)} collective-permute-done((f32[2,208,128]{2,1,0:T(8,128)S(1)}, f32[2,208,128]{2,1,0:T(8,128)S(1)}, u32[]{:S(2)}, u32[]{:S(2)}) %collective-permute-start.1) | collective-permute-done | bytes 213024 | tf_op jit(solution)/shard_map/ppermute | solution.py:604
  54.5 5.7 %shard_map.89 = (f32[18432,128]{1,0:T(8,128)S(1)}, f32[2,3,3,208,128]{4,3,2,1,0:T(8,128)S(1)}, f32[2,3,3,208,128]{4,3,2,1,0:T(8,128)S(1)}) custom-call(s32[1]{0:T(128)} %bitcast.c_ref, s32[64,8]{1,0:T(8,128)S(1)} %convert_bitcast_fusion.idx_ref, f32[3584,128]{1,0:T(8,128)} %bitcast.12.p_ref), custom_call_target="tpu_custom_call" | custom-call | flops 100000000 | bytes 15108100 | tf_op jit(solution)/shard_map/pallas_call | solution.py:24
  61.1 3.5 %collective-permute-done.3.got_ref = f32[2,3,3,208,128]{4,3,2,1,0:T(8,128)S(1)} collective-permute-done((f32[2,3,3,208,128]{4,3,2,1,0:T(8,128)S(1)}, f32[2,3,3,208,128]{4,3,2,1,0:T(8,128)S(1)}, u32[]{:S(2)}, u32[]{:S(2)}) %collective-permute-start.3) | collective-permute-done | bytes 1916960 | tf_op jit(solution)/shard_map/ppermute | solution.py:601
  66.2 6.9 %collective-permute-start.5 = (f32[3,3,208,128]{3,2,1,0:T(8,128)S(1)}, f32[3,3,208,128]{3,2,1,0:T(8,128)S(1)}, u32[]{:S(2)}, u32[]{:S(2)}) collective-permute-start(f32[3,3,208,128]{3,2,1,0:T(8,128)S(1)} %get-tuple-element.118.refs_2_), channel_id=1, source_target_pairs={{1,0},{2,1},{3,2},{4,3},{5,4},{6,5},{7,6},{8,7},{9,8},{10,9},{11,1... | collective-permute-start | bytes 2875400 | tf_op jit(solution)/shard_map/ppermute | solution.py:604
  73.2 20.9 %collective-permute-done.4.refs_4_ = f32[3,3,208,128]{3,2,1,0:T(8,128)S(1)} collective-permute-done((f32[3,3,208,128]{3,2,1,0:T(8,128)S(1)}, f32[3,3,208,128]{3,2,1,0:T(8,128)S(1)}, u32[]{:S(2)}, u32[]{:S(2)}) %collective-permute-start.4) | collective-permute-done | bytes 958496 | tf_op jit(solution)/shard_map/ppermute | solution.py:604
  94.1 2.9 shard_map.92
  97.0 6.9 %collective-permute-start.7 = (f32[3,3,208,128]{3,2,1,0:T(8,128)S(1)}, f32[3,3,208,128]{3,2,1,0:T(8,128)S(1)}, u32[]{:S(2)}, u32[]{:S(2)}) collective-permute-start(f32[3,3,208,128]{3,2,1,0:T(8,128)S(1)} %get-tuple-element.126.refs_2_), channel_id=1, source_target_pairs={{1,0},{2,1},{3,2},{4,3},{5,4},{6,5},{7,6},{8,7},{9,8},{10,9},{11,1... | collective-permute-start | bytes 2875400 | tf_op jit(solution)/shard_map/ppermute | solution.py:604
  105.2 1.7 collective-permute-start.13
  106.8 17.1 %collective-permute-done.6.refs_4_ = f32[3,3,208,128]{3,2,1,0:T(8,128)S(1)} collective-permute-done((f32[3,3,208,128]{3,2,1,0:T(8,128)S(1)}, f32[3,3,208,128]{3,2,1,0:T(8,128)S(1)}, u32[]{:S(2)}, u32[]{:S(2)}) %collective-permute-start.6) | collective-permute-done | bytes 958496 | tf_op jit(solution)/shard_map/ppermute | solution.py:604
  124.0 2.6 shard_map.93
  126.6 6.9 %collective-permute-start.9 = (f32[2,3,208,128]{3,2,1,0:T(8,128)S(1)}, f32[2,3,208,128]{3,2,1,0:T(8,128)S(1)}, u32[]{:S(2)}, u32[]{:S(2)}) collective-permute-start(f32[2,3,208,128]{3,2,1,0:T(8,128)S(1)} %get-tuple-element.131.ss), channel_id=1, source_target_pairs={{1,0},{2,1},{3,2},{4,3},{5,4},{6,5},{7,6},{8,7},{9,8},{10,9},{11,1... | collective-permute-start | bytes 1916936 | tf_op jit(solution)/shard_map/ppermute | solution.py:604
  133.5 12.3 %collective-permute-done.8.rs = f32[2,3,208,128]{3,2,1,0:T(8,128)S(1)} collective-permute-done((f32[2,3,208,128]{3,2,1,0:T(8,128)S(1)}, f32[2,3,208,128]{3,2,1,0:T(8,128)S(1)}, u32[]{:S(2)}, u32[]{:S(2)}) %collective-permute-start.8) | collective-permute-done | bytes 639008 | tf_op jit(solution)/shard_map/ppermute | solution.py:604
  145.8 3.0 shard_map.94
  148.8 6.9 %collective-permute-start.11 = (f32[2,3,208,128]{3,2,1,0:T(8,128)S(1)}, f32[2,3,208,128]{3,2,1,0:T(8,128)S(1)}, u32[]{:S(2)}, u32[]{:S(2)}) collective-permute-start(f32[2,3,208,128]{3,2,1,0:T(8,128)S(1)} %get-tuple-element.137.ss), channel_id=1, source_target_pairs={{1,0},{2,1},{3,2},{4,3},{5,4},{6,5},{7,6},{8,7},{9,8},{10,9},{11,1... | collective-permute-start | bytes 1916936 | tf_op jit(solution)/shard_map/ppermute | solution.py:604
  156.2 10.9 %collective-permute-done.10.rs = f32[2,3,208,128]{3,2,1,0:T(8,128)S(1)} collective-permute-done((f32[2,3,208,128]{3,2,1,0:T(8,128)S(1)}, f32[2,3,208,128]{3,2,1,0:T(8,128)S(1)}, u32[]{:S(2)}, u32[]{:S(2)}) %collective-permute-start.10) | collective-permute-done | bytes 639008 | tf_op jit(solution)/shard_map/ppermute | solution.py:604
  167.1 2.6 shard_map.95
  169.6 4.1 %collective-permute-start.12 = (f32[3,16,16,128]{3,2,1,0:T(8,128)S(1)}, f32[3,16,16,128]{3,2,1,0:T(8,128)S(1)}, u32[]{:S(2)}, u32[]{:S(2)}) collective-permute-start(f32[3,16,16,128]{3,2,1,0:T(8,128)S(1)} %get-tuple-element.143), channel_id=1, source_target_pairs={{0,64},{64,0},{1,65},{65,1},{2,66},{66,2},{3,67},{67,3},{4,68},{68... | collective-permute-start | bytes 1179656 | tf_op jit(solution)/shard_map/ppermute | solution.py:601
  173.8 7.0 %collective-permute-start.17 = (f32[2,3,208,128]{3,2,1,0:T(8,128)S(1)}, f32[2,3,208,128]{3,2,1,0:T(8,128)S(1)}, u32[]{:S(2)}, u32[]{:S(2)}) collective-permute-start(f32[2,3,208,128]{3,2,1,0:T(8,128)S(1)} %pad_maximum_fusion.1), channel_id=1, source_target_pairs={{1,0},{2,1},{3,2},{4,3},{5,4},{6,5},{7,6},{8,7},{9,8},{10,9},{11,1... | collective-permute-start | bytes 1916936 | tf_op jit(solution)/shard_map/ppermute | solution.py:604
  182.2 6.9 %collective-permute-start.15 = (f32[2,3,208,128]{3,2,1,0:T(8,128)S(1)}, f32[2,3,208,128]{3,2,1,0:T(8,128)S(1)}, u32[]{:S(2)}, u32[]{:S(2)}) collective-permute-start(f32[2,3,208,128]{3,2,1,0:T(8,128)S(1)} %get-tuple-element.149.refs_2_), channel_id=1, source_target_pairs={{1,0},{2,1},{3,2},{4,3},{5,4},{6,5},{7,6},{8,7},{9,8},{10,9},{11,1... | collective-permute-start | bytes 1916936 | tf_op jit(solution)/shard_map/ppermute | solution.py:604
  189.1 5.4 %collective-permute-done.17.dn = f32[2,3,208,128]{3,2,1,0:T(8,128)S(1)} collective-permute-done((f32[2,3,208,128]{3,2,1,0:T(8,128)S(1)}, f32[2,3,208,128]{3,2,1,0:T(8,128)S(1)}, u32[]{:S(2)}, u32[]{:S(2)}) %collective-permute-start.17) | collective-permute-done | bytes 639008 | tf_op jit(solution)/shard_map/ppermute | solution.py:604
  194.6 7.4 %collective-permute-done.16.ds = f32[2,3,208,128]{3,2,1,0:T(8,128)S(1)} collective-permute-done((f32[2,3,208,128]{3,2,1,0:T(8,128)S(1)}, f32[2,3,208,128]{3,2,1,0:T(8,128)S(1)}, u32[]{:S(2)}, u32[]{:S(2)}) %collective-permute-start.16) | collective-permute-done | bytes 639008 | tf_op jit(solution)/shard_map/ppermute | solution.py:604
  202.7 13.0 %collective-permute-done.14.refs_4_ = f32[2,3,208,128]{3,2,1,0:T(8,128)S(1)} collective-permute-done((f32[2,3,208,128]{3,2,1,0:T(8,128)S(1)}, f32[2,3,208,128]{3,2,1,0:T(8,128)S(1)}, u32[]{:S(2)}, u32[]{:S(2)}) %collective-permute-start.14) | collective-permute-done | bytes 639008 | tf_op jit(solution)/shard_map/ppermute | solution.py:604
  215.7 2.9 shard_map.100
  218.6 6.9 %collective-permute-start.19 = (f32[2,3,208,128]{3,2,1,0:T(8,128)S(1)}, f32[2,3,208,128]{3,2,1,0:T(8,128)S(1)}, u32[]{:S(2)}, u32[]{:S(2)}) collective-permute-start(f32[2,3,208,128]{3,2,1,0:T(8,128)S(1)} %get-tuple-element.158.refs_2_), channel_id=1, source_target_pairs={{1,0},{2,1},{3,2},{4,3},{5,4},{6,5},{7,6},{8,7},{9,8},{10,9},{11,1... | collective-permute-start | bytes 1916936 | tf_op jit(solution)/shard_map/ppermute | solution.py:604
  225.5 13.3 %collective-permute-done.18.refs_4_ = f32[2,3,208,128]{3,2,1,0:T(8,128)S(1)} collective-permute-done((f32[2,3,208,128]{3,2,1,0:T(8,128)S(1)}, f32[2,3,208,128]{3,2,1,0:T(8,128)S(1)}, u32[]{:S(2)}, u32[]{:S(2)}) %collective-permute-start.18) | collective-permute-done | bytes 639008 | tf_op jit(solution)/shard_map/ppermute | solution.py:604
  238.8 2.5 shard_map.101
  241.4 6.9 %collective-permute-start.21 = (f32[2,3,208,128]{3,2,1,0:T(8,128)S(1)}, f32[2,3,208,128]{3,2,1,0:T(8,128)S(1)}, u32[]{:S(2)}, u32[]{:S(2)}) collective-permute-start(f32[2,3,208,128]{3,2,1,0:T(8,128)S(1)} %get-tuple-element.162.ss), channel_id=1, source_target_pairs={{1,0},{2,1},{3,2},{4,3},{5,4},{6,5},{7,6},{8,7},{9,8},{10,9},{11,1... | collective-permute-start | bytes 1916936 | tf_op jit(solution)/shard_map/ppermute | solution.py:604
  248.3 12.4 %collective-permute-done.20.rs = f32[2,3,208,128]{3,2,1,0:T(8,128)S(1)} collective-permute-done((f32[2,3,208,128]{3,2,1,0:T(8,128)S(1)}, f32[2,3,208,128]{3,2,1,0:T(8,128)S(1)}, u32[]{:S(2)}, u32[]{:S(2)}) %collective-permute-start.20) | collective-permute-done | bytes 639008 | tf_op jit(solution)/shard_map/ppermute | solution.py:604
  260.7 3.0 shard_map.102
  263.7 6.9 %collective-permute-start.23 = (f32[2,3,208,128]{3,2,1,0:T(8,128)S(1)}, f32[2,3,208,128]{3,2,1,0:T(8,128)S(1)}, u32[]{:S(2)}, u32[]{:S(2)}) collective-permute-start(f32[2,3,208,128]{3,2,1,0:T(8,128)S(1)} %get-tuple-element.167.ss), channel_id=1, source_target_pairs={{1,0},{2,1},{3,2},{4,3},{5,4},{6,5},{7,6},{8,7},{9,8},{10,9},{11,1... | collective-permute-start | bytes 1916936 | tf_op jit(solution)/shard_map/ppermute | solution.py:604
  270.6 11.4 %collective-permute-done.22.rs = f32[2,3,208,128]{3,2,1,0:T(8,128)S(1)} collective-permute-done((f32[2,3,208,128]{3,2,1,0:T(8,128)S(1)}, f32[2,3,208,128]{3,2,1,0:T(8,128)S(1)}, u32[]{:S(2)}, u32[]{:S(2)}) %collective-permute-start.22) | collective-permute-done | bytes 639008 | tf_op jit(solution)/shard_map/ppermute | solution.py:604
  282.1 2.6 shard_map.103
  284.6 4.0 %collective-permute-start.24 = (f32[3,16,16,128]{3,2,1,0:T(8,128)S(1)}, f32[3,16,16,128]{3,2,1,0:T(8,128)S(1)}, u32[]{:S(2)}, u32[]{:S(2)}) collective-permute-start(f32[3,16,16,128]{3,2,1,0:T(8,128)S(1)} %get-tuple-element.173), channel_id=1, source_target_pairs={{0,64},{64,0},{1,65},{65,1},{2,66},{66,2},{3,67},{67,3},{4,68},{68... | collective-permute-start | bytes 1179656 | tf_op jit(solution)/shard_map/ppermute | solution.py:601
  291.0 2.7 collective-permute-start.28
  298.0 6.1 %collective-permute-start.30 = (f32[2,3,208,128]{3,2,1,0:T(8,128)S(1)}, f32[2,3,208,128]{3,2,1,0:T(8,128)S(1)}, u32[]{:S(2)}, u32[]{:S(2)}) collective-permute-start(f32[2,3,208,128]{3,2,1,0:T(8,128)S(1)} %get-tuple-element.180.refs_2_), channel_id=1, source_target_pairs={{1,0},{2,1},{3,2},{4,3},{5,4},{6,5},{7,6},{8,7},{9,8},{10,9},{11,1... | collective-permute-start | bytes 1916936 | tf_op jit(solution)/shard_map/ppermute | solution.py:604
  304.1 2.7 collective-permute-start.33
  308.3 4.6 %collective-permute-done.33.d = f32[1,128]{1,0:T(1,128)S(1)} collective-permute-done((f32[1,128]{1,0:T(1,128)S(1)}, f32[1,128]{1,0:T(1,128)S(1)}, u32[]{:S(2)}, u32[]{:S(2)}) %collective-permute-start.33) | collective-permute-done | bytes 544 | tf_op jit(solution)/shard_map/ppermute | solution.py:614
  312.9 4.1 %collective-permute-done.29.refs_4_ = f32[2,3,208,128]{3,2,1,0:T(8,128)S(1)} collective-permute-done((f32[2,3,208,128]{3,2,1,0:T(8,128)S(1)}, f32[2,3,208,128]{3,2,1,0:T(8,128)S(1)}, u32[]{:S(2)}, u32[]{:S(2)}) %collective-permute-start.29) | collective-permute-done | bytes 639008 | tf_op jit(solution)/shard_map/ppermute | solution.py:604
  317.1 2.9 shard_map.112
  320.0 6.9 %collective-permute-start.39 = (f32[2,3,208,128]{3,2,1,0:T(8,128)S(1)}, f32[2,3,208,128]{3,2,1,0:T(8,128)S(1)}, u32[]{:S(2)}, u32[]{:S(2)}) collective-permute-start(f32[2,3,208,128]{3,2,1,0:T(8,128)S(1)} %get-tuple-element.189.refs_2_), channel_id=1, source_target_pairs={{1,0},{2,1},{3,2},{4,3},{5,4},{6,5},{7,6},{8,7},{9,8},{10,9},{11,1... | collective-permute-start | bytes 1916936 | tf_op jit(solution)/shard_map/ppermute | solution.py:604
  326.9 2.7 collective-permute-start.36
  331.1 7.0 %collective-permute-done.36.d = f32[1,128]{1,0:T(1,128)S(1)} collective-permute-done((f32[1,128]{1,0:T(1,128)S(1)}, f32[1,128]{1,0:T(1,128)S(1)}, u32[]{:S(2)}, u32[]{:S(2)}) %collective-permute-start.36) | collective-permute-done | bytes 544 | tf_op jit(solution)/shard_map/ppermute | solution.py:614
  339.6 3.6 %collective-permute-start.37 = (f32[2,3,3,192,128]{4,3,2,1,0:T(8,128)S(1)}, f32[2,3,3,192,128]{4,3,2,1,0:T(8,128)S(1)}, u32[]{:S(2)}, u32[]{:S(2)}) collective-permute-start(f32[2,3,3,192,128]{4,3,2,1,0:T(8,128)S(1)} %get-tuple-element.187), channel_id=1, source_target_pairs={{0,64},{64,0},{1,65},{65,1},{2,66},{66,2},{3,67},{67,3},{4,68},{68... | collective-permute-start | bytes 5308424 | tf_op jit(solution)/shard_map/ppermute | solution.py:601
  343.2 1.9 shard_map.117
  346.5 1.8 shard_map.116
  349.9 1.8 shard_map.119
  (108 shorter events, 38.3 us)
Async XLA Ops:
  0.6 1.3 copy-start.4
  2.7 4.8 %copy-start.5 = (f32[1,1,64,8,384]{4,3,2,1,0:T(8,128)S(1)}, f32[1,1,64,8,384]{4,3,2,1,0:T(8,128)}, u32[]{:S(2)}) copy-start(f32[1,1,64,8,384]{4,3,2,1,0:T(8,128)} %param.10) | copy-start | bytes 2359300
  5.2 16.5 %collective-permute-start = (f32[2,2,3,208,128]{4,3,2,1,0:T(8,128)}, f32[2,2,3,208,128]{4,3,2,1,0:T(8,128)S(1)}, u32[]{:S(2)}, u32[]{:S(2)}) collective-permute-start(f32[2,2,3,208,128]{4,3,2,1,0:T(8,128)} %get-tuple-element.101), channel_id=1, source_target_pairs={{0,64},{64,0},{1,65},{65,1},{2,66},{66,2},{3,67},{67,3},{4,68},{68... | collective-permute-start | bytes 3833864 | tf_op jit(solution)/shard_map/ppermute | solution.py:601
  7.5 1.1 copy-start.6
  10.0 16.5 %copy-start.8 = (f32[128,128]{1,0:T(8,128)S(1)}, f32[128,128]{1,0:T(8,128)}, u32[]{:S(2)}) copy-start(f32[128,128]{1,0:T(8,128)} %m_ref.1) | copy-start | bytes 196612
  10.0 43.0 %all-to-all-start = ((f32[64,7,8,128]{3,2,1,0:T(8,128)}), f32[64,7,8,128]{3,2,1,0:T(8,128)}, u32[]{:S(2)}, u32[]{:S(2)}) async-start(f32[64,7,8,128]{3,2,1,0:T(8,128)} %shard_map.86), calls=%async_computation | async-start | bytes 3670016 | tf_op jit(solution)/shard_map/all_to_all | solution.py:640
  22.7 1.3 copy-start.1
  24.0 1.3 copy-start.3
  25.5 27.4 %collective-permute-start.1 = (f32[2,208,128]{2,1,0:T(8,128)S(1)}, f32[2,208,128]{2,1,0:T(8,128)S(1)}, u32[]{:S(2)}, u32[]{:S(2)}) collective-permute-start(f32[2,208,128]{2,1,0:T(8,128)S(1)} %get-tuple-element.102), channel_id=1, source_target_pairs={{0,1},{1,2},{2,3},{3,4},{4,5},{5,6},{6,7},{7,8},{8,9},{9,10},{10,1... | collective-permute-start | bytes 638984 | tf_op jit(solution)/shard_map/ppermute | solution.py:604
  29.1 23.8 %collective-permute-start.2 = (f32[2,208,128]{2,1,0:T(8,128)S(1)}, f32[2,208,128]{2,1,0:T(8,128)S(1)}, u32[]{:S(2)}, u32[]{:S(2)}) collective-permute-start(f32[2,208,128]{2,1,0:T(8,128)S(1)} %get-tuple-element.103), channel_id=1, source_target_pairs={{1,0},{2,1},{3,2},{4,3},{5,4},{6,5},{7,6},{8,7},{9,8},{10,9},{11,1... | collective-permute-start | bytes 638984 | tf_op jit(solution)/shard_map/ppermute | solution.py:604
  60.2 4.4 %collective-permute-start.3 = (f32[2,3,3,208,128]{4,3,2,1,0:T(8,128)S(1)}, f32[2,3,3,208,128]{4,3,2,1,0:T(8,128)S(1)}, u32[]{:S(2)}, u32[]{:S(2)}) collective-permute-start(f32[2,3,3,208,128]{4,3,2,1,0:T(8,128)S(1)} %get-tuple-element.112), channel_id=1, source_target_pairs={{0,64},{64,0},{1,65},{65,1},{2,66},{66,2},{3,67},{67,3},{4,68},{68... | collective-permute-start | bytes 5750792 | tf_op jit(solution)/shard_map/ppermute | solution.py:601
  66.1 27.9 %collective-permute-start.4 = (f32[3,3,208,128]{3,2,1,0:T(8,128)S(1)}, f32[3,3,208,128]{3,2,1,0:T(8,128)S(1)}, u32[]{:S(2)}, u32[]{:S(2)}) collective-permute-start(f32[3,3,208,128]{3,2,1,0:T(8,128)S(1)} %get-tuple-element.119.refs_3_), channel_id=1, source_target_pairs={{0,1},{1,2},{2,3},{3,4},{4,5},{5,6},{6,7},{7,8},{8,9},{9,10},{10,1... | collective-permute-start | bytes 2875400 | tf_op jit(solution)/shard_map/ppermute | solution.py:604
  66.2 27.9 %collective-permute-start.5 = (f32[3,3,208,128]{3,2,1,0:T(8,128)S(1)}, f32[3,3,208,128]{3,2,1,0:T(8,128)S(1)}, u32[]{:S(2)}, u32[]{:S(2)}) collective-permute-start(f32[3,3,208,128]{3,2,1,0:T(8,128)S(1)} %get-tuple-element.118.refs_2_), channel_id=1, source_target_pairs={{1,0},{2,1},{3,2},{4,3},{5,4},{6,5},{7,6},{8,7},{9,8},{10,9},{11,1... | collective-permute-start | bytes 2875400 | tf_op jit(solution)/shard_map/ppermute | solution.py:604
  96.9 27.0 %collective-permute-start.6 = (f32[3,3,208,128]{3,2,1,0:T(8,128)S(1)}, f32[3,3,208,128]{3,2,1,0:T(8,128)S(1)}, u32[]{:S(2)}, u32[]{:S(2)}) collective-permute-start(f32[3,3,208,128]{3,2,1,0:T(8,128)S(1)} %get-tuple-element.127.refs_3_), channel_id=1, source_target_pairs={{0,1},{1,2},{2,3},{3,4},{4,5},{5,6},{6,7},{7,8},{8,9},{9,10},{10,1... | collective-permute-start | bytes 2875400 | tf_op jit(solution)/shard_map/ppermute | solution.py:604
  97.0 26.9 %collective-permute-start.7 = (f32[3,3,208,128]{3,2,1,0:T(8,128)S(1)}, f32[3,3,208,128]{3,2,1,0:T(8,128)S(1)}, u32[]{:S(2)}, u32[]{:S(2)}) collective-permute-start(f32[3,3,208,128]{3,2,1,0:T(8,128)S(1)} %get-tuple-element.126.refs_2_), channel_id=1, source_target_pairs={{1,0},{2,1},{3,2},{4,3},{5,4},{6,5},{7,6},{8,7},{9,8},{10,9},{11,1... | collective-permute-start | bytes 2875400 | tf_op jit(solution)/shard_map/ppermute | solution.py:604
  105.2 50.6 %collective-permute-start.13 = (f32[2,3,3,208,128]{4,3,2,1,0:T(8,128)S(1)}, f32[2,3,3,208,128]{4,3,2,1,0:T(8,128)S(1)}, u32[]{:S(2)}, u32[]{:S(2)}) collective-permute-start(f32[2,3,3,208,128]{4,3,2,1,0:T(8,128)S(1)} %get-tuple-element.146), channel_id=1, source_target_pairs={{0,64},{64,0},{1,65},{65,1},{2,66},{66,2},{3,67},{67,3},{4,68},{68... | collective-permute-start | bytes 5750792 | tf_op jit(solution)/shard_map/ppermute | solution.py:601
  126.5 19.2 %collective-permute-start.8 = (f32[2,3,208,128]{3,2,1,0:T(8,128)S(1)}, f32[2,3,208,128]{3,2,1,0:T(8,128)S(1)}, u32[]{:S(2)}, u32[]{:S(2)}) collective-permute-start(f32[2,3,208,128]{3,2,1,0:T(8,128)S(1)} %get-tuple-element.132.sn), channel_id=1, source_target_pairs={{0,1},{1,2},{2,3},{3,4},{4,5},{5,6},{6,7},{7,8},{8,9},{9,10},{10,1... | collective-permute-start | bytes 1916936 | tf_op jit(solution)/shard_map/ppermute | solution.py:604
  126.6 19.2 %collective-permute-start.9 = (f32[2,3,208,128]{3,2,1,0:T(8,128)S(1)}, f32[2,3,208,128]{3,2,1,0:T(8,128)S(1)}, u32[]{:S(2)}, u32[]{:S(2)}) collective-permute-start(f32[2,3,208,128]{3,2,1,0:T(8,128)S(1)} %get-tuple-element.131.ss), channel_id=1, source_target_pairs={{1,0},{2,1},{3,2},{4,3},{5,4},{6,5},{7,6},{8,7},{9,8},{10,9},{11,1... | collective-permute-start | bytes 1916936 | tf_op jit(solution)/shard_map/ppermute | solution.py:604
  148.7 18.3 %collective-permute-start.10 = (f32[2,3,208,128]{3,2,1,0:T(8,128)S(1)}, f32[2,3,208,128]{3,2,1,0:T(8,128)S(1)}, u32[]{:S(2)}, u32[]{:S(2)}) collective-permute-start(f32[2,3,208,128]{3,2,1,0:T(8,128)S(1)} %get-tuple-element.138.sn), channel_id=1, source_target_pairs={{0,1},{1,2},{2,3},{3,4},{4,5},{5,6},{6,7},{7,8},{8,9},{9,10},{10,1... | collective-permute-start | bytes 1916936 | tf_op jit(solution)/shard_map/ppermute | solution.py:604
  148.8 18.2 %collective-permute-start.11 = (f32[2,3,208,128]{3,2,1,0:T(8,128)S(1)}, f32[2,3,208,128]{3,2,1,0:T(8,128)S(1)}, u32[]{:S(2)}, u32[]{:S(2)}) collective-permute-start(f32[2,3,208,128]{3,2,1,0:T(8,128)S(1)} %get-tuple-element.137.ss), channel_id=1, source_target_pairs={{1,0},{2,1},{3,2},{4,3},{5,4},{6,5},{7,6},{8,7},{9,8},{10,9},{11,1... | collective-permute-start | bytes 1916936 | tf_op jit(solution)/shard_map/ppermute | solution.py:604
  169.6 11.2 %collective-permute-start.12 = (f32[3,16,16,128]{3,2,1,0:T(8,128)S(1)}, f32[3,16,16,128]{3,2,1,0:T(8,128)S(1)}, u32[]{:S(2)}, u32[]{:S(2)}) collective-permute-start(f32[3,16,16,128]{3,2,1,0:T(8,128)S(1)} %get-tuple-element.143), channel_id=1, source_target_pairs={{0,64},{64,0},{1,65},{65,1},{2,66},{66,2},{3,67},{67,3},{4,68},{68... | collective-permute-start | bytes 1179656 | tf_op jit(solution)/shard_map/ppermute | solution.py:601
  173.8 20.8 %collective-permute-start.17 = (f32[2,3,208,128]{3,2,1,0:T(8,128)S(1)}, f32[2,3,208,128]{3,2,1,0:T(8,128)S(1)}, u32[]{:S(2)}, u32[]{:S(2)}) collective-permute-start(f32[2,3,208,128]{3,2,1,0:T(8,128)S(1)} %pad_maximum_fusion.1), channel_id=1, source_target_pairs={{1,0},{2,1},{3,2},{4,3},{5,4},{6,5},{7,6},{8,7},{9,8},{10,9},{11,1... | collective-permute-start | bytes 1916936 | tf_op jit(solution)/shard_map/ppermute | solution.py:604
  180.8 21.2 %collective-permute-start.16 = (f32[2,3,208,128]{3,2,1,0:T(8,128)S(1)}, f32[2,3,208,128]{3,2,1,0:T(8,128)S(1)}, u32[]{:S(2)}, u32[]{:S(2)}) collective-permute-start(f32[2,3,208,128]{3,2,1,0:T(8,128)S(1)} %pad_maximum_fusion), channel_id=1, source_target_pairs={{0,1},{1,2},{2,3},{3,4},{4,5},{5,6},{6,7},{7,8},{8,9},{9,10},{10,1... | collective-permute-start | bytes 1916936 | tf_op jit(solution)/shard_map/ppermute | solution.py:604
  182.1 33.6 %collective-permute-start.14 = (f32[2,3,208,128]{3,2,1,0:T(8,128)S(1)}, f32[2,3,208,128]{3,2,1,0:T(8,128)S(1)}, u32[]{:S(2)}, u32[]{:S(2)}) collective-permute-start(f32[2,3,208,128]{3,2,1,0:T(8,128)S(1)} %get-tuple-element.150.refs_3_), channel_id=1, source_target_pairs={{0,1},{1,2},{2,3},{3,4},{4,5},{5,6},{6,7},{7,8},{8,9},{9,10},{10,1... | collective-permute-start | bytes 1916936 | tf_op jit(solution)/shard_map/ppermute | solution.py:604
  182.2 33.5 %collective-permute-start.15 = (f32[2,3,208,128]{3,2,1,0:T(8,128)S(1)}, f32[2,3,208,128]{3,2,1,0:T(8,128)S(1)}, u32[]{:S(2)}, u32[]{:S(2)}) collective-permute-start(f32[2,3,208,128]{3,2,1,0:T(8,128)S(1)} %get-tuple-element.149.refs_2_), channel_id=1, source_target_pairs={{1,0},{2,1},{3,2},{4,3},{5,4},{6,5},{7,6},{8,7},{9,8},{10,9},{11,1... | collective-permute-start | bytes 1916936 | tf_op jit(solution)/shard_map/ppermute | solution.py:604
  218.6 20.2 %collective-permute-start.18 = (f32[2,3,208,128]{3,2,1,0:T(8,128)S(1)}, f32[2,3,208,128]{3,2,1,0:T(8,128)S(1)}, u32[]{:S(2)}, u32[]{:S(2)}) collective-permute-start(f32[2,3,208,128]{3,2,1,0:T(8,128)S(1)} %get-tuple-element.159.refs_3_), channel_id=1, source_target_pairs={{0,1},{1,2},{2,3},{3,4},{4,5},{5,6},{6,7},{7,8},{8,9},{9,10},{10,1... | collective-permute-start | bytes 1916936 | tf_op jit(solution)/shard_map/ppermute | solution.py:604
  218.6 20.2 %collective-permute-start.19 = (f32[2,3,208,128]{3,2,1,0:T(8,128)S(1)}, f32[2,3,208,128]{3,2,1,0:T(8,128)S(1)}, u32[]{:S(2)}, u32[]{:S(2)}) collective-permute-start(f32[2,3,208,128]{3,2,1,0:T(8,128)S(1)} %get-tuple-element.158.refs_2_), channel_id=1, source_target_pairs={{1,0},{2,1},{3,2},{4,3},{5,4},{6,5},{7,6},{8,7},{9,8},{10,9},{11,1... | collective-permute-start | bytes 1916936 | tf_op jit(solution)/shard_map/ppermute | solution.py:604
  241.4 19.3 %collective-permute-start.20 = (f32[2,3,208,128]{3,2,1,0:T(8,128)S(1)}, f32[2,3,208,128]{3,2,1,0:T(8,128)S(1)}, u32[]{:S(2)}, u32[]{:S(2)}) collective-permute-start(f32[2,3,208,128]{3,2,1,0:T(8,128)S(1)} %get-tuple-element.163.sn), channel_id=1, source_target_pairs={{0,1},{1,2},{2,3},{3,4},{4,5},{5,6},{6,7},{7,8},{8,9},{9,10},{10,1... | collective-permute-start | bytes 1916936 | tf_op jit(solution)/shard_map/ppermute | solution.py:604
  241.4 19.2 %collective-permute-start.21 = (f32[2,3,208,128]{3,2,1,0:T(8,128)S(1)}, f32[2,3,208,128]{3,2,1,0:T(8,128)S(1)}, u32[]{:S(2)}, u32[]{:S(2)}) collective-permute-start(f32[2,3,208,128]{3,2,1,0:T(8,128)S(1)} %get-tuple-element.162.ss), channel_id=1, source_target_pairs={{1,0},{2,1},{3,2},{4,3},{5,4},{6,5},{7,6},{8,7},{9,8},{10,9},{11,1... | collective-permute-start | bytes 1916936 | tf_op jit(solution)/shard_map/ppermute | solution.py:604
  263.6 18.4 %collective-permute-start.22 = (f32[2,3,208,128]{3,2,1,0:T(8,128)S(1)}, f32[2,3,208,128]{3,2,1,0:T(8,128)S(1)}, u32[]{:S(2)}, u32[]{:S(2)}) collective-permute-start(f32[2,3,208,128]{3,2,1,0:T(8,128)S(1)} %get-tuple-element.168.sn), channel_id=1, source_target_pairs={{0,1},{1,2},{2,3},{3,4},{4,5},{5,6},{6,7},{7,8},{8,9},{9,10},{10,1... | collective-permute-start | bytes 1916936 | tf_op jit(solution)/shard_map/ppermute | solution.py:604
  263.7 18.3 %collective-permute-start.23 = (f32[2,3,208,128]{3,2,1,0:T(8,128)S(1)}, f32[2,3,208,128]{3,2,1,0:T(8,128)S(1)}, u32[]{:S(2)}, u32[]{:S(2)}) collective-permute-start(f32[2,3,208,128]{3,2,1,0:T(8,128)S(1)} %get-tuple-element.167.ss), channel_id=1, source_target_pairs={{1,0},{2,1},{3,2},{4,3},{5,4},{6,5},{7,6},{8,7},{9,8},{10,9},{11,1... | collective-permute-start | bytes 1916936 | tf_op jit(solution)/shard_map/ppermute | solution.py:604
  284.6 10.6 %collective-permute-start.24 = (f32[3,16,16,128]{3,2,1,0:T(8,128)S(1)}, f32[3,16,16,128]{3,2,1,0:T(8,128)S(1)}, u32[]{:S(2)}, u32[]{:S(2)}) collective-permute-start(f32[3,16,16,128]{3,2,1,0:T(8,128)S(1)} %get-tuple-element.173), channel_id=1, source_target_pairs={{0,64},{64,0},{1,65},{65,1},{2,66},{66,2},{3,67},{67,3},{4,68},{68... | collective-permute-start | bytes 1179656 | tf_op jit(solution)/shard_map/ppermute | solution.py:601
  289.8 1.2 collective-permute-start.25
  291.0 3.6 %collective-permute-start.26 = (f32[1,128]{1,0:T(1,128)S(1)}, f32[1,128]{1,0:T(1,128)S(1)}, u32[]{:S(2)}, u32[]{:S(2)}) collective-permute-start(f32[1,128]{1,0:T(1,128)S(1)} %shard_map.107.a), channel_id=1, source_target_pairs={{0,1},{1,2},{2,3},{3,0},{4,5},{5,6},{6,7},{7,4},{8,9},{9,10},{10,1... | collective-permute-start | bytes 1544 | tf_op jit(solution)/shard_map/ppermute | solution.py:614
  291.0 3.9 %collective-permute-start.27 = (f32[1,128]{1,0:T(1,128)S(1)}, f32[1,128]{1,0:T(1,128)S(1)}, u32[]{:S(2)}, u32[]{:S(2)}) collective-permute-start(f32[1,128]{1,0:T(1,128)S(1)} %shard_map.107.a), channel_id=1, source_target_pairs={{0,2},{1,3},{2,0},{3,1},{4,6},{5,7},{6,4},{7,5},{8,10},{9,11},{10,... | collective-permute-start | bytes 1544 | tf_op jit(solution)/shard_map/ppermute | solution.py:614
  291.0 4.2 %collective-permute-start.28 = (f32[1,128]{1,0:T(1,128)S(1)}, f32[1,128]{1,0:T(1,128)S(1)}, u32[]{:S(2)}, u32[]{:S(2)}) collective-permute-start(f32[1,128]{1,0:T(1,128)S(1)} %shard_map.107.a), channel_id=1, source_target_pairs={{0,3},{1,0},{2,1},{3,2},{4,7},{5,4},{6,5},{7,6},{8,11},{9,8},{10,9... | collective-permute-start | bytes 1544 | tf_op jit(solution)/shard_map/ppermute | solution.py:614
  296.4 20.6 %collective-permute-start.29 = (f32[2,3,208,128]{3,2,1,0:T(8,128)S(1)}, f32[2,3,208,128]{3,2,1,0:T(8,128)S(1)}, u32[]{:S(2)}, u32[]{:S(2)}) collective-permute-start(f32[2,3,208,128]{3,2,1,0:T(8,128)S(1)} %get-tuple-element.181.refs_3_), channel_id=1, source_target_pairs={{0,1},{1,2},{2,3},{3,4},{4,5},{5,6},{6,7},{7,8},{8,9},{9,10},{10,1... | collective-permute-start | bytes 1916936 | tf_op jit(solution)/shard_map/ppermute | solution.py:604
  298.0 19.1 %collective-permute-start.30 = (f32[2,3,208,128]{3,2,1,0:T(8,128)S(1)}, f32[2,3,208,128]{3,2,1,0:T(8,128)S(1)}, u32[]{:S(2)}, u32[]{:S(2)}) collective-permute-start(f32[2,3,208,128]{3,2,1,0:T(8,128)S(1)} %get-tuple-element.180.refs_2_), channel_id=1, source_target_pairs={{1,0},{2,1},{3,2},{4,3},{5,4},{6,5},{7,6},{8,7},{9,8},{10,9},{11,1... | collective-permute-start | bytes 1916936 | tf_op jit(solution)/shard_map/ppermute | solution.py:604
  304.1 3.9 %collective-permute-start.31 = (f32[1,128]{1,0:T(1,128)S(1)}, f32[1,128]{1,0:T(1,128)S(1)}, u32[]{:S(2)}, u32[]{:S(2)}) collective-permute-start(f32[1,128]{1,0:T(1,128)S(1)} %get-tuple-element.184.a), channel_id=1, source_target_pairs={{0,4},{1,5},{2,6},{3,7},{4,8},{5,9},{6,10},{7,11},{8,12},{9,13},{1... | collective-permute-start | bytes 1544 | tf_op jit(solution)/shard_map/ppermute | solution.py:614
  304.1 4.2 %collective-permute-start.32 = (f32[1,128]{1,0:T(1,128)S(1)}, f32[1,128]{1,0:T(1,128)S(1)}, u32[]{:S(2)}, u32[]{:S(2)}) collective-permute-start(f32[1,128]{1,0:T(1,128)S(1)} %get-tuple-element.184.a), channel_id=1, source_target_pairs={{0,8},{1,9},{2,10},{3,11},{4,12},{5,13},{6,14},{7,15},{8,0},{9,1},... | collective-permute-start | bytes 1544 | tf_op jit(solution)/shard_map/ppermute | solution.py:614
  304.1 8.8 %collective-permute-start.33 = (f32[1,128]{1,0:T(1,128)S(1)}, f32[1,128]{1,0:T(1,128)S(1)}, u32[]{:S(2)}, u32[]{:S(2)}) collective-permute-start(f32[1,128]{1,0:T(1,128)S(1)} %get-tuple-element.184.a), channel_id=1, source_target_pairs={{0,12},{1,13},{2,14},{3,15},{4,0},{5,1},{6,2},{7,3},{8,4},{9,5},{1... | collective-permute-start | bytes 1544 | tf_op jit(solution)/shard_map/ppermute | solution.py:614
  320.0 23.2 %collective-permute-start.38 = (f32[2,3,208,128]{3,2,1,0:T(8,128)S(1)}, f32[2,3,208,128]{3,2,1,0:T(8,128)S(1)}, u32[]{:S(2)}, u32[]{:S(2)}) collective-permute-start(f32[2,3,208,128]{3,2,1,0:T(8,128)S(1)} %get-tuple-element.190.refs_3_), channel_id=1, source_target_pairs={{0,1},{1,2},{2,3},{3,4},{4,5},{5,6},{6,7},{7,8},{8,9},{9,10},{10,1... | collective-permute-start | bytes 1916936 | tf_op jit(solution)/shard_map/ppermute | solution.py:604
  320.0 23.1 %collective-permute-start.39 = (f32[2,3,208,128]{3,2,1,0:T(8,128)S(1)}, f32[2,3,208,128]{3,2,1,0:T(8,128)S(1)}, u32[]{:S(2)}, u32[]{:S(2)}) collective-permute-start(f32[2,3,208,128]{3,2,1,0:T(8,128)S(1)} %get-tuple-element.189.refs_2_), channel_id=1, source_target_pairs={{1,0},{2,1},{3,2},{4,3},{5,4},{6,5},{7,6},{8,7},{9,8},{10,9},{11,1... | collective-permute-start | bytes 1916936 | tf_op jit(solution)/shard_map/ppermute | solution.py:604
  326.9 3.6 %collective-permute-start.34 = (f32[1,128]{1,0:T(1,128)S(1)}, f32[1,128]{1,0:T(1,128)S(1)}, u32[]{:S(2)}, u32[]{:S(2)}) collective-permute-start(f32[1,128]{1,0:T(1,128)S(1)} %get-tuple-element.185.a), channel_id=1, source_target_pairs={{0,16},{1,17},{2,18},{3,19},{4,20},{5,21},{6,22},{7,23},{8,24},{9,... | collective-permute-start | bytes 1544 | tf_op jit(solution)/shard_map/ppermute | solution.py:614
  326.9 4.2 %collective-permute-start.35 = (f32[1,128]{1,0:T(1,128)S(1)}, f32[1,128]{1,0:T(1,128)S(1)}, u32[]{:S(2)}, u32[]{:S(2)}) collective-permute-start(f32[1,128]{1,0:T(1,128)S(1)} %get-tuple-element.185.a), channel_id=1, source_target_pairs={{0,32},{1,33},{2,34},{3,35},{4,36},{5,37},{6,38},{7,39},{8,40},{9,... | collective-permute-start | bytes 1544 | tf_op jit(solution)/shard_map/ppermute | solution.py:614
  326.9 11.2 %collective-permute-start.36 = (f32[1,128]{1,0:T(1,128)S(1)}, f32[1,128]{1,0:T(1,128)S(1)}, u32[]{:S(2)}, u32[]{:S(2)}) collective-permute-start(f32[1,128]{1,0:T(1,128)S(1)} %get-tuple-element.185.a), channel_id=1, source_target_pairs={{0,48},{1,49},{2,50},{3,51},{4,52},{5,53},{6,54},{7,55},{8,56},{9,... | collective-permute-start | bytes 1544 | tf_op jit(solution)/shard_map/ppermute | solution.py:614
  339.6 6.9 %collective-permute-start.37 = (f32[2,3,3,192,128]{4,3,2,1,0:T(8,128)S(1)}, f32[2,3,3,192,128]{4,3,2,1,0:T(8,128)S(1)}, u32[]{:S(2)}, u32[]{:S(2)}) collective-permute-start(f32[2,3,3,192,128]{4,3,2,1,0:T(8,128)S(1)} %get-tuple-element.187), channel_id=1, source_target_pairs={{0,64},{64,0},{1,65},{65,1},{2,66},{66,2},{3,67},{67,3},{4,68},{68... | collective-permute-start | bytes 5308424 | tf_op jit(solution)/shard_map/ppermute | solution.py:601
  346.2 3.8 %collective-permute-start.40 = (f32[2,3,3,192,128]{4,3,2,1,0:T(8,128)S(1)}, f32[2,3,3,192,128]{4,3,2,1,0:T(8,128)S(1)}, u32[]{:S(2)}, u32[]{:S(2)}) collective-permute-start(f32[2,3,3,192,128]{4,3,2,1,0:T(8,128)S(1)} %get-tuple-element.197), channel_id=1, source_target_pairs={{0,64},{64,0},{1,65},{65,1},{2,66},{66,2},{3,67},{67,3},{4,68},{68... | collective-permute-start | bytes 5308424 | tf_op jit(solution)/shard_map/ppermute | solution.py:601
  (3 other events, 2.9 us)

commit v4 on v3

--- a/solution.py
+++ b/solution.py
@@ -9,7 +9,7 @@
 FIELDS = 3
 MIXC = 0.25
 SCALE_Q = 0.5
-GROUPS = (3,)
+GROUPS = (FIELDS,)
 PAD = 8
 F32 = jnp.float32
 BF16 = jnp.bfloat16
@@ -64,6 +64,23 @@
     return v + (o[:, :lev] + o[:, lev:])
 
 
+class Sides:
+
+    def __init__(self, flag, first, second):
+        self.even = flag > 0.5
+        self.refs = (first, second)
+
+    def south(self, k, f):
+        return jnp.where(self.even, self.refs[1][k, f], self.refs[0][k, f])
+
+    def north(self, k, f):
+        return jnp.where(self.even, self.refs[0][k, f], self.refs[1][k, f])
+
+    def put(self, k, f, south, north):
+        self.refs[0][k, f] = jnp.where(self.even, north, south)
+        self.refs[1][k, f] = jnp.where(self.even, south, north)
+
+
 def adj_local(w, c):
     ap, am, _, _, c0 = c
     return c0 * w + earlier(ap * w) + later(am * w)
@@ -74,23 +91,26 @@
     return c0 * u + ap * later(u) + am * earlier(u)
 
 
-def adj_pre(f, rows, w_ref, rhs, mid_ref, ss_ref, sn_ref):
+def adj_pre(f, rows, w_ref, rhs, mid_ref, out):
     w = [mixed(x, rhs) for x in rows]
     c = [coef(w_ref, i) for i in range(3)]
     mid_ref[f] = adj_local(w[1], c[1]) + c[2][2] * w[2] + c[0][3] * w[0]
-    ss_ref[0, f] = adj_local(w[0], c[0]) + c[1][2] * w[1]
-    ss_ref[1, f] = c[0][2] * w[0]
-    sn_ref[0, f] = adj_local(w[2], c[2]) + c[1][3] * w[1]
-    sn_ref[1, f] = c[2][3] * w[2]
-
-
-def adj_post(f, mid_ref, ss_ref, sn_ref, rs_ref, rn_ref, fs, fn):
+    out.put(
+        0,
+        f,
+        adj_local(w[0], c[0]) + c[1][2] * w[1],
+        adj_local(w[2], c[2]) + c[1][3] * w[1],
+    )
+    out.put(1, f, c[0][2] * w[0], c[2][3] * w[2])
+
+
+def adj_post(f, mid_ref, own, got, fs, fn):
     return [
-        (rs_ref[0, f] + ss_ref[1, f]) * fs,
-        ss_ref[0, f] + rs_ref[1, f] * fs,
+        (got.south(0, f) + own.south(1, f)) * fs,
+        own.south(0, f) + got.south(1, f) * fs,
         mid_ref[f],
-        sn_ref[0, f] + rn_ref[1, f] * fn,
-        (rn_ref[0, f] + sn_ref[1, f]) * fn,
+        own.north(0, f) + got.north(1, f) * fn,
+        (got.north(0, f) + own.north(1, f)) * fn,
     ]
 
 
@@ -104,24 +124,27 @@
     ]
 
 
-def fwd_pre(f, u, w_ref, mid_ref, ss_ref, sn_ref):
+def fwd_pre(f, u, w_ref, mid_ref, out):
     c = [coef(w_ref, i) for i in range(3)]
     mid_ref[f] = fwd_local(u[1], c[1]) + c[1][2] * u[0] + c[1][3] * u[2]
-    ss_ref[0, f] = u[0]
-    ss_ref[1, f] = fwd_local(u[0], c[0]) + c[0][3] * u[1]
-    sn_ref[0, f] = u[2]
-    sn_ref[1, f] = fwd_local(u[2], c[2]) + c[2][2] * u[1]
-
-
-def fwd_post(f, mid_ref, ss_ref, sn_ref, rs_ref, rn_ref, w_ref, wh_ref, fs, fn, rhs):
+    out.put(0, f, u[0], u[2])
+    out.put(
+        1,
+        f,
+        fwd_local(u[0], c[0]) + c[0][3] * u[1],
+        fwd_local(u[2], c[2]) + c[2][2] * u[1],
+    )
+
+
+def fwd_post(f, mid_ref, own, got, w_ref, wh_ref, fs, fn, rhs):
     b0 = w_ref[1, 0]
     b2 = w_ref[1, 2]
     m = [
-        rs_ref[1, f] * fs + wh_ref[0] * ss_ref[0, f],
-        ss_ref[1, f] + jnp.maximum(b0, 0.0) * (rs_ref[0, f] * fs),
+        got.south(1, f) * fs + wh_ref[0] * own.south(0, f),
+        own.south(1, f) + jnp.maximum(b0, 0.0) * (got.south(0, f) * fs),
         mid_ref[f],
-        sn_ref[1, f] + jnp.maximum(-b2, 0.0) * (rn_ref[0, f] * fn),
-        rn_ref[1, f] * fn + wh_ref[1] * sn_ref[0, f],
+        own.north(1, f) + jnp.maximum(-b2, 0.0) * (got.north(0, f) * fn),
+        got.north(1, f) * fn + wh_ref[1] * own.north(0, f),
     ]
     return [mixed(x, rhs) for x in m]
 
@@ -168,7 +191,8 @@
         snd_ref[idx] = low
 
 
-def pack_body(w_ref, d_ref, i_ref, o_ref):
+def pack_body(w_ref, d_ref, i_ref, o_ref, t_ref):
+    t_ref[...] = jnp.zeros_like(t_ref)
     lev = o_ref.shape[-1]
     live = i_ref[...] >= 0.0
     for f in range(FIELDS):
@@ -192,10 +216,20 @@
         lax.fori_loop(0, 3, one, 0)
 
 
-def scatter_body(half, c_ref, idx_ref, p_ref, acc, go_ref, gs_ref):
-    owners, slots = idx_ref.shape
+def scatter_body(half, slots, c_ref, p_ref, acc, go_ref, gs_ref, idx_v, idx_s, sem):
     blocks = 2 * FIELDS + 1
+    owners = p_ref.shape[0] // (blocks * slots)
     lev = p_ref.shape[1]
+    lane = lanes((slots, lev))
+
+    def column(o, vals):
+        at = pl.multiple_of((o * blocks + blocks - 1) * slots, slots)
+        return jnp.where(lane == o, p_ref[pl.ds(at, slots), :], vals)
+
+    vals = lax.fori_loop(0, owners, column, jnp.zeros((slots, lev), F32))
+    idx_v[...] = jnp.maximum(vals, 0.0).astype(jnp.int32)
+    copy = pltpu.make_async_copy(idx_v, idx_s, sem)
+    copy.start()
     cells = acc.shape[0] // 8
     chunk = 64
 
@@ -207,9 +241,11 @@
 
     lax.fori_loop(0, cells // chunk, clear, 0)
 
+    copy.wait()
+
     def put(o, carry):
         for s in range(slots):
-            row = pl.multiple_of(idx_ref[o, s] * 8, 8)
+            row = pl.multiple_of(idx_s[s, o] * 8, 8)
             x = p_ref[pl.ds(o * (blocks * slots) + s, blocks, stride=slots), :]
             acc[pl.ds(row, blocks), :] += x
         return carry
@@ -222,7 +258,7 @@
     emit(half, c_ref[0], acc, 0, do_ref, ds_ref)
 
 
-def wind_body(half, c_ref, w_ref, m_ref, o_ref, s_ref, ra_ref, rf_ref):
+def wind_body(half, c_ref, w_ref, m_ref, t_ref, o_ref, s_ref, ra_ref, rf_ref):
     c = c_ref[0]
     for w in range(2):
 
@@ -266,20 +302,20 @@
         sn[k] = jnp.maximum(-w[1, 2], 0.0)
 
 
-def turn_first_body(g3_ref, g2_ref, w3_ref, ra_ref, mid_ref, ss_ref, sn_ref):
+def turn_first_body(fl, g3_ref, g2_ref, w3_ref, ra_ref, mid_ref, ss_ref, sn_ref):
     rhs = ra_ref[...]
+    out = Sides(fl[2], ss_ref, sn_ref)
 
     def one(f):
-        adj_pre(f, [g3_ref[f, i] for i in range(3)], w3_ref, rhs, mid_ref, ss_ref, sn_ref)
-        ss_ref[2, f] = g2_ref[f, 0]
-        sn_ref[2, f] = g2_ref[f, 2]
+        adj_pre(f, [g3_ref[f, i] for i in range(3)], w3_ref, rhs, mid_ref, out)
+        out.put(2, f, g2_ref[f, 0], g2_ref[f, 2])
 
     fields(g3_ref.shape[0], one)
 
 
-def five(f, f_ref, rs_ref, rn_ref, ext):
+def five(f, f_ref, got, ext):
     if ext:
-        return [rs_ref[2, f]] + [f_ref[f, i] for i in range(3)] + [rn_ref[2, f]]
+        return [got.south(2, f)] + [f_ref[f, i] for i in range(3)] + [got.north(2, f)]
     return [f_ref[f, i] for i in range(5)]
 
 
@@ -295,56 +331,72 @@
     g3, g2, mid_o, ss_o, sn_o = refs[n:]
     fs, fn = fl[0], fl[1]
     rhs = ra[...]
+    own, got, out_o = Sides(fl[2], ss, sn), Sides(fl[2], rs, rn), Sides(fl[2], ss_o, sn_o)
 
     def one(f):
-        lam = adj_post(f, mid, ss, sn, rs, rn, fs, fn)
+        lam = adj_post(f, mid, own, got, fs, fn)
         for i in range(5):
             g3[f, i] = lam[i] * SCALE_Q
-        src = five(f, f2, rs, rn, ext)
+        src = five(f, f2, got, ext)
         out = adj_second([lam[i] + src[i] for i in range(5)], w2, wh2, rhs)
         for i in range(3):
             g2[f, i] = out[i] * SCALE_Q
-        adj_pre(f, [out[i] + f1[f, i] for i in range(3)], w1, rhs, mid_o, ss_o, sn_o)
+        adj_pre(f, [out[i] + f1[f, i] for i in range(3)], w1, rhs, mid_o, out_o)
         if ext:
-            ss_o[2, f] = g0[f, 0]
-            sn_o[2, f] = g0[f, 2]
+            out_o.put(2, f, g0[f, 0], g0[f, 2])
 
     fields(mid.shape[0], one)
 
 
 def adj_last_body(mode, *refs):
     (fl, mid, ss, sn, rs, rn, f0, w0, wh0, ra) = refs[:10]
-    outs = refs[10:]
+    n = 10
+    if mode == 0:
+        d2 = refs[n]
+        n += 1
+    outs = refs[n:]
     fs, fn = fl[0], fl[1]
     rhs = ra[...]
+    own, got = Sides(fl[2], ss, sn), Sides(fl[2], rs, rn)
+    if mode < 2:
+        out_o = Sides(fl[2], outs[3], outs[4])
 
     def one(f):
-        lam = adj_post(f, mid, ss, sn, rs, rn, fs, fn)
-        src = five(f, f0, rs, rn, mode == 0)
+        lam = adj_post(f, mid, own, got, fs, fn)
+        src = five(f, f0, got, mode == 0)
         out = adj_second([lam[i] + src[i] for i in range(5)], w0, wh0, rhs)
         for i in range(5):
             outs[1][f, i] = lam[i] * SCALE_Q
         for i in range(3):
             outs[0][f, i] = out[i]
         if mode < 2:
-            fwd_pre(f, out, w0, *outs[2:5])
+            fwd_pre(f, out, w0, outs[2], out_o)
+        if mode == 0:
+            out_o.put(2, f, d2[f, 0], d2[f, 2])
 
     fields(mid.shape[0], one)
 
 
-def fwd_first_body(fl, mid, ss, sn, rs, rn, v1, v2, w0, wh0, w1, w2, rf, *outs):
+def fwd_first_body(ride, fl, mid, ss, sn, rs, rn, v1, v2, w0, wh0, w1, w2, rf, *outs):
+    if ride:
+        d0, outs, halo = outs[0], outs[1:6], outs[6]
     x0, x1, mid_o, ss_o, sn_o = outs
     fs, fn = fl[0], fl[1]
     rhs = rf[...]
+    own, got, out_o = Sides(fl[2], ss, sn), Sides(fl[2], rs, rn), Sides(fl[2], ss_o, sn_o)
 
     def one(f):
-        x5 = fwd_post(f, mid, ss, sn, rs, rn, w0, wh0, fs, fn, rhs)
+        x5 = fwd_post(f, mid, own, got, w0, wh0, fs, fn, rhs)
         for i in range(5):
             x0[f, i] = x5[i]
         x3 = fwd_second([x5[i] + SCALE_Q * v1[f, i] for i in range(5)], w1, rhs)
         for i in range(3):
             x1[f, i] = x3[i]
-        fwd_pre(f, [x3[i] + SCALE_Q * v2[f, i] for i in range(3)], w2, mid_o, ss_o, sn_o)
+        fwd_pre(f, [x3[i] + SCALE_Q * v2[f, i] for i in range(3)], w2, mid_o, out_o)
+        if ride:
+            out_o.put(2, f, d0[f, 0], d0[f, 2])
+            halo[0, f] = got.south(2, f)
+            halo[1, f] = got.north(2, f)
 
     fields(mid.shape[0], one)
 
@@ -354,12 +406,13 @@
 
 
 def fwd_last_body(half, fl, mid, ss, sn, rs, rn, v3, x0, x1, w2, wh2, w3, rf, *outs):
-    x2, x3, eg = outs
+    x2, x3, eg = outs[:3]
     fs, fn = fl[0], fl[1]
     rhs = rf[...]
+    own, got = Sides(fl[2], ss, sn), Sides(fl[2], rs, rn)
 
     def one(f):
-        x5 = fwd_post(f, mid, ss, sn, rs, rn, w2, wh2, fs, fn, rhs)
+        x5 = fwd_post(f, mid, own, got, w2, wh2, fs, fn, rhs)
         for i in range(5):
             x2[f, i] = x5[i]
             eg[f, 8 + i] = edge(x5[i], half)
@@ -369,6 +422,9 @@
             x3[f, i] = y3[i]
             eg[f, 13 + i] = edge(y3[i], half)
             eg[f, 5 + i] = edge(x1[f, i], half)
+        if len(outs) > 3:
+            outs[3][0, f] = got.south(2, f)
+            outs[3][1, f] = got.north(2, f)
 
     fields(mid.shape[0], one)
 
@@ -377,12 +433,13 @@
     return jnp.concatenate([e[:PAD], x[PAD:-PAD], e[PAD:]], axis=0)
 
 
-def turn_body(carry, sc, x3, eg, d3, w3, ra, *outs):
+def turn_body(carry, fl, sc, x3, eg, d3, w3, ra, *outs):
     if carry:
         outs[4][...] = outs[0][...]
         outs = outs[1:4]
     mid, ss, sn = outs[:3]
     q = None if carry else outs[3]
+    out = Sides(fl[2], ss, sn)
     rhs = ra[...]
     if q is not None:
         q[...] = jnp.zeros_like(q)
@@ -396,28 +453,28 @@
             if q is not None:
                 q[...] += fold(t * y)
             rows.append(t * scale)
-        adj_pre(f, rows, w3, rhs, mid, ss, sn)
+        adj_pre(f, rows, w3, rhs, mid, out)
 
     fields(x3.shape[0], one)
 
 
-def rest_body(sc, x0, x1, x2, eg, d0, d1, d2, ds, dn, f0, f1, f2, q=None):
+def rest_body(sc, x0, x1, x2, eg, d0, d1, d2, h0, h2, f0, f1, f2, q=None):
     if q is not None:
         q[...] = jnp.zeros_like(q)
     scale = sc[0]
 
     def one(f):
-        for x, rows, at, d, w, f_o in (
-            (x0, 5, 0, d0, 0, f0),
+        for x, rows, at, d, h, f_o in (
+            (x0, 5, 0, d0, h0, f0),
             (x1, 3, 5, d1, None, f1),
-            (x2, 5, 8, d2, 1, f2),
+            (x2, 5, 8, d2, h2, f2),
         ):
             for i in range(rows):
                 y = fixed(x[f, i], eg[f, at + i])
                 if rows == 5 and i == 0:
-                    t = ds[w, f] * y
+                    t = h[0, f] * y
                 elif rows == 5 and i == 4:
-                    t = dn[w, f] * y
+                    t = h[1, f] * y
                 else:
                     t = d[f, i - (rows == 5)] * y
                     if q is not None:
@@ -520,65 +577,64 @@
     out[...] = w
 
 
-def final_body(kind, c_ref, k_ref, *refs):
+def outbound_body(c_ref, v0, v1, v2, v3, out):
+    v = (v0, v1, v2, v3)
+
+    def put(first):
+        for k in (first, first + 1):
+            off = k % 2
+            for f in range(out.shape[1]):
+                for i in range(3):
+                    out[k % 2, f, i] = v[k][f, i + off][PAD:-PAD]
+
+    @pl.when(c_ref[0] == 0)
+    def _():
+        put(2)
+
+    @pl.when(c_ref[0] != 0)
+    def _():
+        put(0)
+
+
+def final_body(half, c_ref, k_ref, *refs):
+    g, z, w = refs[0:4], refs[4:8], refs[8:12]
+    og, oz, ow = refs[12:15]
+    inc, res, ib, rb, sem = refs[15:]
     row = k_ref[...]
     at = lanes(row.shape)
-
-    def pick(k):
-        return jnp.sum(jnp.where(at == k, row, 0.0), axis=1, keepdims=True)
-
-    g, z = refs[0:4], refs[4:8]
-    n = 8
-    if kind == "res":
-        w = refs[8:12]
-        n = 12
-        kg, kz, kw = pick(2), pick(3), pick(4)
-    else:
-        kg, kz = pick(0), pick(1)
-    keep, send = refs[n:]
+    ig, iz, rg, rz, rw = [
+        jnp.sum(jnp.where(at == k, row, 0.0), axis=1, keepdims=True) for k in range(5)
+    ]
     c = c_ref[0]
-
-    def one(f):
-        for k in range(4):
-            off = k % 2
-            for i in range(3):
-                val = kg * g[k][f, i + off][PAD:-PAD] + kz * z[k][f, i + off][PAD:-PAD]
-                if kind == "res":
-                    val = val + kw * w[k][f, i + off][PAD:-PAD]
-
-                @pl.when(c == k // 2)
-                def _():
-                    keep[k % 2, f, i] = val
-
-                @pl.when(c != k // 2)
-                def _():
-                    send[k % 2, f, i] = val
-
-    fields(g[0].shape[0], one)
-
-
-def join_body(half, n, c_ref, *refs):
-    keep, other, out, sem = refs[:n], refs[n : 2 * n], refs[2 * n], refs[2 * n + 1]
-    mine = pl.multiple_of(c_ref[0] * half, PAD)
-    theirs = pl.multiple_of((1 - c_ref[0]) * half, PAD)
-    copies = []
-    for src, at in ((keep, mine), (other, theirs)):
-        f0 = 0
-        for s in src:
-            nf = s.shape[1]
-            for w in range(2):
-                copies.append(
-                    pltpu.make_async_copy(
-                        s.at[w],
-                        out.at[w, 0, pl.ds(f0, nf), :, pl.ds(at, half), :],
-                        sem.at[len(copies)],
+    nf = og.shape[1]
+
+    def put(first, mine, theirs):
+        copies = []
+        for k in (first, first + 1):
+            n, off = k % 2, k % 2
+            for f in range(nf):
+                for i in range(3):
+                    x = [v[k][f, i + off][PAD:-PAD] for v in (g, z, w)]
+                    y = [v[n, f, i] for v in (og, oz, ow)]
+                    for (a, b, d), lo in ((x, mine), (y, theirs)):
+                        ib[n, f, i, lo : lo + half] = ig * a + iz * b
+                        rb[n, f, i, lo : lo + half] = rg * a + rz * b + rw * d
+                for src, dst in ((ib, inc), (rb, res)):
+                    copy = pltpu.make_async_copy(
+                        src.at[n, f], dst.at[n, 0, f], sem.at[len(copies)]
                     )
-                )
-            f0 += nf
-    for cp in copies:
-        cp.start()
-    for cp in copies:
-        cp.wait()
+                    copy.start()
+                    copies.append(copy)
+        for copy in copies:
+            copy.wait()
+
+    @pl.when(c == 0)
+    def _():
+        put(0, 0, half)
+
+    @pl.when(c != 0)
+    def _():
+        put(2, half, 0)
 
 
 def per_device(winds, mixing, innovations, obs_weight, obs_sub, obs_col, obs_count):
@@ -593,15 +649,16 @@
     bands = lax.axis_size("space")
     c_arr = c.reshape(1)
     pos_arr = pos.astype(jnp.int32).reshape(1)
-    flags = jnp.stack([(pos > 0), (pos < bands - 1)]).astype(F32)
-    north = [(i, (i + 1) % bands) for i in range(bands)]
-    south = [((i + 1) % bands, i) for i in range(bands)]
+    even = pos % 2 == 0
+    flags = jnp.stack([pos > 0, pos < bands - 1, even]).astype(F32)
+    first_pairs = [(i, i ^ 1) for i in range(bands)]
+    second_pairs = [(i, (((i + 1) ^ 1) - 1) % bands) for i in range(bands)]
 
     def swap(x):
         return lax.ppermute(x, "tm", [(0, 1), (1, 0)])
 
-    def exchange(ss, sn):
-        return lax.ppermute(sn, "space", north), lax.ppermute(ss, "space", south)
+    def exchange(a, b):
+        return lax.ppermute(a, "space", first_pairs), lax.ppermute(b, "space", second_pairs)
 
     def ring_sum(row, step):
         shifts = []
@@ -627,7 +684,7 @@
     place = jnp.where(live, place, -1).astype(F32)
     place = jnp.broadcast_to(place[..., None], (owners, slots, lev))
     blocks = 2 * FIELDS + 1
-    packed = call(
+    packed, token = call(
         pack_body,
         (
             obs_weight.reshape(owners, slots, -1),
@@ -635,14 +692,14 @@
             place,
         ),
         [VM] * 3,
-        [sds(owners, blocks, slots, lev)],
-    )[0]
+        [sds(owners, blocks, slots, lev), sds(8, lev)],
+    )
     got = lax.all_to_all(packed, "space", split_axis=0, concat_axis=0, tiled=True)
 
     w_own, w_snd, ra, rf = call(
         functools.partial(wind_body, half),
-        (c_arr, winds[:, 0], mixing),
-        [SM, VM, VM],
+        (c_arr, winds[:, 0], mixing, token),
+        [SM] + [VM] * 3,
         [sds(2, 2, 3, wide, lev)] * 2 + [sds(2 * lev, 2 * lev, dtype=BF16)] * 2,
     )
     w_got = swap(w_snd)
@@ -652,9 +709,9 @@
         [SM, VM, VM],
         [sds(2, 3, wide, lev)] * 4 + [sds(2, wide, lev)] * 2,
     )
-    from_s, from_n = exchange(down, up)
-    from_s = jnp.where(pos > 0, from_s, 0.0)
-    from_n = jnp.where(pos < bands - 1, from_n, 0.0)
+    one_side, other_side = exchange(jnp.where(even, up, down), jnp.where(even, down, up))
+    from_s = jnp.where(pos > 0, jnp.where(even, other_side, one_side), 0.0)
+    from_n = jnp.where(pos < bands - 1, jnp.where(even, one_side, other_side), 0.0)
     wh0 = jnp.stack([from_s[0], from_n[0]])
     wh2 = jnp.stack([from_s[1], from_n[1]])
 
@@ -667,16 +724,21 @@
     one_arr = jnp.ones((1,), F32)
     span = jnp.stack([sig, 1.0 / sig])
 
-    idx = jnp.maximum(got[:, 2 * FIELDS, :, 0], 0.0).astype(jnp.int32)
-    idx, wh0, wh2, w0, w1, w2, w3, sig_arr, span = lax.optimization_barrier(
-        (idx, wh0, wh2, w0, w1, w2, w3, sig_arr, span)
+    flat = got.reshape(owners * blocks * slots, lev)
+    flat, wh0, wh2, w0, w1, w2, w3, sig_arr, span = lax.optimization_barrier(
+        (flat, wh0, wh2, w0, w1, w2, w3, sig_arr, span)
     )
     halves = [sds(2, FIELDS, 3, wide, lev)] * 2
     acc, g_own, g_snd = call(
-        functools.partial(scatter_body, half),
-        (c_arr, idx, got.reshape(owners * blocks * slots, lev)),
-        [SM, SM, VM],
+        functools.partial(scatter_body, half, slots),
+        (c_arr, flat),
+        [SM, VM],
         [sds(2 * cells * 8, lev)] + halves,
+        scratch=[
+            pltpu.VMEM((slots, lev), jnp.int32),
+            pltpu.SMEM((slots, lev), jnp.int32),
+            pltpu.SemaphoreType.DMA(()),
+        ],
     )
     g_got = swap(g_snd)
     d_own, d_snd = call(functools.partial(diag_body, half), (c_arr, acc), [SM, VM], halves)
@@ -688,10 +750,7 @@
         pick = functools.partial(pick_body, f0)
         gg = call(pick, (c_arr, g_own, g_got), [SM, VM, VM], shapes)
         dd = call(pick, (c_arr, d_own, d_got), [SM, VM, VM], shapes)
-        ds, dn = exchange(
-            jnp.stack([dd[0][:, 0], dd[2][:, 0]]), jnp.stack([dd[0][:, 2], dd[2][:, 2]])
-        )
-        groups.append((nf, gg, dd, ds, dn))
+        groups.append((nf, gg, dd))
         f0 += nf
 
     part = sds(8, lev)
@@ -724,30 +783,33 @@
             return o[0], o[1], tuple(o[2:5]), o[5]
         return o[0], o[1], tuple(o[2:])
 
-    def adj_last(mode, state, f0):
+    def adj_last(mode, state, f0, ride=()):
         mid, ss, sn = state
         nf = mid.shape[0]
         rs, rn = exchange(ss, sn)
-        ins = (flags, mid, ss, sn, rs, rn, f0, w0, wh0, ra)
-        specs = [SM] + [VM] * 9
-        outs = [row3(nf), row5(nf)] + (state_of(nf, 2) if mode < 2 else [])
+        ins = (flags, mid, ss, sn, rs, rn, f0, w0, wh0, ra) + tuple(ride)
+        specs = [SM] + [VM] * (len(ins) - 1)
+        outs = [row3(nf), row5(nf)]
+        outs += state_of(nf, 3 if mode == 0 else 2) if mode < 2 else []
         o = call(functools.partial(adj_last_body, mode), ins, specs, outs)
         return o[0], o[1], tuple(o[2:])
 
-    def fwd_first(state, v1, v2):
+    def fwd_first(state, v1, v2, ride=()):
         mid, ss, sn = state
         nf = mid.shape[0]
         rs, rn = exchange(ss, sn)
-        ins = (flags, mid, ss, sn, rs, rn, v1, v2, w0, wh0, w1, w2, rf)
+        ins = (flags, mid, ss, sn, rs, rn, v1, v2, w0, wh0, w1, w2, rf) + ride
         o = call(
-            fwd_first_body,
+            functools.partial(fwd_first_body, len(ride) > 0),
             ins,
-            [SM] + [VM] * 12,
-            [row5(nf), row3(nf)] + state_of(nf, 2),
+            [SM] + [VM] * (len(ins) - 1),
+            [row5(nf), row3(nf)]
+            + state_of(nf, 3 if ride else 2)
+            + ([sds(2, nf, wide, lev)] if ride else []),
         )
-        return o[0], o[1], tuple(o[2:])
-
-    def fwd_last(state, v3, x0, x1):
+        return o[0], o[1], tuple(o[2:5]), o[5:]
+
+    def fwd_last(state, v3, x0, x1, ride):
         mid, ss, sn = state
         nf = mid.shape[0]
         rs, rn = exchange(ss, sn)
@@ -756,65 +818,70 @@
             functools.partial(fwd_last_body, half),
             ins,
             [SM] + [VM] * 12,
-            [row5(nf), row3(nf), sds(nf, 16, 2 * PAD, lev)],
+            [row5(nf), row3(nf), sds(nf, 16, 2 * PAD, lev)]
+            + ([sds(2, nf, wide, lev)] if ride else []),
         )
 
-    def turn(xs, eg, dd, ds, dn, scale, row=None):
+    def turn(xs, eg, dd, halo, scale, row=None):
         eg = swap(eg)
         x0, x1, x2, x3 = xs
         nf = x3.shape[0]
         carry = row is not None
         o = call(
             functools.partial(turn_body, carry),
-            (scale, x3, eg, dd[3], w3, ra) + ((row,) if carry else ()),
-            [SM] + [VM] * (6 if carry else 5),
+            (flags, scale, x3, eg, dd[3], w3, ra) + ((row,) if carry else ()),
+            [SM] * 2 + [VM] * (6 if carry else 5),
             state_of(nf, 2) + [sds(1, lev) if carry else part],
         )
         r = call(
             rest_body,
-            (scale, x0, x1, x2, eg, dd[0], dd[1], dd[2], ds, dn),
+            (scale, x0, x1, x2, eg, dd[0], dd[1], dd[2]) + halo,
             [SM] + [VM] * 9,
             [row5(nf), row3(nf), row5(nf)] + ([] if carry else [part]),
         )
         return tuple(o[:3]), tuple(r[:3]), (o[3] if carry else (o[3], r[3]))
 
-    def forward(state, v):
-        x0, x1, state = fwd_first(state, v[1], v[2])
-        x2, x3, eg = fwd_last(state, v[3], x0, x1)
-        return (x0, x1, x2, x3), eg
+    def forward(state, v, ride=()):
+        x0, x1, state, halo2 = fwd_first(state, v[1], v[2], ride)
+        o = fwd_last(state, v[3], x0, x1, len(ride) > 0)
+        return (x0, x1) + tuple(o[:2]), o[2], tuple(o[3:]) + tuple(halo2)
 
     def norm(v):
         return call(norm_body, tuple(v), [VM] * 4, [part])[0]
 
     chains = []
-    for nf, gg, dd, ds, dn in groups:
+    for nf, gg, dd in groups:
         state = tuple(
-            call(turn_first_body, (gg[3], gg[2], w3, ra), [VM] * 4, state_of(nf, 3))
+            call(
+                turn_first_body,
+                (flags, gg[3], gg[2], w3, ra),
+                [SM] + [VM] * 4,
+                state_of(nf, 3),
+            )
         )
         g3, g2, state = adj_mid(state, gg[2], gg[1], gg[0])
-        g0, g1, state = adj_last(0, state, gg[0])
+        g0, g1, state = adj_last(0, state, gg[0], (dd[2],))
         g = (g0, g1, g2, g3)
-        xs, eg = forward(state, g)
-        state, fs, bg = turn(xs, eg, dd, ds, dn, sig_arr)
+        xs, eg, halo = forward(state, g, (dd[0],))
+        state, fs, bg = turn(xs, eg, dd, halo, sig_arr)
         z3, z2, state = adj_mid(state, fs[2], fs[1])
         z0, z1, state = adj_last(1, state, fs[0])
         z = (z0, z1, z2, z3)
-        xs, eg = forward(state, z)
-        chains.append((g, z, xs, eg, norm(g), bg, norm(z)))
+        xs, eg, _ = forward(state, z)
+        chains.append((g, z, xs, eg, norm(g), bg, norm(z), halo))
     ins = [ch[4] for ch in chains] + [q for ch in chains for q in ch[5]]
     ins += [ch[6] for ch in chains]
-    for ch, (_, _, dd, _, _) in zip(chains, groups):
+    for ch, (_, _, dd) in zip(chains, groups):
         ins += list(ch[2]) + list(dd)
     row = call(
         functools.partial(sums_body, len(chains)), tuple(ins), [VM] * len(ins), [sds(1, lev)]
     )[0]
     row = call(add_body, (row, swap(row)), [VM] * 2, [sds(1, lev)], flops=1e5)[0]
-    row = ring_sum(row, 1)
     states = []
-    for ch, (nf, gg, dd, ds, dn) in zip(chains, groups):
-        state, fs, row = turn(ch[2], ch[3], dd, ds, dn, one_arr, row)
+    for ch, (nf, gg, dd) in zip(chains, groups):
+        state, fs, row = turn(ch[2], ch[3], dd, ch[7], one_arr, row)
         states.append((state, fs))
-    row = ring_sum(row, 4)
+    row = ring_sum(ring_sum(row, 1), 4)
     mids = []
     for state, fs in states:
         w3z, w2z, state, row = adj_mid(state, fs[2], fs[1], None, row)
@@ -822,36 +889,32 @@
     row = ring_sum(row, 16)
     weights = call(solve_body, (span, row), [SM, VM], [sds(1, lev)], flops=1e5)[0]
 
-    def final(kind, *vecs):
-        nf = vecs[0][0].shape[0]
-        ins = (c_arr, weights) + tuple(x for v in vecs for x in v)
-        shape = sds(2, nf, 3, half, lev)
-        keep, send = call(
-            functools.partial(final_body, kind),
-            ins,
-            [SM] + [VM] * (len(ins) - 1),
-            [shape, shape],
+    g, z = chains[0][0], chains[0][1]
+    w3z, w2z, state, fs = mids[0]
+    w0z, w1z, _ = adj_last(2, state, fs[0])
+    w = (w0z, w1z, w2z, w3z)
+    shape = sds(2, FIELDS, 3, half, lev)
+
+    def other(v):
+        return swap(
+            call(outbound_body, (c_arr,) + tuple(v), [SM] + [VM] * 4, [shape])[0]
         )
-        return keep, swap(send)
-
-    def join(parts):
-        n = len(parts)
-        ins = (c_arr,) + tuple(p[0] for p in parts) + tuple(p[1] for p in parts)
-        return call(
-            functools.partial(join_body, half, n),
-            ins,
-            [SM] + [VM] * (2 * n),
-            [sds(2, 1, FIELDS, 3, cols, lev)],
-            scratch=[pltpu.SemaphoreType.DMA((4 * n,))],
-            out_specs=[pl.BlockSpec(memory_space=pl.ANY)],
-        )[0]
-
-    increment = join([final("inc", ch[0], ch[1]) for ch in chains])
-    ends = []
-    for ch, (w3z, w2z, state, fs) in zip(chains, mids):
-        w0z, w1z, _ = adj_last(2, state, fs[0])
-        ends.append(final("res", ch[0], ch[1], (w0z, w1z, w2z, w3z)))
-    return increment, join(ends)
+
+    ins = (c_arr, weights) + tuple(g) + tuple(z) + w + (other(g), other(z), other(w))
+    full = (2, FIELDS, 3, cols, lev)
+    return call(
+        functools.partial(final_body, half),
+        ins,
+        [SM] + [VM] * (len(ins) - 1),
+        [sds(2, 1, FIELDS, 3, cols, lev)] * 2,
+        scratch=[
+            pltpu.VMEM(full, F32),
+            pltpu.VMEM(full, F32),
+            pltpu.SemaphoreType.DMA((4 * FIELDS,)),
+        ],
+        out_specs=[pl.BlockSpec(memory_space=pl.ANY)] * 2,
+        vmem=12 * 2**20,
+    )
 
 
 def solution(mesh):

time: 352 us -> 350 us (level)
  starting transfers between devices: 120 us -> 66.6 us
  waiting for transfers between devices: 168 us -> 218 us
    ppermute x24 -> x22, starting transfers between devices: 84.3 us -> 30 us  [the longest x11 29.2 us: exchange(): lax.ppermute(b, 'space', second_pairs)]
    ppermute x24 -> x22, waiting for transfers between devices: 146 us -> 195 us  [the longest x11 110 us: exchange(): lax.ppermute(a, 'space', first_pairs)]
    ppermute x8 -> x9, starting transfers between devices: 15.7 us -> 19 us  [swap(): return lax.ppermute(x, 'tm', [(0, 1), (1, 0)])]
    unnamed x19 -> x16, local copies, waits for them, and re-layouts: 8.38 us -> 6.96 us
  transfers between devices with their start and end apart: 42 -> 41, of which waited for: 25 -> 30; matrix products, arithmetic and copies ran while one was open for 1% -> 1% of each run, Pallas kernels for 5% -> 3%
where the time goes in v4:
time: 350 us; the launch traced here: 349 us
  waiting for transfers between devices  218 us (62%)
  starting transfers between devices  66.6 us (19%)
  Pallas kernels  50.4 us (14%)
  local copies, waits for them, and re-layouts  7.2 us (2%)
  other arithmetic  4.12 us (1%)
    ppermute x11, waiting for transfers between devices, exchange(): lax.ppermute(a, 'space', first_pairs)  110 us
    ppermute x11, waiting for transfers between devices, exchange(): lax.ppermute(b, 'space', second_pairs)  84.5 us
    pallas_call x34, Pallas kernels, call(): pl.pallas_call(body, out_shape=outs, in_specs=specs, out_specs=out_specs...  50.4 us
    ppermute x11, starting transfers between devices, exchange(): lax.ppermute(b, 'space', second_pairs)  29.2 us
    ppermute x9, starting transfers between devices, swap(): return lax.ppermute(x, 'tm', [(0, 1), (1, 0)])  19 us
    ppermute x9, waiting for transfers between devices, ring_sum(): got = tuple((lax.ppermute(row, 'space', p) for p in shifts))  17.4 us
    all_to_all x1, starting transfers between devices, per_device(): lax.all_to_all(packed, 'space', split_axis=0, concat_axis=0, tiled=True)  11.4 us
  transfers between devices with their start and end apart: 41, of which 30 were waited for; matrix products, arithmetic and copies ran while one was open for 1% of the time, Pallas kernels for 3%

profile of v4, /device:TPU:1, one launch (start us, length us, event | category | flops | bytes accessed | tf_op | source)
XLA Modules:
  0.0 348.6 jit_solution(15699367554711091808)
XLA Ops:
  8.2 11.4 %all-to-all-start = ((f32[64,7,8,128]{3,2,1,0:T(8,128)}), f32[64,7,8,128]{3,2,1,0:T(8,128)}, u32[]{:S(2)}, u32[]{:S(2)}) async-start(f32[64,7,8,128]{3,2,1,0:T(8,128)} %get-tuple-element.100), calls=%async_computation | async-start | bytes 3670016 | tf_op jit(solution)/shard_map/all_to_all | solution.py:697
  24.4 6.7 %collective-permute-start.1 = (f32[2,208,128]{2,1,0:T(8,128)}, f32[2,208,128]{2,1,0:T(8,128)S(1)}, u32[]{:S(2)}, u32[]{:S(2)}) collective-permute-start(f32[2,208,128]{2,1,0:T(8,128)} %get-tuple-element.202), channel_id=1, source_target_pairs={{0,63},{1,2},{2,1},{3,4},{4,3},{5,6},{6,5},{7,8},{8,7},{9,10},{10,... | collective-permute-start | bytes 638984 | tf_op jit(solution)/shard_map/ppermute | solution.py:661
  33.7 17.2 %collective-permute-done.1 = f32[2,208,128]{2,1,0:T(8,128)S(1)} collective-permute-done((f32[2,208,128]{2,1,0:T(8,128)}, f32[2,208,128]{2,1,0:T(8,128)S(1)}, u32[]{:S(2)}, u32[]{:S(2)}) %collective-permute-start.1) | collective-permute-done | bytes 213024 | tf_op jit(solution)/shard_map/ppermute | solution.py:661
  52.0 6.0 %shard_map.89 = (f32[18432,128]{1,0:T(8,128)S(1)}, f32[2,3,3,208,128]{4,3,2,1,0:T(8,128)S(1)}, f32[2,3,3,208,128]{4,3,2,1,0:T(8,128)S(1)}) custom-call(s32[1]{0:T(128)} %bitcast.c_ref, f32[3584,128]{1,0:T(8,128)} %bitcast.5.p_ref), custom_call_target="tpu_custom_call" | custom-call | flops 100000000 | bytes 15106052 | tf_op jit(solution)/shard_map/pallas_call | solution.py:24
  59.0 3.5 collective-permute-done.3.got_ref
  64.6 2.2 collective-permute-start.5
  68.6 18.4 %collective-permute-done.4.refs_4_ = f32[3,3,208,128]{3,2,1,0:T(8,128)S(1)} collective-permute-done((f32[3,3,208,128]{3,2,1,0:T(8,128)S(1)}, f32[3,3,208,128]{3,2,1,0:T(8,128)S(1)}, u32[]{:S(2)}, u32[]{:S(2)}) %collective-permute-start.4) | collective-permute-done | bytes 958496 | tf_op jit(solution)/shard_map/ppermute | solution.py:661
  87.0 5.5 %collective-permute-done.5.refs_5_ = f32[3,3,208,128]{3,2,1,0:T(8,128)S(1)} collective-permute-done((f32[3,3,208,128]{3,2,1,0:T(8,128)S(1)}, f32[3,3,208,128]{3,2,1,0:T(8,128)S(1)}, u32[]{:S(2)}, u32[]{:S(2)}) %collective-permute-start.5) | collective-permute-done | bytes 958496 | tf_op jit(solution)/shard_map/ppermute | solution.py:661
  92.5 3.1 shard_map.92
  95.7 2.2 collective-permute-start.7
  98.2 19.0 %collective-permute-done.6.refs_4_ = f32[3,3,208,128]{3,2,1,0:T(8,128)S(1)} collective-permute-done((f32[3,3,208,128]{3,2,1,0:T(8,128)S(1)}, f32[3,3,208,128]{3,2,1,0:T(8,128)S(1)}, u32[]{:S(2)}, u32[]{:S(2)}) %collective-permute-start.6) | collective-permute-done | bytes 958496 | tf_op jit(solution)/shard_map/ppermute | solution.py:661
  117.2 5.5 %collective-permute-done.7.refs_5_ = f32[3,3,208,128]{3,2,1,0:T(8,128)S(1)} collective-permute-done((f32[3,3,208,128]{3,2,1,0:T(8,128)S(1)}, f32[3,3,208,128]{3,2,1,0:T(8,128)S(1)}, u32[]{:S(2)}, u32[]{:S(2)}) %collective-permute-start.7) | collective-permute-done | bytes 958496 | tf_op jit(solution)/shard_map/ppermute | solution.py:661
  122.7 2.8 shard_map.95
  125.5 2.2 collective-permute-start.10
  127.7 23.9 %collective-permute-done.10.rn = f32[3,3,208,128]{3,2,1,0:T(8,128)S(1)} collective-permute-done((f32[3,3,208,128]{3,2,1,0:T(8,128)S(1)}, f32[3,3,208,128]{3,2,1,0:T(8,128)S(1)}, u32[]{:S(2)}, u32[]{:S(2)}) %collective-permute-start.10) | collective-permute-done | bytes 958496 | tf_op jit(solution)/shard_map/ppermute | solution.py:661
  151.6 3.2 shard_map.96
  154.9 2.2 collective-permute-start.12
  157.1 17.4 %collective-permute-done.11.rs = f32[3,3,208,128]{3,2,1,0:T(8,128)S(1)} collective-permute-done((f32[3,3,208,128]{3,2,1,0:T(8,128)S(1)}, f32[3,3,208,128]{3,2,1,0:T(8,128)S(1)}, u32[]{:S(2)}, u32[]{:S(2)}) %collective-permute-start.11) | collective-permute-done | bytes 958496 | tf_op jit(solution)/shard_map/ppermute | solution.py:661
  174.6 5.5 %collective-permute-done.12.rn = f32[3,3,208,128]{3,2,1,0:T(8,128)S(1)} collective-permute-done((f32[3,3,208,128]{3,2,1,0:T(8,128)S(1)}, f32[3,3,208,128]{3,2,1,0:T(8,128)S(1)}, u32[]{:S(2)}, u32[]{:S(2)}) %collective-permute-start.12) | collective-permute-done | bytes 958496 | tf_op jit(solution)/shard_map/ppermute | solution.py:661
  180.1 2.8 shard_map.97
  182.9 4.2 %collective-permute-start.13 = (f32[3,16,16,128]{3,2,1,0:T(8,128)S(1)}, f32[3,16,16,128]{3,2,1,0:T(8,128)S(1)}, u32[]{:S(2)}, u32[]{:S(2)}) collective-permute-start(f32[3,16,16,128]{3,2,1,0:T(8,128)S(1)} %get-tuple-element.150), channel_id=1, source_target_pairs={{0,64},{64,0},{1,65},{65,1},{2,66},{66,2},{3,67},{67,3},{4,68},{68... | collective-permute-start | bytes 1179656 | tf_op jit(solution)/shard_map/ppermute | solution.py:658
  190.3 2.2 collective-permute-start.15
  193.3 12.6 %collective-permute-done.14.refs_4_ = f32[2,3,208,128]{3,2,1,0:T(8,128)S(1)} collective-permute-done((f32[2,3,208,128]{3,2,1,0:T(8,128)S(1)}, f32[2,3,208,128]{3,2,1,0:T(8,128)S(1)}, u32[]{:S(2)}, u32[]{:S(2)}) %collective-permute-start.14) | collective-permute-done | bytes 639008 | tf_op jit(solution)/shard_map/ppermute | solution.py:661
  205.9 5.5 %collective-permute-done.15.refs_5_ = f32[2,3,208,128]{3,2,1,0:T(8,128)S(1)} collective-permute-done((f32[2,3,208,128]{3,2,1,0:T(8,128)S(1)}, f32[2,3,208,128]{3,2,1,0:T(8,128)S(1)}, u32[]{:S(2)}, u32[]{:S(2)}) %collective-permute-start.15) | collective-permute-done | bytes 639008 | tf_op jit(solution)/shard_map/ppermute | solution.py:661
  211.4 3.1 shard_map.100
  214.6 2.2 collective-permute-start.17
  216.8 12.5 %collective-permute-done.16.refs_4_ = f32[2,3,208,128]{3,2,1,0:T(8,128)S(1)} collective-permute-done((f32[2,3,208,128]{3,2,1,0:T(8,128)S(1)}, f32[2,3,208,128]{3,2,1,0:T(8,128)S(1)}, u32[]{:S(2)}, u32[]{:S(2)}) %collective-permute-start.16) | collective-permute-done | bytes 639008 | tf_op jit(solution)/shard_map/ppermute | solution.py:661
  229.3 5.5 %collective-permute-done.17.refs_5_ = f32[2,3,208,128]{3,2,1,0:T(8,128)S(1)} collective-permute-done((f32[2,3,208,128]{3,2,1,0:T(8,128)S(1)}, f32[2,3,208,128]{3,2,1,0:T(8,128)S(1)}, u32[]{:S(2)}, u32[]{:S(2)}) %collective-permute-start.17) | collective-permute-done | bytes 639008 | tf_op jit(solution)/shard_map/ppermute | solution.py:661
  234.8 2.7 shard_map.101
  237.6 2.2 collective-permute-start.19
  239.8 11.5 %collective-permute-done.18.rs = f32[2,3,208,128]{3,2,1,0:T(8,128)S(1)} collective-permute-done((f32[2,3,208,128]{3,2,1,0:T(8,128)S(1)}, f32[2,3,208,128]{3,2,1,0:T(8,128)S(1)}, u32[]{:S(2)}, u32[]{:S(2)}) %collective-permute-start.18) | collective-permute-done | bytes 639008 | tf_op jit(solution)/shard_map/ppermute | solution.py:661
  251.3 5.5 %collective-permute-done.19.rn = f32[2,3,208,128]{3,2,1,0:T(8,128)S(1)} collective-permute-done((f32[2,3,208,128]{3,2,1,0:T(8,128)S(1)}, f32[2,3,208,128]{3,2,1,0:T(8,128)S(1)}, u32[]{:S(2)}, u32[]{:S(2)}) %collective-permute-start.19) | collective-permute-done | bytes 639008 | tf_op jit(solution)/shard_map/ppermute | solution.py:661
  256.9 3.2 shard_map.102
  260.2 2.2 collective-permute-start.21
  262.4 10.6 %collective-permute-done.20.rs = f32[2,3,208,128]{3,2,1,0:T(8,128)S(1)} collective-permute-done((f32[2,3,208,128]{3,2,1,0:T(8,128)S(1)}, f32[2,3,208,128]{3,2,1,0:T(8,128)S(1)}, u32[]{:S(2)}, u32[]{:S(2)}) %collective-permute-start.20) | collective-permute-done | bytes 639008 | tf_op jit(solution)/shard_map/ppermute | solution.py:661
  273.0 5.5 %collective-permute-done.21.rn = f32[2,3,208,128]{3,2,1,0:T(8,128)S(1)} collective-permute-done((f32[2,3,208,128]{3,2,1,0:T(8,128)S(1)}, f32[2,3,208,128]{3,2,1,0:T(8,128)S(1)}, u32[]{:S(2)}, u32[]{:S(2)}) %collective-permute-start.21) | collective-permute-done | bytes 639008 | tf_op jit(solution)/shard_map/ppermute | solution.py:661
  278.5 2.7 shard_map.103
  281.2 4.0 %collective-permute-start.22 = (f32[3,16,16,128]{3,2,1,0:T(8,128)S(1)}, f32[3,16,16,128]{3,2,1,0:T(8,128)S(1)}, u32[]{:S(2)}, u32[]{:S(2)}) collective-permute-start(f32[3,16,16,128]{3,2,1,0:T(8,128)S(1)} %get-tuple-element.177), channel_id=1, source_target_pairs={{0,64},{64,0},{1,65},{65,1},{2,66},{66,2},{3,67},{67,3},{4,68},{68... | collective-permute-start | bytes 1179656 | tf_op jit(solution)/shard_map/ppermute | solution.py:658
  294.8 8.6 %collective-permute-done.26.b = f32[1,128]{1,0:T(1,128)S(1)} collective-permute-done((f32[1,128]{1,0:T(1,128)S(1)}, f32[1,128]{1,0:T(1,128)S(1)}, u32[]{:S(2)}, u32[]{:S(2)}) %collective-permute-start.26) | collective-permute-done | bytes 544 | tf_op jit(solution)/shard_map/ppermute | solution.py:671
  305.5 2.6 collective-permute-start.31
  310.8 3.1 shard_map.112
  314.0 2.7 collective-permute-start.36
  316.8 3.5 collective-permute-start.37
  320.7 7.8 %collective-permute-done.35.refs_4_ = f32[2,3,208,128]{3,2,1,0:T(8,128)S(1)} collective-permute-done((f32[2,3,208,128]{3,2,1,0:T(8,128)S(1)}, f32[2,3,208,128]{3,2,1,0:T(8,128)S(1)}, u32[]{:S(2)}, u32[]{:S(2)}) %collective-permute-start.35) | collective-permute-done | bytes 639008 | tf_op jit(solution)/shard_map/ppermute | solution.py:661
  328.5 3.9 %collective-permute-done.36.refs_5_ = f32[2,3,208,128]{3,2,1,0:T(8,128)S(1)} collective-permute-done((f32[2,3,208,128]{3,2,1,0:T(8,128)S(1)}, f32[2,3,208,128]{3,2,1,0:T(8,128)S(1)}, u32[]{:S(2)}, u32[]{:S(2)}) %collective-permute-start.36) | collective-permute-done | bytes 639008 | tf_op jit(solution)/shard_map/ppermute | solution.py:661
  334.6 4.0 %collective-permute-start.39 = (f32[2,3,3,192,128]{4,3,2,1,0:T(8,128)S(1)}, f32[2,3,3,192,128]{4,3,2,1,0:T(8,128)S(1)}, u32[]{:S(2)}, u32[]{:S(2)}) collective-permute-start(f32[2,3,3,192,128]{4,3,2,1,0:T(8,128)S(1)} %shard_map.118), channel_id=1, source_target_pairs={{0,64},{64,0},{1,65},{65,1},{2,66},{66,2},{3,67},{67,3},{4,68},{68... | collective-permute-start | bytes 5308424 | tf_op jit(solution)/shard_map/ppermute | solution.py:658
  338.9 3.3 collective-permute-done.32.b
  345.3 3.2 shard_map.119
  (97 shorter events, 44.6 us)
Async XLA Ops:
  0.6 4.7 %copy-start.4 = (bf16[2,1,2,3,384,128]{5,4,3,2,1,0:T(8,128)(2,1)S(1)}, bf16[2,1,2,3,384,128]{5,4,3,2,1,0:T(8,128)(2,1)}, u32[]{:S(2)}) copy-start(bf16[2,1,2,3,384,128]{5,4,3,2,1,0:T(8,128)(2,1)} %param.7) | copy-start | bytes 3538948
  1.7 1.1 copy-start.5
  2.8 1.1 copy-start.6
  3.9 1.4 copy-start.7
  5.7 1.0 copy-start
  6.8 12.9 %collective-permute-start = (f32[2,2,3,208,128]{4,3,2,1,0:T(8,128)S(1)}, f32[2,2,3,208,128]{4,3,2,1,0:T(8,128)S(1)}, u32[]{:S(2)}, u32[]{:S(2)}) collective-permute-start(f32[2,2,3,208,128]{4,3,2,1,0:T(8,128)S(1)} %get-tuple-element.103), channel_id=1, source_target_pairs={{0,64},{64,0},{1,65},{65,1},{2,66},{66,2},{3,67},{67,3},{4,68},{68... | collective-permute-start | bytes 3833864 | tf_op jit(solution)/shard_map/ppermute | solution.py:658
  8.2 43.8 %all-to-all-start = ((f32[64,7,8,128]{3,2,1,0:T(8,128)}), f32[64,7,8,128]{3,2,1,0:T(8,128)}, u32[]{:S(2)}, u32[]{:S(2)}) async-start(f32[64,7,8,128]{3,2,1,0:T(8,128)} %get-tuple-element.100), calls=%async_computation | async-start | bytes 3670016 | tf_op jit(solution)/shard_map/all_to_all | solution.py:697
  20.7 1.3 copy-start.1
  22.0 1.3 copy-start.3
  24.4 26.6 %collective-permute-start.1 = (f32[2,208,128]{2,1,0:T(8,128)}, f32[2,208,128]{2,1,0:T(8,128)S(1)}, u32[]{:S(2)}, u32[]{:S(2)}) collective-permute-start(f32[2,208,128]{2,1,0:T(8,128)} %get-tuple-element.202), channel_id=1, source_target_pairs={{0,63},{1,2},{2,1},{3,4},{4,3},{5,6},{6,5},{7,8},{8,7},{9,10},{10,... | collective-permute-start | bytes 638984 | tf_op jit(solution)/shard_map/ppermute | solution.py:661
  31.0 19.9 %collective-permute-start.2 = (f32[2,208,128]{2,1,0:T(8,128)}, f32[2,208,128]{2,1,0:T(8,128)}, u32[]{:S(2)}, u32[]{:S(2)}) collective-permute-start(f32[2,208,128]{2,1,0:T(8,128)} %get-tuple-element.203), channel_id=1, source_target_pairs={{0,1},{1,0},{2,3},{3,2},{4,5},{5,4},{6,7},{7,6},{8,9},{9,8},{10,11... | collective-permute-start | bytes 638984 | tf_op jit(solution)/shard_map/ppermute | solution.py:661
  58.0 4.4 %collective-permute-start.3 = (f32[2,3,3,208,128]{4,3,2,1,0:T(8,128)S(1)}, f32[2,3,3,208,128]{4,3,2,1,0:T(8,128)S(1)}, u32[]{:S(2)}, u32[]{:S(2)}) collective-permute-start(f32[2,3,3,208,128]{4,3,2,1,0:T(8,128)S(1)} %get-tuple-element.114), channel_id=1, source_target_pairs={{0,64},{64,0},{1,65},{65,1},{2,66},{66,2},{3,67},{67,3},{4,68},{68... | collective-permute-start | bytes 5750792 | tf_op jit(solution)/shard_map/ppermute | solution.py:658
  64.5 22.5 %collective-permute-start.4 = (f32[3,3,208,128]{3,2,1,0:T(8,128)S(1)}, f32[3,3,208,128]{3,2,1,0:T(8,128)S(1)}, u32[]{:S(2)}, u32[]{:S(2)}) collective-permute-start(f32[3,3,208,128]{3,2,1,0:T(8,128)S(1)} %get-tuple-element.120.refs_2_), channel_id=1, source_target_pairs={{0,1},{1,0},{2,3},{3,2},{4,5},{5,4},{6,7},{7,6},{8,9},{9,8},{10,11... | collective-permute-start | bytes 2875400 | tf_op jit(solution)/shard_map/ppermute | solution.py:661
  64.6 27.9 %collective-permute-start.5 = (f32[3,3,208,128]{3,2,1,0:T(8,128)S(1)}, f32[3,3,208,128]{3,2,1,0:T(8,128)S(1)}, u32[]{:S(2)}, u32[]{:S(2)}) collective-permute-start(f32[3,3,208,128]{3,2,1,0:T(8,128)S(1)} %get-tuple-element.121.refs_3_), channel_id=1, source_target_pairs={{0,63},{1,2},{2,1},{3,4},{4,3},{5,6},{6,5},{7,8},{8,7},{9,10},{10,... | collective-permute-start | bytes 2875400 | tf_op jit(solution)/shard_map/ppermute | solution.py:661
  68.0 29.9 %collective-permute-start.8 = (f32[2,3,3,208,128]{4,3,2,1,0:T(8,128)S(1)}, f32[2,3,3,208,128]{4,3,2,1,0:T(8,128)S(1)}, u32[]{:S(2)}, u32[]{:S(2)}) collective-permute-start(f32[2,3,3,208,128]{4,3,2,1,0:T(8,128)S(1)} %get-tuple-element.134), channel_id=1, source_target_pairs={{0,64},{64,0},{1,65},{65,1},{2,66},{66,2},{3,67},{67,3},{4,68},{68... | collective-permute-start | bytes 5750792 | tf_op jit(solution)/shard_map/ppermute | solution.py:658
  95.6 21.6 %collective-permute-start.6 = (f32[3,3,208,128]{3,2,1,0:T(8,128)S(1)}, f32[3,3,208,128]{3,2,1,0:T(8,128)S(1)}, u32[]{:S(2)}, u32[]{:S(2)}) collective-permute-start(f32[3,3,208,128]{3,2,1,0:T(8,128)S(1)} %get-tuple-element.128.refs_2_), channel_id=1, source_target_pairs={{0,1},{1,0},{2,3},{3,2},{4,5},{5,4},{6,7},{7,6},{8,9},{9,8},{10,11... | collective-permute-start | bytes 2875400 | tf_op jit(solution)/shard_map/ppermute | solution.py:661
  95.7 27.0 %collective-permute-start.7 = (f32[3,3,208,128]{3,2,1,0:T(8,128)S(1)}, f32[3,3,208,128]{3,2,1,0:T(8,128)S(1)}, u32[]{:S(2)}, u32[]{:S(2)}) collective-permute-start(f32[3,3,208,128]{3,2,1,0:T(8,128)S(1)} %get-tuple-element.129.refs_3_), channel_id=1, source_target_pairs={{0,63},{1,2},{2,1},{3,4},{4,3},{5,6},{6,5},{7,8},{8,7},{9,10},{10,... | collective-permute-start | bytes 2875400 | tf_op jit(solution)/shard_map/ppermute | solution.py:661
  125.5 26.1 %collective-permute-start.10 = (f32[3,3,208,128]{3,2,1,0:T(8,128)S(1)}, f32[3,3,208,128]{3,2,1,0:T(8,128)S(1)}, u32[]{:S(2)}, u32[]{:S(2)}) collective-permute-start(f32[3,3,208,128]{3,2,1,0:T(8,128)S(1)} %get-tuple-element.138.sn), channel_id=1, source_target_pairs={{0,63},{1,2},{2,1},{3,4},{4,3},{5,6},{6,5},{7,8},{8,7},{9,10},{10,... | collective-permute-start | bytes 2875400 | tf_op jit(solution)/shard_map/ppermute | solution.py:661
  127.7 23.9 %collective-permute-start.9 = (f32[3,3,208,128]{3,2,1,0:T(8,128)S(1)}, f32[3,3,208,128]{3,2,1,0:T(8,128)S(1)}, u32[]{:S(2)}, u32[]{:S(2)}) collective-permute-start(f32[3,3,208,128]{3,2,1,0:T(8,128)S(1)} %get-tuple-element.137.ss), channel_id=1, source_target_pairs={{0,1},{1,0},{2,3},{3,2},{4,5},{5,4},{6,7},{7,6},{8,9},{9,8},{10,11... | collective-permute-start | bytes 2875400 | tf_op jit(solution)/shard_map/ppermute | solution.py:661
  154.8 19.7 %collective-permute-start.11 = (f32[3,3,208,128]{3,2,1,0:T(8,128)S(1)}, f32[3,3,208,128]{3,2,1,0:T(8,128)S(1)}, u32[]{:S(2)}, u32[]{:S(2)}) collective-permute-start(f32[3,3,208,128]{3,2,1,0:T(8,128)S(1)} %get-tuple-element.144.ss), channel_id=1, source_target_pairs={{0,1},{1,0},{2,3},{3,2},{4,5},{5,4},{6,7},{7,6},{8,9},{9,8},{10,11... | collective-permute-start | bytes 2875400 | tf_op jit(solution)/shard_map/ppermute | solution.py:661
  154.9 25.2 %collective-permute-start.12 = (f32[3,3,208,128]{3,2,1,0:T(8,128)S(1)}, f32[3,3,208,128]{3,2,1,0:T(8,128)S(1)}, u32[]{:S(2)}, u32[]{:S(2)}) collective-permute-start(f32[3,3,208,128]{3,2,1,0:T(8,128)S(1)} %get-tuple-element.145.sn), channel_id=1, source_target_pairs={{0,63},{1,2},{2,1},{3,4},{4,3},{5,6},{6,5},{7,8},{8,7},{9,10},{10,... | collective-permute-start | bytes 2875400 | tf_op jit(solution)/shard_map/ppermute | solution.py:661
  182.9 5.6 %collective-permute-start.13 = (f32[3,16,16,128]{3,2,1,0:T(8,128)S(1)}, f32[3,16,16,128]{3,2,1,0:T(8,128)S(1)}, u32[]{:S(2)}, u32[]{:S(2)}) collective-permute-start(f32[3,16,16,128]{3,2,1,0:T(8,128)S(1)} %get-tuple-element.150), channel_id=1, source_target_pairs={{0,64},{64,0},{1,65},{65,1},{2,66},{66,2},{3,67},{67,3},{4,68},{68... | collective-permute-start | bytes 1179656 | tf_op jit(solution)/shard_map/ppermute | solution.py:658
  190.2 15.7 %collective-permute-start.14 = (f32[2,3,208,128]{3,2,1,0:T(8,128)S(1)}, f32[2,3,208,128]{3,2,1,0:T(8,128)S(1)}, u32[]{:S(2)}, u32[]{:S(2)}) collective-permute-start(f32[2,3,208,128]{3,2,1,0:T(8,128)S(1)} %get-tuple-element.153.refs_2_), channel_id=1, source_target_pairs={{0,1},{1,0},{2,3},{3,2},{4,5},{5,4},{6,7},{7,6},{8,9},{9,8},{10,11... | collective-permute-start | bytes 1916936 | tf_op jit(solution)/shard_map/ppermute | solution.py:661
  190.3 21.1 %collective-permute-start.15 = (f32[2,3,208,128]{3,2,1,0:T(8,128)S(1)}, f32[2,3,208,128]{3,2,1,0:T(8,128)S(1)}, u32[]{:S(2)}, u32[]{:S(2)}) collective-permute-start(f32[2,3,208,128]{3,2,1,0:T(8,128)S(1)} %get-tuple-element.154.refs_3_), channel_id=1, source_target_pairs={{0,63},{1,2},{2,1},{3,4},{4,3},{5,6},{6,5},{7,8},{8,7},{9,10},{10,... | collective-permute-start | bytes 1916936 | tf_op jit(solution)/shard_map/ppermute | solution.py:661
  214.5 14.8 %collective-permute-start.16 = (f32[2,3,208,128]{3,2,1,0:T(8,128)S(1)}, f32[2,3,208,128]{3,2,1,0:T(8,128)S(1)}, u32[]{:S(2)}, u32[]{:S(2)}) collective-permute-start(f32[2,3,208,128]{3,2,1,0:T(8,128)S(1)} %get-tuple-element.162.refs_2_), channel_id=1, source_target_pairs={{0,1},{1,0},{2,3},{3,2},{4,5},{5,4},{6,7},{7,6},{8,9},{9,8},{10,11... | collective-permute-start | bytes 1916936 | tf_op jit(solution)/shard_map/ppermute | solution.py:661
  214.6 20.2 %collective-permute-start.17 = (f32[2,3,208,128]{3,2,1,0:T(8,128)S(1)}, f32[2,3,208,128]{3,2,1,0:T(8,128)S(1)}, u32[]{:S(2)}, u32[]{:S(2)}) collective-permute-start(f32[2,3,208,128]{3,2,1,0:T(8,128)S(1)} %get-tuple-element.163.refs_3_), channel_id=1, source_target_pairs={{0,63},{1,2},{2,1},{3,4},{4,3},{5,6},{6,5},{7,8},{8,7},{9,10},{10,... | collective-permute-start | bytes 1916936 | tf_op jit(solution)/shard_map/ppermute | solution.py:661
  237.5 13.8 %collective-permute-start.18 = (f32[2,3,208,128]{3,2,1,0:T(8,128)S(1)}, f32[2,3,208,128]{3,2,1,0:T(8,128)S(1)}, u32[]{:S(2)}, u32[]{:S(2)}) collective-permute-start(f32[2,3,208,128]{3,2,1,0:T(8,128)S(1)} %get-tuple-element.166.ss), channel_id=1, source_target_pairs={{0,1},{1,0},{2,3},{3,2},{4,5},{5,4},{6,7},{7,6},{8,9},{9,8},{10,11... | collective-permute-start | bytes 1916936 | tf_op jit(solution)/shard_map/ppermute | solution.py:661
  237.6 19.3 %collective-permute-start.19 = (f32[2,3,208,128]{3,2,1,0:T(8,128)S(1)}, f32[2,3,208,128]{3,2,1,0:T(8,128)S(1)}, u32[]{:S(2)}, u32[]{:S(2)}) collective-permute-start(f32[2,3,208,128]{3,2,1,0:T(8,128)S(1)} %get-tuple-element.167.sn), channel_id=1, source_target_pairs={{0,63},{1,2},{2,1},{3,4},{4,3},{5,6},{6,5},{7,8},{8,7},{9,10},{10,... | collective-permute-start | bytes 1916936 | tf_op jit(solution)/shard_map/ppermute | solution.py:661
  260.1 12.9 %collective-permute-start.20 = (f32[2,3,208,128]{3,2,1,0:T(8,128)S(1)}, f32[2,3,208,128]{3,2,1,0:T(8,128)S(1)}, u32[]{:S(2)}, u32[]{:S(2)}) collective-permute-start(f32[2,3,208,128]{3,2,1,0:T(8,128)S(1)} %get-tuple-element.171.ss), channel_id=1, source_target_pairs={{0,1},{1,0},{2,3},{3,2},{4,5},{5,4},{6,7},{7,6},{8,9},{9,8},{10,11... | collective-permute-start | bytes 1916936 | tf_op jit(solution)/shard_map/ppermute | solution.py:661
  260.2 18.4 %collective-permute-start.21 = (f32[2,3,208,128]{3,2,1,0:T(8,128)S(1)}, f32[2,3,208,128]{3,2,1,0:T(8,128)S(1)}, u32[]{:S(2)}, u32[]{:S(2)}) collective-permute-start(f32[2,3,208,128]{3,2,1,0:T(8,128)S(1)} %get-tuple-element.172.sn), channel_id=1, source_target_pairs={{0,63},{1,2},{2,1},{3,4},{4,3},{5,6},{6,5},{7,8},{8,7},{9,10},{10,... | collective-permute-start | bytes 1916936 | tf_op jit(solution)/shard_map/ppermute | solution.py:661
  281.2 6.4 %collective-permute-start.22 = (f32[3,16,16,128]{3,2,1,0:T(8,128)S(1)}, f32[3,16,16,128]{3,2,1,0:T(8,128)S(1)}, u32[]{:S(2)}, u32[]{:S(2)}) collective-permute-start(f32[3,16,16,128]{3,2,1,0:T(8,128)S(1)} %get-tuple-element.177), channel_id=1, source_target_pairs={{0,64},{64,0},{1,65},{65,1},{2,66},{66,2},{3,67},{67,3},{4,68},{68... | collective-permute-start | bytes 1179656 | tf_op jit(solution)/shard_map/ppermute | solution.py:658
  286.5 1.2 collective-permute-start.23
  289.4 20.5 %collective-permute-start.24 = (f32[2,3,208,128]{3,2,1,0:T(8,128)S(1)}, f32[2,3,208,128]{3,2,1,0:T(8,128)S(1)}, u32[]{:S(2)}, u32[]{:S(2)}) collective-permute-start(f32[2,3,208,128]{3,2,1,0:T(8,128)S(1)} %get-tuple-element.184.refs_2_), channel_id=1, source_target_pairs={{0,1},{1,0},{2,3},{3,2},{4,5},{5,4},{6,7},{7,6},{8,9},{9,8},{10,11... | collective-permute-start | bytes 1916936 | tf_op jit(solution)/shard_map/ppermute | solution.py:661
  289.5 21.3 %collective-permute-start.25 = (f32[2,3,208,128]{3,2,1,0:T(8,128)S(1)}, f32[2,3,208,128]{3,2,1,0:T(8,128)S(1)}, u32[]{:S(2)}, u32[]{:S(2)}) collective-permute-start(f32[2,3,208,128]{3,2,1,0:T(8,128)S(1)} %get-tuple-element.185.refs_3_), channel_id=1, source_target_pairs={{0,63},{1,2},{2,1},{3,4},{4,3},{5,6},{6,5},{7,8},{8,7},{9,10},{10,... | collective-permute-start | bytes 1916936 | tf_op jit(solution)/shard_map/ppermute | solution.py:661
  291.7 11.7 %collective-permute-start.26 = (f32[1,128]{1,0:T(1,128)S(1)}, f32[1,128]{1,0:T(1,128)S(1)}, u32[]{:S(2)}, u32[]{:S(2)}) collective-permute-start(f32[1,128]{1,0:T(1,128)S(1)} %get-tuple-element.188.a), channel_id=1, source_target_pairs={{0,1},{1,2},{2,3},{3,0},{4,5},{5,6},{6,7},{7,4},{8,9},{9,10},{10,1... | collective-permute-start | bytes 1544 | tf_op jit(solution)/shard_map/ppermute | solution.py:671
  291.7 11.7 %collective-permute-start.27 = (f32[1,128]{1,0:T(1,128)S(1)}, f32[1,128]{1,0:T(1,128)S(1)}, u32[]{:S(2)}, u32[]{:S(2)}) collective-permute-start(f32[1,128]{1,0:T(1,128)S(1)} %get-tuple-element.188.a), channel_id=1, source_target_pairs={{0,2},{1,3},{2,0},{3,1},{4,6},{5,7},{6,4},{7,5},{8,10},{9,11},{10,... | collective-permute-start | bytes 1544 | tf_op jit(solution)/shard_map/ppermute | solution.py:671
  292.8 12.5 %collective-permute-start.28 = (f32[1,128]{1,0:T(1,128)S(1)}, f32[1,128]{1,0:T(1,128)S(1)}, u32[]{:S(2)}, u32[]{:S(2)}) collective-permute-start(f32[1,128]{1,0:T(1,128)S(1)} %get-tuple-element.188.a), channel_id=1, source_target_pairs={{0,3},{1,0},{2,1},{3,2},{4,7},{5,4},{6,5},{7,6},{8,11},{9,8},{10,9... | collective-permute-start | bytes 1544 | tf_op jit(solution)/shard_map/ppermute | solution.py:671
  305.3 4.0 %collective-permute-start.29 = (f32[1,128]{1,0:T(1,128)S(1)}, f32[1,128]{1,0:T(1,128)S(1)}, u32[]{:S(2)}, u32[]{:S(2)}) collective-permute-start(f32[1,128]{1,0:T(1,128)S(1)} %shard_map.110.a), channel_id=1, source_target_pairs={{0,4},{1,5},{2,6},{3,7},{4,8},{5,9},{6,10},{7,11},{8,12},{9,13},{1... | collective-permute-start | bytes 1544 | tf_op jit(solution)/shard_map/ppermute | solution.py:671
  305.4 4.3 %collective-permute-start.30 = (f32[1,128]{1,0:T(1,128)S(1)}, f32[1,128]{1,0:T(1,128)S(1)}, u32[]{:S(2)}, u32[]{:S(2)}) collective-permute-start(f32[1,128]{1,0:T(1,128)S(1)} %shard_map.110.a), channel_id=1, source_target_pairs={{0,8},{1,9},{2,10},{3,11},{4,12},{5,13},{6,14},{7,15},{8,0},{9,1},... | collective-permute-start | bytes 1544 | tf_op jit(solution)/shard_map/ppermute | solution.py:671
  305.5 4.4 %collective-permute-start.31 = (f32[1,128]{1,0:T(1,128)S(1)}, f32[1,128]{1,0:T(1,128)S(1)}, u32[]{:S(2)}, u32[]{:S(2)}) collective-permute-start(f32[1,128]{1,0:T(1,128)S(1)} %shard_map.110.a), channel_id=1, source_target_pairs={{0,12},{1,13},{2,14},{3,15},{4,0},{5,1},{6,2},{7,3},{8,4},{9,5},{1... | collective-permute-start | bytes 1544 | tf_op jit(solution)/shard_map/ppermute | solution.py:671
  313.9 14.6 %collective-permute-start.35 = (f32[2,3,208,128]{3,2,1,0:T(8,128)S(1)}, f32[2,3,208,128]{3,2,1,0:T(8,128)S(1)}, u32[]{:S(2)}, u32[]{:S(2)}) collective-permute-start(f32[2,3,208,128]{3,2,1,0:T(8,128)S(1)} %get-tuple-element.191.refs_2_), channel_id=1, source_target_pairs={{0,1},{1,0},{2,3},{3,2},{4,5},{5,4},{6,7},{7,6},{8,9},{9,8},{10,11... | collective-permute-start | bytes 1916936 | tf_op jit(solution)/shard_map/ppermute | solution.py:661
  314.0 18.4 %collective-permute-start.36 = (f32[2,3,208,128]{3,2,1,0:T(8,128)S(1)}, f32[2,3,208,128]{3,2,1,0:T(8,128)S(1)}, u32[]{:S(2)}, u32[]{:S(2)}) collective-permute-start(f32[2,3,208,128]{3,2,1,0:T(8,128)S(1)} %get-tuple-element.192.refs_3_), channel_id=1, source_target_pairs={{0,63},{1,2},{2,1},{3,4},{4,3},{5,6},{6,5},{7,8},{8,7},{9,10},{10,... | collective-permute-start | bytes 1916936 | tf_op jit(solution)/shard_map/ppermute | solution.py:661
  316.8 28.4 %collective-permute-start.37 = (f32[2,3,3,192,128]{4,3,2,1,0:T(8,128)S(1)}, f32[2,3,3,192,128]{4,3,2,1,0:T(8,128)S(1)}, u32[]{:S(2)}, u32[]{:S(2)}) collective-permute-start(f32[2,3,3,192,128]{4,3,2,1,0:T(8,128)S(1)} %shard_map.116), channel_id=1, source_target_pairs={{0,64},{64,0},{1,65},{65,1},{2,66},{66,2},{3,67},{67,3},{4,68},{68... | collective-permute-start | bytes 5308424 | tf_op jit(solution)/shard_map/ppermute | solution.py:658
  320.4 24.9 %collective-permute-start.38 = (f32[2,3,3,192,128]{4,3,2,1,0:T(8,128)S(1)}, f32[2,3,3,192,128]{4,3,2,1,0:T(8,128)S(1)}, u32[]{:S(2)}, u32[]{:S(2)}) collective-permute-start(f32[2,3,3,192,128]{4,3,2,1,0:T(8,128)S(1)} %shard_map.117), channel_id=1, source_target_pairs={{0,64},{64,0},{1,65},{65,1},{2,66},{66,2},{3,67},{67,3},{4,68},{68... | collective-permute-start | bytes 5308424 | tf_op jit(solution)/shard_map/ppermute | solution.py:658
  334.6 10.7 %collective-permute-start.39 = (f32[2,3,3,192,128]{4,3,2,1,0:T(8,128)S(1)}, f32[2,3,3,192,128]{4,3,2,1,0:T(8,128)S(1)}, u32[]{:S(2)}, u32[]{:S(2)}) collective-permute-start(f32[2,3,3,192,128]{4,3,2,1,0:T(8,128)S(1)} %shard_map.118), channel_id=1, source_target_pairs={{0,64},{64,0},{1,65},{65,1},{2,66},{66,2},{3,67},{67,3},{4,68},{68... | collective-permute-start | bytes 5308424 | tf_op jit(solution)/shard_map/ppermute | solution.py:658
  338.6 3.6 %collective-permute-start.32 = (f32[1,128]{1,0:T(1,128)S(1)}, f32[1,128]{1,0:T(1,128)S(1)}, u32[]{:S(2)}, u32[]{:S(2)}) collective-permute-start(f32[1,128]{1,0:T(1,128)S(1)} %get-tuple-element.189.a), channel_id=1, source_target_pairs={{0,16},{1,17},{2,18},{3,19},{4,20},{5,21},{6,22},{7,23},{8,24},{9,... | collective-permute-start | bytes 1544 | tf_op jit(solution)/shard_map/ppermute | solution.py:671
  338.6 3.9 %collective-permute-start.33 = (f32[1,128]{1,0:T(1,128)S(1)}, f32[1,128]{1,0:T(1,128)S(1)}, u32[]{:S(2)}, u32[]{:S(2)}) collective-permute-start(f32[1,128]{1,0:T(1,128)S(1)} %get-tuple-element.189.a), channel_id=1, source_target_pairs={{0,32},{1,33},{2,34},{3,35},{4,36},{5,37},{6,38},{7,39},{8,40},{9,... | collective-permute-start | bytes 1544 | tf_op jit(solution)/shard_map/ppermute | solution.py:671
  342.2 2.4 collective-permute-start.34
  (1 other events, 1.0 us)

commit v5 on v4

--- a/solution.py
+++ b/solution.py
@@ -91,62 +91,62 @@
     return c0 * u + ap * later(u) + am * earlier(u)
 
 
-def adj_pre(f, rows, w_ref, rhs, mid_ref, out):
+def adj_pre(f, rows, w_ref, ends, next_ref, rhs, mid_ref, pp_ref, out):
     w = [mixed(x, rhs) for x in rows]
     c = [coef(w_ref, i) for i in range(3)]
+    low = adj_local(w[0], c[0]) + c[1][2] * w[1]
+    high = adj_local(w[2], c[2]) + c[1][3] * w[1]
     mid_ref[f] = adj_local(w[1], c[1]) + c[2][2] * w[2] + c[0][3] * w[0]
-    out.put(
-        0,
-        f,
-        adj_local(w[0], c[0]) + c[1][2] * w[1],
-        adj_local(w[2], c[2]) + c[1][3] * w[1],
-    )
+    pp_ref[0, f] = low
+    pp_ref[1, f] = high
+    south = jnp.maximum(next_ref[1, 0], 0.0) * mixed(low + ends[0], rhs)
+    north = jnp.maximum(-next_ref[1, 2], 0.0) * mixed(high + ends[1], rhs)
+    out.put(0, f, south, north)
     out.put(1, f, c[0][2] * w[0], c[2][3] * w[2])
 
 
-def adj_post(f, mid_ref, own, got, fs, fn):
+def adj_post(f, mid_ref, pp_ref, got, fs, fn):
     return [
-        (got.south(0, f) + own.south(1, f)) * fs,
-        own.south(0, f) + got.south(1, f) * fs,
+        pp_ref[0, f] + got.south(1, f) * fs,
         mid_ref[f],
-        own.north(0, f) + got.north(1, f) * fn,
-        (got.north(0, f) + own.north(1, f)) * fn,
+        pp_ref[1, f] + got.north(1, f) * fn,
     ]
 
 
-def adj_second(rows5, w_ref, wh_ref, rhs):
-    w = [mixed(x, rhs) for x in rows5]
+def adj_second(f, rows, w_ref, wh_ref, rhs, own, got, fs, fn):
+    w = [mixed(x, rhs) for x in rows]
     c = [coef(w_ref, i) for i in range(3)]
-    up = [c[1][2], c[2][2], wh_ref[1]]
-    down = [wh_ref[0], c[0][3], c[1][3]]
+    below = got.south(0, f) * fs + wh_ref[0] * mixed(own.south(1, f), rhs)
+    above = got.north(0, f) * fn + wh_ref[1] * mixed(own.north(1, f), rhs)
     return [
-        adj_local(w[i + 1], c[i]) + up[i] * w[i + 2] + down[i] * w[i] for i in range(3)
+        adj_local(w[0], c[0]) + c[1][2] * w[1] + below,
+        adj_local(w[1], c[1]) + c[2][2] * w[2] + c[0][3] * w[0],
+        adj_local(w[2], c[2]) + c[1][3] * w[1] + above,
     ]
 
 
-def fwd_pre(f, u, w_ref, mid_ref, out):
+def fwd_pre(f, u, w_ref, ends, rhs, mid_ref, pp_ref, out):
     c = [coef(w_ref, i) for i in range(3)]
+    low = fwd_local(u[0], c[0]) + c[0][3] * u[1]
+    high = fwd_local(u[2], c[2]) + c[2][2] * u[1]
     mid_ref[f] = fwd_local(u[1], c[1]) + c[1][2] * u[0] + c[1][3] * u[2]
+    pp_ref[0, f] = low
+    pp_ref[1, f] = high
     out.put(0, f, u[0], u[2])
-    out.put(
-        1,
-        f,
-        fwd_local(u[0], c[0]) + c[0][3] * u[1],
-        fwd_local(u[2], c[2]) + c[2][2] * u[1],
-    )
-
-
-def fwd_post(f, mid_ref, own, got, w_ref, wh_ref, fs, fn, rhs):
+    out.put(1, f, mixed(low, rhs) + ends[0], mixed(high, rhs) + ends[1])
+
+
+def fwd_post(f, mid_ref, pp_ref, own, got, w_ref, wh_ref, fs, fn, rhs):
     b0 = w_ref[1, 0]
     b2 = w_ref[1, 2]
     m = [
-        got.south(1, f) * fs + wh_ref[0] * own.south(0, f),
-        own.south(1, f) + jnp.maximum(b0, 0.0) * (got.south(0, f) * fs),
+        pp_ref[0, f] + jnp.maximum(b0, 0.0) * (got.south(0, f) * fs),
         mid_ref[f],
-        own.north(1, f) + jnp.maximum(-b2, 0.0) * (got.north(0, f) * fn),
-        got.north(1, f) * fn + wh_ref[1] * own.north(0, f),
+        pp_ref[1, f] + jnp.maximum(-b2, 0.0) * (got.north(0, f) * fn),
     ]
-    return [mixed(x, rhs) for x in m]
+    below = (got.south(1, f) + mixed(wh_ref[0] * own.south(0, f), rhs)) * fs
+    above = (got.north(1, f) + mixed(wh_ref[1] * own.north(0, f), rhs)) * fn
+    return [mixed(x, rhs) for x in m], below, above
 
 
 def fwd_second(u5, w_ref, rhs):
@@ -302,101 +302,82 @@
         sn[k] = jnp.maximum(-w[1, 2], 0.0)
 
 
-def turn_first_body(fl, g3_ref, g2_ref, w3_ref, ra_ref, mid_ref, ss_ref, sn_ref):
-    rhs = ra_ref[...]
-    out = Sides(fl[2], ss_ref, sn_ref)
+def turn_first_body(fl, g3, g2, w3, w2, ra, mid, pp, ss, sn):
+    rhs = ra[...]
+    out = Sides(fl[2], ss, sn)
 
     def one(f):
-        adj_pre(f, [g3_ref[f, i] for i in range(3)], w3_ref, rhs, mid_ref, out)
-        out.put(2, f, g2_ref[f, 0], g2_ref[f, 2])
-
-    fields(g3_ref.shape[0], one)
-
-
-def five(f, f_ref, got, ext):
-    if ext:
-        return [got.south(2, f)] + [f_ref[f, i] for i in range(3)] + [got.north(2, f)]
-    return [f_ref[f, i] for i in range(5)]
-
-
-def adj_mid_body(ext, carry, *refs):
+        rows = [g3[f, i] for i in range(3)]
+        adj_pre(f, rows, w3, (g2[f, 0], g2[f, 2]), w2, rhs, mid, pp, out)
+
+    fields(g3.shape[0], one)
+
+
+def adj_mid_body(carry, *refs):
     if carry:
-        refs[-1][...] = refs[12][...]
-        refs = refs[:12] + refs[13:-1]
-    (fl, mid, ss, sn, rs, rn, f2, f1, w2, wh2, w1, ra) = refs[:12]
-    n = 12
-    if ext:
-        g0 = refs[n]
-        n += 1
-    g3, g2, mid_o, ss_o, sn_o = refs[n:]
+        refs[-1][...] = refs[15][...]
+        refs = refs[:15] + refs[16:-1]
+    (fl, mid, pp, ss, sn, rs, rn, f2, f1, f0, w2, wh2, w1, w0, ra) = refs[:15]
+    g3, g2, mid_o, pp_o, ss_o, sn_o = refs[15:]
     fs, fn = fl[0], fl[1]
     rhs = ra[...]
     own, got, out_o = Sides(fl[2], ss, sn), Sides(fl[2], rs, rn), Sides(fl[2], ss_o, sn_o)
 
     def one(f):
-        lam = adj_post(f, mid, own, got, fs, fn)
-        for i in range(5):
+        lam = adj_post(f, mid, pp, got, fs, fn)
+        for i in range(3):
             g3[f, i] = lam[i] * SCALE_Q
-        src = five(f, f2, got, ext)
-        out = adj_second([lam[i] + src[i] for i in range(5)], w2, wh2, rhs)
+        rows = [lam[i] + f2[f, i] for i in range(3)]
+        out = adj_second(f, rows, w2, wh2, rhs, own, got, fs, fn)
         for i in range(3):
             g2[f, i] = out[i] * SCALE_Q
-        adj_pre(f, [out[i] + f1[f, i] for i in range(3)], w1, rhs, mid_o, out_o)
-        if ext:
-            out_o.put(2, f, g0[f, 0], g0[f, 2])
+        rows = [out[i] + f1[f, i] for i in range(3)]
+        adj_pre(f, rows, w1, (f0[f, 0], f0[f, 2]), w0, rhs, mid_o, pp_o, out_o)
 
     fields(mid.shape[0], one)
 
 
-def adj_last_body(mode, *refs):
-    (fl, mid, ss, sn, rs, rn, f0, w0, wh0, ra) = refs[:10]
-    n = 10
-    if mode == 0:
-        d2 = refs[n]
-        n += 1
-    outs = refs[n:]
+def adj_last_body(more, *refs):
+    (fl, mid, pp, ss, sn, rs, rn, f0, w0, wh0, ra, rf) = refs[:12]
+    outs = refs[12:]
     fs, fn = fl[0], fl[1]
     rhs = ra[...]
     own, got = Sides(fl[2], ss, sn), Sides(fl[2], rs, rn)
-    if mode < 2:
-        out_o = Sides(fl[2], outs[3], outs[4])
+    if more:
+        out_o = Sides(fl[2], outs[4], outs[5])
 
     def one(f):
-        lam = adj_post(f, mid, own, got, fs, fn)
-        src = five(f, f0, got, mode == 0)
-        out = adj_second([lam[i] + src[i] for i in range(5)], w0, wh0, rhs)
-        for i in range(5):
+        lam = adj_post(f, mid, pp, got, fs, fn)
+        rows = [lam[i] + f0[f, i] for i in range(3)]
+        out = adj_second(f, rows, w0, wh0, rhs, own, got, fs, fn)
+        for i in range(3):
             outs[1][f, i] = lam[i] * SCALE_Q
-        for i in range(3):
             outs[0][f, i] = out[i]
-        if mode < 2:
-            fwd_pre(f, out, w0, outs[2], out_o)
-        if mode == 0:
-            out_o.put(2, f, d2[f, 0], d2[f, 2])
+        if more:
+            half = SCALE_Q * SCALE_Q
+            ends = (half * lam[0], half * lam[2])
+            fwd_pre(f, out, w0, ends, rf[...], outs[2], outs[3], out_o)
 
     fields(mid.shape[0], one)
 
 
-def fwd_first_body(ride, fl, mid, ss, sn, rs, rn, v1, v2, w0, wh0, w1, w2, rf, *outs):
-    if ride:
-        d0, outs, halo = outs[0], outs[1:6], outs[6]
-    x0, x1, mid_o, ss_o, sn_o = outs
+def fwd_first_body(fl, mid, pp, ss, sn, rs, rn, v1, v2, v3, w0, wh0, w1, w2, rf, *outs):
+    x0, x1, mid_o, pp_o, ss_o, sn_o = outs
     fs, fn = fl[0], fl[1]
     rhs = rf[...]
     own, got, out_o = Sides(fl[2], ss, sn), Sides(fl[2], rs, rn), Sides(fl[2], ss_o, sn_o)
 
     def one(f):
-        x5 = fwd_post(f, mid, own, got, w0, wh0, fs, fn, rhs)
-        for i in range(5):
-            x0[f, i] = x5[i]
-        x3 = fwd_second([x5[i] + SCALE_Q * v1[f, i] for i in range(5)], w1, rhs)
+        x, below, above = fwd_post(f, mid, pp, own, got, w0, wh0, fs, fn, rhs)
         for i in range(3):
-            x1[f, i] = x3[i]
-        fwd_pre(f, [x3[i] + SCALE_Q * v2[f, i] for i in range(3)], w2, mid_o, out_o)
-        if ride:
-            out_o.put(2, f, d0[f, 0], d0[f, 2])
-            halo[0, f] = got.south(2, f)
-            halo[1, f] = got.north(2, f)
+            x0[f, i] = x[i]
+        u = [x[i] + SCALE_Q * v1[f, i] for i in range(3)]
+        x = fwd_second([below] + u + [above], w1, rhs)
+        for i in range(3):
+            x1[f, i] = x[i]
+        u = [x[i] + SCALE_Q * v2[f, i] for i in range(3)]
+        ends = (SCALE_Q * v3[f, 0], SCALE_Q * v3[f, 2])
+        fwd_pre(f, u, w2, ends, rhs, mid_o, pp_o, out_o)
 
     fields(mid.shape[0], one)
 
@@ -405,26 +386,23 @@
     return jnp.concatenate([x[half : half + PAD], x[PAD : 2 * PAD]], axis=0)
 
 
-def fwd_last_body(half, fl, mid, ss, sn, rs, rn, v3, x0, x1, w2, wh2, w3, rf, *outs):
-    x2, x3, eg = outs[:3]
+def fwd_last_body(half, fl, mid, pp, ss, sn, rs, rn, v3, x0, x1, w2, wh2, w3, rf, *outs):
+    x2, x3, eg = outs
     fs, fn = fl[0], fl[1]
     rhs = rf[...]
     own, got = Sides(fl[2], ss, sn), Sides(fl[2], rs, rn)
 
     def one(f):
-        x5 = fwd_post(f, mid, own, got, w2, wh2, fs, fn, rhs)
-        for i in range(5):
-            x2[f, i] = x5[i]
-            eg[f, 8 + i] = edge(x5[i], half)
+        x, below, above = fwd_post(f, mid, pp, own, got, w2, wh2, fs, fn, rhs)
+        u = [x[i] + SCALE_Q * v3[f, i] for i in range(3)]
+        y = fwd_second([below] + u + [above], w3, rhs)
+        for i in range(3):
+            x2[f, i] = x[i]
+            x3[f, i] = y[i]
             eg[f, i] = edge(x0[f, i], half)
-        y3 = fwd_second([x5[i] + SCALE_Q * v3[f, i] for i in range(5)], w3, rhs)
-        for i in range(3):
-            x3[f, i] = y3[i]
-            eg[f, 13 + i] = edge(y3[i], half)
-            eg[f, 5 + i] = edge(x1[f, i], half)
-        if len(outs) > 3:
-            outs[3][0, f] = got.south(2, f)
-            outs[3][1, f] = got.north(2, f)
+            eg[f, 3 + i] = edge(x1[f, i], half)
+            eg[f, 6 + i] = edge(x[i], half)
+            eg[f, 9 + i] = edge(y[i], half)
 
     fields(mid.shape[0], one)
 
@@ -433,12 +411,12 @@
     return jnp.concatenate([e[:PAD], x[PAD:-PAD], e[PAD:]], axis=0)
 
 
-def turn_body(carry, fl, sc, x3, eg, d3, w3, ra, *outs):
+def turn_body(carry, fl, sc, x3, x2, eg, d3, d2, w3, w2, ra, *outs):
     if carry:
-        outs[4][...] = outs[0][...]
-        outs = outs[1:4]
-    mid, ss, sn = outs[:3]
-    q = None if carry else outs[3]
+        outs[5][...] = outs[0][...]
+        outs = outs[1:5]
+    mid, pp, ss, sn = outs[:4]
+    q = None if carry else outs[4]
     out = Sides(fl[2], ss, sn)
     rhs = ra[...]
     if q is not None:
@@ -448,37 +426,29 @@
     def one(f):
         rows = []
         for i in range(3):
-            y = fixed(x3[f, i], eg[f, 13 + i])
+            y = fixed(x3[f, i], eg[f, 9 + i])
             t = d3[f, i] * y
             if q is not None:
                 q[...] += fold(t * y)
             rows.append(t * scale)
-        adj_pre(f, rows, w3, rhs, mid, out)
+        ends = [d2[f, i] * fixed(x2[f, i], eg[f, 6 + i]) * scale for i in (0, 2)]
+        adj_pre(f, rows, w3, ends, w2, rhs, mid, pp, out)
 
     fields(x3.shape[0], one)
 
 
-def rest_body(sc, x0, x1, x2, eg, d0, d1, d2, h0, h2, f0, f1, f2, q=None):
+def rest_body(sc, x0, x1, x2, eg, d0, d1, d2, f0, f1, f2, q=None):
     if q is not None:
         q[...] = jnp.zeros_like(q)
     scale = sc[0]
 
     def one(f):
-        for x, rows, at, d, h, f_o in (
-            (x0, 5, 0, d0, h0, f0),
-            (x1, 3, 5, d1, None, f1),
-            (x2, 5, 8, d2, h2, f2),
-        ):
-            for i in range(rows):
+        for x, at, d, f_o in ((x0, 0, d0, f0), (x1, 3, d1, f1), (x2, 6, d2, f2)):
+            for i in range(3):
                 y = fixed(x[f, i], eg[f, at + i])
-                if rows == 5 and i == 0:
-                    t = h[0, f] * y
-                elif rows == 5 and i == 4:
-                    t = h[1, f] * y
-                else:
-                    t = d[f, i - (rows == 5)] * y
-                    if q is not None:
-                        q[...] += fold(t * y)
+                t = d[f, i] * y
+                if q is not None:
+                    q[...] += fold(t * y)
                 f_o[f, i] = t * scale
 
     fields(x0.shape[0], one)
@@ -488,9 +458,9 @@
     q[...] = jnp.zeros_like(q)
 
     def one(f):
-        for v, off in ((v0, 0), (v1, 1), (v2, 0), (v3, 1)):
+        for v in (v0, v1, v2, v3):
             for i in range(3):
-                x = v[f, i + off]
+                x = v[f, i]
                 q[...] += fold(x * x)
 
     fields(v0.shape[0], one)
@@ -511,9 +481,8 @@
 
         def one(f, acc):
             for x, d in zip(xs, ds):
-                off = (x.shape[1] - 3) // 2
                 for i in range(3):
-                    v = x[f, i + off]
+                    v = x[f, i]
                     acc = acc + fold(d[f, i] * v * v)
             return acc
 
@@ -582,10 +551,9 @@
 
     def put(first):
         for k in (first, first + 1):
-            off = k % 2
             for f in range(out.shape[1]):
                 for i in range(3):
-                    out[k % 2, f, i] = v[k][f, i + off][PAD:-PAD]
+                    out[k % 2, f, i] = v[k][f, i][PAD:-PAD]
 
     @pl.when(c_ref[0] == 0)
     def _():
@@ -611,10 +579,10 @@
     def put(first, mine, theirs):
         copies = []
         for k in (first, first + 1):
-            n, off = k % 2, k % 2
+            n = k % 2
             for f in range(nf):
                 for i in range(3):
-                    x = [v[k][f, i + off][PAD:-PAD] for v in (g, z, w)]
+                    x = [v[k][f, i][PAD:-PAD] for v in (g, z, w)]
                     y = [v[n, f, i] for v in (og, oz, ow)]
                     for (a, b, d), lo in ((x, mine), (y, theirs)):
                         ib[n, f, i, lo : lo + half] = ig * a + iz * b
@@ -758,93 +726,79 @@
     def row3(nf):
         return sds(nf, 3, wide, lev)
 
-    def row5(nf):
-        return sds(nf, 5, wide, lev)
-
     def state_of(nf, n):
-        return [sds(nf, wide, lev)] + [sds(n, nf, wide, lev)] * 2
-
-    def adj_mid(state, f2, f1, g0=None, row=None):
-        mid, ss, sn = state
+        return [sds(nf, wide, lev)] + [sds(n, nf, wide, lev)] * 3
+
+    def adj_mid(state, f2, f1, f0, row=None):
+        mid, pp, ss, sn = state
         nf = mid.shape[0]
         rs, rn = exchange(ss, sn)
-        ext = g0 is not None
         carry = row is not None
-        n = 3 if ext else 2
-        ins = (flags, mid, ss, sn, rs, rn, f2, f1, w2, wh2, w1, ra) + ((g0,) if ext else ())
+        ins = (flags, mid, pp, ss, sn, rs, rn, f2, f1, f0, w2, wh2, w1, w0, ra)
         ins += (row,) if carry else ()
         o = call(
-            functools.partial(adj_mid_body, ext, carry),
+            functools.partial(adj_mid_body, carry),
             ins,
             [SM] + [VM] * (len(ins) - 1),
-            [row5(nf), row3(nf)] + state_of(nf, n) + ([sds(1, lev)] if carry else []),
+            [row3(nf)] * 2 + state_of(nf, 2) + ([sds(1, lev)] if carry else []),
         )
         if carry:
-            return o[0], o[1], tuple(o[2:5]), o[5]
+            return o[0], o[1], tuple(o[2:6]), o[6]
         return o[0], o[1], tuple(o[2:])
 
-    def adj_last(mode, state, f0, ride=()):
-        mid, ss, sn = state
+    def adj_last(state, f0, more):
+        mid, pp, ss, sn = state
         nf = mid.shape[0]
         rs, rn = exchange(ss, sn)
-        ins = (flags, mid, ss, sn, rs, rn, f0, w0, wh0, ra) + tuple(ride)
-        specs = [SM] + [VM] * (len(ins) - 1)
-        outs = [row3(nf), row5(nf)]
-        outs += state_of(nf, 3 if mode == 0 else 2) if mode < 2 else []
-        o = call(functools.partial(adj_last_body, mode), ins, specs, outs)
+        ins = (flags, mid, pp, ss, sn, rs, rn, f0, w0, wh0, ra, rf)
+        outs = [row3(nf)] * 2 + (state_of(nf, 2) if more else [])
+        o = call(
+            functools.partial(adj_last_body, more), ins, [SM] + [VM] * (len(ins) - 1), outs
+        )
         return o[0], o[1], tuple(o[2:])
 
-    def fwd_first(state, v1, v2, ride=()):
-        mid, ss, sn = state
+    def forward(state, v):
+        mid, pp, ss, sn = state
         nf = mid.shape[0]
         rs, rn = exchange(ss, sn)
-        ins = (flags, mid, ss, sn, rs, rn, v1, v2, w0, wh0, w1, w2, rf) + ride
+        ins = (flags, mid, pp, ss, sn, rs, rn, v[1], v[2], v[3], w0, wh0, w1, w2, rf)
         o = call(
-            functools.partial(fwd_first_body, len(ride) > 0),
+            fwd_first_body,
             ins,
             [SM] + [VM] * (len(ins) - 1),
-            [row5(nf), row3(nf)]
-            + state_of(nf, 3 if ride else 2)
-            + ([sds(2, nf, wide, lev)] if ride else []),
+            [row3(nf)] * 2 + state_of(nf, 2),
         )
-        return o[0], o[1], tuple(o[2:5]), o[5:]
-
-    def fwd_last(state, v3, x0, x1, ride):
-        mid, ss, sn = state
-        nf = mid.shape[0]
+        x0, x1, mid, pp, ss, sn = o
         rs, rn = exchange(ss, sn)
-        ins = (flags, mid, ss, sn, rs, rn, v3, x0, x1, w2, wh2, w3, rf)
-        return call(
+        ins = (flags, mid, pp, ss, sn, rs, rn, v[3], x0, x1, w2, wh2, w3, rf)
+        o = call(
             functools.partial(fwd_last_body, half),
             ins,
-            [SM] + [VM] * 12,
-            [row5(nf), row3(nf), sds(nf, 16, 2 * PAD, lev)]
-            + ([sds(2, nf, wide, lev)] if ride else []),
+            [SM] + [VM] * (len(ins) - 1),
+            [row3(nf)] * 2 + [sds(nf, 12, 2 * PAD, lev)],
         )
-
-    def turn(xs, eg, dd, halo, scale, row=None):
+        return (x0, x1, o[0], o[1]), o[2]
+
+    def turn(xs, eg, dd, scale, row=None):
         eg = swap(eg)
         x0, x1, x2, x3 = xs
         nf = x3.shape[0]
         carry = row is not None
+        ins = (flags, scale, x3, x2, eg, dd[3], dd[2], w3, w2, ra)
+        ins += (row,) if carry else ()
         o = call(
             functools.partial(turn_body, carry),
-            (flags, scale, x3, eg, dd[3], w3, ra) + ((row,) if carry else ()),
-            [SM] * 2 + [VM] * (6 if carry else 5),
+            ins,
+            [SM] * 2 + [VM] * (len(ins) - 2),
             state_of(nf, 2) + [sds(1, lev) if carry else part],
         )
         r = call(
             rest_body,
-            (scale, x0, x1, x2, eg, dd[0], dd[1], dd[2]) + halo,
-            [SM] + [VM] * 9,
-            [row5(nf), row3(nf), row5(nf)] + ([] if carry else [part]),
+            (scale, x0, x1, x2, eg, dd[0], dd[1], dd[2]),
+            [SM] + [VM] * 7,
+            [row3(nf)] * 3 + ([] if carry else [part]),
         )
-        return tuple(o[:3]), tuple(r[:3]), (o[3] if carry else (o[3], r[3]))
-
-    def forward(state, v, ride=()):
-        x0, x1, state, halo2 = fwd_first(state, v[1], v[2], ride)
-        o = fwd_last(state, v[3], x0, x1, len(ride) > 0)
-        return (x0, x1) + tuple(o[:2]), o[2], tuple(o[3:]) + tuple(halo2)
+        return tuple(o[:4]), tuple(r[:3]), (o[4] if carry else (o[4], r[3]))
 
     def norm(v):
         return call(norm_body, tuple(v), [VM] * 4, [part])[0]
@@ -854,21 +808,21 @@
         state = tuple(
             call(
                 turn_first_body,
-                (flags, gg[3], gg[2], w3, ra),
-                [SM] + [VM] * 4,
-                state_of(nf, 3),
+                (flags, gg[3], gg[2], w3, w2, ra),
+                [SM] + [VM] * 5,
+                state_of(nf, 2),
             )
         )
         g3, g2, state = adj_mid(state, gg[2], gg[1], gg[0])
-        g0, g1, state = adj_last(0, state, gg[0], (dd[2],))
+        g0, g1, state = adj_last(state, gg[0], True)
         g = (g0, g1, g2, g3)
-        xs, eg, halo = forward(state, g, (dd[0],))
-        state, fs, bg = turn(xs, eg, dd, halo, sig_arr)
-        z3, z2, state = adj_mid(state, fs[2], fs[1])
-        z0, z1, state = adj_last(1, state, fs[0])
+        xs, eg = forward(state, g)
+        state, fs, bg = turn(xs, eg, dd, sig_arr)
+        z3, z2, state = adj_mid(state, fs[2], fs[1], fs[0])
+        z0, z1, state = adj_last(state, fs[0], True)
         z = (z0, z1, z2, z3)
-        xs, eg, _ = forward(state, z)
-        chains.append((g, z, xs, eg, norm(g), bg, norm(z), halo))
+        xs, eg = forward(state, z)
+        chains.append((g, z, xs, eg, norm(g), bg, norm(z)))
     ins = [ch[4] for ch in chains] + [q for ch in chains for q in ch[5]]
     ins += [ch[6] for ch in chains]
     for ch, (_, _, dd) in zip(chains, groups):
@@ -879,19 +833,19 @@
     row = call(add_body, (row, swap(row)), [VM] * 2, [sds(1, lev)], flops=1e5)[0]
     states = []
     for ch, (nf, gg, dd) in zip(chains, groups):
-        state, fs, row = turn(ch[2], ch[3], dd, ch[7], one_arr, row)
+        state, fs, row = turn(ch[2], ch[3], dd, one_arr, row)
         states.append((state, fs))
     row = ring_sum(ring_sum(row, 1), 4)
     mids = []
     for state, fs in states:
-        w3z, w2z, state, row = adj_mid(state, fs[2], fs[1], None, row)
+        w3z, w2z, state, row = adj_mid(state, fs[2], fs[1], fs[0], row)
         mids.append((w3z, w2z, state, fs))
     row = ring_sum(row, 16)
     weights = call(solve_body, (span, row), [SM, VM], [sds(1, lev)], flops=1e5)[0]
 
     g, z = chains[0][0], chains[0][1]
     w3z, w2z, state, fs = mids[0]
-    w0z, w1z, _ = adj_last(2, state, fs[0])
+    w0z, w1z, _ = adj_last(state, fs[0], False)
     w = (w0z, w1z, w2z, w3z)
     shape = sds(2, FIELDS, 3, half, lev)
 

time: 350 us -> 327 us (0.934)
  waiting for transfers between devices: 218 us -> 192 us
  Pallas kernels: 50.4 us -> 54.4 us
    ppermute x11, waiting for transfers between devices: 84.5 us -> 66.2 us  [exchange(): lax.ppermute(b, 'space', second_pairs)]
    ppermute x11, waiting for transfers between devices: 110 us -> 102 us  [exchange(): lax.ppermute(a, 'space', first_pairs)]
    pallas_call x34, Pallas kernels: 50.4 us -> 54.4 us  [call(): pl.pallas_call(body, out_shape=outs, in_specs=specs, out_specs=out_specs...]
  transfers between devices with their start and end apart: 41 -> 41, of which waited for: 30 -> 31; matrix products, arithmetic and copies ran while one was open for 1% -> 1% of each run, Pallas kernels for 3% -> 5%
where the time goes in v5:
time: 327 us; the launch traced here: 326 us
  waiting for transfers between devices  192 us (59%)
  starting transfers between devices  65.7 us (20%)
  Pallas kernels  54.4 us (17%)
  local copies, waits for them, and re-layouts  7.2 us (2%)
  other arithmetic  4.12 us (1%)
    ppermute x11, waiting for transfers between devices, exchange(): lax.ppermute(a, 'space', first_pairs)  102 us
    ppermute x11, waiting for transfers between devices, exchange(): lax.ppermute(b, 'space', second_pairs)  66.2 us
    pallas_call x34, Pallas kernels, call(): pl.pallas_call(body, out_shape=outs, in_specs=specs, out_specs=out_specs...  54.4 us
    ppermute x11, starting transfers between devices, exchange(): lax.ppermute(b, 'space', second_pairs)  27.4 us
    ppermute x9, starting transfers between devices, swap(): return lax.ppermute(x, 'tm', [(0, 1), (1, 0)])  19.6 us
    ppermute x9, waiting for transfers between devices, ring_sum(): got = tuple((lax.ppermute(row, 'space', p) for p in shifts))  17.8 us
    all_to_all x1, starting transfers between devices, per_device(): lax.all_to_all(packed, 'space', split_axis=0, concat_axis=0, tiled=True)  11.4 us
    unnamed x16, local copies, waits for them, and re-layouts  6.96 us
  transfers between devices with their start and end apart: 41, of which 31 were waited for; matrix products, arithmetic and copies ran while one was open for 1% of the time, Pallas kernels for 5%

profile of v5, /device:TPU:1, one launch (start us, length us, event | category | flops | bytes accessed | tf_op | source)
XLA Modules:
  0.0 325.7 jit_solution(11330973145132190695)
XLA Ops:
  8.2 11.4 %all-to-all-start = ((f32[64,7,8,128]{3,2,1,0:T(8,128)}), f32[64,7,8,128]{3,2,1,0:T(8,128)}, u32[]{:S(2)}, u32[]{:S(2)}) async-start(f32[64,7,8,128]{3,2,1,0:T(8,128)} %get-tuple-element.108), calls=%async_computation | async-start | bytes 3670016 | tf_op jit(solution)/shard_map/all_to_all | solution.py:665
  24.4 6.7 %collective-permute-start.1 = (f32[2,208,128]{2,1,0:T(8,128)}, f32[2,208,128]{2,1,0:T(8,128)S(1)}, u32[]{:S(2)}, u32[]{:S(2)}) collective-permute-start(f32[2,208,128]{2,1,0:T(8,128)} %get-tuple-element.218), channel_id=1, source_target_pairs={{0,63},{1,2},{2,1},{3,4},{4,3},{5,6},{6,5},{7,8},{8,7},{9,10},{10,... | collective-permute-start | bytes 638984 | tf_op jit(solution)/shard_map/ppermute | solution.py:629
  33.7 17.2 %collective-permute-done.1 = f32[2,208,128]{2,1,0:T(8,128)S(1)} collective-permute-done((f32[2,208,128]{2,1,0:T(8,128)}, f32[2,208,128]{2,1,0:T(8,128)S(1)}, u32[]{:S(2)}, u32[]{:S(2)}) %collective-permute-start.1) | collective-permute-done | bytes 213024 | tf_op jit(solution)/shard_map/ppermute | solution.py:629
  52.0 6.0 %shard_map.89 = (f32[18432,128]{1,0:T(8,128)S(1)}, f32[2,3,3,208,128]{4,3,2,1,0:T(8,128)S(1)}, f32[2,3,3,208,128]{4,3,2,1,0:T(8,128)S(1)}) custom-call(s32[1]{0:T(128)} %bitcast.c_ref, f32[3584,128]{1,0:T(8,128)} %bitcast.5.p_ref), custom_call_target="tpu_custom_call" | custom-call | flops 100000000 | bytes 15106052 | tf_op jit(solution)/shard_map/pallas_call | solution.py:24
  59.1 3.5 %collective-permute-done.3.got_ref = f32[2,3,3,208,128]{4,3,2,1,0:T(8,128)S(1)} collective-permute-done((f32[2,3,3,208,128]{4,3,2,1,0:T(8,128)S(1)}, f32[2,3,3,208,128]{4,3,2,1,0:T(8,128)S(1)}, u32[]{:S(2)}, u32[]{:S(2)}) %collective-permute-start.3) | collective-permute-done | bytes 1916960 | tf_op jit(solution)/shard_map/ppermute | solution.py:626
  62.8 2.2 shard_map.91
  65.1 2.0 collective-permute-start.5
  67.2 13.5 %collective-permute-done.4.refs_5_ = f32[2,3,208,128]{3,2,1,0:T(8,128)S(1)} collective-permute-done((f32[2,3,208,128]{3,2,1,0:T(8,128)S(1)}, f32[2,3,208,128]{3,2,1,0:T(8,128)S(1)}, u32[]{:S(2)}, u32[]{:S(2)}) %collective-permute-start.4) | collective-permute-done | bytes 639008 | tf_op jit(solution)/shard_map/ppermute | solution.py:629
  80.7 5.5 %collective-permute-done.5.refs_6_ = f32[2,3,208,128]{3,2,1,0:T(8,128)S(1)} collective-permute-done((f32[2,3,208,128]{3,2,1,0:T(8,128)S(1)}, f32[2,3,208,128]{3,2,1,0:T(8,128)S(1)}, u32[]{:S(2)}, u32[]{:S(2)}) %collective-permute-start.5) | collective-permute-done | bytes 639008 | tf_op jit(solution)/shard_map/ppermute | solution.py:629
  86.2 3.6 %shard_map.92 = (f32[3,3,208,128]{3,2,1,0:T(8,128)S(1)}, f32[3,3,208,128]{3,2,1,0:T(8,128)S(1)}, f32[3,208,128]{2,1,0:T(8,128)S(1)}, f32[2,3,208,128]{3,2,1,0:T(...) custom-call(f32[3]{0:T(128)S(1)} %add_convert_fusion.fl.refs_0_, ...), custom_call_target="tpu_custom_call" | custom-call | flops 100000000 | bytes 12804108 | tf_op jit(solution)/shard_map/pallas_call | solution.py:24
  89.9 2.0 collective-permute-start.7
  94.6 10.0 %collective-permute-done.6.refs_5_ = f32[2,3,208,128]{3,2,1,0:T(8,128)S(1)} collective-permute-done((f32[2,3,208,128]{3,2,1,0:T(8,128)S(1)}, f32[2,3,208,128]{3,2,1,0:T(8,128)S(1)}, u32[]{:S(2)}, u32[]{:S(2)}) %collective-permute-start.6) | collective-permute-done | bytes 639008 | tf_op jit(solution)/shard_map/ppermute | solution.py:629
  104.6 5.5 %collective-permute-done.7.refs_6_ = f32[2,3,208,128]{3,2,1,0:T(8,128)S(1)} collective-permute-done((f32[2,3,208,128]{3,2,1,0:T(8,128)S(1)}, f32[2,3,208,128]{3,2,1,0:T(8,128)S(1)}, u32[]{:S(2)}, u32[]{:S(2)}) %collective-permute-start.7) | collective-permute-done | bytes 639008 | tf_op jit(solution)/shard_map/ppermute | solution.py:629
  110.1 3.1 shard_map.93
  115.4 11.7 %collective-permute-done.8.rs = f32[2,3,208,128]{3,2,1,0:T(8,128)S(1)} collective-permute-done((f32[2,3,208,128]{3,2,1,0:T(8,128)S(1)}, f32[2,3,208,128]{3,2,1,0:T(8,128)S(1)}, u32[]{:S(2)}, u32[]{:S(2)}) %collective-permute-start.8) | collective-permute-done | bytes 639008 | tf_op jit(solution)/shard_map/ppermute | solution.py:629
  127.1 5.5 %collective-permute-done.9.rn = f32[2,3,208,128]{3,2,1,0:T(8,128)S(1)} collective-permute-done((f32[2,3,208,128]{3,2,1,0:T(8,128)S(1)}, f32[2,3,208,128]{3,2,1,0:T(8,128)S(1)}, u32[]{:S(2)}, u32[]{:S(2)}) %collective-permute-start.9) | collective-permute-done | bytes 639008 | tf_op jit(solution)/shard_map/ppermute | solution.py:629
  132.6 3.5 %shard_map.94 = (f32[3,3,208,128]{3,2,1,0:T(8,128)S(1)}, f32[3,3,208,128]{3,2,1,0:T(8,128)S(1)}, f32[3,208,128]{2,1,0:T(8,128)S(1)}, f32[2,3,208,128]{3,2,1,0:T(...) custom-call(f32[3]{0:T(128)S(1)} %add_convert_fusion.fl.refs_0_, ...), custom_call_target="tpu_custom_call" | custom-call | flops 100000000 | bytes 12804108 | tf_op jit(solution)/shard_map/pallas_call | solution.py:24
  138.2 10.8 %collective-permute-done.10.rs = f32[2,3,208,128]{3,2,1,0:T(8,128)S(1)} collective-permute-done((f32[2,3,208,128]{3,2,1,0:T(8,128)S(1)}, f32[2,3,208,128]{3,2,1,0:T(8,128)S(1)}, u32[]{:S(2)}, u32[]{:S(2)}) %collective-permute-start.10) | collective-permute-done | bytes 639008 | tf_op jit(solution)/shard_map/ppermute | solution.py:629
  149.0 5.5 %collective-permute-done.11.rn = f32[2,3,208,128]{3,2,1,0:T(8,128)S(1)} collective-permute-done((f32[2,3,208,128]{3,2,1,0:T(8,128)S(1)}, f32[2,3,208,128]{3,2,1,0:T(8,128)S(1)}, u32[]{:S(2)}, u32[]{:S(2)}) %collective-permute-start.11) | collective-permute-done | bytes 639008 | tf_op jit(solution)/shard_map/ppermute | solution.py:629
  154.5 2.7 shard_map.95
  157.3 4.1 %collective-permute-start.12 = (f32[3,12,16,128]{3,2,1,0:T(8,128)S(1)}, f32[3,12,16,128]{3,2,1,0:T(8,128)S(1)}, u32[]{:S(2)}, u32[]{:S(2)}) collective-permute-start(f32[3,12,16,128]{3,2,1,0:T(8,128)S(1)} %get-tuple-element.158), channel_id=1, source_target_pairs={{0,64},{64,0},{1,65},{65,1},{2,66},{66,2},{3,67},{67,3},{4,68},{68... | collective-permute-start | bytes 884744 | tf_op jit(solution)/shard_map/ppermute | solution.py:626
  162.5 2.3 shard_map.98
  167.6 12.9 %collective-permute-done.14.refs_5_ = f32[2,3,208,128]{3,2,1,0:T(8,128)S(1)} collective-permute-done((f32[2,3,208,128]{3,2,1,0:T(8,128)S(1)}, f32[2,3,208,128]{3,2,1,0:T(8,128)S(1)}, u32[]{:S(2)}, u32[]{:S(2)}) %collective-permute-start.14) | collective-permute-done | bytes 639008 | tf_op jit(solution)/shard_map/ppermute | solution.py:629
  180.5 5.5 %collective-permute-done.15.refs_6_ = f32[2,3,208,128]{3,2,1,0:T(8,128)S(1)} collective-permute-done((f32[2,3,208,128]{3,2,1,0:T(8,128)S(1)}, f32[2,3,208,128]{3,2,1,0:T(8,128)S(1)}, u32[]{:S(2)}, u32[]{:S(2)}) %collective-permute-start.15) | collective-permute-done | bytes 639008 | tf_op jit(solution)/shard_map/ppermute | solution.py:629
  186.0 3.6 %shard_map.100 = (f32[3,3,208,128]{3,2,1,0:T(8,128)S(1)}, f32[3,3,208,128]{3,2,1,0:T(8,128)S(1)}, f32[3,208,128]{2,1,0:T(8,128)S(1)}, f32[2,3,208,128]{3,2,1,0:T...) custom-call(f32[3]{0:T(128)S(1)} %add_convert_fusion.fl.refs_0_, ...), custom_call_target="tpu_custom_call" | custom-call | flops 100000000 | bytes 12804108 | tf_op jit(solution)/shard_map/pallas_call | solution.py:24
  191.7 12.6 %collective-permute-done.16.refs_5_ = f32[2,3,208,128]{3,2,1,0:T(8,128)S(1)} collective-permute-done((f32[2,3,208,128]{3,2,1,0:T(8,128)S(1)}, f32[2,3,208,128]{3,2,1,0:T(8,128)S(1)}, u32[]{:S(2)}, u32[]{:S(2)}) %collective-permute-start.16) | collective-permute-done | bytes 639008 | tf_op jit(solution)/shard_map/ppermute | solution.py:629
  204.4 5.5 %collective-permute-done.17.refs_6_ = f32[2,3,208,128]{3,2,1,0:T(8,128)S(1)} collective-permute-done((f32[2,3,208,128]{3,2,1,0:T(8,128)S(1)}, f32[2,3,208,128]{3,2,1,0:T(8,128)S(1)}, u32[]{:S(2)}, u32[]{:S(2)}) %collective-permute-start.17) | collective-permute-done | bytes 639008 | tf_op jit(solution)/shard_map/ppermute | solution.py:629
  209.9 3.1 shard_map.101
  215.1 11.7 %collective-permute-done.18.rs = f32[2,3,208,128]{3,2,1,0:T(8,128)S(1)} collective-permute-done((f32[2,3,208,128]{3,2,1,0:T(8,128)S(1)}, f32[2,3,208,128]{3,2,1,0:T(8,128)S(1)}, u32[]{:S(2)}, u32[]{:S(2)}) %collective-permute-start.18) | collective-permute-done | bytes 639008 | tf_op jit(solution)/shard_map/ppermute | solution.py:629
  226.9 5.5 %collective-permute-done.19.rn = f32[2,3,208,128]{3,2,1,0:T(8,128)S(1)} collective-permute-done((f32[2,3,208,128]{3,2,1,0:T(8,128)S(1)}, f32[2,3,208,128]{3,2,1,0:T(8,128)S(1)}, u32[]{:S(2)}, u32[]{:S(2)}) %collective-permute-start.19) | collective-permute-done | bytes 639008 | tf_op jit(solution)/shard_map/ppermute | solution.py:629
  232.4 3.5 %shard_map.102 = (f32[3,3,208,128]{3,2,1,0:T(8,128)S(1)}, f32[3,3,208,128]{3,2,1,0:T(8,128)S(1)}, f32[3,208,128]{2,1,0:T(8,128)S(1)}, f32[2,3,208,128]{3,2,1,0:T...) custom-call(f32[3]{0:T(128)S(1)} %add_convert_fusion.fl.refs_0_, ...), custom_call_target="tpu_custom_call" | custom-call | flops 100000000 | bytes 12804108 | tf_op jit(solution)/shard_map/pallas_call | solution.py:24
  238.0 10.8 %collective-permute-done.20.rs = f32[2,3,208,128]{3,2,1,0:T(8,128)S(1)} collective-permute-done((f32[2,3,208,128]{3,2,1,0:T(8,128)S(1)}, f32[2,3,208,128]{3,2,1,0:T(8,128)S(1)}, u32[]{:S(2)}, u32[]{:S(2)}) %collective-permute-start.20) | collective-permute-done | bytes 639008 | tf_op jit(solution)/shard_map/ppermute | solution.py:629
  248.8 5.5 %collective-permute-done.21.rn = f32[2,3,208,128]{3,2,1,0:T(8,128)S(1)} collective-permute-done((f32[2,3,208,128]{3,2,1,0:T(8,128)S(1)}, f32[2,3,208,128]{3,2,1,0:T(8,128)S(1)}, u32[]{:S(2)}, u32[]{:S(2)}) %collective-permute-start.21) | collective-permute-done | bytes 639008 | tf_op jit(solution)/shard_map/ppermute | solution.py:629
  254.3 2.7 shard_map.103
  257.0 4.0 %collective-permute-start.22 = (f32[3,12,16,128]{3,2,1,0:T(8,128)S(1)}, f32[3,12,16,128]{3,2,1,0:T(8,128)S(1)}, u32[]{:S(2)}, u32[]{:S(2)}) collective-permute-start(f32[3,12,16,128]{3,2,1,0:T(8,128)S(1)} %get-tuple-element.192), channel_id=1, source_target_pairs={{0,64},{64,0},{1,65},{65,1},{2,66},{66,2},{3,67},{67,3},{4,68},{68... | collective-permute-start | bytes 884744 | tf_op jit(solution)/shard_map/ppermute | solution.py:626
  263.5 2.3 shard_map.108
  269.1 2.1 collective-permute-start.28
  271.2 8.6 %collective-permute-done.26.b = f32[1,128]{1,0:T(1,128)S(1)} collective-permute-done((f32[1,128]{1,0:T(1,128)S(1)}, f32[1,128]{1,0:T(1,128)S(1)}, u32[]{:S(2)}, u32[]{:S(2)}) %collective-permute-start.26) | collective-permute-done | bytes 544 | tf_op jit(solution)/shard_map/ppermute | solution.py:639
  281.8 2.6 collective-permute-start.31
  287.2 3.6 %shard_map.112 = (f32[3,3,208,128]{3,2,1,0:T(8,128)S(1)}, f32[3,3,208,128]{3,2,1,0:T(8,128)S(1)}, f32[3,208,128]{2,1,0:T(8,128)S(1)}, f32[2,3,208,128]{3,2,1,0:T...) custom-call(f32[3]{0:T(128)S(1)} %add_convert_fusion.fl.refs_0_, ...), custom_call_target="tpu_custom_call" | custom-call | flops 100000000 | bytes 12805132 | tf_op jit(solution)/shard_map/pallas_call | solution.py:24
  291.1 2.5 collective-permute-start.36
  293.7 3.5 %collective-permute-start.37 = (f32[2,3,3,192,128]{4,3,2,1,0:T(8,128)S(1)}, f32[2,3,3,192,128]{4,3,2,1,0:T(8,128)S(1)}, u32[]{:S(2)}, u32[]{:S(2)}) collective-permute-start(f32[2,3,3,192,128]{4,3,2,1,0:T(8,128)S(1)} %shard_map.116), channel_id=1, source_target_pairs={{0,64},{64,0},{1,65},{65,1},{2,66},{66,2},{3,67},{67,3},{4,68},{68... | collective-permute-start | bytes 5308424 | tf_op jit(solution)/shard_map/ppermute | solution.py:626
  297.4 8.2 %collective-permute-done.35.refs_5_ = f32[2,3,208,128]{3,2,1,0:T(8,128)S(1)} collective-permute-done((f32[2,3,208,128]{3,2,1,0:T(8,128)S(1)}, f32[2,3,208,128]{3,2,1,0:T(8,128)S(1)}, u32[]{:S(2)}, u32[]{:S(2)}) %collective-permute-start.35) | collective-permute-done | bytes 639008 | tf_op jit(solution)/shard_map/ppermute | solution.py:629
  305.6 3.9 %collective-permute-done.36.refs_6_ = f32[2,3,208,128]{3,2,1,0:T(8,128)S(1)} collective-permute-done((f32[2,3,208,128]{3,2,1,0:T(8,128)S(1)}, f32[2,3,208,128]{3,2,1,0:T(8,128)S(1)}, u32[]{:S(2)}, u32[]{:S(2)}) %collective-permute-start.36) | collective-permute-done | bytes 639008 | tf_op jit(solution)/shard_map/ppermute | solution.py:629
  311.6 4.0 %collective-permute-start.39 = (f32[2,3,3,192,128]{4,3,2,1,0:T(8,128)S(1)}, f32[2,3,3,192,128]{4,3,2,1,0:T(8,128)S(1)}, u32[]{:S(2)}, u32[]{:S(2)}) collective-permute-start(f32[2,3,3,192,128]{4,3,2,1,0:T(8,128)S(1)} %shard_map.118), channel_id=1, source_target_pairs={{0,64},{64,0},{1,65},{65,1},{2,66},{66,2},{3,67},{67,3},{4,68},{68... | collective-permute-start | bytes 5308424 | tf_op jit(solution)/shard_map/ppermute | solution.py:626
  315.7 3.5 %collective-permute-done.32.b = f32[1,128]{1,0:T(1,128)S(1)} collective-permute-done((f32[1,128]{1,0:T(1,128)S(1)}, f32[1,128]{1,0:T(1,128)S(1)}, u32[]{:S(2)}, u32[]{:S(2)}) %collective-permute-start.32) | collective-permute-done | bytes 544 | tf_op jit(solution)/shard_map/ppermute | solution.py:639
  319.5 2.1 collective-permute-done.34.d
  322.3 3.2 shard_map.119
  (97 shorter events, 47.6 us)
Async XLA Ops:
  0.6 4.7 %copy-start.4 = (bf16[2,1,2,3,384,128]{5,4,3,2,1,0:T(8,128)(2,1)S(1)}, bf16[2,1,2,3,384,128]{5,4,3,2,1,0:T(8,128)(2,1)}, u32[]{:S(2)}) copy-start(bf16[2,1,2,3,384,128]{5,4,3,2,1,0:T(8,128)(2,1)} %param.7) | copy-start | bytes 3538948
  1.7 1.1 copy-start.5
  2.8 1.1 copy-start.6
  3.9 1.4 copy-start.7
  5.7 1.0 copy-start
  6.8 12.9 %collective-permute-start = (f32[2,2,3,208,128]{4,3,2,1,0:T(8,128)S(1)}, f32[2,2,3,208,128]{4,3,2,1,0:T(8,128)S(1)}, u32[]{:S(2)}, u32[]{:S(2)}) collective-permute-start(f32[2,2,3,208,128]{4,3,2,1,0:T(8,128)S(1)} %get-tuple-element.111), channel_id=1, source_target_pairs={{0,64},{64,0},{1,65},{65,1},{2,66},{66,2},{3,67},{67,3},{4,68},{68... | collective-permute-start | bytes 3833864 | tf_op jit(solution)/shard_map/ppermute | solution.py:626
  8.2 43.8 %all-to-all-start = ((f32[64,7,8,128]{3,2,1,0:T(8,128)}), f32[64,7,8,128]{3,2,1,0:T(8,128)}, u32[]{:S(2)}, u32[]{:S(2)}) async-start(f32[64,7,8,128]{3,2,1,0:T(8,128)} %get-tuple-element.108), calls=%async_computation | async-start | bytes 3670016 | tf_op jit(solution)/shard_map/all_to_all | solution.py:665
  20.7 1.3 copy-start.1
  22.0 1.3 copy-start.3
  24.4 26.6 %collective-permute-start.1 = (f32[2,208,128]{2,1,0:T(8,128)}, f32[2,208,128]{2,1,0:T(8,128)S(1)}, u32[]{:S(2)}, u32[]{:S(2)}) collective-permute-start(f32[2,208,128]{2,1,0:T(8,128)} %get-tuple-element.218), channel_id=1, source_target_pairs={{0,63},{1,2},{2,1},{3,4},{4,3},{5,6},{6,5},{7,8},{8,7},{9,10},{10,... | collective-permute-start | bytes 638984 | tf_op jit(solution)/shard_map/ppermute | solution.py:629
  31.0 19.9 %collective-permute-start.2 = (f32[2,208,128]{2,1,0:T(8,128)}, f32[2,208,128]{2,1,0:T(8,128)}, u32[]{:S(2)}, u32[]{:S(2)}) collective-permute-start(f32[2,208,128]{2,1,0:T(8,128)} %get-tuple-element.219), channel_id=1, source_target_pairs={{0,1},{1,0},{2,3},{3,2},{4,5},{5,4},{6,7},{7,6},{8,9},{9,8},{10,11... | collective-permute-start | bytes 638984 | tf_op jit(solution)/shard_map/ppermute | solution.py:629
  58.0 4.6 %collective-permute-start.3 = (f32[2,3,3,208,128]{4,3,2,1,0:T(8,128)S(1)}, f32[2,3,3,208,128]{4,3,2,1,0:T(8,128)S(1)}, u32[]{:S(2)}, u32[]{:S(2)}) collective-permute-start(f32[2,3,3,208,128]{4,3,2,1,0:T(8,128)S(1)} %get-tuple-element.122), channel_id=1, source_target_pairs={{0,64},{64,0},{1,65},{65,1},{2,66},{66,2},{3,67},{67,3},{4,68},{68... | collective-permute-start | bytes 5750792 | tf_op jit(solution)/shard_map/ppermute | solution.py:626
  65.0 15.7 %collective-permute-start.4 = (f32[2,3,208,128]{3,2,1,0:T(8,128)S(1)}, f32[2,3,208,128]{3,2,1,0:T(8,128)S(1)}, u32[]{:S(2)}, u32[]{:S(2)}) collective-permute-start(f32[2,3,208,128]{3,2,1,0:T(8,128)S(1)} %get-tuple-element.130.refs_3_), channel_id=1, source_target_pairs={{0,1},{1,0},{2,3},{3,2},{4,5},{5,4},{6,7},{7,6},{8,9},{9,8},{10,11... | collective-permute-start | bytes 1916936 | tf_op jit(solution)/shard_map/ppermute | solution.py:629
  65.1 21.1 %collective-permute-start.5 = (f32[2,3,208,128]{3,2,1,0:T(8,128)S(1)}, f32[2,3,208,128]{3,2,1,0:T(8,128)S(1)}, u32[]{:S(2)}, u32[]{:S(2)}) collective-permute-start(f32[2,3,208,128]{3,2,1,0:T(8,128)S(1)} %get-tuple-element.131.refs_4_), channel_id=1, source_target_pairs={{0,63},{1,2},{2,1},{3,4},{4,3},{5,6},{6,5},{7,8},{8,7},{9,10},{10,... | collective-permute-start | bytes 1916936 | tf_op jit(solution)/shard_map/ppermute | solution.py:629
  89.8 14.7 %collective-permute-start.6 = (f32[2,3,208,128]{3,2,1,0:T(8,128)S(1)}, f32[2,3,208,128]{3,2,1,0:T(8,128)S(1)}, u32[]{:S(2)}, u32[]{:S(2)}) collective-permute-start(f32[2,3,208,128]{3,2,1,0:T(8,128)S(1)} %get-tuple-element.139.refs_3_), channel_id=1, source_target_pairs={{0,1},{1,0},{2,3},{3,2},{4,5},{5,4},{6,7},{7,6},{8,9},{9,8},{10,11... | collective-permute-start | bytes 1916936 | tf_op jit(solution)/shard_map/ppermute | solution.py:629
  89.9 20.2 %collective-permute-start.7 = (f32[2,3,208,128]{3,2,1,0:T(8,128)S(1)}, f32[2,3,208,128]{3,2,1,0:T(8,128)S(1)}, u32[]{:S(2)}, u32[]{:S(2)}) collective-permute-start(f32[2,3,208,128]{3,2,1,0:T(8,128)S(1)} %get-tuple-element.140.refs_4_), channel_id=1, source_target_pairs={{0,63},{1,2},{2,1},{3,4},{4,3},{5,6},{6,5},{7,8},{8,7},{9,10},{10,... | collective-permute-start | bytes 1916936 | tf_op jit(solution)/shard_map/ppermute | solution.py:629
  93.2 68.1 %collective-permute-start.13 = (f32[2,3,3,208,128]{4,3,2,1,0:T(8,128)S(1)}, f32[2,3,3,208,128]{4,3,2,1,0:T(8,128)S(1)}, u32[]{:S(2)}, u32[]{:S(2)}) collective-permute-start(f32[2,3,3,208,128]{4,3,2,1,0:T(8,128)S(1)} %get-tuple-element.161), channel_id=1, source_target_pairs={{0,64},{64,0},{1,65},{65,1},{2,66},{66,2},{3,67},{67,3},{4,68},{68... | collective-permute-start | bytes 5750792 | tf_op jit(solution)/shard_map/ppermute | solution.py:626
  113.2 13.8 %collective-permute-start.8 = (f32[2,3,208,128]{3,2,1,0:T(8,128)S(1)}, f32[2,3,208,128]{3,2,1,0:T(8,128)S(1)}, u32[]{:S(2)}, u32[]{:S(2)}) collective-permute-start(f32[2,3,208,128]{3,2,1,0:T(8,128)S(1)} %get-tuple-element.145.ss), channel_id=1, source_target_pairs={{0,1},{1,0},{2,3},{3,2},{4,5},{5,4},{6,7},{7,6},{8,9},{9,8},{10,11... | collective-permute-start | bytes 1916936 | tf_op jit(solution)/shard_map/ppermute | solution.py:629
  113.3 19.3 %collective-permute-start.9 = (f32[2,3,208,128]{3,2,1,0:T(8,128)S(1)}, f32[2,3,208,128]{3,2,1,0:T(8,128)S(1)}, u32[]{:S(2)}, u32[]{:S(2)}) collective-permute-start(f32[2,3,208,128]{3,2,1,0:T(8,128)S(1)} %get-tuple-element.146.sn), channel_id=1, source_target_pairs={{0,63},{1,2},{2,1},{3,4},{4,3},{5,6},{6,5},{7,8},{8,7},{9,10},{10,... | collective-permute-start | bytes 1916936 | tf_op jit(solution)/shard_map/ppermute | solution.py:629
  136.1 12.9 %collective-permute-start.10 = (f32[2,3,208,128]{3,2,1,0:T(8,128)S(1)}, f32[2,3,208,128]{3,2,1,0:T(8,128)S(1)}, u32[]{:S(2)}, u32[]{:S(2)}) collective-permute-start(f32[2,3,208,128]{3,2,1,0:T(8,128)S(1)} %get-tuple-element.152.ss), channel_id=1, source_target_pairs={{0,1},{1,0},{2,3},{3,2},{4,5},{5,4},{6,7},{7,6},{8,9},{9,8},{10,11... | collective-permute-start | bytes 1916936 | tf_op jit(solution)/shard_map/ppermute | solution.py:629
  136.2 18.3 %collective-permute-start.11 = (f32[2,3,208,128]{3,2,1,0:T(8,128)S(1)}, f32[2,3,208,128]{3,2,1,0:T(8,128)S(1)}, u32[]{:S(2)}, u32[]{:S(2)}) collective-permute-start(f32[2,3,208,128]{3,2,1,0:T(8,128)S(1)} %get-tuple-element.153.sn), channel_id=1, source_target_pairs={{0,63},{1,2},{2,1},{3,4},{4,3},{5,6},{6,5},{7,8},{8,7},{9,10},{10,... | collective-permute-start | bytes 1916936 | tf_op jit(solution)/shard_map/ppermute | solution.py:629
  157.3 5.3 %collective-permute-start.12 = (f32[3,12,16,128]{3,2,1,0:T(8,128)S(1)}, f32[3,12,16,128]{3,2,1,0:T(8,128)S(1)}, u32[]{:S(2)}, u32[]{:S(2)}) collective-permute-start(f32[3,12,16,128]{3,2,1,0:T(8,128)S(1)} %get-tuple-element.158), channel_id=1, source_target_pairs={{0,64},{64,0},{1,65},{65,1},{2,66},{66,2},{3,67},{67,3},{4,68},{68... | collective-permute-start | bytes 884744 | tf_op jit(solution)/shard_map/ppermute | solution.py:626
  164.8 15.7 %collective-permute-start.14 = (f32[2,3,208,128]{3,2,1,0:T(8,128)S(1)}, f32[2,3,208,128]{3,2,1,0:T(8,128)S(1)}, u32[]{:S(2)}, u32[]{:S(2)}) collective-permute-start(f32[2,3,208,128]{3,2,1,0:T(8,128)S(1)} %get-tuple-element.166.refs_3_), channel_id=1, source_target_pairs={{0,1},{1,0},{2,3},{3,2},{4,5},{5,4},{6,7},{7,6},{8,9},{9,8},{10,11... | collective-permute-start | bytes 1916936 | tf_op jit(solution)/shard_map/ppermute | solution.py:629
  164.9 21.1 %collective-permute-start.15 = (f32[2,3,208,128]{3,2,1,0:T(8,128)S(1)}, f32[2,3,208,128]{3,2,1,0:T(8,128)S(1)}, u32[]{:S(2)}, u32[]{:S(2)}) collective-permute-start(f32[2,3,208,128]{3,2,1,0:T(8,128)S(1)} %get-tuple-element.167.refs_4_), channel_id=1, source_target_pairs={{0,63},{1,2},{2,1},{3,4},{4,3},{5,6},{6,5},{7,8},{8,7},{9,10},{10,... | collective-permute-start | bytes 1916936 | tf_op jit(solution)/shard_map/ppermute | solution.py:629
  189.6 14.8 %collective-permute-start.16 = (f32[2,3,208,128]{3,2,1,0:T(8,128)S(1)}, f32[2,3,208,128]{3,2,1,0:T(8,128)S(1)}, u32[]{:S(2)}, u32[]{:S(2)}) collective-permute-start(f32[2,3,208,128]{3,2,1,0:T(8,128)S(1)} %get-tuple-element.175.refs_3_), channel_id=1, source_target_pairs={{0,1},{1,0},{2,3},{3,2},{4,5},{5,4},{6,7},{7,6},{8,9},{9,8},{10,11... | collective-permute-start | bytes 1916936 | tf_op jit(solution)/shard_map/ppermute | solution.py:629
  189.7 20.2 %collective-permute-start.17 = (f32[2,3,208,128]{3,2,1,0:T(8,128)S(1)}, f32[2,3,208,128]{3,2,1,0:T(8,128)S(1)}, u32[]{:S(2)}, u32[]{:S(2)}) collective-permute-start(f32[2,3,208,128]{3,2,1,0:T(8,128)S(1)} %get-tuple-element.176.refs_4_), channel_id=1, source_target_pairs={{0,63},{1,2},{2,1},{3,4},{4,3},{5,6},{6,5},{7,8},{8,7},{9,10},{10,... | collective-permute-start | bytes 1916936 | tf_op jit(solution)/shard_map/ppermute | solution.py:629
  213.0 13.8 %collective-permute-start.18 = (f32[2,3,208,128]{3,2,1,0:T(8,128)S(1)}, f32[2,3,208,128]{3,2,1,0:T(8,128)S(1)}, u32[]{:S(2)}, u32[]{:S(2)}) collective-permute-start(f32[2,3,208,128]{3,2,1,0:T(8,128)S(1)} %get-tuple-element.179.ss), channel_id=1, source_target_pairs={{0,1},{1,0},{2,3},{3,2},{4,5},{5,4},{6,7},{7,6},{8,9},{9,8},{10,11... | collective-permute-start | bytes 1916936 | tf_op jit(solution)/shard_map/ppermute | solution.py:629
  213.1 19.3 %collective-permute-start.19 = (f32[2,3,208,128]{3,2,1,0:T(8,128)S(1)}, f32[2,3,208,128]{3,2,1,0:T(8,128)S(1)}, u32[]{:S(2)}, u32[]{:S(2)}) collective-permute-start(f32[2,3,208,128]{3,2,1,0:T(8,128)S(1)} %get-tuple-element.180.sn), channel_id=1, source_target_pairs={{0,63},{1,2},{2,1},{3,4},{4,3},{5,6},{6,5},{7,8},{8,7},{9,10},{10,... | collective-permute-start | bytes 1916936 | tf_op jit(solution)/shard_map/ppermute | solution.py:629
  235.9 12.9 %collective-permute-start.20 = (f32[2,3,208,128]{3,2,1,0:T(8,128)S(1)}, f32[2,3,208,128]{3,2,1,0:T(8,128)S(1)}, u32[]{:S(2)}, u32[]{:S(2)}) collective-permute-start(f32[2,3,208,128]{3,2,1,0:T(8,128)S(1)} %get-tuple-element.186.ss), channel_id=1, source_target_pairs={{0,1},{1,0},{2,3},{3,2},{4,5},{5,4},{6,7},{7,6},{8,9},{9,8},{10,11... | collective-permute-start | bytes 1916936 | tf_op jit(solution)/shard_map/ppermute | solution.py:629
  236.0 18.3 %collective-permute-start.21 = (f32[2,3,208,128]{3,2,1,0:T(8,128)S(1)}, f32[2,3,208,128]{3,2,1,0:T(8,128)S(1)}, u32[]{:S(2)}, u32[]{:S(2)}) collective-permute-start(f32[2,3,208,128]{3,2,1,0:T(8,128)S(1)} %get-tuple-element.187.sn), channel_id=1, source_target_pairs={{0,63},{1,2},{2,1},{3,4},{4,3},{5,6},{6,5},{7,8},{8,7},{9,10},{10,... | collective-permute-start | bytes 1916936 | tf_op jit(solution)/shard_map/ppermute | solution.py:629
  257.0 6.5 %collective-permute-start.22 = (f32[3,12,16,128]{3,2,1,0:T(8,128)S(1)}, f32[3,12,16,128]{3,2,1,0:T(8,128)S(1)}, u32[]{:S(2)}, u32[]{:S(2)}) collective-permute-start(f32[3,12,16,128]{3,2,1,0:T(8,128)S(1)} %get-tuple-element.192), channel_id=1, source_target_pairs={{0,64},{64,0},{1,65},{65,1},{2,66},{66,2},{3,67},{67,3},{4,68},{68... | collective-permute-start | bytes 884744 | tf_op jit(solution)/shard_map/ppermute | solution.py:626
  262.3 1.2 collective-permute-start.23
  265.8 20.5 %collective-permute-start.24 = (f32[2,3,208,128]{3,2,1,0:T(8,128)S(1)}, f32[2,3,208,128]{3,2,1,0:T(8,128)S(1)}, u32[]{:S(2)}, u32[]{:S(2)}) collective-permute-start(f32[2,3,208,128]{3,2,1,0:T(8,128)S(1)} %get-tuple-element.199.refs_3_), channel_id=1, source_target_pairs={{0,1},{1,0},{2,3},{3,2},{4,5},{5,4},{6,7},{7,6},{8,9},{9,8},{10,11... | collective-permute-start | bytes 1916936 | tf_op jit(solution)/shard_map/ppermute | solution.py:629
  265.9 21.3 %collective-permute-start.25 = (f32[2,3,208,128]{3,2,1,0:T(8,128)S(1)}, f32[2,3,208,128]{3,2,1,0:T(8,128)S(1)}, u32[]{:S(2)}, u32[]{:S(2)}) collective-permute-start(f32[2,3,208,128]{3,2,1,0:T(8,128)S(1)} %get-tuple-element.200.refs_4_), channel_id=1, source_target_pairs={{0,63},{1,2},{2,1},{3,4},{4,3},{5,6},{6,5},{7,8},{8,7},{9,10},{10,... | collective-permute-start | bytes 1916936 | tf_op jit(solution)/shard_map/ppermute | solution.py:629
  267.9 11.9 %collective-permute-start.26 = (f32[1,128]{1,0:T(1,128)S(1)}, f32[1,128]{1,0:T(1,128)S(1)}, u32[]{:S(2)}, u32[]{:S(2)}) collective-permute-start(f32[1,128]{1,0:T(1,128)S(1)} %get-tuple-element.204.a), channel_id=1, source_target_pairs={{0,1},{1,2},{2,3},{3,0},{4,5},{5,6},{6,7},{7,4},{8,9},{9,10},{10,1... | collective-permute-start | bytes 1544 | tf_op jit(solution)/shard_map/ppermute | solution.py:639
  267.9 11.9 %collective-permute-start.27 = (f32[1,128]{1,0:T(1,128)S(1)}, f32[1,128]{1,0:T(1,128)S(1)}, u32[]{:S(2)}, u32[]{:S(2)}) collective-permute-start(f32[1,128]{1,0:T(1,128)S(1)} %get-tuple-element.204.a), channel_id=1, source_target_pairs={{0,2},{1,3},{2,0},{3,1},{4,6},{5,7},{6,4},{7,5},{8,10},{9,11},{10,... | collective-permute-start | bytes 1544 | tf_op jit(solution)/shard_map/ppermute | solution.py:639
  269.1 12.5 %collective-permute-start.28 = (f32[1,128]{1,0:T(1,128)S(1)}, f32[1,128]{1,0:T(1,128)S(1)}, u32[]{:S(2)}, u32[]{:S(2)}) collective-permute-start(f32[1,128]{1,0:T(1,128)S(1)} %get-tuple-element.204.a), channel_id=1, source_target_pairs={{0,3},{1,0},{2,1},{3,2},{4,7},{5,4},{6,5},{7,6},{8,11},{9,8},{10,9... | collective-permute-start | bytes 1544 | tf_op jit(solution)/shard_map/ppermute | solution.py:639
  281.7 4.0 %collective-permute-start.29 = (f32[1,128]{1,0:T(1,128)S(1)}, f32[1,128]{1,0:T(1,128)S(1)}, u32[]{:S(2)}, u32[]{:S(2)}) collective-permute-start(f32[1,128]{1,0:T(1,128)S(1)} %shard_map.110.a), channel_id=1, source_target_pairs={{0,4},{1,5},{2,6},{3,7},{4,8},{5,9},{6,10},{7,11},{8,12},{9,13},{1... | collective-permute-start | bytes 1544 | tf_op jit(solution)/shard_map/ppermute | solution.py:639
  281.7 4.3 %collective-permute-start.30 = (f32[1,128]{1,0:T(1,128)S(1)}, f32[1,128]{1,0:T(1,128)S(1)}, u32[]{:S(2)}, u32[]{:S(2)}) collective-permute-start(f32[1,128]{1,0:T(1,128)S(1)} %shard_map.110.a), channel_id=1, source_target_pairs={{0,8},{1,9},{2,10},{3,11},{4,12},{5,13},{6,14},{7,15},{8,0},{9,1},... | collective-permute-start | bytes 1544 | tf_op jit(solution)/shard_map/ppermute | solution.py:639
  281.8 4.4 %collective-permute-start.31 = (f32[1,128]{1,0:T(1,128)S(1)}, f32[1,128]{1,0:T(1,128)S(1)}, u32[]{:S(2)}, u32[]{:S(2)}) collective-permute-start(f32[1,128]{1,0:T(1,128)S(1)} %shard_map.110.a), channel_id=1, source_target_pairs={{0,12},{1,13},{2,14},{3,15},{4,0},{5,1},{6,2},{7,3},{8,4},{9,5},{1... | collective-permute-start | bytes 1544 | tf_op jit(solution)/shard_map/ppermute | solution.py:639
  290.7 14.8 %collective-permute-start.35 = (f32[2,3,208,128]{3,2,1,0:T(8,128)S(1)}, f32[2,3,208,128]{3,2,1,0:T(8,128)S(1)}, u32[]{:S(2)}, u32[]{:S(2)}) collective-permute-start(f32[2,3,208,128]{3,2,1,0:T(8,128)S(1)} %get-tuple-element.208.refs_3_), channel_id=1, source_target_pairs={{0,1},{1,0},{2,3},{3,2},{4,5},{5,4},{6,7},{7,6},{8,9},{9,8},{10,11... | collective-permute-start | bytes 1916936 | tf_op jit(solution)/shard_map/ppermute | solution.py:629
  291.1 18.4 %collective-permute-start.36 = (f32[2,3,208,128]{3,2,1,0:T(8,128)S(1)}, f32[2,3,208,128]{3,2,1,0:T(8,128)S(1)}, u32[]{:S(2)}, u32[]{:S(2)}) collective-permute-start(f32[2,3,208,128]{3,2,1,0:T(8,128)S(1)} %get-tuple-element.209.refs_4_), channel_id=1, source_target_pairs={{0,63},{1,2},{2,1},{3,4},{4,3},{5,6},{6,5},{7,8},{8,7},{9,10},{10,... | collective-permute-start | bytes 1916936 | tf_op jit(solution)/shard_map/ppermute | solution.py:629
  293.7 28.6 %collective-permute-start.37 = (f32[2,3,3,192,128]{4,3,2,1,0:T(8,128)S(1)}, f32[2,3,3,192,128]{4,3,2,1,0:T(8,128)S(1)}, u32[]{:S(2)}, u32[]{:S(2)}) collective-permute-start(f32[2,3,3,192,128]{4,3,2,1,0:T(8,128)S(1)} %shard_map.116), channel_id=1, source_target_pairs={{0,64},{64,0},{1,65},{65,1},{2,66},{66,2},{3,67},{67,3},{4,68},{68... | collective-permute-start | bytes 5308424 | tf_op jit(solution)/shard_map/ppermute | solution.py:626
  297.3 25.0 %collective-permute-start.38 = (f32[2,3,3,192,128]{4,3,2,1,0:T(8,128)S(1)}, f32[2,3,3,192,128]{4,3,2,1,0:T(8,128)S(1)}, u32[]{:S(2)}, u32[]{:S(2)}) collective-permute-start(f32[2,3,3,192,128]{4,3,2,1,0:T(8,128)S(1)} %shard_map.117), channel_id=1, source_target_pairs={{0,64},{64,0},{1,65},{65,1},{2,66},{66,2},{3,67},{67,3},{4,68},{68... | collective-permute-start | bytes 5308424 | tf_op jit(solution)/shard_map/ppermute | solution.py:626
  311.6 10.7 %collective-permute-start.39 = (f32[2,3,3,192,128]{4,3,2,1,0:T(8,128)S(1)}, f32[2,3,3,192,128]{4,3,2,1,0:T(8,128)S(1)}, u32[]{:S(2)}, u32[]{:S(2)}) collective-permute-start(f32[2,3,3,192,128]{4,3,2,1,0:T(8,128)S(1)} %shard_map.118), channel_id=1, source_target_pairs={{0,64},{64,0},{1,65},{65,1},{2,66},{66,2},{3,67},{67,3},{4,68},{68... | collective-permute-start | bytes 5308424 | tf_op jit(solution)/shard_map/ppermute | solution.py:626
  315.6 3.6 %collective-permute-start.32 = (f32[1,128]{1,0:T(1,128)S(1)}, f32[1,128]{1,0:T(1,128)S(1)}, u32[]{:S(2)}, u32[]{:S(2)}) collective-permute-start(f32[1,128]{1,0:T(1,128)S(1)} %get-tuple-element.205.a), channel_id=1, source_target_pairs={{0,16},{1,17},{2,18},{3,19},{4,20},{5,21},{6,22},{7,23},{8,24},{9,... | collective-permute-start | bytes 1544 | tf_op jit(solution)/shard_map/ppermute | solution.py:639
  315.6 3.9 %collective-permute-start.33 = (f32[1,128]{1,0:T(1,128)S(1)}, f32[1,128]{1,0:T(1,128)S(1)}, u32[]{:S(2)}, u32[]{:S(2)}) collective-permute-start(f32[1,128]{1,0:T(1,128)S(1)} %get-tuple-element.205.a), channel_id=1, source_target_pairs={{0,32},{1,33},{2,34},{3,35},{4,36},{5,37},{6,38},{7,39},{8,40},{9,... | collective-permute-start | bytes 1544 | tf_op jit(solution)/shard_map/ppermute | solution.py:639
  319.2 2.4 collective-permute-start.34
  (1 other events, 1.0 us)

commit v6 on v5

--- a/solution.py
+++ b/solution.py
@@ -617,10 +617,10 @@
     bands = lax.axis_size("space")
     c_arr = c.reshape(1)
     pos_arr = pos.astype(jnp.int32).reshape(1)
-    even = pos % 2 == 0
+    even = pos % 2 == 1
     flags = jnp.stack([pos > 0, pos < bands - 1, even]).astype(F32)
-    first_pairs = [(i, i ^ 1) for i in range(bands)]
-    second_pairs = [(i, (((i + 1) ^ 1) - 1) % bands) for i in range(bands)]
+    first_pairs = [(i, (((i + 1) ^ 1) - 1) % bands) for i in range(bands)]
+    second_pairs = [(i, i ^ 1) for i in range(bands)]
 
     def swap(x):
         return lax.ppermute(x, "tm", [(0, 1), (1, 0)])

time: 327 us -> 327 us (level)
  waiting for transfers between devices: 192 us -> 181 us
  starting transfers between devices: 65.7 us -> 76.6 us
    ppermute x11, waiting for transfers between devices: 66.2 us -> 12.4 us  [exchange(): lax.ppermute(b, 'space', second_pairs)]
    ppermute x11, waiting for transfers between devices: 102 us -> 149 us  [exchange(): lax.ppermute(a, 'space', first_pairs)]
    ppermute x11, starting transfers between devices: 1.08 us -> 34.1 us  [exchange(): lax.ppermute(a, 'space', first_pairs)]
    ppermute x11, starting transfers between devices: 27.4 us -> 0.97 us  [exchange(): lax.ppermute(b, 'space', second_pairs)]
    ppermute x9, starting transfers between devices: 6.14 us -> 11.7 us  [ring_sum(): got = tuple((lax.ppermute(row, 'space', p) for p in shifts))]
    ppermute x9, waiting for transfers between devices: 17.8 us -> 13.9 us  [ring_sum(): got = tuple((lax.ppermute(row, 'space', p) for p in shifts))]
  transfers between devices with their start and end apart: 41 -> 41, of which waited for: 31 -> 20; matrix products, arithmetic and copies ran while one was open for 1% -> 1% of each run, Pallas kernels for 5% -> 5%
where the time goes in v6:
time: 327 us; the launch traced here: 326 us
  waiting for transfers between devices  181 us (55%)
  starting transfers between devices  76.6 us (23%)
  Pallas kernels  54.3 us (17%)
  local copies, waits for them, and re-layouts  7.2 us (2%)
  other arithmetic  4.12 us (1%)
    ppermute x11, waiting for transfers between devices, exchange(): lax.ppermute(a, 'space', first_pairs)  149 us
    pallas_call x34, Pallas kernels, call(): pl.pallas_call(body, out_shape=outs, in_specs=specs, out_specs=out_specs...  54.3 us
    ppermute x11, starting transfers between devices, exchange(): lax.ppermute(a, 'space', first_pairs)  34.1 us
    ppermute x9, starting transfers between devices, swap(): return lax.ppermute(x, 'tm', [(0, 1), (1, 0)])  18.4 us
    ppermute x9, waiting for transfers between devices, ring_sum(): got = tuple((lax.ppermute(row, 'space', p) for p in shifts))  13.9 us
    ppermute x11, waiting for transfers between devices, exchange(): lax.ppermute(b, 'space', second_pairs)  12.4 us
    ppermute x9, starting transfers between devices, ring_sum(): got = tuple((lax.ppermute(row, 'space', p) for p in shifts))  11.7 us
    all_to_all x1, starting transfers between devices, per_device(): lax.all_to_all(packed, 'space', split_axis=0, concat_axis=0, tiled=True)  11.4 us
  transfers between devices with their start and end apart: 41, of which 20 were waited for; matrix products, arithmetic and copies ran while one was open for 1% of the time, Pallas kernels for 5%

profile of v6, /device:TPU:1, one launch (start us, length us, event | category | flops | bytes accessed | tf_op | source)
XLA Modules:
  0.0 325.7 jit_solution(11941320104678050437)
XLA Ops:
  8.2 11.4 %all-to-all-start = ((f32[64,7,8,128]{3,2,1,0:T(8,128)}), f32[64,7,8,128]{3,2,1,0:T(8,128)}, u32[]{:S(2)}, u32[]{:S(2)}) async-start(f32[64,7,8,128]{3,2,1,0:T(8,128)} %get-tuple-element.108), calls=%async_computation | async-start | bytes 3670016 | tf_op jit(solution)/shard_map/all_to_all | solution.py:665
  25.3 6.3 %collective-permute-start.2 = (f32[2,208,128]{2,1,0:T(8,128)}, f32[2,208,128]{2,1,0:T(8,128)}, u32[]{:S(2)}, u32[]{:S(2)}) collective-permute-start(f32[2,208,128]{2,1,0:T(8,128)} %get-tuple-element.219), channel_id=1, source_target_pairs={{0,63},{1,2},{2,1},{3,4},{4,3},{5,6},{6,5},{7,8},{8,7},{9,10},{10,... | collective-permute-start | bytes 638984 | tf_op jit(solution)/shard_map/ppermute | solution.py:629
  34.3 12.3 %collective-permute-done.1 = f32[2,208,128]{2,1,0:T(8,128)S(1)} collective-permute-done((f32[2,208,128]{2,1,0:T(8,128)}, f32[2,208,128]{2,1,0:T(8,128)S(1)}, u32[]{:S(2)}, u32[]{:S(2)}) %collective-permute-start.1) | collective-permute-done | bytes 213024 | tf_op jit(solution)/shard_map/ppermute | solution.py:629
  46.6 4.4 %collective-permute-done.2 = f32[2,208,128]{2,1,0:T(8,128)} collective-permute-done((f32[2,208,128]{2,1,0:T(8,128)}, f32[2,208,128]{2,1,0:T(8,128)}, u32[]{:S(2)}, u32[]{:S(2)}) %collective-permute-start.2) | collective-permute-done | bytes 213024 | tf_op jit(solution)/shard_map/ppermute | solution.py:629
  52.1 5.9 %shard_map.89 = (f32[18432,128]{1,0:T(8,128)S(1)}, f32[2,3,3,208,128]{4,3,2,1,0:T(8,128)S(1)}, f32[2,3,3,208,128]{4,3,2,1,0:T(8,128)S(1)}) custom-call(s32[1]{0:T(128)} %bitcast.c_ref, f32[3584,128]{1,0:T(8,128)} %bitcast.5.p_ref), custom_call_target="tpu_custom_call" | custom-call | flops 100000000 | bytes 15106052 | tf_op jit(solution)/shard_map/pallas_call | solution.py:24
  58.4 3.6 %collective-permute-done.3.got_ref = f32[2,3,3,208,128]{4,3,2,1,0:T(8,128)S(1)} collective-permute-done((f32[2,3,3,208,128]{4,3,2,1,0:T(8,128)S(1)}, f32[2,3,3,208,128]{4,3,2,1,0:T(8,128)S(1)}, u32[]{:S(2)}, u32[]{:S(2)}) %collective-permute-start.3) | collective-permute-done | bytes 1916960 | tf_op jit(solution)/shard_map/ppermute | solution.py:626
  62.2 2.2 shard_map.91
  64.5 2.7 collective-permute-start.4
  67.2 18.5 %collective-permute-done.4.refs_5_ = f32[2,3,208,128]{3,2,1,0:T(8,128)S(1)} collective-permute-done((f32[2,3,208,128]{3,2,1,0:T(8,128)S(1)}, f32[2,3,208,128]{3,2,1,0:T(8,128)S(1)}, u32[]{:S(2)}, u32[]{:S(2)}) %collective-permute-start.4) | collective-permute-done | bytes 639008 | tf_op jit(solution)/shard_map/ppermute | solution.py:629
  85.7 3.6 %shard_map.92 = (f32[3,3,208,128]{3,2,1,0:T(8,128)S(1)}, f32[3,3,208,128]{3,2,1,0:T(8,128)S(1)}, f32[3,208,128]{2,1,0:T(8,128)S(1)}, f32[2,3,208,128]{3,2,1,0:T(...) custom-call(f32[3]{0:T(128)S(1)} %add_convert_fusion.fl.refs_0_, ...), custom_call_target="tpu_custom_call" | custom-call | flops 100000000 | bytes 12804108 | tf_op jit(solution)/shard_map/pallas_call | solution.py:24
  89.3 2.6 collective-permute-start.6
  94.5 15.0 %collective-permute-done.6.refs_5_ = f32[2,3,208,128]{3,2,1,0:T(8,128)S(1)} collective-permute-done((f32[2,3,208,128]{3,2,1,0:T(8,128)S(1)}, f32[2,3,208,128]{3,2,1,0:T(8,128)S(1)}, u32[]{:S(2)}, u32[]{:S(2)}) %collective-permute-start.6) | collective-permute-done | bytes 639008 | tf_op jit(solution)/shard_map/ppermute | solution.py:629
  109.6 3.1 shard_map.93
  112.7 2.5 collective-permute-start.8
  115.2 16.9 %collective-permute-done.8.rs = f32[2,3,208,128]{3,2,1,0:T(8,128)S(1)} collective-permute-done((f32[2,3,208,128]{3,2,1,0:T(8,128)S(1)}, f32[2,3,208,128]{3,2,1,0:T(8,128)S(1)}, u32[]{:S(2)}, u32[]{:S(2)}) %collective-permute-start.8) | collective-permute-done | bytes 639008 | tf_op jit(solution)/shard_map/ppermute | solution.py:629
  132.1 3.5 %shard_map.94 = (f32[3,3,208,128]{3,2,1,0:T(8,128)S(1)}, f32[3,3,208,128]{3,2,1,0:T(8,128)S(1)}, f32[3,208,128]{2,1,0:T(8,128)S(1)}, f32[2,3,208,128]{3,2,1,0:T(...) custom-call(f32[3]{0:T(128)S(1)} %add_convert_fusion.fl.refs_0_, ...), custom_call_target="tpu_custom_call" | custom-call | flops 100000000 | bytes 12804108 | tf_op jit(solution)/shard_map/pallas_call | solution.py:24
  135.6 2.4 collective-permute-start.10
  138.0 16.1 %collective-permute-done.10.rs = f32[2,3,208,128]{3,2,1,0:T(8,128)S(1)} collective-permute-done((f32[2,3,208,128]{3,2,1,0:T(8,128)S(1)}, f32[2,3,208,128]{3,2,1,0:T(8,128)S(1)}, u32[]{:S(2)}, u32[]{:S(2)}) %collective-permute-start.10) | collective-permute-done | bytes 639008 | tf_op jit(solution)/shard_map/ppermute | solution.py:629
  154.0 2.7 shard_map.95
  156.8 3.9 %collective-permute-start.12 = (f32[3,12,16,128]{3,2,1,0:T(8,128)S(1)}, f32[3,12,16,128]{3,2,1,0:T(8,128)S(1)}, u32[]{:S(2)}, u32[]{:S(2)}) collective-permute-start(f32[3,12,16,128]{3,2,1,0:T(8,128)S(1)} %get-tuple-element.158), channel_id=1, source_target_pairs={{0,64},{64,0},{1,65},{65,1},{2,66},{66,2},{3,67},{67,3},{4,68},{68... | collective-permute-start | bytes 884744 | tf_op jit(solution)/shard_map/ppermute | solution.py:626
  161.9 2.3 shard_map.98
  164.2 2.4 collective-permute-start.14
  167.2 18.1 %collective-permute-done.14.refs_5_ = f32[2,3,208,128]{3,2,1,0:T(8,128)S(1)} collective-permute-done((f32[2,3,208,128]{3,2,1,0:T(8,128)S(1)}, f32[2,3,208,128]{3,2,1,0:T(8,128)S(1)}, u32[]{:S(2)}, u32[]{:S(2)}) %collective-permute-start.14) | collective-permute-done | bytes 639008 | tf_op jit(solution)/shard_map/ppermute | solution.py:629
  185.3 3.6 %shard_map.100 = (f32[3,3,208,128]{3,2,1,0:T(8,128)S(1)}, f32[3,3,208,128]{3,2,1,0:T(8,128)S(1)}, f32[3,208,128]{2,1,0:T(8,128)S(1)}, f32[2,3,208,128]{3,2,1,0:T...) custom-call(f32[3]{0:T(128)S(1)} %add_convert_fusion.fl.refs_0_, ...), custom_call_target="tpu_custom_call" | custom-call | flops 100000000 | bytes 12804108 | tf_op jit(solution)/shard_map/pallas_call | solution.py:24
  188.9 2.4 collective-permute-start.16
  191.3 17.8 %collective-permute-done.16.refs_5_ = f32[2,3,208,128]{3,2,1,0:T(8,128)S(1)} collective-permute-done((f32[2,3,208,128]{3,2,1,0:T(8,128)S(1)}, f32[2,3,208,128]{3,2,1,0:T(8,128)S(1)}, u32[]{:S(2)}, u32[]{:S(2)}) %collective-permute-start.16) | collective-permute-done | bytes 639008 | tf_op jit(solution)/shard_map/ppermute | solution.py:629
  209.1 3.1 shard_map.101
  212.2 2.4 collective-permute-start.18
  214.6 16.8 %collective-permute-done.18.rs = f32[2,3,208,128]{3,2,1,0:T(8,128)S(1)} collective-permute-done((f32[2,3,208,128]{3,2,1,0:T(8,128)S(1)}, f32[2,3,208,128]{3,2,1,0:T(8,128)S(1)}, u32[]{:S(2)}, u32[]{:S(2)}) %collective-permute-start.18) | collective-permute-done | bytes 639008 | tf_op jit(solution)/shard_map/ppermute | solution.py:629
  231.5 3.5 %shard_map.102 = (f32[3,3,208,128]{3,2,1,0:T(8,128)S(1)}, f32[3,3,208,128]{3,2,1,0:T(8,128)S(1)}, f32[3,208,128]{2,1,0:T(8,128)S(1)}, f32[2,3,208,128]{3,2,1,0:T...) custom-call(f32[3]{0:T(128)S(1)} %add_convert_fusion.fl.refs_0_, ...), custom_call_target="tpu_custom_call" | custom-call | flops 100000000 | bytes 12804108 | tf_op jit(solution)/shard_map/pallas_call | solution.py:24
  235.0 2.4 collective-permute-start.20
  237.4 15.9 %collective-permute-done.20.rs = f32[2,3,208,128]{3,2,1,0:T(8,128)S(1)} collective-permute-done((f32[2,3,208,128]{3,2,1,0:T(8,128)S(1)}, f32[2,3,208,128]{3,2,1,0:T(8,128)S(1)}, u32[]{:S(2)}, u32[]{:S(2)}) %collective-permute-start.20) | collective-permute-done | bytes 639008 | tf_op jit(solution)/shard_map/ppermute | solution.py:629
  253.3 2.7 shard_map.103
  256.0 4.1 %collective-permute-start.22 = (f32[3,12,16,128]{3,2,1,0:T(8,128)S(1)}, f32[3,12,16,128]{3,2,1,0:T(8,128)S(1)}, u32[]{:S(2)}, u32[]{:S(2)}) collective-permute-start(f32[3,12,16,128]{3,2,1,0:T(8,128)S(1)} %get-tuple-element.192), channel_id=1, source_target_pairs={{0,64},{64,0},{1,65},{65,1},{2,66},{66,2},{3,67},{67,3},{4,68},{68... | collective-permute-start | bytes 884744 | tf_op jit(solution)/shard_map/ppermute | solution.py:626
  262.5 2.3 shard_map.108
  264.8 2.4 collective-permute-start.24
  268.7 2.4 collective-permute-start.28
  271.1 9.8 %collective-permute-done.26.b = f32[1,128]{1,0:T(1,128)S(1)} collective-permute-done((f32[1,128]{1,0:T(1,128)S(1)}, f32[1,128]{1,0:T(1,128)S(1)}, u32[]{:S(2)}, u32[]{:S(2)}) %collective-permute-start.26) | collective-permute-done | bytes 544 | tf_op jit(solution)/shard_map/ppermute | solution.py:639
  280.8 1.8 collective-permute-done.28.d
  282.8 2.6 collective-permute-start.31
  287.0 3.6 %shard_map.112 = (f32[3,3,208,128]{3,2,1,0:T(8,128)S(1)}, f32[3,3,208,128]{3,2,1,0:T(8,128)S(1)}, f32[3,208,128]{2,1,0:T(8,128)S(1)}, f32[2,3,208,128]{3,2,1,0:T...) custom-call(f32[3]{0:T(128)S(1)} %add_convert_fusion.fl.refs_0_, ...), custom_call_target="tpu_custom_call" | custom-call | flops 100000000 | bytes 12805132 | tf_op jit(solution)/shard_map/pallas_call | solution.py:24
  290.6 5.5 %collective-permute-start.35 = (f32[2,3,208,128]{3,2,1,0:T(8,128)S(1)}, f32[2,3,208,128]{3,2,1,0:T(8,128)S(1)}, u32[]{:S(2)}, u32[]{:S(2)}) collective-permute-start(f32[2,3,208,128]{3,2,1,0:T(8,128)S(1)} %get-tuple-element.208.refs_3_), channel_id=1, source_target_pairs={{0,63},{1,2},{2,1},{3,4},{4,3},{5,6},{6,5},{7,8},{8,7},{9,10},{10,... | collective-permute-start | bytes 1916936 | tf_op jit(solution)/shard_map/ppermute | solution.py:629
  296.2 3.2 collective-permute-start.37
  299.6 9.7 %collective-permute-done.35.refs_5_ = f32[2,3,208,128]{3,2,1,0:T(8,128)S(1)} collective-permute-done((f32[2,3,208,128]{3,2,1,0:T(8,128)S(1)}, f32[2,3,208,128]{3,2,1,0:T(8,128)S(1)}, u32[]{:S(2)}, u32[]{:S(2)}) %collective-permute-start.35) | collective-permute-done | bytes 639008 | tf_op jit(solution)/shard_map/ppermute | solution.py:629
  309.3 2.0 shard_map.115
  311.5 3.8 %collective-permute-start.39 = (f32[2,3,3,192,128]{4,3,2,1,0:T(8,128)S(1)}, f32[2,3,3,192,128]{4,3,2,1,0:T(8,128)S(1)}, u32[]{:S(2)}, u32[]{:S(2)}) collective-permute-start(f32[2,3,3,192,128]{4,3,2,1,0:T(8,128)S(1)} %shard_map.118), channel_id=1, source_target_pairs={{0,64},{64,0},{1,65},{65,1},{2,66},{66,2},{3,67},{67,3},{4,68},{68... | collective-permute-start | bytes 5308424 | tf_op jit(solution)/shard_map/ppermute | solution.py:626
  315.3 3.9 %collective-permute-start.33 = (f32[1,128]{1,0:T(1,128)S(1)}, f32[1,128]{1,0:T(1,128)S(1)}, u32[]{:S(2)}, u32[]{:S(2)}) collective-permute-start(f32[1,128]{1,0:T(1,128)S(1)} %get-tuple-element.205.a), channel_id=1, source_target_pairs={{0,32},{1,33},{2,34},{3,35},{4,36},{5,37},{6,38},{7,39},{8,40},{9,... | collective-permute-start | bytes 1544 | tf_op jit(solution)/shard_map/ppermute | solution.py:639
  322.4 3.2 shard_map.119
  (97 shorter events, 29.9 us)
Async XLA Ops:
  0.6 4.7 %copy-start.4 = (bf16[2,1,2,3,384,128]{5,4,3,2,1,0:T(8,128)(2,1)S(1)}, bf16[2,1,2,3,384,128]{5,4,3,2,1,0:T(8,128)(2,1)}, u32[]{:S(2)}) copy-start(bf16[2,1,2,3,384,128]{5,4,3,2,1,0:T(8,128)(2,1)} %param.7) | copy-start | bytes 3538948
  1.7 1.1 copy-start.5
  2.8 1.1 copy-start.6
  3.9 1.4 copy-start.7
  5.7 1.0 copy-start
  6.8 12.9 %collective-permute-start = (f32[2,2,3,208,128]{4,3,2,1,0:T(8,128)S(1)}, f32[2,2,3,208,128]{4,3,2,1,0:T(8,128)S(1)}, u32[]{:S(2)}, u32[]{:S(2)}) collective-permute-start(f32[2,2,3,208,128]{4,3,2,1,0:T(8,128)S(1)} %get-tuple-element.111), channel_id=1, source_target_pairs={{0,64},{64,0},{1,65},{65,1},{2,66},{66,2},{3,67},{67,3},{4,68},{68... | collective-permute-start | bytes 3833864 | tf_op jit(solution)/shard_map/ppermute | solution.py:626
  8.2 43.9 %all-to-all-start = ((f32[64,7,8,128]{3,2,1,0:T(8,128)}), f32[64,7,8,128]{3,2,1,0:T(8,128)}, u32[]{:S(2)}, u32[]{:S(2)}) async-start(f32[64,7,8,128]{3,2,1,0:T(8,128)} %get-tuple-element.108), calls=%async_computation | async-start | bytes 3670016 | tf_op jit(solution)/shard_map/all_to_all | solution.py:665
  20.7 1.3 copy-start.1
  22.0 1.3 copy-start.3
  24.4 22.3 %collective-permute-start.1 = (f32[2,208,128]{2,1,0:T(8,128)}, f32[2,208,128]{2,1,0:T(8,128)S(1)}, u32[]{:S(2)}, u32[]{:S(2)}) collective-permute-start(f32[2,208,128]{2,1,0:T(8,128)} %get-tuple-element.218), channel_id=1, source_target_pairs={{0,1},{1,0},{2,3},{3,2},{4,5},{5,4},{6,7},{7,6},{8,9},{9,8},{10,11... | collective-permute-start | bytes 638984 | tf_op jit(solution)/shard_map/ppermute | solution.py:629
  25.3 25.8 %collective-permute-start.2 = (f32[2,208,128]{2,1,0:T(8,128)}, f32[2,208,128]{2,1,0:T(8,128)}, u32[]{:S(2)}, u32[]{:S(2)}) collective-permute-start(f32[2,208,128]{2,1,0:T(8,128)} %get-tuple-element.219), channel_id=1, source_target_pairs={{0,63},{1,2},{2,1},{3,4},{4,3},{5,6},{6,5},{7,8},{8,7},{9,10},{10,... | collective-permute-start | bytes 638984 | tf_op jit(solution)/shard_map/ppermute | solution.py:629
  58.0 4.0 %collective-permute-start.3 = (f32[2,3,3,208,128]{4,3,2,1,0:T(8,128)S(1)}, f32[2,3,3,208,128]{4,3,2,1,0:T(8,128)S(1)}, u32[]{:S(2)}, u32[]{:S(2)}) collective-permute-start(f32[2,3,3,208,128]{4,3,2,1,0:T(8,128)S(1)} %get-tuple-element.122), channel_id=1, source_target_pairs={{0,64},{64,0},{1,65},{65,1},{2,66},{66,2},{3,67},{67,3},{4,68},{68... | collective-permute-start | bytes 5750792 | tf_op jit(solution)/shard_map/ppermute | solution.py:626
  64.5 21.2 %collective-permute-start.4 = (f32[2,3,208,128]{3,2,1,0:T(8,128)S(1)}, f32[2,3,208,128]{3,2,1,0:T(8,128)S(1)}, u32[]{:S(2)}, u32[]{:S(2)}) collective-permute-start(f32[2,3,208,128]{3,2,1,0:T(8,128)S(1)} %get-tuple-element.130.refs_3_), channel_id=1, source_target_pairs={{0,63},{1,2},{2,1},{3,4},{4,3},{5,6},{6,5},{7,8},{8,7},{9,10},{10,... | collective-permute-start | bytes 1916936 | tf_op jit(solution)/shard_map/ppermute | solution.py:629
  67.2 18.5 %collective-permute-start.5 = (f32[2,3,208,128]{3,2,1,0:T(8,128)S(1)}, f32[2,3,208,128]{3,2,1,0:T(8,128)S(1)}, u32[]{:S(2)}, u32[]{:S(2)}) collective-permute-start(f32[2,3,208,128]{3,2,1,0:T(8,128)S(1)} %get-tuple-element.131.refs_4_), channel_id=1, source_target_pairs={{0,1},{1,0},{2,3},{3,2},{4,5},{5,4},{6,7},{7,6},{8,9},{9,8},{10,11... | collective-permute-start | bytes 1916936 | tf_op jit(solution)/shard_map/ppermute | solution.py:629
  89.3 20.3 %collective-permute-start.6 = (f32[2,3,208,128]{3,2,1,0:T(8,128)S(1)}, f32[2,3,208,128]{3,2,1,0:T(8,128)S(1)}, u32[]{:S(2)}, u32[]{:S(2)}) collective-permute-start(f32[2,3,208,128]{3,2,1,0:T(8,128)S(1)} %get-tuple-element.139.refs_3_), channel_id=1, source_target_pairs={{0,63},{1,2},{2,1},{3,4},{4,3},{5,6},{6,5},{7,8},{8,7},{9,10},{10,... | collective-permute-start | bytes 1916936 | tf_op jit(solution)/shard_map/ppermute | solution.py:629
  91.9 17.7 %collective-permute-start.7 = (f32[2,3,208,128]{3,2,1,0:T(8,128)S(1)}, f32[2,3,208,128]{3,2,1,0:T(8,128)S(1)}, u32[]{:S(2)}, u32[]{:S(2)}) collective-permute-start(f32[2,3,208,128]{3,2,1,0:T(8,128)S(1)} %get-tuple-element.140.refs_4_), channel_id=1, source_target_pairs={{0,1},{1,0},{2,3},{3,2},{4,5},{5,4},{6,7},{7,6},{8,9},{9,8},{10,11... | collective-permute-start | bytes 1916936 | tf_op jit(solution)/shard_map/ppermute | solution.py:629
  93.1 67.6 %collective-permute-start.13 = (f32[2,3,3,208,128]{4,3,2,1,0:T(8,128)S(1)}, f32[2,3,3,208,128]{4,3,2,1,0:T(8,128)S(1)}, u32[]{:S(2)}, u32[]{:S(2)}) collective-permute-start(f32[2,3,3,208,128]{4,3,2,1,0:T(8,128)S(1)} %get-tuple-element.161), channel_id=1, source_target_pairs={{0,64},{64,0},{1,65},{65,1},{2,66},{66,2},{3,67},{67,3},{4,68},{68... | collective-permute-start | bytes 5750792 | tf_op jit(solution)/shard_map/ppermute | solution.py:626
  112.7 19.4 %collective-permute-start.8 = (f32[2,3,208,128]{3,2,1,0:T(8,128)S(1)}, f32[2,3,208,128]{3,2,1,0:T(8,128)S(1)}, u32[]{:S(2)}, u32[]{:S(2)}) collective-permute-start(f32[2,3,208,128]{3,2,1,0:T(8,128)S(1)} %get-tuple-element.145.ss), channel_id=1, source_target_pairs={{0,63},{1,2},{2,1},{3,4},{4,3},{5,6},{6,5},{7,8},{8,7},{9,10},{10,... | collective-permute-start | bytes 1916936 | tf_op jit(solution)/shard_map/ppermute | solution.py:629
  115.2 16.9 %collective-permute-start.9 = (f32[2,3,208,128]{3,2,1,0:T(8,128)S(1)}, f32[2,3,208,128]{3,2,1,0:T(8,128)S(1)}, u32[]{:S(2)}, u32[]{:S(2)}) collective-permute-start(f32[2,3,208,128]{3,2,1,0:T(8,128)S(1)} %get-tuple-element.146.sn), channel_id=1, source_target_pairs={{0,1},{1,0},{2,3},{3,2},{4,5},{5,4},{6,7},{7,6},{8,9},{9,8},{10,11... | collective-permute-start | bytes 1916936 | tf_op jit(solution)/shard_map/ppermute | solution.py:629
  135.6 18.4 %collective-permute-start.10 = (f32[2,3,208,128]{3,2,1,0:T(8,128)S(1)}, f32[2,3,208,128]{3,2,1,0:T(8,128)S(1)}, u32[]{:S(2)}, u32[]{:S(2)}) collective-permute-start(f32[2,3,208,128]{3,2,1,0:T(8,128)S(1)} %get-tuple-element.152.ss), channel_id=1, source_target_pairs={{0,63},{1,2},{2,1},{3,4},{4,3},{5,6},{6,5},{7,8},{8,7},{9,10},{10,... | collective-permute-start | bytes 1916936 | tf_op jit(solution)/shard_map/ppermute | solution.py:629
  138.0 16.1 %collective-permute-start.11 = (f32[2,3,208,128]{3,2,1,0:T(8,128)S(1)}, f32[2,3,208,128]{3,2,1,0:T(8,128)S(1)}, u32[]{:S(2)}, u32[]{:S(2)}) collective-permute-start(f32[2,3,208,128]{3,2,1,0:T(8,128)S(1)} %get-tuple-element.153.sn), channel_id=1, source_target_pairs={{0,1},{1,0},{2,3},{3,2},{4,5},{5,4},{6,7},{7,6},{8,9},{9,8},{10,11... | collective-permute-start | bytes 1916936 | tf_op jit(solution)/shard_map/ppermute | solution.py:629
  156.8 5.1 %collective-permute-start.12 = (f32[3,12,16,128]{3,2,1,0:T(8,128)S(1)}, f32[3,12,16,128]{3,2,1,0:T(8,128)S(1)}, u32[]{:S(2)}, u32[]{:S(2)}) collective-permute-start(f32[3,12,16,128]{3,2,1,0:T(8,128)S(1)} %get-tuple-element.158), channel_id=1, source_target_pairs={{0,64},{64,0},{1,65},{65,1},{2,66},{66,2},{3,67},{67,3},{4,68},{68... | collective-permute-start | bytes 884744 | tf_op jit(solution)/shard_map/ppermute | solution.py:626
  164.2 21.1 %collective-permute-start.14 = (f32[2,3,208,128]{3,2,1,0:T(8,128)S(1)}, f32[2,3,208,128]{3,2,1,0:T(8,128)S(1)}, u32[]{:S(2)}, u32[]{:S(2)}) collective-permute-start(f32[2,3,208,128]{3,2,1,0:T(8,128)S(1)} %get-tuple-element.166.refs_3_), channel_id=1, source_target_pairs={{0,63},{1,2},{2,1},{3,4},{4,3},{5,6},{6,5},{7,8},{8,7},{9,10},{10,... | collective-permute-start | bytes 1916936 | tf_op jit(solution)/shard_map/ppermute | solution.py:629
  166.6 18.7 %collective-permute-start.15 = (f32[2,3,208,128]{3,2,1,0:T(8,128)S(1)}, f32[2,3,208,128]{3,2,1,0:T(8,128)S(1)}, u32[]{:S(2)}, u32[]{:S(2)}) collective-permute-start(f32[2,3,208,128]{3,2,1,0:T(8,128)S(1)} %get-tuple-element.167.refs_4_), channel_id=1, source_target_pairs={{0,1},{1,0},{2,3},{3,2},{4,5},{5,4},{6,7},{7,6},{8,9},{9,8},{10,11... | collective-permute-start | bytes 1916936 | tf_op jit(solution)/shard_map/ppermute | solution.py:629
  188.9 20.2 %collective-permute-start.16 = (f32[2,3,208,128]{3,2,1,0:T(8,128)S(1)}, f32[2,3,208,128]{3,2,1,0:T(8,128)S(1)}, u32[]{:S(2)}, u32[]{:S(2)}) collective-permute-start(f32[2,3,208,128]{3,2,1,0:T(8,128)S(1)} %get-tuple-element.175.refs_3_), channel_id=1, source_target_pairs={{0,63},{1,2},{2,1},{3,4},{4,3},{5,6},{6,5},{7,8},{8,7},{9,10},{10,... | collective-permute-start | bytes 1916936 | tf_op jit(solution)/shard_map/ppermute | solution.py:629
  191.3 17.8 %collective-permute-start.17 = (f32[2,3,208,128]{3,2,1,0:T(8,128)S(1)}, f32[2,3,208,128]{3,2,1,0:T(8,128)S(1)}, u32[]{:S(2)}, u32[]{:S(2)}) collective-permute-start(f32[2,3,208,128]{3,2,1,0:T(8,128)S(1)} %get-tuple-element.176.refs_4_), channel_id=1, source_target_pairs={{0,1},{1,0},{2,3},{3,2},{4,5},{5,4},{6,7},{7,6},{8,9},{9,8},{10,11... | collective-permute-start | bytes 1916936 | tf_op jit(solution)/shard_map/ppermute | solution.py:629
  212.2 19.2 %collective-permute-start.18 = (f32[2,3,208,128]{3,2,1,0:T(8,128)S(1)}, f32[2,3,208,128]{3,2,1,0:T(8,128)S(1)}, u32[]{:S(2)}, u32[]{:S(2)}) collective-permute-start(f32[2,3,208,128]{3,2,1,0:T(8,128)S(1)} %get-tuple-element.179.ss), channel_id=1, source_target_pairs={{0,63},{1,2},{2,1},{3,4},{4,3},{5,6},{6,5},{7,8},{8,7},{9,10},{10,... | collective-permute-start | bytes 1916936 | tf_op jit(solution)/shard_map/ppermute | solution.py:629
  214.6 16.8 %collective-permute-start.19 = (f32[2,3,208,128]{3,2,1,0:T(8,128)S(1)}, f32[2,3,208,128]{3,2,1,0:T(8,128)S(1)}, u32[]{:S(2)}, u32[]{:S(2)}) collective-permute-start(f32[2,3,208,128]{3,2,1,0:T(8,128)S(1)} %get-tuple-element.180.sn), channel_id=1, source_target_pairs={{0,1},{1,0},{2,3},{3,2},{4,5},{5,4},{6,7},{7,6},{8,9},{9,8},{10,11... | collective-permute-start | bytes 1916936 | tf_op jit(solution)/shard_map/ppermute | solution.py:629
  235.0 18.3 %collective-permute-start.20 = (f32[2,3,208,128]{3,2,1,0:T(8,128)S(1)}, f32[2,3,208,128]{3,2,1,0:T(8,128)S(1)}, u32[]{:S(2)}, u32[]{:S(2)}) collective-permute-start(f32[2,3,208,128]{3,2,1,0:T(8,128)S(1)} %get-tuple-element.186.ss), channel_id=1, source_target_pairs={{0,63},{1,2},{2,1},{3,4},{4,3},{5,6},{6,5},{7,8},{8,7},{9,10},{10,... | collective-permute-start | bytes 1916936 | tf_op jit(solution)/shard_map/ppermute | solution.py:629
  237.4 15.9 %collective-permute-start.21 = (f32[2,3,208,128]{3,2,1,0:T(8,128)S(1)}, f32[2,3,208,128]{3,2,1,0:T(8,128)S(1)}, u32[]{:S(2)}, u32[]{:S(2)}) collective-permute-start(f32[2,3,208,128]{3,2,1,0:T(8,128)S(1)} %get-tuple-element.187.sn), channel_id=1, source_target_pairs={{0,1},{1,0},{2,3},{3,2},{4,5},{5,4},{6,7},{7,6},{8,9},{9,8},{10,11... | collective-permute-start | bytes 1916936 | tf_op jit(solution)/shard_map/ppermute | solution.py:629
  256.0 6.5 %collective-permute-start.22 = (f32[3,12,16,128]{3,2,1,0:T(8,128)S(1)}, f32[3,12,16,128]{3,2,1,0:T(8,128)S(1)}, u32[]{:S(2)}, u32[]{:S(2)}) collective-permute-start(f32[3,12,16,128]{3,2,1,0:T(8,128)S(1)} %get-tuple-element.192), channel_id=1, source_target_pairs={{0,64},{64,0},{1,65},{65,1},{2,66},{66,2},{3,67},{67,3},{4,68},{68... | collective-permute-start | bytes 884744 | tf_op jit(solution)/shard_map/ppermute | solution.py:626
  261.3 1.2 collective-permute-start.23
  264.8 22.2 %collective-permute-start.24 = (f32[2,3,208,128]{3,2,1,0:T(8,128)S(1)}, f32[2,3,208,128]{3,2,1,0:T(8,128)S(1)}, u32[]{:S(2)}, u32[]{:S(2)}) collective-permute-start(f32[2,3,208,128]{3,2,1,0:T(8,128)S(1)} %get-tuple-element.199.refs_3_), channel_id=1, source_target_pairs={{0,63},{1,2},{2,1},{3,4},{4,3},{5,6},{6,5},{7,8},{8,7},{9,10},{10,... | collective-permute-start | bytes 1916936 | tf_op jit(solution)/shard_map/ppermute | solution.py:629
  267.2 19.8 %collective-permute-start.25 = (f32[2,3,208,128]{3,2,1,0:T(8,128)S(1)}, f32[2,3,208,128]{3,2,1,0:T(8,128)S(1)}, u32[]{:S(2)}, u32[]{:S(2)}) collective-permute-start(f32[2,3,208,128]{3,2,1,0:T(8,128)S(1)} %get-tuple-element.200.refs_4_), channel_id=1, source_target_pairs={{0,1},{1,0},{2,3},{3,2},{4,5},{5,4},{6,7},{7,6},{8,9},{9,8},{10,11... | collective-permute-start | bytes 1916936 | tf_op jit(solution)/shard_map/ppermute | solution.py:629
  267.2 13.6 %collective-permute-start.26 = (f32[1,128]{1,0:T(1,128)S(1)}, f32[1,128]{1,0:T(1,128)S(1)}, u32[]{:S(2)}, u32[]{:S(2)}) collective-permute-start(f32[1,128]{1,0:T(1,128)S(1)} %get-tuple-element.204.a), channel_id=1, source_target_pairs={{0,1},{1,2},{2,3},{3,0},{4,5},{5,6},{6,7},{7,4},{8,9},{9,10},{10,1... | collective-permute-start | bytes 1544 | tf_op jit(solution)/shard_map/ppermute | solution.py:639
  268.7 12.2 %collective-permute-start.27 = (f32[1,128]{1,0:T(1,128)S(1)}, f32[1,128]{1,0:T(1,128)S(1)}, u32[]{:S(2)}, u32[]{:S(2)}) collective-permute-start(f32[1,128]{1,0:T(1,128)S(1)} %get-tuple-element.204.a), channel_id=1, source_target_pairs={{0,2},{1,3},{2,0},{3,1},{4,6},{5,7},{6,4},{7,5},{8,10},{9,11},{10,... | collective-permute-start | bytes 1544 | tf_op jit(solution)/shard_map/ppermute | solution.py:639
  268.7 14.0 %collective-permute-start.28 = (f32[1,128]{1,0:T(1,128)S(1)}, f32[1,128]{1,0:T(1,128)S(1)}, u32[]{:S(2)}, u32[]{:S(2)}) collective-permute-start(f32[1,128]{1,0:T(1,128)S(1)} %get-tuple-element.204.a), channel_id=1, source_target_pairs={{0,3},{1,0},{2,1},{3,2},{4,7},{5,4},{6,5},{7,6},{8,11},{9,8},{10,9... | collective-permute-start | bytes 1544 | tf_op jit(solution)/shard_map/ppermute | solution.py:639
  282.7 4.0 %collective-permute-start.29 = (f32[1,128]{1,0:T(1,128)S(1)}, f32[1,128]{1,0:T(1,128)S(1)}, u32[]{:S(2)}, u32[]{:S(2)}) collective-permute-start(f32[1,128]{1,0:T(1,128)S(1)} %shard_map.110.a), channel_id=1, source_target_pairs={{0,4},{1,5},{2,6},{3,7},{4,8},{5,9},{6,10},{7,11},{8,12},{9,13},{1... | collective-permute-start | bytes 1544 | tf_op jit(solution)/shard_map/ppermute | solution.py:639
  282.8 4.0 %collective-permute-start.30 = (f32[1,128]{1,0:T(1,128)S(1)}, f32[1,128]{1,0:T(1,128)S(1)}, u32[]{:S(2)}, u32[]{:S(2)}) collective-permute-start(f32[1,128]{1,0:T(1,128)S(1)} %shard_map.110.a), channel_id=1, source_target_pairs={{0,8},{1,9},{2,10},{3,11},{4,12},{5,13},{6,14},{7,15},{8,0},{9,1},... | collective-permute-start | bytes 1544 | tf_op jit(solution)/shard_map/ppermute | solution.py:639
  282.8 4.1 %collective-permute-start.31 = (f32[1,128]{1,0:T(1,128)S(1)}, f32[1,128]{1,0:T(1,128)S(1)}, u32[]{:S(2)}, u32[]{:S(2)}) collective-permute-start(f32[1,128]{1,0:T(1,128)S(1)} %shard_map.110.a), channel_id=1, source_target_pairs={{0,12},{1,13},{2,14},{3,15},{4,0},{5,1},{6,2},{7,3},{8,4},{9,5},{1... | collective-permute-start | bytes 1544 | tf_op jit(solution)/shard_map/ppermute | solution.py:639
  290.6 18.8 %collective-permute-start.35 = (f32[2,3,208,128]{3,2,1,0:T(8,128)S(1)}, f32[2,3,208,128]{3,2,1,0:T(8,128)S(1)}, u32[]{:S(2)}, u32[]{:S(2)}) collective-permute-start(f32[2,3,208,128]{3,2,1,0:T(8,128)S(1)} %get-tuple-element.208.refs_3_), channel_id=1, source_target_pairs={{0,63},{1,2},{2,1},{3,4},{4,3},{5,6},{6,5},{7,8},{8,7},{9,10},{10,... | collective-permute-start | bytes 1916936 | tf_op jit(solution)/shard_map/ppermute | solution.py:629
  296.0 13.3 %collective-permute-start.36 = (f32[2,3,208,128]{3,2,1,0:T(8,128)S(1)}, f32[2,3,208,128]{3,2,1,0:T(8,128)S(1)}, u32[]{:S(2)}, u32[]{:S(2)}) collective-permute-start(f32[2,3,208,128]{3,2,1,0:T(8,128)S(1)} %get-tuple-element.209.refs_4_), channel_id=1, source_target_pairs={{0,1},{1,0},{2,3},{3,2},{4,5},{5,4},{6,7},{7,6},{8,9},{9,8},{10,11... | collective-permute-start | bytes 1916936 | tf_op jit(solution)/shard_map/ppermute | solution.py:629
  296.2 26.2 %collective-permute-start.37 = (f32[2,3,3,192,128]{4,3,2,1,0:T(8,128)S(1)}, f32[2,3,3,192,128]{4,3,2,1,0:T(8,128)S(1)}, u32[]{:S(2)}, u32[]{:S(2)}) collective-permute-start(f32[2,3,3,192,128]{4,3,2,1,0:T(8,128)S(1)} %shard_map.116), channel_id=1, source_target_pairs={{0,64},{64,0},{1,65},{65,1},{2,66},{66,2},{3,67},{67,3},{4,68},{68... | collective-permute-start | bytes 5308424 | tf_op jit(solution)/shard_map/ppermute | solution.py:626
  299.5 22.9 %collective-permute-start.38 = (f32[2,3,3,192,128]{4,3,2,1,0:T(8,128)S(1)}, f32[2,3,3,192,128]{4,3,2,1,0:T(8,128)S(1)}, u32[]{:S(2)}, u32[]{:S(2)}) collective-permute-start(f32[2,3,3,192,128]{4,3,2,1,0:T(8,128)S(1)} %shard_map.117), channel_id=1, source_target_pairs={{0,64},{64,0},{1,65},{65,1},{2,66},{66,2},{3,67},{67,3},{4,68},{68... | collective-permute-start | bytes 5308424 | tf_op jit(solution)/shard_map/ppermute | solution.py:626
  311.5 10.9 %collective-permute-start.39 = (f32[2,3,3,192,128]{4,3,2,1,0:T(8,128)S(1)}, f32[2,3,3,192,128]{4,3,2,1,0:T(8,128)S(1)}, u32[]{:S(2)}, u32[]{:S(2)}) collective-permute-start(f32[2,3,3,192,128]{4,3,2,1,0:T(8,128)S(1)} %shard_map.118), channel_id=1, source_target_pairs={{0,64},{64,0},{1,65},{65,1},{2,66},{66,2},{3,67},{67,3},{4,68},{68... | collective-permute-start | bytes 5308424 | tf_op jit(solution)/shard_map/ppermute | solution.py:626
  315.3 3.9 %collective-permute-start.32 = (f32[1,128]{1,0:T(1,128)S(1)}, f32[1,128]{1,0:T(1,128)S(1)}, u32[]{:S(2)}, u32[]{:S(2)}) collective-permute-start(f32[1,128]{1,0:T(1,128)S(1)} %get-tuple-element.205.a), channel_id=1, source_target_pairs={{0,16},{1,17},{2,18},{3,19},{4,20},{5,21},{6,22},{7,23},{8,24},{9,... | collective-permute-start | bytes 1544 | tf_op jit(solution)/shard_map/ppermute | solution.py:639
  315.3 5.1 %collective-permute-start.33 = (f32[1,128]{1,0:T(1,128)S(1)}, f32[1,128]{1,0:T(1,128)S(1)}, u32[]{:S(2)}, u32[]{:S(2)}) collective-permute-start(f32[1,128]{1,0:T(1,128)S(1)} %get-tuple-element.205.a), channel_id=1, source_target_pairs={{0,32},{1,33},{2,34},{3,35},{4,36},{5,37},{6,38},{7,39},{8,40},{9,... | collective-permute-start | bytes 1544 | tf_op jit(solution)/shard_map/ppermute | solution.py:639
  319.3 2.4 collective-permute-start.34
  (1 other events, 1.0 us)
